TPU v7x, 32 devices: a whole 2x2x4 slice. The times are simulated.
32 devices in a mesh: ctx: 8 (over y, x, core), wt: 4 (over z).
Axes of the slice: x: 2, y: 2, z: 4, core: 2. Of those that a mesh axis runs over, the one named last changes fastest.
Arguments:
- hidden_in: bfloat16 [4, 1024, 2048], P('wt', 'ctx'), may hold values from -6 to 6
- doc_lengths: int32 [4, 2], P('wt'), may hold values from 1 to 768, 1024 in all within a row
- routes: int32 [4, 1024, 8], P('wt', 'ctx'), may hold values from 0 to 31, all different within a row; in each aligned block of 128 rows (0 to 127, 128 to 255, ..., all dimensions but the last counted through in order) at most 64 rows name the same one
- gain_attn: float32 [2048], replicated, may hold values from 0.1 to 1.9
- w_query: bfloat16 [2048, 4096], P(('ctx', 'wt')), may hold values from -0.125 to 0.125
- key_weight: bfloat16 [2048, 512], P(('ctx', 'wt')), may hold values from -0.125 to 0.125
- value_weight: bfloat16 [2048, 512], P(('ctx', 'wt')), may hold values from -0.125 to 0.125
- gain_query: float32 [128], replicated, may hold values from 0.1 to 1.9
- gain_key: float32 [128], replicated, may hold values from 0.1 to 1.9
- w_out: bfloat16 [4096, 2048], P(('ctx', 'wt')), may hold values from -1.5 to 1.5
- gain_moe: float32 [2048], replicated, may hold values from 0.1 to 1.9
- w_router: bfloat16 [2048, 32], P(('ctx', 'wt')), may hold values from -0.0625 to 0.0625
- expert_gate: bfloat16 [32, 2048, 768], P(('ctx', 'wt')), may hold values from -0.125 to 0.125
- expert_up: bfloat16 [32, 2048, 768], P(('ctx', 'wt')), may hold values from -0.125 to 0.125
- expert_down: bfloat16 [32, 768, 2048], P(('ctx', 'wt')), may hold values from -0.625 to 0.625
- out_grad: bfloat16 [4, 1024, 2048], P('wt', 'ctx'), may hold values from -6 to 6
Outputs:
- hidden_out: float32 [4, 1024, 2048], P('wt', 'ctx')
- grad_in: float32 [4, 1024, 2048], P('wt', 'ctx')
- grad_gain_attn: float32 [2048], replicated
- grad_w_query: float32 [2048, 4096], P(('ctx', 'wt'))
- grad_w_key: float32 [2048, 512], P(('ctx', 'wt'))
- grad_w_value: float32 [2048, 512], P(('ctx', 'wt'))
- grad_gain_query: float32 [128], replicated
- grad_gain_key: float32 [128], replicated
- grad_w_out: float32 [4096, 2048], P(('ctx', 'wt'))
- grad_gain_moe: float32 [2048], replicated
- grad_w_router: float32 [2048, 32], P(('ctx', 'wt'))
- grad_expert_gate: float32 [32, 2048, 768], P(('ctx', 'wt'))
- grad_expert_up: float32 [32, 2048, 768], P(('ctx', 'wt'))
- grad_expert_down: float32 [32, 768, 2048], P(('ctx', 'wt'))
Inputs may be any that keep to these rules, and one draw needn't show every extreme that they name: `doc_lengths`: the 2 lengths of a stream sum to 1024; the longest is at most 768. `routes`: A token names 8 different experts. Within the rows of one device, no expert is named more than 64 times; on some device an expert is named exactly 64 times.
All inputs are finite; a program needn't handle non-finite values.
Results may differ from a plain program's by a relative error of at most 0.018.
Values may be sent and summed in bfloat16 or wider, within the bound.
A program may use at most 256 MiB of HBM per device.

v0:
```python
import math

import jax
import jax.numpy as jnp
from jax import lax
from jax.sharding import PartitionSpec as P

EPS = 1e-06
THETA = 1000000.0
MASKED = -1e30


def entering(value, axis, combine, identity):
    size, position = (lax.axis_size(axis), lax.axis_index(axis))
    everything = lax.all_gather(value, axis)
    start = jnp.broadcast_to(jnp.asarray(identity, value.dtype), value.shape)

    def step(k, before):
        reached = k < position
        new = combine(before, everything[k])
        return jnp.where(reached, new, before)

    return lax.fori_loop(0, size, step, start)


def norm_rows(value_rows, gain_vec):
    return (
        value_rows
        * lax.rsqrt(jnp.mean(value_rows * value_rows, axis=-1, keepdims=True) + EPS)
        * gain_vec
    )


def norm_back(value_rows, gain_vec, upstream):
    factor = lax.rsqrt(jnp.mean(value_rows * value_rows, axis=-1, keepdims=True) + EPS)
    normalized_input = value_rows * factor
    weighted = upstream * gain_vec
    inner_mean = jnp.mean(weighted * normalized_input, axis=-1, keepdims=True)
    return (factor * (weighted - normalized_input * inner_mean), upstream * normalized_input)


def rotary_tables(positions, head_dim):
    half_dim = head_dim // 2
    frequency = jnp.exp(
        jnp.arange(half_dim, dtype=jnp.float32) * (-2.0 * math.log(THETA) / head_dim)
    )
    angles = positions.astype(jnp.float32)[:, None] * frequency[None, :]
    angles = jnp.concatenate([angles, angles], axis=1)
    return (jnp.cos(angles)[:, None, :], jnp.sin(angles)[:, None, :])


def rotate(value_rows, cosine_table, sine_table):
    half_dim = value_rows.shape[-1] // 2
    turned = jnp.concatenate([-value_rows[..., half_dim:], value_rows[..., :half_dim]], axis=-1)
    return value_rows * cosine_table + turned * sine_table


def matmul(left_side, right_side):
    return jnp.dot(left_side, right_side, preferred_element_type=jnp.float32)


def contract_rows(left_side, right_side):
    return lax.dot_general(
        left_side, right_side, (((0,), (0,)), ((), ())), preferred_element_type=jnp.float32
    )


def contract_cols(left_side, right_side):
    return lax.dot_general(
        left_side, right_side, (((1,), (1,)), ((), ())), preferred_element_type=jnp.float32
    )


def add_counts(earlier, later):
    return earlier + later


def on_device(
    hidden_in,
    doc_lengths,
    routes,
    gain_attn,
    w_query,
    key_weight,
    value_weight,
    gain_query,
    gain_key,
    w_out,
    gain_moe,
    w_router,
    expert_gate,
    expert_up,
    expert_down,
    out_grad,
):
    block_rows = 512
    tokens = hidden_in.shape[1]
    model_width = hidden_in.shape[2]
    ctx_size = lax.axis_size("ctx")
    wt_size = lax.axis_size("wt")
    devices = ctx_size * wt_size
    seq_len = tokens * ctx_size
    head_dim = gain_query.shape[0]
    q_width = w_query.shape[1]
    kv_width = key_weight.shape[1]
    query_heads = q_width // head_dim
    key_heads = kv_width // head_dim
    group_width = query_heads // key_heads
    expert_count = w_router.shape[1]
    top_count = routes.shape[2]
    local_count = expert_gate.shape[0]
    send_slots = 2 * tokens * top_count // expert_count
    capacity = tokens * top_count // (local_count * wt_size)
    cap_rows = wt_size * capacity
    score_scale = head_dim ** (-0.5)
    ctx_index = lax.axis_index("ctx")
    stream_index = lax.axis_index("wt")
    doc_ends = jnp.cumsum(doc_lengths[0])
    all_positions = jnp.arange(seq_len, dtype=jnp.int32)
    doc_all = jnp.sum((doc_ends[None, :] <= all_positions[:, None]).astype(jnp.int32), axis=1)
    first_pos = ctx_index * tokens
    my_positions = first_pos + jnp.arange(tokens, dtype=jnp.int32)
    my_docs = lax.dynamic_slice_in_dim(doc_all, first_pos, tokens)
    cosine_table, sine_table = rotary_tables(my_positions, head_dim)
    resid_in = hidden_in[0].astype(jnp.float32)
    normed_in = norm_rows(resid_in, gain_attn).astype(jnp.bfloat16)
    pieces = (
        lax.all_gather(w_query, ("ctx", "wt"), axis=0, tiled=True),
        lax.all_gather(key_weight, ("ctx", "wt"), axis=0, tiled=True),
        lax.all_gather(value_weight, ("ctx", "wt"), axis=0, tiled=True),
        lax.all_gather(w_router, ("ctx", "wt"), axis=0, tiled=True),
    )
    columns = normed_in
    query_sum = matmul(columns, pieces[0]).reshape(tokens, query_heads, head_dim)
    key_sum = matmul(columns, pieces[1]).reshape(tokens, key_heads, head_dim)
    router_full = pieces[3]
    query_low = (
        rotate(norm_rows(query_sum, gain_query), cosine_table, sine_table)
        .reshape(tokens, q_width)
        .astype(jnp.bfloat16)
    )
    key_low = (
        rotate(norm_rows(key_sum, gain_key), cosine_table, sine_table)
        .reshape(tokens, kv_width)
        .astype(jnp.bfloat16)
    )
    value_low = matmul(columns, pieces[2]).astype(jnp.bfloat16)
    keys_all, values_all = (
        lax.all_gather(key_low, "ctx", axis=0, tiled=True),
        lax.all_gather(value_low, "ctx", axis=0, tiled=True),
    )
    head_grouped = query_low.reshape(tokens, key_heads, group_width, head_dim)
    block_count = seq_len // block_rows

    def block_scores(block_index):
        key_begin = block_index * block_rows
        key_block = lax.dynamic_slice_in_dim(keys_all, key_begin, block_rows, 0).reshape(
            block_rows, key_heads, head_dim
        )
        value_block = lax.dynamic_slice_in_dim(values_all, key_begin, block_rows, 0).reshape(
            block_rows, key_heads, head_dim
        )
        scores = (
            jnp.einsum(
                "qkgd,skd->kgqs", head_grouped, key_block, preferred_element_type=jnp.float32
            )
            * score_scale
        )
        key_pos = key_begin + jnp.arange(block_rows, dtype=jnp.int32)
        key_doc = lax.dynamic_slice_in_dim(doc_all, key_begin, block_rows)
        allowed = (key_pos[None, :] <= my_positions[:, None]) & (
            key_doc[None, :] == my_docs[:, None]
        )
        return (jnp.where(allowed, scores, MASKED), allowed, key_block, value_block)

    def lse_step(running, block_index):
        row_peak, row_total = running
        scores, allowed, key_block, value_block = block_scores(block_index)
        new_peak = jnp.maximum(row_peak, jnp.max(scores, axis=-1))
        weights = jnp.where(allowed, jnp.exp(scores - new_peak[..., None]), 0.0)
        return (
            (new_peak, row_total * jnp.exp(row_peak - new_peak) + jnp.sum(weights, axis=-1)),
            None,
        )

    stat_shape = (key_heads, group_width, tokens)
    (row_peak, row_total), unused = lax.scan(
        lse_step,
        (jnp.full(stat_shape, MASKED, jnp.float32), jnp.zeros(stat_shape, jnp.float32)),
        jnp.arange(block_count),
    )
    log_total = row_peak + jnp.log(row_total)

    def mix_step(running, block_index):
        scores, allowed, key_block, value_block = block_scores(block_index)
        weights = jnp.where(allowed, jnp.exp(scores - log_total[..., None]), 0.0).astype(
            jnp.bfloat16
        )
        return (
            running
            + jnp.einsum(
                "kgqs,skd->qkgd", weights, value_block, preferred_element_type=jnp.float32
            ),
            None,
        )

    mixed, unused = lax.scan(
        mix_step,
        jnp.zeros((tokens, key_heads, group_width, head_dim), jnp.float32),
        jnp.arange(block_count),
    )
    mixed_low = mixed.reshape(tokens, q_width).astype(jnp.bfloat16)
    columns = mixed_low
    sums = matmul(columns, lax.all_gather(w_out, ("ctx", "wt"), axis=0, tiled=True))
    resid_mid = resid_in + sums
    normed_mid = norm_rows(resid_mid, gain_moe).astype(jnp.bfloat16)
    logits = matmul(normed_mid, router_full)
    logit_exp = jnp.exp(logits - jnp.max(logits, axis=-1, keepdims=True))
    router_probs = logit_exp / jnp.sum(logit_exp, axis=-1, keepdims=True)
    expert_ids = jnp.arange(expert_count, dtype=jnp.int32)
    chosen_ids = routes[0]
    picked = chosen_ids[:, :, None] == expert_ids[None, None, :]
    picked_int = picked.astype(jnp.int32)
    picked_float = picked.astype(jnp.float32)
    chosen = jnp.sum(picked_float * router_probs[:, None, :], axis=2)
    chosen_total = jnp.sum(chosen, axis=1, keepdims=True)
    expert_hits = jnp.sum(picked_int, axis=1)
    local_before = jnp.cumsum(expert_hits, axis=0) - expert_hits
    offsets = entering(
        jnp.sum(expert_hits, axis=0), "ctx", add_counts, jnp.zeros((expert_count,), jnp.int32)
    )
    local_rank = jnp.sum(picked_int * local_before[:, None, :], axis=2)
    slot_index = local_rank + jnp.sum(picked_int * offsets[None, None, :], axis=2).astype(jnp.int32)
    kept_mask = slot_index < capacity
    keep_float = kept_mask.astype(jnp.float32)
    gate_kept = chosen / chosen_total * keep_float
    dest_row = jnp.where(kept_mask, stream_index * capacity + slot_index, cap_rows).reshape(-1)
    send_pos = (chosen_ids * send_slots + local_rank).reshape(-1)

    def to_owners(pair_rows):
        placed = (
            jnp.zeros((expert_count * send_slots, model_width), jnp.bfloat16)
            .at[send_pos]
            .set(pair_rows)
        )
        return placed.reshape(devices, local_count * send_slots, model_width)

    def by_expert(stacked):
        return (
            stacked.reshape(devices, local_count, send_slots, model_width)
            .transpose(1, 0, 2, 3)
            .reshape(local_count, devices * send_slots, model_width)
        )

    def from_expert(stacked):
        return (
            stacked.reshape(local_count, devices, send_slots, model_width)
            .transpose(1, 0, 2, 3)
            .reshape(devices, local_count * send_slots, model_width)
        )

    def to_pairs(returned):
        return (
            returned.reshape(expert_count * send_slots, model_width)[send_pos]
            .reshape(tokens, top_count, model_width)
            .astype(jnp.float32)
        )

    pair_rows = jnp.broadcast_to(normed_mid[:, None, :], (tokens, top_count, model_width)).reshape(
        -1, model_width
    )
    dest_sent = (
        jnp.full((expert_count * send_slots,), cap_rows, jnp.int32)
        .at[send_pos]
        .set(dest_row)
        .reshape(devices, local_count * send_slots)
    )
    arrived, arrived_dest = (
        lax.all_to_all(
            to_owners(pair_rows), ("ctx", "wt"), split_axis=0, concat_axis=0, tiled=True
        ),
        lax.all_to_all(dest_sent, ("ctx", "wt"), split_axis=0, concat_axis=0, tiled=True),
    )
    dest_local = (
        arrived_dest.reshape(devices, local_count, send_slots)
        .transpose(1, 0, 2)
        .reshape(local_count, devices * send_slots)
    )
    rows_local = by_expert(arrived)
    kept_inputs, kept_gates, kept_ups, kept_hidden, back_rows = ([], [], [], [], [])
    local_expert = 0
    dest_rows = dest_local[local_expert]
    valid_rows = dest_rows < cap_rows
    filled = (
        jnp.zeros((cap_rows, model_width), jnp.bfloat16)
        .at[dest_rows]
        .set(rows_local[local_expert], mode="drop")
    )
    gate_h = matmul(filled, expert_gate[local_expert])
    up_h = matmul(filled, expert_up[local_expert])
    hidden_h = (gate_h * jax.nn.sigmoid(gate_h) * up_h).astype(jnp.bfloat16)
    result_rows = matmul(hidden_h, expert_down[local_expert]).astype(jnp.bfloat16)
    back_rows.append(
        jnp.where(
            valid_rows[:, None],
            result_rows[jnp.minimum(dest_rows, cap_rows - 1)],
            jnp.zeros((), jnp.bfloat16),
        )
    )
    kept_inputs.append(filled)
    kept_gates.append(gate_h)
    kept_ups.append(up_h)
    kept_hidden.append(hidden_h)
    returned = lax.all_to_all(
        from_expert(jnp.stack(back_rows)), ("ctx", "wt"), split_axis=0, concat_axis=0, tiled=True
    )
    expert_out = to_pairs(returned)
    hidden_out = resid_mid + jnp.sum(gate_kept[:, :, None] * expert_out, axis=1)
    out_cot = out_grad[0].astype(jnp.float32)
    gate_cot = jnp.sum(expert_out * out_cot[:, None, :], axis=2)
    pair_cot = (
        (gate_kept[:, :, None] * out_cot[:, None, :]).astype(jnp.bfloat16).reshape(-1, model_width)
    )
    arrived_cot = lax.all_to_all(
        to_owners(pair_cot), ("ctx", "wt"), split_axis=0, concat_axis=0, tiled=True
    )
    cot_local = by_expert(arrived_cot)
    grads_gate, grads_up, grads_down, back_cots = ([], [], [], [])
    local_expert = 0
    dest_rows = dest_local[local_expert]
    valid_rows = dest_rows < cap_rows
    out_rows_cot = (
        jnp.zeros((cap_rows, model_width), jnp.bfloat16)
        .at[dest_rows]
        .set(cot_local[local_expert], mode="drop")
    )
    hidden_cot = contract_cols(out_rows_cot, expert_down[local_expert])
    grads_down.append(contract_rows(kept_hidden[local_expert], out_rows_cot))
    gate_h = kept_gates[local_expert]
    sigma_h = jax.nn.sigmoid(gate_h)
    gate_cot_h = (
        hidden_cot * kept_ups[local_expert] * sigma_h * (1.0 + gate_h * (1.0 - sigma_h))
    ).astype(jnp.bfloat16)
    up_cot_h = (hidden_cot * gate_h * sigma_h).astype(jnp.bfloat16)
    grads_gate.append(contract_rows(kept_inputs[local_expert], gate_cot_h))
    grads_up.append(contract_rows(kept_inputs[local_expert], up_cot_h))
    in_rows_cot = (
        contract_cols(gate_cot_h, expert_gate[local_expert])
        + contract_cols(up_cot_h, expert_up[local_expert])
    ).astype(jnp.bfloat16)
    back_cots.append(
        jnp.where(
            valid_rows[:, None],
            in_rows_cot[jnp.minimum(dest_rows, cap_rows - 1)],
            jnp.zeros((), jnp.bfloat16),
        )
    )
    returned_cot = lax.all_to_all(
        from_expert(jnp.stack(back_cots)), ("ctx", "wt"), split_axis=0, concat_axis=0, tiled=True
    )
    mid_cot = jnp.sum(to_pairs(returned_cot), axis=1)
    kept_cot = gate_cot * keep_float
    chosen_cot = kept_cot / chosen_total - jnp.sum(kept_cot * chosen, axis=1, keepdims=True) / (
        chosen_total * chosen_total
    )
    probs_cot = jnp.sum(picked_float * chosen_cot[:, :, None], axis=1)
    logit_cot = (
        router_probs * (probs_cot - jnp.sum(router_probs * probs_cot, axis=1, keepdims=True))
    ).astype(jnp.bfloat16)
    mid_cot = mid_cot + contract_cols(logit_cot, router_full)
    mid_norm_cot, gain_moe_terms = norm_back(resid_mid, gain_moe, mid_cot)
    resid_cot = out_cot + mid_norm_cot
    attn_cot = resid_cot.astype(jnp.bfloat16)
    mixed_cot = contract_cols(attn_cot, lax.all_gather(w_out, ("ctx", "wt"), axis=0, tiled=True))
    grad_w_out = lax.psum_scatter(
        contract_rows(mixed_low, attn_cot), ("ctx", "wt"), scatter_dimension=0, tiled=True
    )
    cot_grouped = mixed_cot.astype(jnp.bfloat16).reshape(tokens, key_heads, group_width, head_dim)
    row_delta = jnp.sum(cot_grouped.astype(jnp.float32) * mixed, axis=-1).transpose(1, 2, 0)

    def back_step(query_cot, block_index):
        scores, allowed, key_block, value_block = block_scores(block_index)
        weights = jnp.where(allowed, jnp.exp(scores - log_total[..., None]), 0.0)
        value_cot = jnp.einsum(
            "kgqs,qkgd->skd",
            weights.astype(jnp.bfloat16),
            cot_grouped,
            preferred_element_type=jnp.float32,
        )
        weight_cot = jnp.einsum(
            "qkgd,skd->kgqs", cot_grouped, value_block, preferred_element_type=jnp.float32
        )
        score_cot = (weights * (weight_cot - row_delta[..., None])).astype(jnp.bfloat16)
        query_cot = (
            query_cot
            + jnp.einsum("kgqs,skd->qkgd", score_cot, key_block, preferred_element_type=jnp.float32)
            * score_scale
        )
        key_cot = (
            jnp.einsum(
                "kgqs,qkgd->skd", score_cot, head_grouped, preferred_element_type=jnp.float32
            )
            * score_scale
        )
        return (
            query_cot,
            (key_cot.reshape(block_rows, kv_width), value_cot.reshape(block_rows, kv_width)),
        )

    query_cot, (key_cots, value_cots) = lax.scan(
        back_step,
        jnp.zeros((tokens, key_heads, group_width, head_dim), jnp.float32),
        jnp.arange(block_count),
    )
    key_mine, value_mine = (
        lax.psum_scatter(
            key_cots.reshape(seq_len, kv_width).astype(jnp.bfloat16),
            "ctx",
            scatter_dimension=0,
            tiled=True,
        ).astype(jnp.float32),
        lax.psum_scatter(
            value_cots.reshape(seq_len, kv_width).astype(jnp.bfloat16),
            "ctx",
            scatter_dimension=0,
            tiled=True,
        ).astype(jnp.float32),
    )
    query_pre, gain_query_terms = norm_back(
        query_sum,
        gain_query,
        rotate(query_cot.reshape(tokens, query_heads, head_dim), cosine_table, -sine_table),
    )
    key_pre, gain_key_terms = norm_back(
        key_sum,
        gain_key,
        rotate(key_mine.reshape(tokens, key_heads, head_dim), cosine_table, -sine_table),
    )
    query_cot_low = query_pre.reshape(tokens, q_width).astype(jnp.bfloat16)
    key_cot_low = key_pre.reshape(tokens, kv_width).astype(jnp.bfloat16)
    value_cot_low = value_mine.astype(jnp.bfloat16)
    pieces = lax.all_gather((w_query, key_weight, value_weight), ("ctx", "wt"), axis=0, tiled=True)
    in_cot = (
        contract_cols(query_cot_low, pieces[0])
        + contract_cols(key_cot_low, pieces[1])
        + contract_cols(value_cot_low, pieces[2])
    )
    proj_cols = q_width + 2 * kv_width + expert_count
    proj_grads = lax.psum_scatter(
        jnp.concatenate(
            [
                contract_rows(normed_in, query_cot_low),
                contract_rows(normed_in, key_cot_low),
                contract_rows(normed_in, value_cot_low),
                contract_rows(normed_mid, logit_cot),
            ],
            axis=1,
        ),
        ("ctx", "wt"),
        scatter_dimension=0,
        tiled=True,
    )
    grad_w_query = proj_grads[:, :q_width]
    grad_w_key = proj_grads[:, q_width : q_width + kv_width]
    grad_w_value = proj_grads[:, q_width + kv_width : q_width + 2 * kv_width]
    grad_w_router = proj_grads[:, q_width + 2 * kv_width : proj_cols]
    in_norm_cot, gain_attn_terms = norm_back(resid_in, gain_attn, in_cot)
    grad_in = resid_cot + in_norm_cot
    grad_gain_attn, grad_gain_query, grad_gain_key, grad_gain_moe = lax.psum(
        (
            jnp.sum(gain_attn_terms, axis=0),
            jnp.sum(gain_query_terms, axis=(0, 1)),
            jnp.sum(gain_key_terms, axis=(0, 1)),
            jnp.sum(gain_moe_terms, axis=0),
        ),
        ("ctx", "wt"),
    )
    return (
        hidden_out[None],
        grad_in[None],
        grad_gain_attn,
        grad_w_query,
        grad_w_key,
        grad_w_value,
        grad_gain_query,
        grad_gain_key,
        grad_w_out,
        grad_gain_moe,
        grad_w_router,
        jnp.stack(grads_gate),
        jnp.stack(grads_up),
        jnp.stack(grads_down),
    )


def solution(mesh):
    in_specs = (
        P("wt", "ctx", None),
        P("wt", None),
        P("wt", "ctx", None),
        P(),
        P(("ctx", "wt"), None),
        P(("ctx", "wt"), None),
        P(("ctx", "wt"), None),
        P(),
        P(),
        P(("ctx", "wt"), None),
        P(),
        P(("ctx", "wt"), None),
        P(("ctx", "wt"), None, None),
        P(("ctx", "wt"), None, None),
        P(("ctx", "wt"), None, None),
        P("wt", "ctx", None),
    )
    out_specs = (
        P("wt", "ctx", None),
        P("wt", "ctx", None),
        P(),
        P(("ctx", "wt"), None),
        P(("ctx", "wt"), None),
        P(("ctx", "wt"), None),
        P(),
        P(),
        P(("ctx", "wt"), None),
        P(),
        P(("ctx", "wt"), None),
        P(("ctx", "wt"), None, None),
        P(("ctx", "wt"), None, None),
        P(("ctx", "wt"), None, None),
    )
    return jax.shard_map(
        on_device, mesh=mesh, in_specs=in_specs, out_specs=out_specs, check_vma=False
    )
```

profile of v0, /device:TPU:0, one launch (start us, length us, event | category | flops | bytes accessed | tf_op | source)
XLA Modules:
  0.0 3125.6 jit_solution(14378632185446623608)
XLA Ops:
  10.0 60.1 %all-gather.9.cloned.1.call-done = bf16[2048,512]{1,0:T(8,128)(2,1)} async-done(((bf16[64,512]{1,0:T(8,128)(2,1)}), bf16[2048,512]{1,0:T(8,128)(2,1)}) %all-gather.9.cloned.1.call-update) | async-done | bytes 2097168 | tf_op jit(solution)/shard_map/all_gather | solution.py:130
  74.6 53.6 %all-gather.13.cloned.1.call-done = bf16[2048,512]{1,0:T(8,128)(2,1)} async-done(((bf16[64,512]{1,0:T(8,128)(2,1)}), bf16[2048,512]{1,0:T(8,128)(2,1)}) %all-gather.13.cloned.1.call-update) | async-done | bytes 2097168 | tf_op jit(solution)/shard_map/all_gather | solution.py:129
  128.2 3.9 copy.182
  138.9 7.3 all-reduce
  147.3 70.6 %all-gather.1 = bf16[32,64,32]{1,2,0:T(8,128)(2,1)S(1)} all-gather(bf16[1,64,32]{1,2,0:T(8,128)(2,1)} %bitcast.382), channel_id=1, replica_groups=mesh['ctx'=8,'wt'=4] {'ctx','wt'}, dimensions={0}, use_global_device_ids=true | all-gather | bytes 135168 | tf_op jit(solution)/shard_map/all_gather | solution.py:131
  222.7 49.3 %all-gather.17.cloned.1.call-done = bf16[2048,4096]{1,0:T(8,128)(2,1)} async-done(((bf16[64,4096]{1,0:T(8,128)(2,1)}), bf16[2048,4096]{1,0:T(8,128)(2,1)}) %all-gather.17.cloned.1.call-update) | async-done | bytes 16777232 | tf_op jit(solution)/shard_map/all_gather | solution.py:128
  272.0 22.6 copy.183
  294.7 8.4 multiply_reduce_fusion.3
  308.4 26.3 while.53
  311.0 5.9 fusion.188
  316.9 4.6 select_reduce_fusion.7
  324.2 5.9 fusion.188
  330.1 4.5 select_reduce_fusion.7
  334.7 19.8 while.54
  338.5 5.7 bitcast_add_fusion.4
  348.0 6.4 bitcast_add_fusion.4
  357.3 56.0 %all-gather.19.cloned.1.call-done = bf16[4096,2048]{1,0:T(8,128)(2,1)} async-done(((bf16[128,2048]{1,0:T(8,128)(2,1)}), bf16[4096,2048]{1,0:T(8,128)(2,1)}) %all-gather.19.cloned.1.call-update) | async-done | bytes 16777232 | tf_op jit(solution)/shard_map/all_gather | solution.py:214
  413.3 8.6 multiply_reduce_fusion.6
  425.1 4.3 scatter_custom_fusion
  432.9 11.7 scatter_custom_fusion.1
  444.6 6.2 all-to-all-start.1
  453.2 12.1 scatter_custom_fusion.3
  465.2 167.0 %all-to-all-done.1 = bf16[32,64,2048]{2,1,0:T(8,128)(2,1)} async-done(((bf16[32,64,2048]{2,1,0:T(8,128)(2,1)}), bf16[32,64,2048]{2,1,0:T(8,128)(2,1)}, u32[]{:S(2)}, u32[]{:S(2)}) %all-to-all-start.1) | async-done | bytes 8388640 | tf_op jit(solution)/shard_map/all_to_all | solution.py:279
  632.2 8.5 all-to-all-start.3
  642.0 16.1 scatter_custom_fusion.2
  658.1 8.4 fusion.54
  666.5 5.1 fusion.50
  671.6 150.5 %all-to-all-done.3 = bf16[32,64,2048]{2,1,0:T(8,128)(2,1)} async-done(((bf16[32,64,2048]{2,1,0:T(8,128)(2,1)}), bf16[32,64,2048]{2,1,0:T(8,128)(2,1)}, u32[]{:S(2)}, u32[]{:S(2)}) %all-to-all-start.3) | async-done | bytes 8388640 | tf_op jit(solution)/shard_map/all_to_all | solution.py:324
  822.1 16.0 scatter_custom_fusion.4
  838.1 8.6 multiply_convert_fusion
  850.2 4.9 convolution_convert_fusion.1
  855.1 5.0 add_convert_fusion
  860.1 19.1 gather_fusion.2
  879.2 19.1 gather_fusion
  898.3 9.2 broadcast_select_fusion.2
  907.5 190.5 %all_to_all.29 = bf16[32,64,2048]{2,1,0:T(8,128)(2,1)} all-to-all(bf16[32,64,2048]{2,1,0:T(8,128)(2,1)S(1)} %get-tuple-element.812), channel_id=1, replica_groups=mesh['ctx'=8,'wt'=4] {'ctx','wt'}, dimensions={0} | all-to-all | bytes 16777216 | tf_op jit(solution)/shard_map/all_to_all | solution.py:358
  1098.0 4.7 all-to-all-start.2
  1102.8 13.3 gather_fusion.3
  1116.0 6.0 convert_reduce_fusion
  1122.1 162.0 %all-to-all-done.2 = bf16[32,64,2048]{2,1,0:T(8,128)(2,1)} async-done(((bf16[32,64,2048]{2,1,0:T(8,128)(2,1)}), bf16[32,64,2048]{2,1,0:T(8,128)(2,1)}, u32[]{:S(2)}, u32[]{:S(2)}) %all-to-all-start.2) | async-done | bytes 8388640 | tf_op jit(solution)/shard_map/all_to_all | solution.py:314
  1284.1 13.3 gather_fusion.1
  1297.5 6.1 fusion.36
  1309.8 12.7 convolution_convert_fusion
  1327.0 56.6 %while.56 = (s32[]{:T(128)}, f32[128,4,8,128]{0,3,2,1:T(8,128)S(1)}, bf16[2,512,512]{2,1,0:T(8,128)(2,1)}, bf16[2,512,512]{2,1,0:T(8,128)(2,1)}, s32[2]{0:T(128)...) while((s32[]{:T(128)}, ...), condition=%wide.region_37.38_spmd.clone, body=%wide.region_36.37_spmd.clone.sunk | while | flops 2711814656 | bytes 130805624 | solution.py:410
  1335.7 4.5 fusion.205
  1340.2 3.5 bitcast_add_fusion.5
  1348.4 4.8 fusion.207
  1363.8 4.5 fusion.205
  1368.3 3.5 bitcast_add_fusion.5
  1376.5 4.8 fusion.207
  1388.0 13.9 fusion.86
  1402.3 21.2 reduce-scatter.5.cloned.1.call-done
  1426.2 3.5 fusion.84
  1429.7 33.0 %reduce-scatter.7.cloned.1.call-done = bf16[128,512]{1,0:T(8,128)(2,1)} async-done(((bf16[1024,512]{1,0:T(8,128)(2,1)}), bf16[128,512]{1,0:T(8,128)(2,1)}) %reduce-scatter.7.cloned.1.call-update) | async-done | bytes 131088 | tf_op jit(solution)/shard_map/reduce_scatter | solution.py:422
  1462.7 3.7 fusion.94
  1466.4 28.9 pad_maximum_fusion
  1496.8 14.1 fusion.91
  1512.4 8.6 convolution_bitcast_fusion.3
  1521.0 5.5 convolution_bitcast_fusion.2
  1526.5 5.6 convolution_bitcast_fusion.1
  1532.1 12.6 fusion.114
  1548.9 45.4 %all-reduce.1 = (f32[2048]{0:T(1024)}, f32[128]{0:T(128)}, f32[128]{0:T(128)}, f32[2048]{0:T(1024)}) all-reduce(f32[2048]{0:T(1024)S(1)} %get-tuple-element.694, f32[128]{0:T(128)S(1)} %copy-done.67, f32[128]{0:T(128)S(1)} %get-tuple-element.696, f32[2048]{0:T(1024)S(1)} %copy-done.48), channel_id=1, replica_groups=mesh['ctx'=8,'wt'=4] {'ctx','wt'}, use_global_device_ids=true, to_apply=%region_44.45 | all-reduce | flops 4352 | bytes 34816 | tf_op jit(solution)/shard_map/psum | solution.py:469
  1597.3 806.4 %reduce-scatter.9.cloned.1.call-done = f32[64,5152]{1,0:T(8,128)} async-done(((f32[2048,5152]{1,0:T(8,128)}), f32[64,5152]{1,0:T(8,128)}) %reduce-scatter.9.cloned.1.call-update) | async-done | bytes 1318928 | tf_op jit(solution)/shard_map/reduce_scatter | solution.py:449
  2409.1 709.5 %reduce-scatter.11.cloned.1.call-done = f32[128,2048]{1,0:T(8,128)} async-done(((f32[4096,2048]{1,0:T(8,128)}), f32[128,2048]{1,0:T(8,128)}) %reduce-scatter.11.cloned.1.call-update) | async-done | bytes 1048592 | tf_op jit(solution)/shard_map/reduce_scatter | solution.py:375
  (352 shorter events, 113.9 us)
Async XLA Ops:
  7.2 830.9 %copy-start = (bf16[1,768,2048]{2,1,0:T(8,128)(2,1)S(1)}, bf16[1,768,2048]{2,1,0:T(8,128)(2,1)}, u32[]{:S(2)}) copy-start(bf16[1,768,2048]{2,1,0:T(8,128)(2,1)} %param.38) | copy-start | bytes 9437188
  7.2 62.9 %all-gather.9.cloned.1.call-start = ((), (), s32[]{:S(2)}) async-start(), calls=%async_computation.9 | async-start | bytes 2162688 | tf_op jit(solution)/shard_map/all_gather | solution.py:130
  7.9 120.3 %all-gather.13.cloned.1.call-start = ((), (), s32[]{:S(2)}) async-start(), calls=%async_computation.11 | async-start | bytes 2162688 | tf_op jit(solution)/shard_map/all_gather | solution.py:129
  8.7 123.5 %copy-start.31 = (f32[2048]{0:T(1024)S(1)}, f32[2048]{0:T(1024)}, u32[]{:S(2)}) copy-start(f32[2048]{0:T(1024)} %param.27) | copy-start | bytes 24580
  8.7 211.5 %all-gather.11.cloned.1.call-start = ((), (), s32[]{:S(2)}) async-start(), calls=%async_computation.10 | async-start | bytes 1179648 | tf_op jit(solution)/shard_map/all_gather | solution.py:150
  10.0 284.7 %copy-start.49 = (f32[128]{0:T(128)}, f32[128]{0:T(128)S(1)}, u32[]{:S(2)}) copy-start(f32[128]{0:T(128)S(1)} %add_rsqrt_fusion.3) | copy-start | bytes 1540
  73.0 61.8 %copy-start.60 = (f32[128]{0:T(128)S(1)}, f32[128]{0:T(128)}, u32[]{:S(2)}) copy-start(f32[128]{0:T(128)} %param.32) | copy-start | bytes 1540
  73.0 199.0 %all-gather.17.cloned.1.call-start = ((), (), s32[]{:S(2)}) async-start(), calls=%async_computation.13 | async-start | bytes 17301504 | tf_op jit(solution)/shard_map/all_gather | solution.py:128
  73.6 234.8 %all-gather.15.cloned.1.call-start = ((), (), s32[]{:S(2)}) async-start(), calls=%async_computation.12 | async-start | bytes 1179648 | tf_op jit(solution)/shard_map/all_gather | solution.py:149
  74.6 229.1 %copy-start.23 = (f32[128,128]{0,1:T(8,128)}, f32[128,128]{0,1:T(8,128)S(1)}, u32[]{:S(2)}) copy-start(f32[128,128]{0,1:T(8,128)S(1)} %get-tuple-element.809) | copy-start | bytes 196612
  128.2 8.7 copy-start.71
  128.2 8.8 copy-start.41
  128.2 9.1 copy-start.72
  136.2 277.0 %all-gather.19.cloned.1.call-start = ((), (), s32[]{:S(2)}) async-start(), calls=%async_computation.14 | async-start | bytes 17301504 | tf_op jit(solution)/shard_map/all_gather | solution.py:214
  220.0 203.0 %copy-start.27 = (bf16[2048,32]{0,1:T(8,128)(2,1)}, bf16[2048,32]{0,1:T(8,128)(2,1)S(1)}, u32[]{:S(2)}) copy-start(bf16[2048,32]{0,1:T(8,128)(2,1)S(1)} %reshape.662) | copy-start | bytes 393220
  294.6 8.5 copy-start.61
  354.5 67.3 %copy-start.37 = (s32[1024]{0:T(1024)}, s32[1024]{0:T(1024)S(1)}, u32[]{:S(2)}) copy-start(s32[1024]{0:T(1024)S(1)} %get-tuple-element.1258) | copy-start | bytes 12292
  354.5 67.3 %copy-start.39 = (s32[128]{0:T(128)}, s32[128]{0:T(128)S(1)}, u32[]{:S(2)}) copy-start(s32[128]{0:T(128)S(1)} %get-tuple-element.1264) | copy-start | bytes 1540
  354.5 67.3 %copy-start.52 = (f32[4,8,128]{2,1,0:T(8,128)}, f32[4,8,128]{2,1,0:T(8,128)S(1)}, u32[]{:S(2)}) copy-start(f32[4,8,128]{2,1,0:T(8,128)S(1)} %get-tuple-element.1269) | copy-start | bytes 49156
  413.3 9.6 copy-start.43
  424.7 19.9 copy-start.58
  424.8 19.8 copy-start.46
  424.8 19.8 copy-start.65
  424.8 19.8 copy-start.54
  430.1 14.6 all-to-all-start
  444.6 187.6 %all-to-all-start.1 = ((bf16[32,64,2048]{2,1,0:T(8,128)(2,1)}), bf16[32,64,2048]{2,1,0:T(8,128)(2,1)}, u32[]{:S(2)}, u32[]{:S(2)}) async-start(bf16[32,64,2048]{2,1,0:T(8,128)(2,1)} %bitcast.351), calls=%async_computation.1 | async-start | bytes 16777216 | tf_op jit(solution)/shard_map/all_to_all | solution.py:279
  632.2 189.9 %all-to-all-start.3 = ((bf16[32,64,2048]{2,1,0:T(8,128)(2,1)}), bf16[32,64,2048]{2,1,0:T(8,128)(2,1)}, u32[]{:S(2)}, u32[]{:S(2)}) async-start(bf16[32,64,2048]{2,1,0:T(8,128)(2,1)} %bitcast.350), calls=%async_computation.3 | async-start | bytes 16777216 | tf_op jit(solution)/shard_map/all_to_all | solution.py:324
  658.1 8.4 copy-start.17
  658.1 8.4 copy-start.69
  838.0 8.7 copy-start.68
  846.7 8.4 copy-start.75
  850.2 5.0 copy-start.70
  1098.0 186.1 %all-to-all-start.2 = ((bf16[32,64,2048]{2,1,0:T(8,128)(2,1)}), bf16[32,64,2048]{2,1,0:T(8,128)(2,1)}, u32[]{:S(2)}, u32[]{:S(2)}) async-start(bf16[32,64,2048]{2,1,0:T(8,128)(2,1)} %get-tuple-element.813), calls=%async_computation.2 | async-start | bytes 16777216 | tf_op jit(solution)/shard_map/all_to_all | solution.py:314
  1102.7 320.8 %reduce-scatter.5.cloned.1.call-start = ((), (), s32[]{:S(2)}) async-start(), calls=%async_computation.15 | async-start | bytes 1179648 | tf_op jit(solution)/shard_map/reduce_scatter | solution.py:416
  1297.4 6.2 copy-start.47
  1297.4 6.2 copy-start.55
  1297.4 6.3 copy-start.66
  1297.4 6.3 copy-start.42
  1297.4 6.3 copy-start.36
  1297.4 6.3 copy-start.57
  1297.4 6.3 copy-start.59
  1297.4 6.4 copy-start.28
  1297.4 6.4 copy-start.44
  1297.4 6.4 copy-start.64
  1297.4 9.0 copy-start.21
  1322.5 4.5 copy-start.38
  1322.5 4.5 copy-start.40
  1322.5 4.5 copy-start.53
  1329.8 5.9 copy-start.16
  1340.2 4.6 copy-start.3
  1357.9 5.9 copy-start.16
  1368.2 4.6 copy-start.3
  1383.7 79.0 %reduce-scatter.7.cloned.1.call-start = ((), (), s32[]{:S(2)}) async-start(), calls=%async_computation.16 | async-start | bytes 1179648 | tf_op jit(solution)/shard_map/reduce_scatter | solution.py:422
  1387.7 1016.0 %reduce-scatter.9.cloned.1.call-start = ((), (), s32[]{:S(2)}) async-start(), calls=%async_computation.17 | async-start | bytes 44335104 | tf_op jit(solution)/shard_map/reduce_scatter | solution.py:449
  1388.0 13.9 copy-start.14
  1388.0 36.5 %copy-start.20 = (f32[128,4,128]{0,2,1:T(8,128)S(1)}, f32[128,4,128]{0,2,1:T(8,128)}, u32[]{:S(2)}) copy-start(f32[128,4,128]{0,2,1:T(8,128)} %copy-done.19) | copy-start | bytes 786436
  1402.3 60.4 %copy-start.51 = (f32[128]{0:T(128)S(1)}, f32[128]{0:T(128)}, u32[]{:S(2)}) copy-start(f32[128]{0:T(128)} %copy-done.49) | copy-start | bytes 1540
  1495.3 1623.2 %reduce-scatter.11.cloned.1.call-start = ((), (), s32[]{:S(2)}) async-start(), calls=%async_computation.18 | async-start | bytes 34603008 | tf_op jit(solution)/shard_map/reduce_scatter | solution.py:375
  1512.4 8.6 copy-start.18
  1512.4 8.6 copy-start.76
  1521.0 5.5 copy-start.9
  1521.0 5.5 copy-start.26
  1532.1 12.6 copy-start.15
  1547.0 1571.6 %copy-start.1 = (bf16[1,768,2048]{2,1,0:T(8,128)(2,1)S(1)}, bf16[1,768,2048]{2,1,0:T(8,128)(2,1)}, u32[]{:S(2)}) copy-start(bf16[1,768,2048]{2,1,0:T(8,128)(2,1)} %param.38) | copy-start | bytes 9437188
  (31 other events, 56.5 us)
Sparse Core Ops, SparseCore 0:
  10.9 59.0 all-gather.8
  73.0 55.1 all-gather.12
  130.7 22.2 all-gather.10
  155.8 116.1 all-gather.16
  274.3 21.6 all-gather.14
  298.9 114.3 all-gather.18
  1383.8 39.6 reduce-scatter.4
  1426.7 35.9 reduce-scatter.6
  1495.4 908.1 reduce-scatter.8
  2406.4 712.0 reduce-scatter.10
where the time goes:
time: 3130 us
  waiting for transfers between devices  2270 us (73%)
  blocking collectives  314 us (10%)
  matrix products  207 us (7%)
  local copies, waits for them, and re-layouts  193 us (6%)
  other arithmetic  97.4 us (3%)
    reduce_scatter x1, waiting for transfers between devices, on_device(): lax.psum_scatter(jnp.concatenate([contract_rows(normed_in, query_cot_low)...  806 us
    reduce_scatter x1, waiting for transfers between devices, on_device(): lax.psum_scatter(contract_rows(mixed_low, attn_cot), ('ctx', 'wt'), scatt...  709 us
    all_to_all x1, blocking collectives, on_device(): lax.all_to_all(from_expert(jnp.stack(back_cots)), ('ctx', 'wt'), split_ax...  191 us
    all_to_all x1, waiting for transfers between devices, on_device(): lax.all_to_all(to_owners(pair_rows), ('ctx', 'wt'), split_axis=0, concat_...  167 us
    all_to_all x1, waiting for transfers between devices, on_device(): lax.all_to_all(from_expert(jnp.stack(back_rows)), ('ctx', 'wt'), split_ax...  162 us
    all_to_all x1, waiting for transfers between devices, on_device(): lax.all_to_all(to_owners(pair_cot), ('ctx', 'wt'), split_axis=0, concat_a...  150 us
    all_gather x1, blocking collectives, on_device(): lax.all_gather(w_router, ('ctx', 'wt'), axis=0, tiled=True)  70.6 us
  transfers between devices with their start and end apart: 14, of which 11 were waited for; matrix products, arithmetic and copies ran while one was open for 8% of the time, Pallas kernels for 0%

commit v1 on v0

v1 whole, which is shorter than its diff:
```python
import math

import jax
import jax.numpy as jnp
from jax import lax
from jax.sharding import PartitionSpec as P

EPS = 1e-06
THETA = 1000000.0
MASKED = -1e30


def norm_rows(value_rows, gain_vec):
    return (
        value_rows
        * lax.rsqrt(jnp.mean(value_rows * value_rows, axis=-1, keepdims=True) + EPS)
        * gain_vec
    )


def norm_back(value_rows, gain_vec, upstream):
    factor = lax.rsqrt(jnp.mean(value_rows * value_rows, axis=-1, keepdims=True) + EPS)
    normalized_input = value_rows * factor
    weighted = upstream * gain_vec
    inner_mean = jnp.mean(weighted * normalized_input, axis=-1, keepdims=True)
    return (factor * (weighted - normalized_input * inner_mean), upstream * normalized_input)


def rotary_tables(positions, head_dim):
    half_dim = head_dim // 2
    frequency = jnp.exp(
        jnp.arange(half_dim, dtype=jnp.float32) * (-2.0 * math.log(THETA) / head_dim)
    )
    angles = positions.astype(jnp.float32)[:, None] * frequency[None, :]
    angles = jnp.concatenate([angles, angles], axis=1)
    return (jnp.cos(angles)[:, None, :], jnp.sin(angles)[:, None, :])


def rotate(value_rows, cosine_table, sine_table):
    half_dim = value_rows.shape[-1] // 2
    turned = jnp.concatenate([-value_rows[..., half_dim:], value_rows[..., :half_dim]], axis=-1)
    return value_rows * cosine_table + turned * sine_table


def matmul(left_side, right_side):
    return jnp.dot(left_side, right_side, preferred_element_type=jnp.float32)


def contract_rows(left_side, right_side):
    return lax.dot_general(
        left_side, right_side, (((0,), (0,)), ((), ())), preferred_element_type=jnp.float32
    )


def contract_cols(left_side, right_side):
    return lax.dot_general(
        left_side, right_side, (((1,), (1,)), ((), ())), preferred_element_type=jnp.float32
    )


def sum_everywhere(vector):
    devices = lax.axis_size("ctx") * lax.axis_size("wt")
    spread = jnp.broadcast_to(vector[None, :], (devices, vector.shape[0]))
    return jnp.sum(
        lax.all_to_all(spread, ("ctx", "wt"), split_axis=0, concat_axis=0, tiled=True), axis=0
    )


def on_device(
    hidden_in,
    doc_lengths,
    routes,
    gain_attn,
    w_query,
    key_weight,
    value_weight,
    gain_query,
    gain_key,
    w_out,
    gain_moe,
    w_router,
    expert_gate,
    expert_up,
    expert_down,
    out_grad,
):
    block_rows = 512
    tokens = hidden_in.shape[1]
    model_width = hidden_in.shape[2]
    ctx_size = lax.axis_size("ctx")
    wt_size = lax.axis_size("wt")
    devices = ctx_size * wt_size
    seq_len = tokens * ctx_size
    head_dim = gain_query.shape[0]
    q_width = w_query.shape[1]
    kv_width = key_weight.shape[1]
    query_heads = q_width // head_dim
    key_heads = kv_width // head_dim
    group_width = query_heads // key_heads
    expert_count = w_router.shape[1]
    top_count = routes.shape[2]
    assert expert_gate.shape[0] == 1 and expert_count == devices
    send_slots = 2 * tokens * top_count // expert_count
    capacity = tokens * top_count // wt_size
    score_scale = head_dim ** (-0.5)
    ctx_index = lax.axis_index("ctx")
    both = ("ctx", "wt")
    by_stream = ("wt", "ctx")

    def gather(value, axes):
        return lax.all_gather(value, axes, axis=0, tiled=True)

    def exchange(value, axes):
        return lax.all_to_all(value, axes, split_axis=0, concat_axis=0, tiled=True)

    doc_ends = jnp.cumsum(doc_lengths[0])
    all_positions = jnp.arange(seq_len, dtype=jnp.int32)
    doc_all = jnp.sum((doc_ends[None, :] <= all_positions[:, None]).astype(jnp.int32), axis=1)
    first_pos = ctx_index * tokens
    my_positions = first_pos + jnp.arange(tokens, dtype=jnp.int32)
    my_docs = lax.dynamic_slice_in_dim(doc_all, first_pos, tokens)
    cosine_table, sine_table = rotary_tables(my_positions, head_dim)

    expert_ids = jnp.arange(expert_count, dtype=jnp.int32)
    hits = jnp.sum((routes[0][:, :, None] == expert_ids[None, None, :]).astype(jnp.int32), axis=1)
    local_rank = jnp.cumsum(hits, axis=0) - hits
    counts = lax.all_gather(jnp.sum(hits, axis=0), "ctx")
    earlier = jnp.arange(ctx_size, dtype=jnp.int32)[:, None] < ctx_index
    offsets = jnp.sum(jnp.where(earlier, counts, 0), axis=0)
    kept = (hits > 0) & (local_rank + offsets[None, :] < capacity)
    keep_float = kept.astype(jnp.float32)
    hits_float = hits.astype(jnp.float32)

    def to_owner_rows(table):
        return table.reshape(tokens, ctx_size, wt_size).transpose(2, 1, 0).reshape(devices, tokens)

    def from_owner_rows(table):
        return table.reshape(wt_size, ctx_size, tokens).transpose(2, 1, 0).reshape(tokens, devices)

    hit_mine = exchange(to_owner_rows(hits), by_stream).reshape(wt_size, seq_len)
    slot_mine = jnp.cumsum(hit_mine, axis=1) - hit_mine
    slot_mine = jnp.where((hit_mine > 0) & (slot_mine < capacity), slot_mine, -1)
    block_hits = jnp.sum(hit_mine.reshape(wt_size, ctx_size, tokens), axis=2)
    block_first = jnp.cumsum(block_hits, axis=1) - block_hits
    slot_ids = jnp.arange(capacity, dtype=jnp.int32)
    place = slot_mine[:, None, :] == slot_ids[None, :, None]
    place_low = place.astype(jnp.bfloat16)
    send_ids = jnp.arange(send_slots, dtype=jnp.int32)
    send_slot = jnp.where(
        send_ids[None, None, :] < block_hits[:, :, None],
        block_first[:, :, None] + send_ids[None, None, :],
        -1,
    ).reshape(wt_size, ctx_size * send_slots)
    send_low = (send_slot[:, :, None] == slot_ids[None, None, :]).astype(jnp.bfloat16)

    resid_in = hidden_in[0].astype(jnp.float32)
    normed_in = norm_rows(resid_in, gain_attn).astype(jnp.bfloat16)
    router_pad = -expert_count % head_dim
    side_weights = gather(
        jnp.concatenate(
            [key_weight, value_weight, jnp.pad(w_router, ((0, 0), (0, router_pad)))], axis=1
        ),
        both,
    )
    query_full = gather(w_query, both)
    key_full = side_weights[:, :kv_width]
    value_full = side_weights[:, kv_width : 2 * kv_width]
    router_full = side_weights[:, 2 * kv_width : 2 * kv_width + expert_count]
    key_sum = matmul(normed_in, key_full).reshape(tokens, key_heads, head_dim)
    value_low = matmul(normed_in, value_full).astype(jnp.bfloat16)
    key_low = (
        rotate(norm_rows(key_sum, gain_key), cosine_table, sine_table)
        .reshape(tokens, kv_width)
        .astype(jnp.bfloat16)
    )
    pairs_all = gather(jnp.concatenate([key_low, value_low], axis=1), "ctx")
    keys_all = pairs_all[:, :kv_width]
    values_all = pairs_all[:, kv_width:]
    query_sum = matmul(normed_in, query_full).reshape(tokens, query_heads, head_dim)
    query_low = (
        rotate(norm_rows(query_sum, gain_query), cosine_table, sine_table)
        .reshape(tokens, q_width)
        .astype(jnp.bfloat16)
    )
    out_full = gather(w_out, both)
    head_grouped = query_low.reshape(tokens, key_heads, group_width, head_dim)
    block_count = seq_len // block_rows

    def block_scores(block_index):
        key_begin = block_index * block_rows
        key_block = lax.dynamic_slice_in_dim(keys_all, key_begin, block_rows, 0).reshape(
            block_rows, key_heads, head_dim
        )
        value_block = lax.dynamic_slice_in_dim(values_all, key_begin, block_rows, 0).reshape(
            block_rows, key_heads, head_dim
        )
        scores = (
            jnp.einsum(
                "qkgd,skd->kgqs", head_grouped, key_block, preferred_element_type=jnp.float32
            )
            * score_scale
        )
        key_pos = key_begin + jnp.arange(block_rows, dtype=jnp.int32)
        key_doc = lax.dynamic_slice_in_dim(doc_all, key_begin, block_rows)
        allowed = (key_pos[None, :] <= my_positions[:, None]) & (
            key_doc[None, :] == my_docs[:, None]
        )
        return (jnp.where(allowed, scores, MASKED), allowed, key_block, value_block)

    def lse_step(running, block_index):
        row_peak, row_total = running
        scores, allowed, key_block, value_block = block_scores(block_index)
        new_peak = jnp.maximum(row_peak, jnp.max(scores, axis=-1))
        weights = jnp.where(allowed, jnp.exp(scores - new_peak[..., None]), 0.0)
        return (
            (new_peak, row_total * jnp.exp(row_peak - new_peak) + jnp.sum(weights, axis=-1)),
            None,
        )

    stat_shape = (key_heads, group_width, tokens)
    (row_peak, row_total), unused = lax.scan(
        lse_step,
        (jnp.full(stat_shape, MASKED, jnp.float32), jnp.zeros(stat_shape, jnp.float32)),
        jnp.arange(block_count),
    )
    log_total = row_peak + jnp.log(row_total)

    def mix_step(running, block_index):
        scores, allowed, key_block, value_block = block_scores(block_index)
        weights = jnp.where(allowed, jnp.exp(scores - log_total[..., None]), 0.0).astype(
            jnp.bfloat16
        )
        return (
            running
            + jnp.einsum(
                "kgqs,skd->qkgd", weights, value_block, preferred_element_type=jnp.float32
            ),
            None,
        )

    mixed, unused = lax.scan(
        mix_step,
        jnp.zeros((tokens, key_heads, group_width, head_dim), jnp.float32),
        jnp.arange(block_count),
    )
    mixed_low = mixed.reshape(tokens, q_width).astype(jnp.bfloat16)
    resid_mid = resid_in + matmul(mixed_low, out_full)
    normed_mid = norm_rows(resid_mid, gain_moe).astype(jnp.bfloat16)

    mid_all = gather(normed_mid, by_stream).reshape(wt_size, seq_len, model_width)
    cot_all = gather(out_grad[0], by_stream).reshape(wt_size, seq_len, model_width)
    logits = matmul(normed_mid, router_full)
    logit_exp = jnp.exp(logits - jnp.max(logits, axis=-1, keepdims=True))
    router_probs = logit_exp / jnp.sum(logit_exp, axis=-1, keepdims=True)
    chosen_total = jnp.sum(hits_float * router_probs, axis=1, keepdims=True)
    gate_kept = jnp.where(kept, router_probs / chosen_total, 0.0)
    gate_mine = exchange(to_owner_rows(gate_kept), by_stream).reshape(wt_size, seq_len)

    def pick_rows(table):
        return (
            jnp.einsum("wkt,wtd->wkd", place_low, table, preferred_element_type=jnp.float32)
            .astype(jnp.bfloat16)
            .reshape(wt_size * capacity, model_width)
        )

    filled = pick_rows(mid_all)
    gate_h = matmul(filled, expert_gate[0])
    up_h = matmul(filled, expert_up[0])
    sigma_h = jax.nn.sigmoid(gate_h)
    hidden_h = (gate_h * sigma_h * up_h).astype(jnp.bfloat16)
    result_rows = matmul(hidden_h, expert_down[0]).astype(jnp.bfloat16)
    cot_rows = pick_rows(cot_all)
    gate_rows = jnp.sum(jnp.where(place, gate_mine[:, None, :], 0.0), axis=2).reshape(-1)
    gate_cot_rows = jnp.sum(
        result_rows.astype(jnp.float32) * cot_rows.astype(jnp.float32), axis=1
    ).reshape(wt_size, capacity)
    gate_cot_mine = jnp.sum(jnp.where(place, gate_cot_rows[:, :, None], 0.0), axis=1)
    out_rows_cot = (gate_rows[:, None] * cot_rows.astype(jnp.float32)).astype(jnp.bfloat16)
    hidden_cot = contract_cols(out_rows_cot, expert_down[0])
    grad_down = contract_rows(hidden_h, out_rows_cot)
    gate_cot_h = (hidden_cot * up_h * sigma_h * (1.0 + gate_h * (1.0 - sigma_h))).astype(
        jnp.bfloat16
    )
    up_cot_h = (hidden_cot * gate_h * sigma_h).astype(jnp.bfloat16)
    grad_gate = contract_rows(filled, gate_cot_h)
    grad_up = contract_rows(filled, up_cot_h)
    in_rows_cot = (
        contract_cols(gate_cot_h, expert_gate[0]) + contract_cols(up_cot_h, expert_up[0])
    ).astype(jnp.bfloat16)

    def to_tokens(rows):
        sent = jnp.einsum(
            "wjk,wkd->wjd",
            send_low,
            rows.reshape(wt_size, capacity, model_width),
            preferred_element_type=jnp.float32,
        ).astype(jnp.bfloat16)
        return exchange(
            sent.reshape(devices, send_slots, model_width), by_stream
        ).reshape(devices * send_slots, model_width)

    gate_cot = from_owner_rows(exchange(gate_cot_mine.reshape(devices, tokens), by_stream))
    returned_cot = to_tokens(in_rows_cot)
    returned = to_tokens(result_rows)

    def by_source(table):
        return table.reshape(tokens, ctx_size, wt_size).transpose(0, 2, 1).reshape(tokens, devices)

    where_kept = by_source(jnp.where(kept, local_rank, -1))[:, :, None] == send_ids[None, None, :]
    take = where_kept.astype(jnp.bfloat16).reshape(tokens, devices * send_slots)
    gates_wide = jnp.where(where_kept, by_source(gate_kept)[:, :, None], 0.0).reshape(
        tokens, devices * send_slots
    )
    gates_high = lax.reduce_precision(gates_wide, 8, 7)
    gates_low = (gates_wide - gates_high).astype(jnp.bfloat16)
    hidden_out = (
        resid_mid + matmul(gates_high.astype(jnp.bfloat16), returned) + matmul(gates_low, returned)
    )
    out_cot = out_grad[0].astype(jnp.float32)

    kept_cot = gate_cot * keep_float
    chosen_cot = kept_cot / chosen_total - jnp.sum(
        kept_cot * router_probs, axis=1, keepdims=True
    ) / (chosen_total * chosen_total)
    probs_cot = hits_float * chosen_cot
    logit_cot = (
        router_probs * (probs_cot - jnp.sum(router_probs * probs_cot, axis=1, keepdims=True))
    ).astype(jnp.bfloat16)
    mid_cot = matmul(take, returned_cot) + contract_cols(logit_cot, router_full)
    mid_norm_cot, gain_moe_terms = norm_back(resid_mid, gain_moe, mid_cot)
    resid_cot = out_cot + mid_norm_cot
    attn_cot = resid_cot.astype(jnp.bfloat16)
    router_parts = exchange(
        contract_rows(normed_mid, logit_cot).reshape(devices, -1), both
    )
    grad_w_router = jnp.sum(router_parts, axis=0).reshape(w_router.shape)

    def column_blocks(value):
        width = value.shape[1] // ctx_size
        blocks = value.reshape(tokens, ctx_size, width).transpose(1, 0, 2)
        return exchange(blocks, "ctx").reshape(seq_len, width)

    mixed_cot = contract_cols(attn_cot, out_full)
    attn_cot_all = gather(attn_cot, "ctx")
    mixed_columns = column_blocks(mixed_low)
    grad_w_out = lax.psum_scatter(
        contract_rows(mixed_columns, attn_cot_all).astype(jnp.bfloat16),
        "wt",
        scatter_dimension=0,
        tiled=True,
    ).astype(jnp.float32)

    cot_grouped = mixed_cot.astype(jnp.bfloat16).reshape(tokens, key_heads, group_width, head_dim)
    row_delta = jnp.sum(cot_grouped.astype(jnp.float32) * mixed, axis=-1).transpose(1, 2, 0)

    def back_step(query_cot, block_index):
        scores, allowed, key_block, value_block = block_scores(block_index)
        weights = jnp.where(allowed, jnp.exp(scores - log_total[..., None]), 0.0)
        value_cot = jnp.einsum(
            "kgqs,qkgd->skd",
            weights.astype(jnp.bfloat16),
            cot_grouped,
            preferred_element_type=jnp.float32,
        )
        weight_cot = jnp.einsum(
            "qkgd,skd->kgqs", cot_grouped, value_block, preferred_element_type=jnp.float32
        )
        score_cot = (weights * (weight_cot - row_delta[..., None])).astype(jnp.bfloat16)
        query_cot = (
            query_cot
            + jnp.einsum("kgqs,skd->qkgd", score_cot, key_block, preferred_element_type=jnp.float32)
            * score_scale
        )
        key_cot = (
            jnp.einsum(
                "kgqs,qkgd->skd", score_cot, head_grouped, preferred_element_type=jnp.float32
            )
            * score_scale
        )
        return (
            query_cot,
            jnp.concatenate(
                [key_cot.reshape(block_rows, kv_width), value_cot.reshape(block_rows, kv_width)],
                axis=1,
            ).astype(jnp.bfloat16),
        )

    query_cot, pair_cots = lax.scan(
        back_step,
        jnp.zeros((tokens, key_heads, group_width, head_dim), jnp.float32),
        jnp.arange(block_count),
    )
    pair_mine = lax.psum_scatter(
        pair_cots.reshape(seq_len, 2 * kv_width), "ctx", scatter_dimension=0, tiled=True
    )
    key_mine = pair_mine[:, :kv_width].astype(jnp.float32)
    value_cot_low = pair_mine[:, kv_width:]
    query_pre, gain_query_terms = norm_back(
        query_sum,
        gain_query,
        rotate(query_cot.reshape(tokens, query_heads, head_dim), cosine_table, -sine_table),
    )
    key_pre, gain_key_terms = norm_back(
        key_sum,
        gain_key,
        rotate(key_mine.reshape(tokens, key_heads, head_dim), cosine_table, -sine_table),
    )
    query_cot_low = query_pre.reshape(tokens, q_width).astype(jnp.bfloat16)
    key_cot_low = key_pre.reshape(tokens, kv_width).astype(jnp.bfloat16)
    pair_cot_low = jnp.concatenate([key_cot_low, value_cot_low], axis=1)

    normed_in_all = gather(normed_in, "ctx")

    def weight_grad(cots):
        width = cots.shape[1] // ctx_size
        block = contract_rows(normed_in_all, column_blocks(cots)).astype(jnp.bfloat16)
        block = block.reshape(ctx_size, wt_size, -1, width).transpose(1, 0, 2, 3)
        mine = lax.psum_scatter(
            block.reshape(model_width, width), "wt", scatter_dimension=0, tiled=True
        )
        rows = exchange(mine.reshape(ctx_size, -1, width), "ctx")
        return rows.transpose(1, 0, 2).reshape(-1, width * ctx_size).astype(jnp.float32)

    grad_w_query = weight_grad(query_cot_low)
    grad_pair = weight_grad(pair_cot_low)
    grad_w_key = grad_pair[:, :kv_width]
    grad_w_value = grad_pair[:, kv_width:]
    in_cot = contract_cols(query_cot_low, query_full) + contract_cols(
        pair_cot_low, side_weights[:, : 2 * kv_width]
    )
    in_norm_cot, gain_attn_terms = norm_back(resid_in, gain_attn, in_cot)
    grad_in = resid_cot + in_norm_cot
    gains = sum_everywhere(
        jnp.concatenate(
            [
                jnp.sum(gain_attn_terms, axis=0),
                jnp.sum(gain_query_terms, axis=(0, 1)),
                jnp.sum(gain_key_terms, axis=(0, 1)),
                jnp.sum(gain_moe_terms, axis=0),
            ]
        )
    )
    grad_gain_attn = gains[:model_width]
    grad_gain_query = gains[model_width : model_width + head_dim]
    grad_gain_key = gains[model_width + head_dim : model_width + 2 * head_dim]
    grad_gain_moe = gains[model_width + 2 * head_dim :]
    return (
        hidden_out[None],
        grad_in[None],
        grad_gain_attn,
        grad_w_query,
        grad_w_key,
        grad_w_value,
        grad_gain_query,
        grad_gain_key,
        grad_w_out,
        grad_gain_moe,
        grad_w_router,
        grad_gate[None],
        grad_up[None],
        grad_down[None],
    )


def solution(mesh):
    in_specs = (
        P("wt", "ctx", None),
        P("wt", None),
        P("wt", "ctx", None),
        P(),
        P(("ctx", "wt"), None),
        P(("ctx", "wt"), None),
        P(("ctx", "wt"), None),
        P(),
        P(),
        P(("ctx", "wt"), None),
        P(),
        P(("ctx", "wt"), None),
        P(("ctx", "wt"), None, None),
        P(("ctx", "wt"), None, None),
        P(("ctx", "wt"), None, None),
        P("wt", "ctx", None),
    )
    out_specs = (
        P("wt", "ctx", None),
        P("wt", "ctx", None),
        P(),
        P(("ctx", "wt"), None),
        P(("ctx", "wt"), None),
        P(("ctx", "wt"), None),
        P(),
        P(),
        P(("ctx", "wt"), None),
        P(),
        P(("ctx", "wt"), None),
        P(("ctx", "wt"), None, None),
        P(("ctx", "wt"), None, None),
        P(("ctx", "wt"), None, None),
    )
    return jax.shard_map(
        on_device, mesh=mesh, in_specs=in_specs, out_specs=out_specs, check_vma=False
    )
```

time: 3130 us -> 1310 us (0.42)
  waiting for transfers between devices: 2270 us -> 879 us
  blocking collectives: 314 us -> 8.24 us
  local copies, waits for them, and re-layouts: 193 us -> 84.8 us
  other arithmetic: 97.4 us -> 51.6 us
    reduce_scatter x4, waiting for transfers between devices: 1570 us -> 10.7 us  [the longest x1 10.7 us: on_device(): lax.psum_scatter(pair_cots.reshape(seq_len, 2 * kv_width), 'ctx', scatter...]
    all_gather x6 -> x8, waiting for transfers between devices: 219 us -> 490 us  [gather(): return lax.all_gather(value, axes, axis=0, tiled=True)]
    all_to_all x1 -> x0, blocking collectives: 191 us -> none  [on_device(): lax.all_to_all(from_expert(jnp.stack(back_cots)), ('ctx', 'wt'), split_ax...]
    all_to_all x4 -> x12, waiting for transfers between devices: 479 us -> 376 us  [the longest x11 368 us: exchange(): return lax.all_to_all(value, axes, split_axis=0, concat_axis=0, tiled=True)]
    all_gather x1 -> x0, blocking collectives: 70.6 us -> none  [on_device(): lax.all_gather(w_router, ('ctx', 'wt'), axis=0, tiled=True)]
    gather x4 -> x0, local copies, waits for them, and re-layouts: 64.7 us -> none  [the longest x2 26.5 us: to_pairs(): returned.reshape(expert_count * send_slots, model_width)[send_pos]]
    scatter x4 -> x0, local copies, waits for them, and re-layouts: 48.1 us -> none  [the longest x1 16.1 us: on_device(): filled = jnp.zeros((cap_rows, model_width), jnp.bfloat16).at[dest_rows].s...]
    psum x1 -> x0, blocking collectives: 45.4 us -> none  [on_device(): lax.psum((jnp.sum(gain_attn_terms, axis=0), jnp.sum(gain_query_terms, axi...]
  transfers between devices with their start and end apart: 14 -> 24, of which waited for: 11 -> 19; matrix products, arithmetic and copies ran while one was open for 8% -> 17% of each run, Pallas kernels for 0% -> 0%
where the time goes in v1:
time: 1310 us; the launch traced here: 1300 us
  waiting for transfers between devices  879 us (67%)
  matrix products  215 us (16%)
  local copies, waits for them, and re-layouts  84.8 us (6%)
  other arithmetic  51.6 us (4%)
  starting transfers between devices  42.3 us (3%)
  between operations  16.3 us (1%)
    all_gather x8, waiting for transfers between devices, gather(): return lax.all_gather(value, axes, axis=0, tiled=True)  490 us
    all_to_all x11, waiting for transfers between devices, exchange(): return lax.all_to_all(value, axes, split_axis=0, concat_axis=0, tiled=True)  368 us
    dot_general x11, matrix products, matmul(): return jnp.dot(left_side, right_side, preferred_element_type=jnp.float32)  52.6 us
    dot_general x7, matrix products, contract_cols(): lax.dot_general(left_side, right_side, (((1,), (1,)), ((), ())), preferre...  43.8 us
    all_to_all x11, starting transfers between devices, exchange(): return lax.all_to_all(value, axes, split_axis=0, concat_axis=0, tiled=True)  38.1 us
    dot_general x7, matrix products, contract_rows(): lax.dot_general(left_side, right_side, (((0,), (0,)), ((), ())), preferre...  31.9 us
    dot_general x3, local copies, waits for them, and re-layouts, matmul(): return jnp.dot(left_side, right_side, preferred_element_type=jnp.float32)  29.6 us
  transfers between devices with their start and end apart: 24, of which 19 were waited for; matrix products, arithmetic and copies ran while one was open for 17% of the time, Pallas kernels for 0%

profile of v1, /device:TPU:0, one launch (start us, length us, event | category | flops | bytes accessed | tf_op | source)
XLA Modules:
  0.0 1301.8 jit_solution(2163464706377161490)
XLA Ops:
  14.1 63.6 %all-gather.11.cloned.1.call-done = bf16[2048,1152]{1,0:T(8,128)(2,1)} async-done(((bf16[64,1152]{1,0:T(8,128)(2,1)}), bf16[2048,1152]{1,0:T(8,128)(2,1)}) %all-gather.11.cloned.1.call-update) | async-done | bytes 4718608 | tf_op jit(solution)/shard_map/all_gather | solution.py:111
  80.8 3.9 copy.277
  93.8 23.7 %all-gather.13.cloned.1.call-done = bf16[1024,1024]{1,0:T(8,128)(2,1)} async-done(((bf16[128,1024]{1,0:T(8,128)(2,1)}), bf16[1024,1024]{1,0:T(8,128)(2,1)}) %all-gather.13.cloned.1.call-update) | async-done | bytes 2097168 | tf_op jit(solution)/shard_map/all_gather | solution.py:111
  124.9 109.9 %all-gather.15.cloned.1.call-done = bf16[2048,4096]{1,0:T(8,128)(2,1)} async-done(((bf16[64,4096]{1,0:T(8,128)(2,1)}), bf16[2048,4096]{1,0:T(8,128)(2,1)}) %all-gather.15.cloned.1.call-update) | async-done | bytes 16777232 | tf_op jit(solution)/shard_map/all_gather | solution.py:111
  234.8 22.7 %copy.279 = bf16[4096,2048]{1,0:T(8,128)(2,1)} copy(bf16[4096,2048]{0,1:T(8,128)(2,1)} %bitcast.420) | data formatting | bytes 33554432 | tf_op jit(solution)/shard_map/dot_general | solution.py:46
  257.5 8.4 multiply_reduce_fusion.3
  271.1 26.3 %while.37 = (s32[]{:T(128)}, f32[4,8,128]{2,1,0:T(8,128)S(1)}, f32[4,8,128]{2,1,0:T(8,128)S(1)}, s32[2]{0:T(128)S(1)}, s32[1024]{0:T(1024)S(1)}, /*index=5*/s32[...) while((s32[]{:T(128)}, f32[4,8,128]{2,1,0:T(8,128)S(1)}, ...), condition=%wide.region_8.9_spmd.clone, body=%wide.region_5.8_spmd.clone.sunk | while | flops 553865856 | bytes 19820240 | solution.py:221
  273.7 5.9 fusion.220
  279.6 4.5 select_reduce_fusion.5
  286.9 5.9 fusion.220
  292.8 4.5 select_reduce_fusion.5
  297.4 20.0 %while.38 = (s32[]{:T(128)}, f32[128,4,8,128]{0,3,2,1:T(8,128)}, s32[2]{0:T(128)S(1)}, bf16[1024,512]{0,1:T(8,128)(2,1)}, s32[1024]{0:T(1024)S(1)}, /*index=5*/s...) while((s32[]{:T(128)}, f32[128,4,8,128]{0,3,2,1:T(8,128)}, ...), condition=%wide.region_10.11_spmd.clone, body=%wide.region_9.10_spmd.clone.sunk | while | flops 1085473408 | bytes 8548057 | solution.py:241
  301.2 5.7 bitcast_add_fusion.4
  310.8 6.4 bitcast_add_fusion.4
  320.1 30.1 %all-gather.17.cloned.1.call-done = bf16[4096,2048]{1,0:T(8,128)(2,1)} async-done(((bf16[128,2048]{1,0:T(8,128)(2,1)}), bf16[4096,2048]{1,0:T(8,128)(2,1)}) %all-gather.17.cloned.1.call-update) | async-done | bytes 16777232 | tf_op jit(solution)/shard_map/all_gather | solution.py:111
  350.3 8.6 multiply_reduce_fusion.6
  366.5 8.2 all-reduce.1
  381.0 92.6 %all-gather.19.cloned.1.call-done = bf16[4096,2048]{1,0:T(8,128)(2,1)} async-done(((bf16[128,2048]{1,0:T(8,128)(2,1)}), bf16[4096,2048]{1,0:T(8,128)(2,1)}) %all-gather.19.cloned.1.call-update) | async-done | bytes 16777232 | tf_op jit(solution)/shard_map/all_gather | solution.py:111
  473.6 10.6 fusion.49
  484.2 3.4 fusion.59
  487.7 5.2 multiply_convert_fusion.2
  494.0 5.3 convolution_convert_fusion.3
  499.4 89.8 %all-gather.25.cloned.1.call-done = bf16[1,4096,2048]{2,1,0:T(8,128)(2,1)} async-done(((bf16[1,128,2048]{2,1,0:T(8,128)(2,1)}), bf16[1,4096,2048]{2,1,0:T(8,128)(2,1)}) %all-gather.25.cloned.1.call-update) | async-done | bytes 16777232 | tf_op jit(solution)/shard_map/all_gather | solution.py:111
  589.1 13.7 %fusion.43 = (f32[1024]{0:T(1024)S(1)}, bf16[4,256,2048]{2,1,0:T(8,128)(2,1)}) fusion(bf16[1024,2048]{1,0:T(8,128)(2,1)} %convolution_convert_fusion.3, bf16[4,1024,2048]{2,1,0:T(8,128)(2,1)} %bitcast.423, s32[4,1024]{1,0:T(4,128)S(1)} %and_select_fusion), kind=kOutput, calls=%fused_computation.60 | convolution fusion | flops 4306500608 | bytes 25186304 | tf_op jit(solution)/shard_map/wkt,wtd->wkd/dot_general | solution.py:261
  607.1 7.1 all-to-all-done.4
  617.7 7.2 all-to-all-done.2
  630.8 4.4 multiply_convert_fusion
  635.2 3.4 fusion.57
  638.7 3.7 add_convert_fusion
  642.4 4.6 convolution_convert_fusion
  647.0 3.7 all-to-all-start.3
  651.1 185.6 %all-to-all-done.3 = bf16[32,64,2048]{2,1,0:T(8,128)(2,1)} async-done(((bf16[32,64,2048]{2,1,0:T(8,128)(2,1)}), bf16[32,64,2048]{2,1,0:T(8,128)(2,1)}, u32[]{:S(2)}, u32[]{:S(2)}) %all-to-all-start.3) | async-done | bytes 8388640 | tf_op jit(solution)/shard_map/all_to_all | solution.py:114
  836.7 4.8 convolution_bitcast_fusion.4
  844.7 12.4 convolution_convert_fusion.2
  861.1 36.0 %while.39 = (s32[]{:T(128)}, f32[128,4,8,128]{0,3,2,1:T(8,128)}, bf16[2,512,1024]{2,1,0:T(8,128)(2,1)}, s32[2]{0:T(128)S(1)}, bf16[1024,512]{0,1:T(8,128)(2,1)},...) while((s32[]{:T(128)}, f32[128,4,8,128]{0,3,2,1:T(8,128)}, ...), condition=%wide.region_31.32_spmd.clone, body=%wide.region_30.31_spmd.clone.sunk | while | flops 2714173952 | bytes 86765936 | solution.py:388
  874.2 4.6 bitcast_add_fusion.5
  891.9 5.2 bitcast_add_fusion.5
  897.9 4.4 all-to-all-start.10
  909.8 8.0 all-to-all-done.10
  924.6 10.7 reduce-scatter.5.cloned.1.call-done
  936.4 3.6 all-to-all-start.6
  941.2 19.7 %all-to-all-done.6 = bf16[8,128,512]{2,1,0:T(8,128)(2,1)S(1)} async-done(((bf16[8,128,512]{2,1,0:T(8,128)(2,1)}), bf16[8,128,512]{2,1,0:T(8,128)(2,1)S(1)}, u32[]{:S(2)}, u32[]{:S(2)}) %all-to-all-start.6) | async-done | bytes 1048608 | tf_op jit(solution)/shard_map/all_to_all | solution.py:114
  960.9 3.6 all-to-all-start.8
  964.5 7.6 convolution_convert_fusion.1
  974.2 4.0 all-to-all-start.1
  979.0 4.7 all-gather.21.cloned.1.call-done
  983.8 3.5 convolution_convert_fusion.6
  988.2 4.6 convolution_convert_fusion.5
  999.8 5.5 convolution_bitcast_fusion.2
  1005.2 5.5 convolution_bitcast_fusion.3
  1010.7 5.6 convolution_bitcast_fusion.1
  1017.2 75.5 %all-gather.23.cloned.1.call-done = bf16[1024,2048]{1,0:T(8,128)(2,1)} async-done(((bf16[128,2048]{1,0:T(8,128)(2,1)}), bf16[1024,2048]{1,0:T(8,128)(2,1)}) %all-gather.23.cloned.1.call-update) | async-done | bytes 4194320 | tf_op jit(solution)/shard_map/all_gather | solution.py:111
  1092.7 6.0 convolution_convert_fusion.4
  1098.7 124.7 %all-to-all-done.1 = bf16[32,64,2048]{2,1,0:T(8,128)(2,1)} async-done(((bf16[32,64,2048]{2,1,0:T(8,128)(2,1)}), bf16[32,64,2048]{2,1,0:T(8,128)(2,1)}, u32[]{:S(2)}, u32[]{:S(2)}) %all-to-all-start.1) | async-done | bytes 8388640 | tf_op jit(solution)/shard_map/all_to_all | solution.py:114
  1223.4 4.7 fusion.64
  1228.2 12.6 fusion.141
  1240.8 5.1 fusion.89
  1247.1 3.3 all-to-all-start.5
  1250.5 5.8 fusion.66
  1258.0 7.3 all-to-all-done.5
  1267.3 3.7 all-to-all-start.9
  1271.5 5.0 all-to-all-done.9
  1276.5 4.1 all-to-all-start.7
  1281.4 9.0 all-to-all-done.7
  (367 shorter events, 143.8 us)
Async XLA Ops:
  7.2 486.9 %copy-start = (bf16[1,768,2048]{2,1,0:T(8,128)(2,1)S(1)}, bf16[1,768,2048]{2,1,0:T(8,128)(2,1)}, u32[]{:S(2)}) copy-start(bf16[1,768,2048]{2,1,0:T(8,128)(2,1)} %param.36) | copy-start | bytes 9437188
  7.2 70.5 %all-gather.11.cloned.1.call-start = ((), (), s32[]{:S(2)}) async-start(), calls=%async_computation.16 | async-start | bytes 4866048 | tf_op jit(solution)/shard_map/all_gather | solution.py:111
  9.8 107.7 %all-gather.13.cloned.1.call-start = ((), (), s32[]{:S(2)}) async-start(), calls=%async_computation.17 | async-start | bytes 2359296 | tf_op jit(solution)/shard_map/all_gather | solution.py:111
  10.8 255.7 %copy-start.24 = (f32[128,128]{0,1:T(8,128)}, f32[128,128]{0,1:T(8,128)S(1)}, u32[]{:S(2)}) copy-start(f32[128,128]{0,1:T(8,128)S(1)} %get-tuple-element.714) | copy-start | bytes 196612
  12.1 72.6 %copy-start.50 = (f32[128]{0:T(128)}, f32[128]{0:T(128)S(1)}, u32[]{:S(2)}) copy-start(f32[128]{0:T(128)S(1)} %add_rsqrt_fusion.3) | copy-start | bytes 1540
  14.1 70.6 %copy-start.36 = (f32[2048]{0:T(1024)S(1)}, f32[2048]{0:T(1024)}, u32[]{:S(2)}) copy-start(f32[2048]{0:T(1024)} %param.25) | copy-start | bytes 24580
  80.8 6.5 copy-start.46
  91.2 143.6 %all-gather.15.cloned.1.call-start = ((), (), s32[]{:S(2)}) async-start(), calls=%async_computation.18 | async-start | bytes 17301504 | tf_op jit(solution)/shard_map/all_gather | solution.py:111
  91.9 258.3 %all-gather.17.cloned.1.call-start = ((), (), s32[]{:S(2)}) async-start(), calls=%async_computation.19 | async-start | bytes 17301504 | tf_op jit(solution)/shard_map/all_gather | solution.py:111
  92.5 381.0 %all-gather.19.cloned.1.call-start = ((), (), s32[]{:S(2)}) async-start(), calls=%async_computation.20 | async-start | bytes 17301504 | tf_op jit(solution)/shard_map/all_gather | solution.py:111
  234.8 22.7 %copy-start.37 = (f32[2048]{0:T(1024)S(1)}, f32[2048]{0:T(1024)}, u32[]{:S(2)}) copy-start(f32[2048]{0:T(1024)} %param.25) | copy-start | bytes 24580
  234.8 22.7 %copy-start.51 = (f32[128]{0:T(128)S(1)}, f32[128]{0:T(128)}, u32[]{:S(2)}) copy-start(f32[128]{0:T(128)} %copy-done.50) | copy-start | bytes 1540
  257.5 8.4 copy-start.48
  350.3 9.6 copy-start.34
  350.3 11.2 copy-start.53
  350.3 14.7 %copy-start.62 = (u32[32]{0:T(128)S(1)}, u32[32]{0:T(128)}, u32[]{:S(2)}) copy-start(u32[32]{0:T(128)} %constant.132) | copy-start | bytes 388
  358.9 484.9 %copy-start.44 = (f32[128]{0:T(128)}, f32[128]{0:T(128)S(1)}, u32[]{:S(2)}) copy-start(f32[128]{0:T(128)S(1)} %add_rsqrt_fusion.2) | copy-start | bytes 1540
  360.8 228.3 %all-gather.25.cloned.1.call-start = ((), (), s32[]{:S(2)}) async-start(), calls=%async_computation.27 | async-start | bytes 17301504 | tf_op jit(solution)/shard_map/all_gather | solution.py:111
  362.2 13.2 %all-to-all-start = ((s32[32,1,128]{2,1,0:T(1,128)}), s32[32,1,128]{2,1,0:T(1,128)S(1)}, u32[]{:S(2)}, u32[]{:S(2)}) async-start(s32[32,1,128]{2,1,0:T(1,128)} %bitcast.23), calls=%async_computation | async-start | bytes 32768 | tf_op jit(solution)/shard_map/all_to_all | solution.py:114
  473.6 10.7 copy-start.56
  604.2 9.9 all-to-all-start.4
  614.9 10.0 all-to-all-start.2
  647.0 189.7 %all-to-all-start.3 = ((bf16[32,64,2048]{2,1,0:T(8,128)(2,1)}), bf16[32,64,2048]{2,1,0:T(8,128)(2,1)}, u32[]{:S(2)}, u32[]{:S(2)}) async-start(bf16[32,64,2048]{2,1,0:T(8,128)(2,1)} %bitcast.422), calls=%async_computation.3 | async-start | bytes 16777216 | tf_op jit(solution)/shard_map/all_to_all | solution.py:114
  650.7 284.6 %reduce-scatter.5.cloned.1.call-start = ((), (), s32[]{:S(2)}) async-start(), calls=%async_computation.21 | async-start | bytes 2359296 | tf_op jit(solution)/shard_map/reduce_scatter | solution.py:393
  651.1 190.5 %copy-start.28 = (s32[128,4,8]{0,2,1:T(8,128)}, s32[128,4,8]{0,2,1:T(8,128)S(1)}, u32[]{:S(2)}) copy-start(s32[128,4,8]{0,2,1:T(8,128)S(1)} %copy.359) | copy-start | bytes 49156
  836.7 7.1 copy-start.17
  843.8 13.4 %copy-start.54 = (f32[128]{0:T(128)}, f32[128]{0:T(128)S(1)}, u32[]{:S(2)}) copy-start(f32[128]{0:T(128)S(1)} %broadcast_multiply_fusion.4) | copy-start | bytes 1540
  844.1 13.0 copy-start.19
  861.1 9.3 copy-start.20
  878.8 9.3 copy-start.20
  897.1 9.0 copy-start.3
  897.2 86.6 %all-gather.21.cloned.1.call-start = ((), (), s32[]{:S(2)}) async-start(), calls=%async_computation.22 | async-start | bytes 4718592 | tf_op jit(solution)/shard_map/all_gather | solution.py:111
  897.9 8.4 copy-start.25
  897.9 8.4 copy-start.31
  897.9 8.4 copy-start.33
  897.9 8.4 copy-start.49
  897.9 19.8 %all-to-all-start.10 = ((bf16[8,128,512]{1,2,0:T(8,128)(2,1)}), bf16[8,128,512]{1,2,0:T(8,128)(2,1)}, u32[]{:S(2)}, u32[]{:S(2)}) async-start(bf16[8,128,512]{1,2,0:T(8,128)(2,1)} %bitcast.431), calls=%async_computation.13 | async-start | bytes 2097152 | tf_op jit(solution)/shard_map/all_to_all | solution.py:114
  917.8 18.6 %all-to-all-start.11 = ((f32[32,1,2048]{2,1,0:T(1,128)}), f32[32,1,2048]{2,1,0:T(1,128)S(1)}, u32[]{:S(2)}, u32[]{:S(2)}) async-start(f32[32,1,2048]{2,1,0:T(1,128)} %all_to_all.65), calls=%async_computation.15 | async-start | bytes 524288 | tf_op jit(solution)/shard_map/all_to_all | solution.py:114
  923.3 16.8 %copy-start.23 = (f32[128,4,128]{0,2,1:T(8,128)S(1)}, f32[128,4,128]{0,2,1:T(8,128)}, u32[]{:S(2)}) copy-start(f32[128,4,128]{0,2,1:T(8,128)} %copy-done.22) | copy-start | bytes 786436
  923.3 16.8 %copy-start.40 = (f32[128,4]{0,1:T(4,128)S(1)}, f32[128,4]{0,1:T(4,128)}, u32[]{:S(2)}) copy-start(f32[128,4]{0,1:T(4,128)} %copy-done.39) | copy-start | bytes 6148
  923.3 16.8 %copy-start.47 = (f32[128]{0:T(128)S(1)}, f32[128]{0:T(128)}, u32[]{:S(2)}) copy-start(f32[128]{0:T(128)} %param.30) | copy-start | bytes 1540
  936.4 24.5 %all-to-all-start.6 = ((bf16[8,128,512]{2,1,0:T(8,128)(2,1)}), bf16[8,128,512]{2,1,0:T(8,128)(2,1)S(1)}, u32[]{:S(2)}, u32[]{:S(2)}) async-start(bf16[8,128,512]{2,1,0:T(8,128)(2,1)} %bitcast.56), calls=%async_computation.7 | async-start | bytes 2097152 | tf_op jit(solution)/shard_map/all_to_all | solution.py:114
  960.9 13.3 %all-to-all-start.8 = ((bf16[8,128,128]{2,1,0:T(8,128)(2,1)}), bf16[8,128,128]{2,1,0:T(8,128)(2,1)S(1)}, u32[]{:S(2)}, u32[]{:S(2)}) async-start(bf16[8,128,128]{2,1,0:T(8,128)(2,1)} %bitcast_bitcast_fusion), calls=%async_computation.10 | async-start | bytes 524288 | tf_op jit(solution)/shard_map/all_to_all | solution.py:114
  974.2 249.2 %all-to-all-start.1 = ((bf16[32,64,2048]{2,1,0:T(8,128)(2,1)}), bf16[32,64,2048]{2,1,0:T(8,128)(2,1)}, u32[]{:S(2)}, u32[]{:S(2)}) async-start(bf16[32,64,2048]{2,1,0:T(8,128)(2,1)} %bitcast.421), calls=%async_computation.1 | async-start | bytes 16777216 | tf_op jit(solution)/shard_map/all_to_all | solution.py:114
  978.2 114.4 %all-gather.23.cloned.1.call-start = ((), (), s32[]{:S(2)}) async-start(), calls=%async_computation.25 | async-start | bytes 4718592 | tf_op jit(solution)/shard_map/all_gather | solution.py:111
  979.0 288.3 %reduce-scatter.9.cloned.1.call-start = ((), (), s32[]{:S(2)}) async-start(), calls=%async_computation.24 | async-start | bytes 655360 | tf_op jit(solution)/shard_map/reduce_scatter | solution.py:418
  988.2 288.3 %reduce-scatter.7.cloned.1.call-start = ((), (), s32[]{:S(2)}) async-start(), calls=%async_computation.23 | async-start | bytes 2621440 | tf_op jit(solution)/shard_map/reduce_scatter | solution.py:418
  994.2 298.3 %reduce-scatter.11.cloned.1.call-start = ((), (), s32[]{:S(2)}) async-start(), calls=%async_computation.26 | async-start | bytes 2621440 | tf_op jit(solution)/shard_map/reduce_scatter | solution.py:346
  1092.7 130.7 %copy-start.10 = (f32[128,2048]{1,0:T(8,128)S(1)}, f32[128,2048]{1,0:T(8,128)}, u32[]{:S(2)}) copy-start(f32[128,2048]{1,0:T(8,128)} %copy-done.8) | copy-start | bytes 3145732
  1092.7 130.7 %copy-start.29 = (s32[128,4,8]{0,2,1:T(8,128)S(1)}, s32[128,4,8]{0,2,1:T(8,128)}, u32[]{:S(2)}) copy-start(s32[128,4,8]{0,2,1:T(8,128)} %copy-done.28) | copy-start | bytes 49156
  1228.2 12.6 copy-start.12
  1228.2 12.6 copy-start.38
  1228.2 12.6 copy-start.52
  1247.1 18.2 %all-to-all-start.5 = ((f32[32,1,4352]{2,1,0:T(1,128)}), f32[32,1,4352]{2,1,0:T(1,128)}, u32[]{:S(2)}, u32[]{:S(2)}) async-start(f32[32,1,4352]{2,1,0:T(1,128)} %broadcast_in_dim.209), calls=%async_computation.6 | async-start | bytes 1114112 | tf_op jit(solution)/shard_map/all_to_all | solution.py:65
  1250.4 5.9 copy-start.11
  1250.4 5.9 copy-start.13
  1250.4 5.9 copy-start.15
  1250.4 5.9 copy-start.18
  1250.4 5.9 copy-start.30
  1250.5 5.9 copy-start.35
  1250.5 5.9 copy-start.45
  1256.4 38.3 %copy-start.1 = (bf16[1,768,2048]{2,1,0:T(8,128)(2,1)S(1)}, bf16[1,768,2048]{2,1,0:T(8,128)(2,1)}, u32[]{:S(2)}) copy-start(bf16[1,768,2048]{2,1,0:T(8,128)(2,1)} %param.36) | copy-start | bytes 9437188
  1267.3 9.2 all-to-all-start.9
  1276.5 13.9 %all-to-all-start.7 = ((bf16[8,64,512]{2,1,0:T(8,128)(2,1)}), bf16[8,64,512]{2,1,0:T(8,128)(2,1)}, u32[]{:S(2)}, u32[]{:S(2)}) async-start(bf16[8,64,512]{2,1,0:T(8,128)(2,1)} %bitcast.452), calls=%async_computation.9 | async-start | bytes 1048576 | tf_op jit(solution)/shard_map/all_to_all | solution.py:114
  (34 other events, 120.6 us)
Sparse Core Ops, SparseCore 0:
  11.4 66.2 all-gather.10
  91.3 26.0 all-gather.12
  120.4 114.3 all-gather.14
  237.7 112.5 all-gather.16
  361.0 112.5 all-gather.18
  476.3 112.8 all-gather.24
  897.3 37.9 reduce-scatter.4
  937.2 46.5 all-gather.20
  985.7 106.9 all-gather.22
  1094.8 39.2 reduce-scatter.8
  1136.4 50.3 reduce-scatter.6
  1189.0 54.1 reduce-scatter.10

commit v2 on v1

v2 whole, which is shorter than its diff:
```python
import functools
import math

import jax
import jax.numpy as jnp
from jax import lax
from jax.experimental import pallas as pl
from jax.experimental.pallas import tpu as pltpu
from jax.sharding import PartitionSpec as P


EPS = 1e-06
THETA = 1000000.0
MASKED = -1e30


def norm_rows(value_rows, gain_vec):
    return (
        value_rows
        * lax.rsqrt(jnp.mean(value_rows * value_rows, axis=-1, keepdims=True) + EPS)
        * gain_vec
    )


def norm_back(value_rows, gain_vec, upstream):
    factor = lax.rsqrt(jnp.mean(value_rows * value_rows, axis=-1, keepdims=True) + EPS)
    normalized_input = value_rows * factor
    weighted = upstream * gain_vec
    inner_mean = jnp.mean(weighted * normalized_input, axis=-1, keepdims=True)
    return (factor * (weighted - normalized_input * inner_mean), upstream * normalized_input)


def rotary_tables(positions, head_dim):
    half_dim = head_dim // 2
    frequency = jnp.exp(
        jnp.arange(half_dim, dtype=jnp.float32) * (-2.0 * math.log(THETA) / head_dim)
    )
    angles = positions.astype(jnp.float32)[:, None] * frequency[None, :]
    angles = jnp.concatenate([angles, angles], axis=1)
    return (jnp.cos(angles)[:, None, :], jnp.sin(angles)[:, None, :])


def rotate(value_rows, cosine_table, sine_table):
    half_dim = value_rows.shape[-1] // 2
    turned = jnp.concatenate([-value_rows[..., half_dim:], value_rows[..., :half_dim]], axis=-1)
    return value_rows * cosine_table + turned * sine_table


def matmul(left_side, right_side):
    return jnp.dot(left_side, right_side, preferred_element_type=jnp.float32)


def contract_rows(left_side, right_side):
    return lax.dot_general(
        left_side, right_side, (((0,), (0,)), ((), ())), preferred_element_type=jnp.float32
    )


def contract_cols(left_side, right_side):
    return lax.dot_general(
        left_side, right_side, (((1,), (1,)), ((), ())), preferred_element_type=jnp.float32
    )


def after(value, earlier):
    return lax.optimization_barrier((value, earlier))[0]


def stack_heads(block, first, head_dim, count):
    return jnp.concatenate(
        [block[:, (first + h) * head_dim : (first + h + 1) * head_dim] for h in range(count)],
        axis=0,
    )


def attend_kernel(
    head_dim,
    together,
    query_ref,
    pairs_ref,
    gain_ref,
    cosine_ref,
    sine_ref,
    query_pos_ref,
    query_doc_ref,
    key_pos_ref,
    key_doc_ref,
    mixed_ref,
    query_low_ref,
    bias_ref,
):
    tokens = query_ref.shape[0]
    heads = query_ref.shape[1] // head_dim
    scale = head_dim ** (-0.5)

    @pl.when(pl.program_id(0) == 0)
    def _():
        allowed = (key_pos_ref[...] <= query_pos_ref[...]) & (
            key_doc_ref[...] == query_doc_ref[...]
        )
        bias_ref[...] = jnp.where(allowed, 0.0, MASKED)

    keys = pairs_ref[:, :head_dim]
    values = pairs_ref[:, head_dim:]
    for first in range(0, heads, together):
        for h in range(first, first + together):
            columns = slice(h * head_dim, (h + 1) * head_dim)
            rows = query_ref[:, columns]
            rows = norm_rows(rows, gain_ref[...])
            turned = pltpu.roll(rows, head_dim // 2, axis=1)
            rows = rows * cosine_ref[...] + turned * sine_ref[...]
            query_low_ref[:, columns] = rows.astype(jnp.bfloat16)
        queries = stack_heads(query_low_ref, first, head_dim, together)
        scores = contract_cols(queries, keys) * scale
        scores = scores + jnp.concatenate([bias_ref[...]] * together, axis=0)
        weights = jnp.exp(scores - jnp.max(scores, axis=1, keepdims=True))
        weights = weights / jnp.sum(weights, axis=1, keepdims=True)
        mixed = matmul(weights.astype(jnp.bfloat16), values)
        for h in range(together):
            columns = slice((first + h) * head_dim, (first + h + 1) * head_dim)
            mixed_ref[:, columns] = mixed[h * tokens : (h + 1) * tokens].astype(jnp.bfloat16)


def attend_back_kernel(
    head_dim,
    together,
    query_ref,
    query_low_ref,
    cot_ref,
    pairs_ref,
    gain_ref,
    cosine_ref,
    sine_ref,
    query_pos_ref,
    query_doc_ref,
    key_pos_ref,
    key_doc_ref,
    query_cot_ref,
    pair_cot_ref,
    gain_cot_ref,
    bias_ref,
    key_sum_ref,
    value_sum_ref,
):
    tokens = query_ref.shape[0]
    heads = query_ref.shape[1] // head_dim
    scale = head_dim ** (-0.5)

    @pl.when(pl.program_id(0) == 0)
    def _():
        allowed = (key_pos_ref[...] <= query_pos_ref[...]) & (
            key_doc_ref[...] == query_doc_ref[...]
        )
        bias_ref[...] = jnp.where(allowed, 0.0, MASKED)

    keys = pairs_ref[:, :head_dim]
    values = pairs_ref[:, head_dim:]
    for first in range(0, heads, together):
        queries = stack_heads(query_low_ref, first, head_dim, together)
        cots = stack_heads(cot_ref, first, head_dim, together)
        scores = contract_cols(keys, queries) * scale
        scores = scores + jnp.concatenate([bias_ref[...]] * together, axis=1)
        weights = jnp.exp(scores - jnp.max(scores, axis=0, keepdims=True))
        weights = weights / jnp.sum(weights, axis=0, keepdims=True)
        weight_cot = contract_cols(values, cots)
        delta = jnp.sum(weights * weight_cot, axis=0, keepdims=True)
        score_cot = (weights * (weight_cot - delta)).astype(jnp.bfloat16)
        value_part = matmul(weights.astype(jnp.bfloat16), cots)
        key_part = matmul(score_cot, queries)
        if first:
            value_sum_ref[...] += value_part
            key_sum_ref[...] += key_part
        else:
            value_sum_ref[...] = value_part
            key_sum_ref[...] = key_part
        query_part = contract_rows(score_cot, keys) * scale
        for h in range(together):
            columns = slice((first + h) * head_dim, (first + h + 1) * head_dim)
            upstream = query_part[h * tokens : (h + 1) * tokens]
            turned = pltpu.roll(upstream, head_dim // 2, axis=1)
            upstream = upstream * cosine_ref[...] - turned * sine_ref[...]
            rows_cot, terms = norm_back(query_ref[:, columns], gain_ref[...], upstream)
            query_cot_ref[:, columns] = rows_cot.astype(jnp.bfloat16)
            gain_cot_ref[first + h : first + h + 1, :] = jnp.sum(terms, axis=0, keepdims=True)
    pair_cot_ref[:, :head_dim] = (key_sum_ref[...] * scale).astype(jnp.bfloat16)
    pair_cot_ref[:, head_dim:] = value_sum_ref[...].astype(jnp.bfloat16)


def attend(query_sum, pairs_all, gain, cosine, sine, query_pos, query_doc, key_pos, key_doc):
    tokens, q_width = query_sum.shape
    seq_len, pair_width = pairs_all.shape
    head_dim = gain.shape[0]
    key_heads = pair_width // (2 * head_dim)
    group = q_width // key_heads
    whole = lambda shape: pl.BlockSpec(shape, lambda g: (0, 0))
    flops = 4 * tokens * seq_len * q_width
    return pl.pallas_call(
        functools.partial(attend_kernel, head_dim, 2),
        grid=(key_heads,),
        in_specs=[
            pl.BlockSpec((tokens, group), lambda g: (0, g)),
            pl.BlockSpec((seq_len, 2 * head_dim), lambda g: (0, g)),
            whole((1, head_dim)),
            whole((tokens, head_dim)),
            whole((tokens, head_dim)),
            whole((tokens, 1)),
            whole((tokens, 1)),
            whole((1, seq_len)),
            whole((1, seq_len)),
        ],
        out_specs=[pl.BlockSpec((tokens, group), lambda g: (0, g))] * 2,
        out_shape=[jax.ShapeDtypeStruct((tokens, q_width), jnp.bfloat16)] * 2,
        scratch_shapes=[pltpu.VMEM((tokens, seq_len), jnp.float32)],
        compiler_params=pltpu.CompilerParams(vmem_limit_bytes=32 << 20),
        cost_estimate=pl.CostEstimate(
            flops=flops, bytes_accessed=8 * tokens * q_width, transcendentals=0
        ),
        name="attend",
    )(
        query_sum,
        pairs_all,
        gain[None, :],
        cosine,
        sine,
        query_pos[:, None],
        query_doc[:, None],
        key_pos[None, :],
        key_doc[None, :],
    )


def attend_back(
    query_sum,
    query_low,
    cots,
    pairs_all,
    gain,
    cosine,
    sine,
    query_pos,
    query_doc,
    key_pos,
    key_doc,
):
    tokens, q_width = query_sum.shape
    seq_len, pair_width = pairs_all.shape
    head_dim = gain.shape[0]
    key_heads = pair_width // (2 * head_dim)
    group = q_width // key_heads
    heads = group // head_dim
    whole = lambda shape: pl.BlockSpec(shape, lambda g: (0, 0))
    flops = 10 * tokens * seq_len * q_width
    return pl.pallas_call(
        functools.partial(attend_back_kernel, head_dim, 2),
        grid=(key_heads,),
        in_specs=[
            pl.BlockSpec((tokens, group), lambda g: (0, g)),
            pl.BlockSpec((tokens, group), lambda g: (0, g)),
            pl.BlockSpec((tokens, group), lambda g: (0, g)),
            pl.BlockSpec((seq_len, 2 * head_dim), lambda g: (0, g)),
            whole((1, head_dim)),
            whole((tokens, head_dim)),
            whole((tokens, head_dim)),
            whole((1, tokens)),
            whole((1, tokens)),
            whole((seq_len, 1)),
            whole((seq_len, 1)),
        ],
        out_specs=[
            pl.BlockSpec((tokens, group), lambda g: (0, g)),
            pl.BlockSpec((seq_len, 2 * head_dim), lambda g: (0, g)),
            pl.BlockSpec((heads, head_dim), lambda g: (g, 0)),
        ],
        out_shape=[
            jax.ShapeDtypeStruct((tokens, q_width), jnp.bfloat16),
            jax.ShapeDtypeStruct((seq_len, pair_width), jnp.bfloat16),
            jax.ShapeDtypeStruct((key_heads * heads, head_dim), jnp.float32),
        ],
        scratch_shapes=[
            pltpu.VMEM((seq_len, tokens), jnp.float32),
            pltpu.VMEM((seq_len, head_dim), jnp.float32),
            pltpu.VMEM((seq_len, head_dim), jnp.float32),
        ],
        compiler_params=pltpu.CompilerParams(vmem_limit_bytes=48 << 20),
        cost_estimate=pl.CostEstimate(
            flops=flops, bytes_accessed=12 * tokens * q_width, transcendentals=0
        ),
        name="attend_back",
    )(
        query_sum,
        query_low,
        cots,
        pairs_all,
        gain[None, :],
        cosine,
        sine,
        query_pos[None, :],
        query_doc[None, :],
        key_pos[:, None],
        key_doc[:, None],
    )


def sum_everywhere(vector):
    devices = lax.axis_size("ctx") * lax.axis_size("wt")
    spread = jnp.broadcast_to(vector[None, :], (devices, vector.shape[0]))
    return jnp.sum(
        lax.all_to_all(spread, ("ctx", "wt"), split_axis=0, concat_axis=0, tiled=True), axis=0
    )


def on_device(
    hidden_in,
    doc_lengths,
    routes,
    gain_attn,
    w_query,
    key_weight,
    value_weight,
    gain_query,
    gain_key,
    w_out,
    gain_moe,
    w_router,
    expert_gate,
    expert_up,
    expert_down,
    out_grad,
):
    tokens = hidden_in.shape[1]
    model_width = hidden_in.shape[2]
    ctx_size = lax.axis_size("ctx")
    wt_size = lax.axis_size("wt")
    devices = ctx_size * wt_size
    seq_len = tokens * ctx_size
    head_dim = gain_query.shape[0]
    kv_width = key_weight.shape[1]
    key_heads = kv_width // head_dim
    expert_count = w_router.shape[1]
    top_count = routes.shape[2]
    assert expert_gate.shape[0] == 1 and expert_count == devices
    capacity = tokens * top_count // wt_size
    ctx_index = lax.axis_index("ctx")
    wt_index = lax.axis_index("wt")
    both = ("ctx", "wt")
    by_stream = ("wt", "ctx")

    def gather(value, axes):
        return lax.all_gather(value, axes, axis=0, tiled=True)

    def exchange(value, axes):
        return lax.all_to_all(value, axes, split_axis=0, concat_axis=0, tiled=True)

    def scatter_sum(value, axes):
        return lax.psum_scatter(value, axes, scatter_dimension=0, tiled=True)

    doc_ends = jnp.cumsum(doc_lengths[0])
    all_positions = jnp.arange(seq_len, dtype=jnp.int32)
    doc_all = jnp.sum((doc_ends[None, :] <= all_positions[:, None]).astype(jnp.int32), axis=1)
    first_pos = ctx_index * tokens
    my_positions = first_pos + jnp.arange(tokens, dtype=jnp.int32)
    my_docs = lax.dynamic_slice_in_dim(doc_all, first_pos, tokens)
    cosine_table, sine_table = rotary_tables(my_positions, head_dim)
    cosine_rows = cosine_table[:, 0, :]
    first_half = jnp.arange(head_dim) < head_dim // 2
    sine_rows = jnp.where(first_half[None, :], -sine_table[:, 0, :], sine_table[:, 0, :])

    expert_ids = jnp.arange(expert_count, dtype=jnp.int32)
    hits = jnp.sum((routes[0][:, :, None] == expert_ids[None, None, :]).astype(jnp.int32), axis=1)
    local_rank = jnp.cumsum(hits, axis=0) - hits
    counts = lax.all_gather(jnp.sum(hits, axis=0), "ctx")
    earlier = jnp.arange(ctx_size, dtype=jnp.int32)[:, None] < ctx_index
    offsets = jnp.sum(jnp.where(earlier, counts, 0), axis=0)
    kept = (hits > 0) & (local_rank + offsets[None, :] < capacity)
    keep_float = kept.astype(jnp.float32)
    hits_float = hits.astype(jnp.float32)

    def to_owner_rows(table):
        return table.reshape(tokens, ctx_size, wt_size).transpose(2, 1, 0).reshape(devices, tokens)

    def from_owner_rows(table):
        return table.reshape(wt_size, ctx_size, tokens).transpose(2, 1, 0).reshape(tokens, devices)

    hit_mine = exchange(to_owner_rows(hits), by_stream).reshape(wt_size, seq_len)
    slot_mine = jnp.cumsum(hit_mine, axis=1) - hit_mine
    slot_mine = jnp.where((hit_mine > 0) & (slot_mine < capacity), slot_mine, -1)
    slot_ids = jnp.arange(capacity, dtype=jnp.int32)
    place = slot_mine[:, None, :] == slot_ids[None, :, None]
    place_low = place.astype(jnp.bfloat16)
    hit_plane = exchange(hits.T.reshape(ctx_size, wt_size, tokens), "ctx").transpose(1, 0, 2)
    hit_plane = hit_plane.reshape(wt_size, seq_len)[
        (wt_index - jnp.arange(wt_size)) % wt_size
    ]
    slot_plane = jnp.cumsum(hit_plane, axis=1) - hit_plane
    slot_plane = jnp.where((hit_plane > 0) & (slot_plane < capacity), slot_plane, -1)
    spread_low = (slot_plane[:, None, :] == slot_ids[None, :, None]).astype(jnp.bfloat16)

    resid_in = hidden_in[0].astype(jnp.float32)
    normed_in = norm_rows(resid_in, gain_attn).astype(jnp.bfloat16)
    router_pad = -expert_count % head_dim
    side_weights = gather(
        jnp.concatenate(
            [key_weight, value_weight, jnp.pad(w_router, ((0, 0), (0, router_pad)))], axis=1
        ),
        both,
    )
    query_full = gather(w_query, both)
    key_full = side_weights[:, :kv_width]
    value_full = side_weights[:, kv_width : 2 * kv_width]
    router_full = side_weights[:, 2 * kv_width : 2 * kv_width + expert_count]
    key_sum = matmul(normed_in, key_full).reshape(tokens, key_heads, head_dim)
    value_low = matmul(normed_in, value_full).astype(jnp.bfloat16)
    key_low = (
        rotate(norm_rows(key_sum, gain_key), cosine_table, sine_table)
        .reshape(tokens, kv_width)
        .astype(jnp.bfloat16)
    )

    def interleave(left, right):
        both_heads = jnp.stack(
            [side.reshape(-1, key_heads, head_dim) for side in (left, right)], axis=2
        )
        return both_heads.reshape(-1, 2 * kv_width)

    pairs_all = gather(interleave(key_low, value_low), "ctx")
    query_sum = lax.optimization_barrier(matmul(normed_in, query_full))
    out_full = gather(w_out, both)
    mixed_low, query_low = attend(
        query_sum,
        pairs_all,
        gain_query,
        cosine_rows,
        sine_rows,
        my_positions,
        my_docs,
        all_positions,
        doc_all,
    )
    resid_mid = resid_in + matmul(mixed_low, out_full)
    normed_mid = norm_rows(resid_mid, gain_moe).astype(jnp.bfloat16)

    mid_all = gather(normed_mid, by_stream).reshape(wt_size, seq_len, model_width)
    logits = matmul(normed_mid, router_full)
    logit_exp = jnp.exp(logits - jnp.max(logits, axis=-1, keepdims=True))
    router_probs = logit_exp / jnp.sum(logit_exp, axis=-1, keepdims=True)
    chosen_total = jnp.sum(hits_float * router_probs, axis=1, keepdims=True)
    gate_kept = jnp.where(kept, router_probs / chosen_total, 0.0)
    gate_mine = exchange(to_owner_rows(gate_kept), by_stream).reshape(wt_size, seq_len)

    def column_blocks(value):
        width = value.shape[1] // ctx_size
        blocks = value.reshape(tokens, ctx_size, width).transpose(1, 0, 2)
        return exchange(blocks, "ctx").reshape(seq_len, width)

    def pick_rows(table):
        return (
            jnp.einsum("wkt,wtd->wkd", place_low, table, preferred_element_type=jnp.float32)
            .astype(jnp.bfloat16)
            .reshape(wt_size * capacity, model_width)
        )

    filled = pick_rows(mid_all)
    gathered_bytes = 2 * devices * tokens * model_width
    own_cot = out_grad[0] if gathered_bytes <= 1 << 25 else after(out_grad[0], filled)
    cot_all = gather(own_cot, by_stream).reshape(wt_size, seq_len, model_width)
    normed_in_all = gather(after(normed_in, filled), "ctx")
    mixed_columns = column_blocks(after(mixed_low, filled))
    gate_h = matmul(filled, expert_gate[0])
    up_h = matmul(filled, expert_up[0])
    sigma_h = jax.nn.sigmoid(gate_h)
    hidden_h = (gate_h * sigma_h * up_h).astype(jnp.bfloat16)
    result_rows = matmul(hidden_h, expert_down[0]).astype(jnp.bfloat16)
    cot_rows = pick_rows(cot_all)
    gate_rows = jnp.sum(jnp.where(place, gate_mine[:, None, :], 0.0), axis=2).reshape(-1)
    gate_cot_rows = jnp.sum(
        result_rows.astype(jnp.float32) * cot_rows.astype(jnp.float32), axis=1
    ).reshape(wt_size, capacity)
    gate_cot_mine = jnp.sum(jnp.where(place, gate_cot_rows[:, :, None], 0.0), axis=1)
    out_rows_cot = (gate_rows[:, None] * cot_rows.astype(jnp.float32)).astype(jnp.bfloat16)
    hidden_cot = contract_cols(out_rows_cot, expert_down[0])
    grad_down = contract_rows(hidden_h, out_rows_cot)
    gate_cot_h = (hidden_cot * up_h * sigma_h * (1.0 + gate_h * (1.0 - sigma_h))).astype(
        jnp.bfloat16
    )
    up_cot_h = (hidden_cot * gate_h * sigma_h).astype(jnp.bfloat16)
    grad_gate = contract_rows(filled, gate_cot_h)
    grad_up = contract_rows(filled, up_cot_h)
    in_rows_cot = (
        contract_cols(gate_cot_h, expert_gate[0]) + contract_cols(up_cot_h, expert_up[0])
    ).astype(jnp.bfloat16)

    def turn(blocks):
        arrived = []
        for step in range(wt_size):
            block = lax.dynamic_index_in_dim(
                blocks, lax.rem(wt_index + step, wt_size), keepdims=False
            )
            if step:
                pairs = [(w, (w + step) % wt_size) for w in range(wt_size)]
                block = lax.ppermute(block, "wt", pairs)
            arrived.append(block)
        return arrived

    def add_pairs(table, stream_rows):
        partial = contract_rows(
            table.reshape(wt_size * capacity, seq_len), jnp.concatenate(stream_rows, axis=0)
        ).astype(jnp.bfloat16)
        return scatter_sum(partial, "ctx").astype(jnp.float32)

    gate_cot = from_owner_rows(exchange(gate_cot_mine.reshape(devices, tokens), by_stream))
    mixed_rows = (gate_rows[:, None] * result_rows.astype(jnp.float32)).astype(jnp.bfloat16)
    in_rows_cot, normed_in_all, mixed_columns = lax.optimization_barrier(
        (in_rows_cot, normed_in_all, mixed_columns)
    )
    blocks_shape = (wt_size, capacity, model_width)
    stream_cots = turn(in_rows_cot.reshape(blocks_shape))
    returned_cot = add_pairs(spread_low, stream_cots)
    stream_mixed = turn(after(mixed_rows, stream_cots).reshape(blocks_shape))
    out_cot = out_grad[0].astype(jnp.float32)

    kept_cot = gate_cot * keep_float
    chosen_cot = kept_cot / chosen_total - jnp.sum(
        kept_cot * router_probs, axis=1, keepdims=True
    ) / (chosen_total * chosen_total)
    probs_cot = hits_float * chosen_cot
    logit_cot = (
        router_probs * (probs_cot - jnp.sum(router_probs * probs_cot, axis=1, keepdims=True))
    ).astype(jnp.bfloat16)
    mid_cot = returned_cot + contract_cols(logit_cot, router_full)
    mid_norm_cot, gain_moe_terms = norm_back(resid_mid, gain_moe, mid_cot)
    resid_cot = out_cot + mid_norm_cot
    attn_cot = resid_cot.astype(jnp.bfloat16)
    router_parts = exchange(contract_rows(normed_mid, logit_cot).reshape(devices, -1), both)
    grad_w_router = jnp.sum(router_parts, axis=0).reshape(w_router.shape)

    mixed_cot = contract_cols(attn_cot, out_full)
    attn_cot_all = gather(attn_cot, "ctx")
    grad_w_out = scatter_sum(
        contract_rows(mixed_columns, attn_cot_all).astype(jnp.bfloat16), "wt"
    ).astype(jnp.float32)

    query_cot_low, pair_cots, gain_query_terms = attend_back(
        query_sum,
        query_low,
        mixed_cot.astype(jnp.bfloat16),
        pairs_all,
        gain_query,
        cosine_rows,
        sine_rows,
        my_positions,
        my_docs,
        all_positions,
        doc_all,
    )
    mixed_mine = add_pairs(after(spread_low, query_cot_low), stream_mixed)
    hidden_out = after(resid_mid, query_cot_low) + mixed_mine
    pair_mine = scatter_sum(pair_cots, "ctx").reshape(tokens, key_heads, 2, head_dim)
    key_mine = pair_mine[:, :, 0].astype(jnp.float32)
    value_cot_low = pair_mine[:, :, 1].reshape(tokens, kv_width)
    key_pre, gain_key_terms = norm_back(
        key_sum,
        gain_key,
        rotate(key_mine, cosine_table, -sine_table),
    )
    key_cot_low = key_pre.reshape(tokens, kv_width).astype(jnp.bfloat16)
    pair_cot_low = jnp.concatenate([key_cot_low, value_cot_low], axis=1)

    def weight_grad(cots):
        width = cots.shape[1] // ctx_size
        block = contract_rows(normed_in_all, column_blocks(cots)).astype(jnp.bfloat16)
        block = block.reshape(ctx_size, wt_size, -1, width).transpose(1, 0, 2, 3)
        mine = scatter_sum(block.reshape(model_width, width), "wt")
        rows = exchange(mine.reshape(ctx_size, -1, width), "ctx")
        return rows.transpose(1, 0, 2).reshape(-1, width * ctx_size).astype(jnp.float32)

    grad_w_query = weight_grad(query_cot_low)
    grad_pair = weight_grad(pair_cot_low)
    grad_w_key = grad_pair[:, :kv_width]
    grad_w_value = grad_pair[:, kv_width:]
    in_cot = contract_cols(query_cot_low, query_full) + contract_cols(
        pair_cot_low, side_weights[:, : 2 * kv_width]
    )
    in_norm_cot, gain_attn_terms = norm_back(resid_in, gain_attn, in_cot)
    grad_in = resid_cot + in_norm_cot
    gains = sum_everywhere(
        jnp.concatenate(
            [
                jnp.sum(gain_attn_terms, axis=0),
                jnp.sum(gain_query_terms, axis=0),
                jnp.sum(gain_key_terms, axis=(0, 1)),
                jnp.sum(gain_moe_terms, axis=0),
            ]
        )
    )
    grad_gain_attn = gains[:model_width]
    grad_gain_query = gains[model_width : model_width + head_dim]
    grad_gain_key = gains[model_width + head_dim : model_width + 2 * head_dim]
    grad_gain_moe = gains[model_width + 2 * head_dim :]
    return (
        hidden_out[None],
        grad_in[None],
        grad_gain_attn,
        grad_w_query,
        grad_w_key,
        grad_w_value,
        grad_gain_query,
        grad_gain_key,
        grad_w_out,
        grad_gain_moe,
        grad_w_router,
        grad_gate[None],
        grad_up[None],
        grad_down[None],
    )


def solution(mesh):
    in_specs = (
        P("wt", "ctx", None),
        P("wt", None),
        P("wt", "ctx", None),
        P(),
        P(("ctx", "wt"), None),
        P(("ctx", "wt"), None),
        P(("ctx", "wt"), None),
        P(),
        P(),
        P(("ctx", "wt"), None),
        P(),
        P(("ctx", "wt"), None),
        P(("ctx", "wt"), None, None),
        P(("ctx", "wt"), None, None),
        P(("ctx", "wt"), None, None),
        P("wt", "ctx", None),
    )
    out_specs = (
        P("wt", "ctx", None),
        P("wt", "ctx", None),
        P(),
        P(("ctx", "wt"), None),
        P(("ctx", "wt"), None),
        P(("ctx", "wt"), None),
        P(),
        P(),
        P(("ctx", "wt"), None),
        P(),
        P(("ctx", "wt"), None),
        P(("ctx", "wt"), None, None),
        P(("ctx", "wt"), None, None),
        P(("ctx", "wt"), None, None),
    )

    return jax.shard_map(
        on_device, mesh=mesh, in_specs=in_specs, out_specs=out_specs, check_vma=False
    )
```

time: 1310 us -> 1200 us (0.916)
  waiting for transfers between devices: 879 us -> 820 us
  matrix products: 215 us -> 163 us
  local copies, waits for them, and re-layouts: 84.8 us -> 47.1 us
  Pallas kernels: 0 us -> 35.8 us
  starting transfers between devices: 42.3 us -> 61.9 us
    all_to_all x11 -> x10, waiting for transfers between devices: 368 us -> 55.5 us  [exchange(): return lax.all_to_all(value, axes, split_axis=0, concat_axis=0, tiled=True)]
    ppermute x0 -> x6, waiting for transfers between devices: none -> 201 us  [turn(): block = lax.ppermute(block, 'wt', pairs)]
    reduce_scatter x4 -> x6, waiting for transfers between devices: 10.7 us -> 90.7 us  [scatter_sum(): return lax.psum_scatter(value, axes, scatter_dimension=0, tiled=True)]
    dot_general x16 -> x0, matrix products: 62.1 us -> none  [the longest x4 14.4 us: block_scores(): jnp.einsum('qkgd,skd->kgqs', head_grouped, key_block, preferred_element_t...]
    pallas_call x0 -> x2, Pallas kernels: none -> 35.8 us  [the longest x1 23.1 us: attend_back(): pl.pallas_call(functools.partial(attend_back_kernel, head_dim, 2), grid=(...]
    all_gather x8, waiting for transfers between devices: 490 us -> 465 us  [gather(): return lax.all_gather(value, axes, axis=0, tiled=True)]
    dot_general x3 -> x2, local copies, waits for them, and re-layouts: 29.6 us -> 6.98 us  [matmul(): return jnp.dot(left_side, right_side, preferred_element_type=jnp.float32)]
    dot_general x7 -> x9, matrix products: 31.9 us -> 53.3 us  [contract_rows(): lax.dot_general(left_side, right_side, (((0,), (0,)), ((), ())), preferre...]
  transfers between devices with their start and end apart: 24 -> 31, of which waited for: 19 -> 21; matrix products, arithmetic and copies ran while one was open for 17% -> 16% of each run, Pallas kernels for 0% -> 1%
where the time goes in v2:
time: 1200 us; the launch traced here: 1190 us
  waiting for transfers between devices  820 us (68%)
  matrix products  163 us (14%)
  starting transfers between devices  61.9 us (5%)
  local copies, waits for them, and re-layouts  47.1 us (4%)
  other arithmetic  41.4 us (3%)
  Pallas kernels  35.8 us (3%)
  between operations  16 us (1%)
    all_gather x8, waiting for transfers between devices, gather(): return lax.all_gather(value, axes, axis=0, tiled=True)  465 us
    ppermute x6, waiting for transfers between devices, turn(): block = lax.ppermute(block, 'wt', pairs)  201 us
    reduce_scatter x6, waiting for transfers between devices, scatter_sum(): return lax.psum_scatter(value, axes, scatter_dimension=0, tiled=True)  90.7 us
    all_to_all x10, waiting for transfers between devices, exchange(): return lax.all_to_all(value, axes, split_axis=0, concat_axis=0, tiled=True)  55.5 us
    dot_general x9, matrix products, contract_rows(): lax.dot_general(left_side, right_side, (((0,), (0,)), ((), ())), preferre...  53.3 us
    all_to_all x10, starting transfers between devices, exchange(): return lax.all_to_all(value, axes, split_axis=0, concat_axis=0, tiled=True)  47.5 us
    dot_general x7, matrix products, contract_cols(): lax.dot_general(left_side, right_side, (((1,), (1,)), ((), ())), preferre...  43.6 us
    dot_general x8, matrix products, matmul(): return jnp.dot(left_side, right_side, preferred_element_type=jnp.float32)  42.4 us
  transfers between devices with their start and end apart: 31, of which 21 were waited for; matrix products, arithmetic and copies ran while one was open for 16% of the time, Pallas kernels for 1%

profile of v2, /device:TPU:0, one launch (start us, length us, event | category | flops | bytes accessed | tf_op | source)
XLA Modules:
  0.0 1193.3 jit_solution(7447935687326969190)
XLA Ops:
  15.2 62.6 %all-gather.13.cloned.1.call-done = bf16[2048,1152]{1,0:T(8,128)(2,1)} async-done(((bf16[64,1152]{1,0:T(8,128)(2,1)}), bf16[2048,1152]{1,0:T(8,128)(2,1)}) %all-gather.13.cloned.1.call-update) | async-done | bytes 4718608 | tf_op jit(solution)/shard_map/all_gather | solution.py:349
  80.7 3.1 slice_bitcast_fusion
  83.8 3.9 copy.152
  87.7 2.7 multiply_reduce_fusion.5
  95.7 97.9 %all-gather.11.cloned.1.call-done = bf16[2048,4096]{1,0:T(8,128)(2,1)} async-done(((bf16[64,4096]{1,0:T(8,128)(2,1)}), bf16[2048,4096]{1,0:T(8,128)(2,1)}) %all-gather.11.cloned.1.call-update) | async-done | bytes 16777232 | tf_op jit(solution)/shard_map/all_gather | solution.py:349
  193.6 9.7 fusion.107.query_ref
  203.3 18.8 %all-gather.15.cloned.1.call-done.pairs_ref = bf16[1024,1024]{1,0:T(8,128)(2,1)} async-done(((bf16[128,1024]{1,0:T(8,128)(2,1)}), bf16[1024,1024]{1,0:T(8,128)(2,1)}) %all-gather.15.cloned.1.call-update) | async-done | bytes 2097168 | tf_op jit(solution)/shard_map/all_gather | solution.py:349
  225.3 12.7 %attend.1 = (bf16[128,4096]{1,0:T(8,128)(2,1)S(1)}, bf16[128,4096]{1,0:T(8,128)(2,1)S(1)}) custom-call(f32[128,4096]{1,0:T(8,128)S(1)} %copy-done.3, bf16[1024,1024]{1,0:T(8,128)(2,1)S(1)} %copy-done.5, f32[1,128]{1,0:T(1,128)S(1)} %bitcast.261, f32[128,128]{1,0:T(8,128)S(1)} %get-tuple-element.144.cosine_ref, f32[128,128]{1,0:T(8,128)S(1)} %get-tuple-element.142.sine_ref, ...), custom_call_target="tpu_custom_call" | custom-call | flops 2147483648 | bytes 4194304 | tf_op jit(solution)/shard_map/attend/pallas_call | solution.py:197
  240.0 99.4 %all-gather.17.cloned.1.call-done = bf16[4096,2048]{1,0:T(8,128)(2,1)} async-done(((bf16[128,2048]{1,0:T(8,128)(2,1)}), bf16[4096,2048]{1,0:T(8,128)(2,1)}) %all-gather.17.cloned.1.call-update) | async-done | bytes 16777232 | tf_op jit(solution)/shard_map/all_gather | solution.py:349
  339.4 9.5 multiply_reduce_fusion.2
  353.1 2.8 all-to-all-start.1
  357.5 8.5 all-reduce.1
  371.6 83.3 %all-gather.25.cloned.1.call-done = bf16[1,4096,2048]{2,1,0:T(8,128)(2,1)} async-done(((bf16[1,128,2048]{2,1,0:T(8,128)(2,1)}), bf16[1,4096,2048]{2,1,0:T(8,128)(2,1)}) %all-gather.25.cloned.1.call-update) | async-done | bytes 16777232 | tf_op jit(solution)/shard_map/all_gather | solution.py:349
  454.9 11.8 fusion.25
  466.7 103.5 %all-gather.19.cloned.1.call-done = bf16[4096,2048]{1,0:T(8,128)(2,1)} async-done(((bf16[128,2048]{1,0:T(8,128)(2,1)}), bf16[4096,2048]{1,0:T(8,128)(2,1)}) %all-gather.19.cloned.1.call-update) | async-done | bytes 16777232 | tf_op jit(solution)/shard_map/all_gather | solution.py:349
  570.2 11.8 fusion.26
  582.1 6.3 fusion.35
  588.4 5.2 multiply_convert_fusion
  593.6 5.2 fusion
  600.3 13.6 %all-to-all-start.4 = ((f32[32,1,128]{2,1,0:T(1,128)}), f32[32,1,128]{2,1,0:T(1,128)S(1)}, u32[]{:S(2)}, u32[]{:S(2)}) async-start(f32[32,1,128]{2,1,0:T(1,128)} %all_to_all.52), calls=%async_computation.5 | async-start | bytes 32768 | tf_op jit(solution)/shard_map/all_to_all | solution.py:352
  613.9 7.1 all-to-all-done.4
  628.9 4.8 all-to-all-done.2
  633.7 4.2 all-to-all-start.3
  639.7 3.1 fusion.2
  643.8 4.4 multiply_convert_fusion.1
  648.2 3.4 fusion.33
  651.7 5.1 add_convert_fusion
  656.8 3.7 dynamic-slice_bitcast_fusion.7
  663.1 4.1 all-to-all-start
  667.3 4.7 all-to-all-done
  674.8 11.6 collective-permute-done.2
  686.4 67.2 %collective-permute-done.1 = bf16[256,2048]{1,0:T(8,128)(2,1)} collective-permute-done((bf16[256,2048]{1,0:T(8,128)(2,1)S(1)}, bf16[256,2048]{1,0:T(8,128)(2,1)}, u32[]{:S(2)}, u32[]{:S(2)}) %collective-permute-start.1) | collective-permute-done | bytes 1048608 | tf_op jit(solution)/shard_map/ppermute | solution.py:500
  753.7 8.4 fusion.30
  763.6 49.1 %reduce-scatter.7.cloned.1.call-done = bf16[128,2048]{1,0:T(8,128)(2,1)} async-done(((bf16[1024,2048]{1,0:T(8,128)(2,1)}), bf16[128,2048]{1,0:T(8,128)(2,1)}) %reduce-scatter.7.cloned.1.call-update) | async-done | bytes 524304 | tf_op jit(solution)/shard_map/reduce_scatter | solution.py:355
  812.7 2.7 multiply_reduce_fusion
  815.4 2.7 fusion.99
  818.1 11.6 convolution_convert_fusion.cot_ref
  830.8 23.1 %attend_back.1 = (bf16[128,4096]{1,0:T(8,128)(2,1)S(1)}, bf16[1024,1024]{1,0:T(8,128)(2,1)}, f32[32,128]{1,0:T(8,128)S(1)}) custom-call(f32[128,4096]{1,0:T(8,128)} %fusion.107.query_ref, bf16[128,4096]{1,0:T(8,128)(2,1)S(1)} %copy-done.8, bf16[128,4096]{1,0:T(8,128)(2,1)S(1)} %convolution_convert_fusion.cot_ref, ...), custom_call_target="tpu_custom_call" | custom-call | flops 5368709120 | bytes 6291456 | tf_op jit(solution)/shard_map/attend_back/pallas_call | solution.py:253
  854.6 40.6 %reduce-scatter.11.cloned.1.call-done = bf16[128,1024]{1,0:T(8,128)(2,1)} async-done(((bf16[1024,1024]{1,0:T(8,128)(2,1)}), bf16[128,1024]{1,0:T(8,128)(2,1)}) %reduce-scatter.11.cloned.1.call-update) | async-done | bytes 262160 | tf_op jit(solution)/shard_map/reduce_scatter | solution.py:355
  898.6 3.4 all-to-all-start.8
  903.1 7.1 all-to-all-done.8
  910.2 3.6 all-to-all-start.6
  914.2 3.5 convolution_convert_fusion.4
  918.6 17.9 %all-to-all-done.6 = bf16[8,128,512]{2,1,0:T(8,128)(2,1)S(1)} async-done(((bf16[8,128,512]{2,1,0:T(8,128)(2,1)}), bf16[8,128,512]{2,1,0:T(8,128)(2,1)S(1)}, u32[]{:S(2)}, u32[]{:S(2)}) %all-to-all-start.6) | async-done | bytes 1048608 | tf_op jit(solution)/shard_map/all_to_all | solution.py:352
  937.5 4.9 convolution_convert_fusion.3
  944.0 6.3 fusion.3
  950.9 3.3 collective-permute-start.5
  956.1 26.6 %collective-permute-done.5 = bf16[256,2048]{1,0:T(8,128)(2,1)S(1)} collective-permute-done((bf16[256,2048]{1,0:T(8,128)(2,1)S(1)}, bf16[256,2048]{1,0:T(8,128)(2,1)S(1)}, u32[]{:S(2)}, u32[]{:S(2)}) %collective-permute-start.5) | collective-permute-done | bytes 1048608 | tf_op jit(solution)/shard_map/ppermute | solution.py:500
  982.7 96.0 %collective-permute-done.4 = bf16[256,2048]{1,0:T(8,128)(2,1)S(1)} collective-permute-done((bf16[256,2048]{1,0:T(8,128)(2,1)S(1)}, bf16[256,2048]{1,0:T(8,128)(2,1)S(1)}, u32[]{:S(2)}, u32[]{:S(2)}) %collective-permute-start.4) | collective-permute-done | bytes 1048608 | tf_op jit(solution)/shard_map/ppermute | solution.py:500
  1078.6 6.2 fusion.27
  1087.3 2.6 all-to-all-start.10
  1090.2 9.4 convolution_bitcast_fusion.2
  1099.6 5.5 convolution_bitcast_fusion.1
  1105.1 6.2 convolution_convert_fusion.2
  1111.4 11.6 fusion.108
  1123.0 4.9 fusion.65
  1129.0 6.0 all-to-all-start.5
  1135.1 9.0 convolution_bitcast_fusion
  1145.0 2.6 fusion.64
  1147.6 4.1 all-to-all-done.5
  1152.6 6.5 all-to-all-start.9
  1159.6 5.0 all-to-all-done.9
  1164.6 4.1 all-to-all-start.7
  1169.5 9.0 all-to-all-done.7
  (263 shorter events, 78.3 us)
Async XLA Ops:
  7.2 586.4 %copy-start = (bf16[1,768,2048]{2,1,0:T(8,128)(2,1)S(1)}, bf16[1,768,2048]{2,1,0:T(8,128)(2,1)}, u32[]{:S(2)}) copy-start(bf16[1,768,2048]{2,1,0:T(8,128)(2,1)} %param.30) | copy-start | bytes 9437188
  7.2 70.5 %all-gather.13.cloned.1.call-start = ((), (), s32[]{:S(2)}) async-start(), calls=%async_computation.18 | async-start | bytes 4866048 | tf_op jit(solution)/shard_map/all_gather | solution.py:349
  9.8 183.9 %all-gather.11.cloned.1.call-start = ((), (), s32[]{:S(2)}) async-start(), calls=%async_computation.17 | async-start | bytes 17301504 | tf_op jit(solution)/shard_map/all_gather | solution.py:349
  10.5 211.6 %all-gather.15.cloned.1.call-start = ((), (), s32[]{:S(2)}) async-start(), calls=%async_computation.19 | async-start | bytes 2359296 | tf_op jit(solution)/shard_map/all_gather | solution.py:349
  11.8 78.8 %copy-start.19 = (f32[128,128]{0,1:T(8,128)}, f32[128,128]{0,1:T(8,128)S(1)}, u32[]{:S(2)}) copy-start(f32[128,128]{0,1:T(8,128)S(1)} %copy.153) | copy-start | bytes 196612
  13.1 74.6 %copy-start.34 = (f32[128]{0:T(128)}, f32[128]{0:T(128)S(1)}, u32[]{:S(2)}) copy-start(f32[128]{0:T(128)S(1)} %add_rsqrt_fusion.2) | copy-start | bytes 1540
  80.7 7.0 copy-start.28
  83.8 6.7 copy-start.32
  87.7 7.5 copy-start.41
  94.0 245.4 %all-gather.17.cloned.1.call-start = ((), (), s32[]{:S(2)}) async-start(), calls=%async_computation.20 | async-start | bytes 17301504 | tf_op jit(solution)/shard_map/all_gather | solution.py:349
  94.6 360.3 %all-gather.25.cloned.1.call-start = ((), (), s32[]{:S(2)}) async-start(), calls=%async_computation.30 | async-start | bytes 17301504 | tf_op jit(solution)/shard_map/all_gather | solution.py:349
  95.2 475.0 %all-gather.19.cloned.1.call-start = ((), (), s32[]{:S(2)}) async-start(), calls=%async_computation.21 | async-start | bytes 17301504 | tf_op jit(solution)/shard_map/all_gather | solution.py:349
  95.7 126.4 %copy-start.6 = (f32[128]{0:T(128)S(1)}, f32[128]{0:T(128)}, u32[]{:S(2)}) copy-start(f32[128]{0:T(128)} %param.23) | copy-start | bytes 1540
  339.4 9.5 copy-start.27
  339.4 11.8 copy-start.33
  339.4 16.6 %copy-start.44 = (u32[32]{0:T(128)S(1)}, u32[32]{0:T(128)}, u32[]{:S(2)}) copy-start(u32[32]{0:T(128)} %constant.116) | copy-start | bytes 388
  353.1 14.1 %all-to-all-start.1 = ((s32[32,1,128]{2,1,0:T(1,128)}), s32[32,1,128]{2,1,0:T(1,128)S(1)}, u32[]{:S(2)}, u32[]{:S(2)}) async-start(s32[32,1,128]{2,1,0:T(1,128)} %bitcast.23), calls=%async_computation.1 | async-start | bytes 32768 | tf_op jit(solution)/shard_map/all_to_all | solution.py:352
  355.9 300.8 %all-gather.21.cloned.1.call-start = ((), (), s32[]{:S(2)}) async-start(), calls=%async_computation.22 | async-start | bytes 4718592 | tf_op jit(solution)/shard_map/all_gather | solution.py:349
  582.0 6.3 copy-start.39
  582.0 6.3 copy-start.42
  588.4 5.2 copy-start.46
  588.4 5.2 copy-start.9
  593.6 5.3 copy-start.17
  600.3 20.7 %all-to-all-start.4 = ((f32[32,1,128]{2,1,0:T(1,128)}), f32[32,1,128]{2,1,0:T(1,128)S(1)}, u32[]{:S(2)}, u32[]{:S(2)}) async-start(f32[32,1,128]{2,1,0:T(1,128)} %all_to_all.52), calls=%async_computation.5 | async-start | bytes 32768 | tf_op jit(solution)/shard_map/all_to_all | solution.py:352
  624.0 9.7 all-to-all-start.2
  633.7 23.1 %all-to-all-start.3 = ((bf16[8,128,512]{2,1,0:T(8,128)(2,1)}), bf16[8,128,512]{2,1,0:T(8,128)(2,1)}, u32[]{:S(2)}, u32[]{:S(2)}) async-start(bf16[8,128,512]{2,1,0:T(8,128)(2,1)} %bitcast.266), calls=%async_computation.3 | async-start | bytes 2097152 | tf_op jit(solution)/shard_map/all_to_all | solution.py:352
  660.5 25.9 %collective-permute-start.2 = (bf16[256,2048]{1,0:T(8,128)(2,1)}, bf16[256,2048]{1,0:T(8,128)(2,1)}, u32[]{:S(2)}, u32[]{:S(2)}) collective-permute-start(bf16[256,2048]{1,0:T(8,128)(2,1)} %get-tuple-element.130), channel_id=1, source_target_pairs={{0,3},{1,0},{2,1},{3,2},{4,7},{5,4},{6,5},{7,6},{8,11},{9,8},{10,9... | collective-permute-start | bytes 3145736 | tf_op jit(solution)/shard_map/ppermute | solution.py:500
  661.1 92.6 %collective-permute-start.1 = (bf16[256,2048]{1,0:T(8,128)(2,1)S(1)}, bf16[256,2048]{1,0:T(8,128)(2,1)}, u32[]{:S(2)}, u32[]{:S(2)}) collective-permute-start(bf16[256,2048]{1,0:T(8,128)(2,1)S(1)} %get-tuple-element.131), channel_id=1, source_target_pairs={{0,2},{1,3},{2,0},{3,1},{4,6},{5,7},{6,4},{7,5},{8,10},{9,11},{10,... | collective-permute-start | bytes 3145736 | tf_op jit(solution)/shard_map/ppermute | solution.py:500
  662.5 91.1 %collective-permute-start = (bf16[256,2048]{1,0:T(8,128)(2,1)S(1)}, bf16[256,2048]{1,0:T(8,128)(2,1)}, u32[]{:S(2)}, u32[]{:S(2)}) collective-permute-start(bf16[256,2048]{1,0:T(8,128)(2,1)S(1)} %get-tuple-element.132), channel_id=1, source_target_pairs={{0,1},{1,2},{2,3},{3,0},{4,5},{5,6},{6,7},{7,4},{8,9},{9,10},{10,1... | collective-permute-start | bytes 3145736 | tf_op jit(solution)/shard_map/ppermute | solution.py:500
  663.1 8.9 all-to-all-start
  667.2 145.5 %reduce-scatter.7.cloned.1.call-start = ((), (), s32[]{:S(2)}) async-start(), calls=%async_computation.23 | async-start | bytes 4718592 | tf_op jit(solution)/shard_map/reduce_scatter | solution.py:355
  762.1 53.3 %copy-start.16 = (bf16[1,128,2048]{2,1,0:T(8,128)(2,1)S(1)}, bf16[1,128,2048]{2,1,0:T(8,128)(2,1)}, u32[]{:S(2)}) copy-start(bf16[1,128,2048]{2,1,0:T(8,128)(2,1)} %param.31) | copy-start | bytes 1572868
  762.1 133.1 %reduce-scatter.11.cloned.1.call-start = ((), (), s32[]{:S(2)}) async-start(), calls=%async_computation.25 | async-start | bytes 2359296 | tf_op jit(solution)/shard_map/reduce_scatter | solution.py:355
  818.1 11.6 copy-start.12
  818.1 11.7 copy-start.8
  830.8 23.7 %copy-start.26 = (f32[128,128]{1,0:T(8,128)S(1)}, f32[128,128]{1,0:T(8,128)}, u32[]{:S(2)}) copy-start(f32[128,128]{1,0:T(8,128)} %get-tuple-element.141) | copy-start | bytes 196612
  853.9 43.2 %copy-start.14 = (f32[128,4,128]{0,2,1:T(8,128)S(1)}, f32[128,4,128]{0,2,1:T(8,128)}, u32[]{:S(2)}) copy-start(f32[128,4,128]{0,2,1:T(8,128)} %copy-done.13) | copy-start | bytes 786436
  853.9 43.2 %copy-start.20 = (f32[128,128]{0,1:T(8,128)S(1)}, f32[128,128]{0,1:T(8,128)}, u32[]{:S(2)}) copy-start(f32[128,128]{0,1:T(8,128)} %copy-done.19) | copy-start | bytes 196612
  853.9 251.2 %all-gather.23.cloned.1.call-start = ((), (), s32[]{:S(2)}) async-start(), calls=%async_computation.28 | async-start | bytes 4718592 | tf_op jit(solution)/shard_map/all_gather | solution.py:349
  897.9 12.4 %copy-start.23 = (bf16[128,4,128]{0,2,1:T(8,128)(2,1)}, bf16[128,4,128]{0,2,1:T(8,128)(2,1)S(1)}, u32[]{:S(2)}) copy-start(bf16[128,4,128]{0,2,1:T(8,128)(2,1)S(1)} %multiply_convert_fusion.4) | copy-start | bytes 393220
  898.6 11.6 all-to-all-start.8
  910.2 26.3 %all-to-all-start.6 = ((bf16[8,128,512]{2,1,0:T(8,128)(2,1)}), bf16[8,128,512]{2,1,0:T(8,128)(2,1)S(1)}, u32[]{:S(2)}, u32[]{:S(2)}) async-start(bf16[8,128,512]{2,1,0:T(8,128)(2,1)} %bitcast.251), calls=%async_computation.9 | async-start | bytes 2097152 | tf_op jit(solution)/shard_map/all_to_all | solution.py:352
  913.8 238.8 %reduce-scatter.15.cloned.1.call-start = ((), (), s32[]{:S(2)}) async-start(), calls=%async_computation.27 | async-start | bytes 655360 | tf_op jit(solution)/shard_map/reduce_scatter | solution.py:355
  918.6 246.0 %reduce-scatter.13.cloned.1.call-start = ((), (), s32[]{:S(2)}) async-start(), calls=%async_computation.26 | async-start | bytes 2621440 | tf_op jit(solution)/shard_map/reduce_scatter | solution.py:355
  944.0 236.8 %reduce-scatter.9.cloned.1.call-start = ((), (), s32[]{:S(2)}) async-start(), calls=%async_computation.24 | async-start | bytes 4718592 | tf_op jit(solution)/shard_map/reduce_scatter | solution.py:355
  950.9 31.8 %collective-permute-start.5 = (bf16[256,2048]{1,0:T(8,128)(2,1)S(1)}, bf16[256,2048]{1,0:T(8,128)(2,1)S(1)}, u32[]{:S(2)}, u32[]{:S(2)}) collective-permute-start(bf16[256,2048]{1,0:T(8,128)(2,1)S(1)} %get-tuple-element.126), channel_id=1, source_target_pairs={{0,3},{1,0},{2,1},{3,2},{4,7},{5,4},{6,5},{7,6},{8,11},{9,8},{10,9... | collective-permute-start | bytes 3145736 | tf_op jit(solution)/shard_map/ppermute | solution.py:500
  954.2 124.4 %collective-permute-start.4 = (bf16[256,2048]{1,0:T(8,128)(2,1)S(1)}, bf16[256,2048]{1,0:T(8,128)(2,1)S(1)}, u32[]{:S(2)}, u32[]{:S(2)}) collective-permute-start(bf16[256,2048]{1,0:T(8,128)(2,1)S(1)} %get-tuple-element.127), channel_id=1, source_target_pairs={{0,2},{1,3},{2,0},{3,1},{4,6},{5,7},{6,4},{7,5},{8,10},{9,11},{10,... | collective-permute-start | bytes 3145736 | tf_op jit(solution)/shard_map/ppermute | solution.py:500
  954.2 124.4 %collective-permute-start.3 = (bf16[256,2048]{1,0:T(8,128)(2,1)S(1)}, bf16[256,2048]{1,0:T(8,128)(2,1)S(1)}, u32[]{:S(2)}, u32[]{:S(2)}) collective-permute-start(bf16[256,2048]{1,0:T(8,128)(2,1)S(1)} %get-tuple-element.128), channel_id=1, source_target_pairs={{0,1},{1,2},{2,3},{3,0},{4,5},{5,6},{6,7},{7,4},{8,9},{9,10},{10,1... | collective-permute-start | bytes 3145736 | tf_op jit(solution)/shard_map/ppermute | solution.py:500
  1087.3 40.6 %all-to-all-start.10 = ((f32[32,1,2048]{2,1,0:T(1,128)}), f32[32,1,2048]{2,1,0:T(1,128)S(1)}, u32[]{:S(2)}, u32[]{:S(2)}) async-start(f32[32,1,2048]{2,1,0:T(1,128)} %all_to_all.61), calls=%async_computation.16 | async-start | bytes 524288 | tf_op jit(solution)/shard_map/all_to_all | solution.py:352
  1089.9 9.7 copy-start.50
  1089.9 94.3 %reduce-scatter.17.cloned.1.call-start = ((), (), s32[]{:S(2)}) async-start(), calls=%async_computation.29 | async-start | bytes 2621440 | tf_op jit(solution)/shard_map/reduce_scatter | solution.py:355
  1090.2 9.4 copy-start.43
  1111.3 11.7 copy-start.11
  1111.3 11.7 copy-start.22
  1111.3 11.7 copy-start.24
  1111.3 11.7 copy-start.29
  1111.4 11.7 copy-start.35
  1129.0 22.7 %all-to-all-start.5 = ((f32[32,1,4352]{2,1,0:T(1,128)}), f32[32,1,4352]{2,1,0:T(1,128)S(1)}, u32[]{:S(2)}, u32[]{:S(2)}) async-start(f32[32,1,4352]{2,1,0:T(1,128)} %broadcast_in_dim.148), calls=%async_computation.8 | async-start | bytes 1114112 | tf_op jit(solution)/shard_map/all_to_all | solution.py:308
  1135.0 10.0 copy-start.15
  1135.1 9.9 copy-start.30
  1135.1 9.9 copy-start.36
  1152.6 12.0 %all-to-all-start.9 = ((bf16[8,64,128]{2,1,0:T(8,128)(2,1)}), bf16[8,64,128]{2,1,0:T(8,128)(2,1)S(1)}, u32[]{:S(2)}, u32[]{:S(2)}) async-start(bf16[8,64,128]{2,1,0:T(8,128)(2,1)} %bitcast.287), calls=%async_computation.14 | async-start | bytes 262144 | tf_op jit(solution)/shard_map/all_to_all | solution.py:352
  1164.6 13.9 %all-to-all-start.7 = ((bf16[8,64,512]{2,1,0:T(8,128)(2,1)}), bf16[8,64,512]{2,1,0:T(8,128)(2,1)}, u32[]{:S(2)}, u32[]{:S(2)}) async-start(bf16[8,64,512]{2,1,0:T(8,128)(2,1)} %bitcast.275), calls=%async_computation.11 | async-start | bytes 1048576 | tf_op jit(solution)/shard_map/all_to_all | solution.py:352
  1168.8 17.6 %copy-start.1 = (bf16[1,768,2048]{2,1,0:T(8,128)(2,1)S(1)}, bf16[1,768,2048]{2,1,0:T(8,128)(2,1)}, u32[]{:S(2)}) copy-start(bf16[1,768,2048]{2,1,0:T(8,128)(2,1)} %param.30) | copy-start | bytes 9437188
  (18 other events, 46.3 us)
Sparse Core Ops, SparseCore 0:
  11.4 66.2 all-gather.12
  80.7 112.8 all-gather.10
  196.1 25.9 all-gather.14
  225.0 114.3 all-gather.16
  342.1 112.7 all-gather.24
  457.6 112.5 all-gather.18
  582.1 34.7 all-gather.20
  762.2 50.4 reduce-scatter.6
  854.0 41.1 reduce-scatter.10
  896.9 44.1 all-gather.22
  943.4 62.2 reduce-scatter.14
  1007.8 75.7 reduce-scatter.12
  1086.9 51.0 reduce-scatter.8
  1140.2 44.0 reduce-scatter.16

commit v3 on v2

--- a/solution.py
+++ b/solution.py
@@ -12,6 +12,7 @@
 EPS = 1e-06
 THETA = 1000000.0
 MASKED = -1e30
+MESH = pl.DeviceIdType.MESH
 
 
 def norm_rows(value_rows, gain_vec):
@@ -60,6 +61,161 @@
     return lax.dot_general(
         left_side, right_side, (((1,), (1,)), ((), ())), preferred_element_type=jnp.float32
     )
+
+
+def spread_kernel(splits, streams_first, *refs):
+    count = len(splits)
+    ins, outs, stages = refs[:count], refs[count : 2 * count], refs[2 * count : 3 * count]
+    send_sems, recv_sems, load_sems, store_sems = refs[3 * count :]
+    ctx = lax.axis_index("ctx")
+    z = lax.axis_index("wt")
+    depth = lax.axis_size("wt")
+    flip_y = ctx + 4 - 8 * (ctx // 4)
+    step_x = 2 - 4 * ((ctx // 2) % 2)
+    step_c = 1 - 2 * (ctx % 2)
+    flip_x = ctx + step_x
+    flip_xy = flip_y + step_x
+
+    barrier = pltpu.get_barrier_semaphore()
+    line = [lax.rem(z + d, depth) for d in range(1, depth)]
+    for peer in line:
+        pl.semaphore_signal(barrier, inc=1, device_id=(ctx, peer), device_id_type=MESH)
+    for peer in (flip_x, flip_y, ctx + step_c):
+        pl.semaphore_signal(barrier, inc=1, device_id=(peer, z), device_id_type=MESH)
+    loads = []
+    for k in range(count):
+        loads.append(pltpu.make_async_copy(ins[k], stages[k], load_sems.at[k]))
+        loads[k].start()
+    pl.semaphore_wait(barrier, depth + 2)
+
+    pieces = []
+    for part in range(max(splits)):
+        for k in range(count):
+            if part < splits[k]:
+                pieces.append((k, part))
+
+    def group(k, owner, rows):
+        view = outs[k]
+        return view.at[:, owner, rows] if streams_first[k] else view.at[owner, :, rows]
+
+    def block(k, rows):
+        view = outs[k]
+        return view.at[z, ctx, rows] if streams_first[k] else view.at[ctx, z, rows]
+
+    def rows_of(k, part):
+        size = ins[k].shape[0] // splits[k]
+        return pl.ds(part * size, size)
+
+    def send(number, slot, source, target, device):
+        copy = pltpu.make_async_remote_copy(
+            src_ref=source,
+            dst_ref=target,
+            send_sem=send_sems.at[number, slot],
+            recv_sem=recv_sems.at[number, slot],
+            device_id=device,
+            device_id_type=MESH,
+        )
+        copy.start()
+        return copy
+
+    along = []
+    for number, (k, part) in enumerate(pieces):
+        rows = rows_of(k, part)
+        along.append(
+            [
+                send(number, d, ins[k].at[rows], block(k, rows), (ctx, peer))
+                for d, peer in enumerate(line)
+            ]
+        )
+    stores = []
+    for k in range(count):
+        loads[k].wait()
+        whole = pl.ds(0, ins[k].shape[0])
+        stores.append(pltpu.make_async_copy(stages[k], block(k, whole), store_sems.at[k]))
+        stores[k].start()
+    for k in range(count):
+        stores[k].wait()
+
+    first_slot = depth - 1
+    crossed, turned, shared = {}, {}, {}
+
+    def owners(number):
+        if number % 2:
+            return flip_x, flip_y
+        return flip_y, flip_x
+
+    def cross(number):
+        k, part = pieces[number]
+        rows = rows_of(k, part)
+        near, far = owners(number)
+        for copy in along[number]:
+            copy.wait_recv()
+        mine = group(k, ctx, rows)
+        crossed[number] = send(number, first_slot, mine, mine, (near, z))
+        turned[number] = [send(number, first_slot + 1, mine, mine, (far, z))]
+        shared[number] = [send(number, first_slot + 3, mine, mine, (ctx + step_c, z))]
+
+    def turn_corner(number):
+        k, part = pieces[number]
+        rows = rows_of(k, part)
+        near, far = owners(number)
+        crossed[number].wait_recv()
+        theirs = group(k, near, rows)
+        turned[number].append(send(number, first_slot + 2, theirs, theirs, (far, z)))
+        shared[number].append(send(number, first_slot + 4, theirs, theirs, (ctx + step_c, z)))
+
+    def share(number):
+        k, part = pieces[number]
+        rows = rows_of(k, part)
+        _, far = owners(number)
+        for slot, (copy, owner) in enumerate(zip(turned[number], (far, flip_xy))):
+            copy.wait_recv()
+            theirs = group(k, owner, rows)
+            shared[number].append(
+                send(number, first_slot + 5 + slot, theirs, theirs, (ctx + step_c, z))
+            )
+
+    total = len(pieces)
+    for step in range(total + 2):
+        if step < total:
+            cross(step)
+        if 0 <= step - 1 < total:
+            turn_corner(step - 1)
+        if 0 <= step - 2 < total:
+            share(step - 2)
+    for number in range(total):
+        for copy in shared[number]:
+            copy.wait_recv()
+        for copy in along[number] + [crossed[number]] + turned[number] + shared[number]:
+            copy.wait_send()
+
+
+def spread(values, splits, streams_first, channel):
+    ctx_size, wt_size = lax.axis_size("ctx"), lax.axis_size("wt")
+    total = sum(splits)
+    heads = [(wt_size, ctx_size) if first else (ctx_size, wt_size) for first in streams_first]
+    size = sum(value.size * value.dtype.itemsize for value in values)
+    results = pl.pallas_call(
+        functools.partial(spread_kernel, splits, streams_first),
+        out_shape=[
+            jax.ShapeDtypeStruct(head + value.shape, value.dtype)
+            for head, value in zip(heads, values)
+        ],
+        in_specs=[pl.BlockSpec(memory_space=pl.ANY)] * len(values),
+        out_specs=[pl.BlockSpec(memory_space=pl.ANY)] * len(values),
+        scratch_shapes=[pltpu.VMEM(value.shape, value.dtype) for value in values]
+        + [
+            pltpu.SemaphoreType.DMA((total, wt_size + 6)),
+            pltpu.SemaphoreType.DMA((total, wt_size + 6)),
+            pltpu.SemaphoreType.DMA((len(values),)),
+            pltpu.SemaphoreType.DMA((len(values),)),
+        ],
+        compiler_params=pltpu.CompilerParams(collective_id=channel, has_side_effects=True),
+        cost_estimate=pl.CostEstimate(
+            flops=0, bytes_accessed=2 * ctx_size * wt_size * size, transcendentals=0
+        ),
+    )(*values)
+    return [result.reshape(-1, result.shape[-1]) for result in results]
 
 
 def after(value, earlier):
@@ -398,13 +554,18 @@
     resid_in = hidden_in[0].astype(jnp.float32)
     normed_in = norm_rows(resid_in, gain_attn).astype(jnp.bfloat16)
     router_pad = -expert_count % head_dim
-    side_weights = gather(
-        jnp.concatenate(
-            [key_weight, value_weight, jnp.pad(w_router, ((0, 0), (0, router_pad)))], axis=1
-        ),
-        both,
-    )
-    query_full = gather(w_query, both)
+    side_mine = jnp.concatenate(
+        [key_weight, value_weight, jnp.pad(w_router, ((0, 0), (0, router_pad)))], axis=1
+    )
+    small_plane = ctx_size == 8
+    if small_plane:
+        side_weights, query_full, out_full = spread(
+            [side_mine, w_query, w_out], (2, 4, 4), (False,) * 3, 1
+        )
+    else:
+        side_weights = gather(side_mine, both)
+        query_full = gather(w_query, both)
+        out_full = gather(w_out, both)
     key_full = side_weights[:, :kv_width]
     value_full = side_weights[:, kv_width : 2 * kv_width]
     router_full = side_weights[:, 2 * kv_width : 2 * kv_width + expert_count]
@@ -423,8 +584,9 @@
         return both_heads.reshape(-1, 2 * kv_width)
 
     pairs_all = gather(interleave(key_low, value_low), "ctx")
+    if small_plane:
+        cot_all = gather(after(out_grad[0], pairs_all), by_stream)
     query_sum = lax.optimization_barrier(matmul(normed_in, query_full))
-    out_full = gather(w_out, both)
     mixed_low, query_low = attend(
         query_sum,
         pairs_all,
@@ -439,7 +601,11 @@
     resid_mid = resid_in + matmul(mixed_low, out_full)
     normed_mid = norm_rows(resid_mid, gain_moe).astype(jnp.bfloat16)
 
-    mid_all = gather(normed_mid, by_stream).reshape(wt_size, seq_len, model_width)
+    if small_plane:
+        (mid_all,) = spread([normed_mid], (4,), (True,), 2)
+    else:
+        mid_all = gather(normed_mid, by_stream)
+    mid_all = mid_all.reshape(wt_size, seq_len, model_width)
     logits = matmul(normed_mid, router_full)
     logit_exp = jnp.exp(logits - jnp.max(logits, axis=-1, keepdims=True))
     router_probs = logit_exp / jnp.sum(logit_exp, axis=-1, keepdims=True)
@@ -460,9 +626,9 @@
         )
 
     filled = pick_rows(mid_all)
-    gathered_bytes = 2 * devices * tokens * model_width
-    own_cot = out_grad[0] if gathered_bytes <= 1 << 25 else after(out_grad[0], filled)
-    cot_all = gather(own_cot, by_stream).reshape(wt_size, seq_len, model_width)
+    if not small_plane:
+        cot_all = gather(after(out_grad[0], filled), by_stream)
+    cot_all = cot_all.reshape(wt_size, seq_len, model_width)
     normed_in_all = gather(after(normed_in, filled), "ctx")
     mixed_columns = column_blocks(after(mixed_low, filled))
     gate_h = matmul(filled, expert_gate[0])

time: 1200 us -> 1080 us (0.900)
  waiting for transfers between devices: 820 us -> 386 us
  Pallas kernels: 35.8 us -> 339 us
    all_gather x8 -> x4, waiting for transfers between devices: 465 us -> 34.4 us  [gather(): return lax.all_gather(value, axes, axis=0, tiled=True)]
    pallas_call x0 -> x2, Pallas kernels: none -> 304 us  [spread(): pl.pallas_call(functools.partial(spread_kernel, splits, streams_first), o...]
  transfers between devices with their start and end apart: 31 -> 27, of which waited for: 21 -> 16; matrix products, arithmetic and copies ran while one was open for 16% -> 18% of each run, Pallas kernels for 1% -> 12%
where the time goes in v3:
time: 1080 us; the launch traced here: 1070 us
  waiting for transfers between devices  386 us (36%)
  Pallas kernels  339 us (31%)
  matrix products  158 us (15%)
  starting transfers between devices  62.5 us (6%)
  other arithmetic  51.7 us (5%)
  local copies, waits for them, and re-layouts  51.2 us (5%)
  between operations  16.3 us (2%)
    pallas_call x2, Pallas kernels, spread(): pl.pallas_call(functools.partial(spread_kernel, splits, streams_first), o...  304 us
    ppermute x6, waiting for transfers between devices, turn(): block = lax.ppermute(block, 'wt', pairs)  201 us
    reduce_scatter x6, waiting for transfers between devices, scatter_sum(): return lax.psum_scatter(value, axes, scatter_dimension=0, tiled=True)  90.4 us
    all_to_all x10, waiting for transfers between devices, exchange(): return lax.all_to_all(value, axes, split_axis=0, concat_axis=0, tiled=True)  55.7 us
    dot_general x9, matrix products, contract_rows(): lax.dot_general(left_side, right_side, (((0,), (0,)), ((), ())), preferre...  53.6 us
    all_to_all x10, starting transfers between devices, exchange(): return lax.all_to_all(value, axes, split_axis=0, concat_axis=0, tiled=True)  48.9 us
    dot_general x7, matrix products, contract_cols(): lax.dot_general(left_side, right_side, (((1,), (1,)), ((), ())), preferre...  43.5 us
    dot_general x8, matrix products, matmul(): return jnp.dot(left_side, right_side, preferred_element_type=jnp.float32)  39.7 us
  transfers between devices with their start and end apart: 27, of which 16 were waited for; matrix products, arithmetic and copies ran while one was open for 18% of the time, Pallas kernels for 12%

profile of v3, /device:TPU:0, one launch (start us, length us, event | category | flops | bytes accessed | tf_op | source)
XLA Modules:
  0.0 1074.4 jit_solution(2299387910124081648)
XLA Ops:
  11.9 182.8 %shard_map.263 = (bf16[8,4,64,1152]{3,2,1,0:T(8,128)(2,1)}, bf16[8,4,64,4096]{3,2,1,0:T(8,128)(2,1)}, bf16[8,4,128,2048]{3,2,1,0:T(8,128)(2,1)}) custom-call(bf16[64,1152]{1,0:T(8,128)(2,1)} %fusion.86.refs_0_, bf16[64,4096]{1,0:T(8,128)(2,1)} %refs_1_.1, bf16[128,2048]{1,0:T(8,128)(2,1)} %refs_2_.1), custom_call_target="tpu_custom_call" | custom-call | bytes 76546048 | tf_op jit(solution)/shard_map/pallas_call | solution.py:198
  194.7 3.1 slice_bitcast_fusion
  201.8 3.9 copy.152
  205.7 2.6 multiply_reduce_fusion.5
  219.6 34.4 %all-gather.6.cloned.1.call-done.pairs_ref = bf16[1024,1024]{1,0:T(8,128)(2,1)} async-done(((bf16[128,1024]{1,0:T(8,128)(2,1)}), bf16[1024,1024]{1,0:T(8,128)(2,1)}) %all-gather.6.cloned.1.call-update) | async-done | bytes 2097168 | tf_op jit(solution)/shard_map/all_gather | solution.py:505
  256.7 4.7 all-to-all-start.1
  265.6 8.9 all-reduce.1
  276.7 9.8 fusion.71.query_ref
  289.7 2.7 reduce-window.31
  296.1 12.7 %attend.1 = (bf16[128,4096]{1,0:T(8,128)(2,1)S(1)}, bf16[128,4096]{1,0:T(8,128)(2,1)S(1)}) custom-call(f32[128,4096]{1,0:T(8,128)S(1)} %copy-done.3, bf16[1024,1024]{1,0:T(8,128)(2,1)S(1)} %copy-done.5, f32[1,128]{1,0:T(1,128)S(1)} %bitcast.264, f32[128,128]{1,0:T(8,128)S(1)} %get-tuple-element.152.cosine_ref, f32[128,128]{1,0:T(8,128)S(1)} %get-tuple-element.150.sine_ref, ...), custom_call_target="tpu_custom_call" | custom-call | flops 2147483648 | bytes 4194304 | tf_op jit(solution)/shard_map/attend/pallas_call | solution.py:353
  308.9 9.9 multiply_reduce_fusion.2
  318.8 2.5 multiply_convert_fusion.3.refs_0_
  321.3 120.7 %shard_map.264 = bf16[4,8,128,2048]{3,2,1,0:T(8,128)(2,1)} custom-call(bf16[128,2048]{1,0:T(8,128)(2,1)} %multiply_convert_fusion.3.refs_0_), custom_call_target="tpu_custom_call" | custom-call | bytes 33554432 | tf_op jit(solution)/shard_map/pallas_call | solution.py:198
  442.1 10.7 fusion.26
  452.8 3.4 fusion.35
  457.8 5.2 multiply_convert_fusion
  464.7 10.6 fusion.25
  475.4 5.0 fusion
  481.8 12.4 %all-to-all-start.4 = ((f32[32,1,128]{2,1,0:T(1,128)}), f32[32,1,128]{2,1,0:T(1,128)S(1)}, u32[]{:S(2)}, u32[]{:S(2)}) async-start(f32[32,1,128]{2,1,0:T(1,128)} %all_to_all.52), calls=%async_computation.5 | async-start | bytes 32768 | tf_op jit(solution)/shard_map/all_to_all | solution.py:508
  494.3 7.1 all-to-all-done.4
  504.3 2.5 all-to-all-start.2
  509.2 4.8 all-to-all-done.2
  514.0 4.5 all-to-all-start.3
  520.2 3.1 fusion.2
  524.3 4.4 multiply_convert_fusion.1
  528.7 3.4 fusion.33
  532.2 5.0 add_convert_fusion
  537.2 3.7 dynamic-slice_bitcast_fusion.7
  543.6 4.2 all-to-all-start
  547.9 4.7 all-to-all-done
  555.8 11.2 %collective-permute-done.2 = bf16[256,2048]{1,0:T(8,128)(2,1)} collective-permute-done((bf16[256,2048]{1,0:T(8,128)(2,1)}, bf16[256,2048]{1,0:T(8,128)(2,1)}, u32[]{:S(2)}, u32[]{:S(2)}) %collective-permute-start.2) | collective-permute-done | bytes 1048608 | tf_op jit(solution)/shard_map/ppermute | solution.py:666
  567.0 67.3 %collective-permute-done.1 = bf16[256,2048]{1,0:T(8,128)(2,1)} collective-permute-done((bf16[256,2048]{1,0:T(8,128)(2,1)S(1)}, bf16[256,2048]{1,0:T(8,128)(2,1)}, u32[]{:S(2)}, u32[]{:S(2)}) %collective-permute-start.1) | collective-permute-done | bytes 1048608 | tf_op jit(solution)/shard_map/ppermute | solution.py:666
  634.2 8.4 fusion.30
  643.8 49.5 %reduce-scatter.7.cloned.1.call-done = bf16[128,2048]{1,0:T(8,128)(2,1)} async-done(((bf16[1024,2048]{1,0:T(8,128)(2,1)}), bf16[128,2048]{1,0:T(8,128)(2,1)}) %reduce-scatter.7.cloned.1.call-update) | async-done | bytes 524304 | tf_op jit(solution)/shard_map/reduce_scatter | solution.py:511
  693.3 2.7 multiply_reduce_fusion
  696.0 2.7 fusion.100
  698.7 11.6 %convolution_convert_fusion.cot_ref = bf16[128,4096]{1,0:T(8,128)(2,1)S(1)} fusion(bf16[128,2048]{1,0:T(8,128)(2,1)S(1)} %get-tuple-element.128, bf16[4096,2048]{1,0:T(8,128)(2,1)} %bitcast.267), kind=kOutput, calls=%fused_computation.10 | convolution fusion | flops 2148007936 | bytes 18350080 | tf_op jit(solution)/shard_map/dot_general | solution.py:61
  711.4 23.1 %attend_back.1 = (bf16[128,4096]{1,0:T(8,128)(2,1)S(1)}, bf16[1024,1024]{1,0:T(8,128)(2,1)}, f32[32,128]{1,0:T(8,128)S(1)}) custom-call(f32[128,4096]{1,0:T(8,128)} %fusion.71.query_ref, bf16[128,4096]{1,0:T(8,128)(2,1)S(1)} %copy-done.8, bf16[128,4096]{1,0:T(8,128)(2,1)S(1)} %convolution_convert_fusion.cot_ref, ...), custom_call_target="tpu_custom_call" | custom-call | flops 5368709120 | bytes 6291456 | tf_op jit(solution)/shard_map/attend_back/pallas_call | solution.py:409
  735.2 40.6 %reduce-scatter.11.cloned.1.call-done = bf16[128,1024]{1,0:T(8,128)(2,1)} async-done(((bf16[1024,1024]{1,0:T(8,128)(2,1)}), bf16[128,1024]{1,0:T(8,128)(2,1)}) %reduce-scatter.11.cloned.1.call-update) | async-done | bytes 262160 | tf_op jit(solution)/shard_map/reduce_scatter | solution.py:511
  779.2 3.4 all-to-all-start.8
  783.7 7.1 all-to-all-done.8
  790.8 3.6 all-to-all-start.6
  794.6 3.5 convolution_convert_fusion.4
  799.1 18.1 %all-to-all-done.6 = bf16[8,128,512]{2,1,0:T(8,128)(2,1)S(1)} async-done(((bf16[8,128,512]{2,1,0:T(8,128)(2,1)}), bf16[8,128,512]{2,1,0:T(8,128)(2,1)S(1)}, u32[]{:S(2)}, u32[]{:S(2)}) %all-to-all-start.6) | async-done | bytes 1048608 | tf_op jit(solution)/shard_map/all_to_all | solution.py:508
  818.1 4.9 convolution_convert_fusion.3
  824.6 6.5 fusion.3
  831.6 3.4 collective-permute-start.5
  836.9 26.4 %collective-permute-done.5 = bf16[256,2048]{1,0:T(8,128)(2,1)S(1)} collective-permute-done((bf16[256,2048]{1,0:T(8,128)(2,1)S(1)}, bf16[256,2048]{1,0:T(8,128)(2,1)S(1)}, u32[]{:S(2)}, u32[]{:S(2)}) %collective-permute-start.5) | collective-permute-done | bytes 1048608 | tf_op jit(solution)/shard_map/ppermute | solution.py:666
  863.3 96.0 %collective-permute-done.4 = bf16[256,2048]{1,0:T(8,128)(2,1)S(1)} collective-permute-done((bf16[256,2048]{1,0:T(8,128)(2,1)S(1)}, bf16[256,2048]{1,0:T(8,128)(2,1)S(1)}, u32[]{:S(2)}, u32[]{:S(2)}) %collective-permute-start.4) | collective-permute-done | bytes 1048608 | tf_op jit(solution)/shard_map/ppermute | solution.py:666
  959.4 6.2 fusion.27
  968.1 2.6 all-to-all-start.10
  970.7 9.4 convolution_bitcast_fusion.2
  980.1 5.7 convolution_bitcast_fusion.1
  985.8 6.2 convolution_convert_fusion.2
  992.1 11.5 %fusion.108 = f32[128,2048]{1,0:T(8,128)S(1)} fusion(bf16[128,4096]{1,0:T(8,128)(2,1)S(1)} %get-tuple-element.40, bf16[2048,4096]{1,0:T(8,128)(2,1)} %bitcast.269), kind=kOutput, calls=%fused_computation.204 | convolution fusion | flops 2147483648 | bytes 18874368 | tf_op jit(solution)/shard_map/dot_general | solution.py:61
  1003.8 4.9 fusion.65
  1009.8 6.1 all-to-all-start.5
  1015.9 9.0 convolution_bitcast_fusion
  1025.8 2.7 fusion.64
  1028.5 4.2 all-to-all-done.5
  1033.7 6.9 all-to-all-start.9
  1041.1 5.0 all-to-all-done.9
  1046.1 4.1 all-to-all-start.7
  1051.0 9.0 all-to-all-done.7
  (255 shorter events, 81.2 us)
Async XLA Ops:
  7.2 468.2 %copy-start = (bf16[1,768,2048]{2,1,0:T(8,128)(2,1)S(1)}, bf16[1,768,2048]{2,1,0:T(8,128)(2,1)}, u32[]{:S(2)}) copy-start(bf16[1,768,2048]{2,1,0:T(8,128)(2,1)} %param.30) | copy-start | bytes 9437188
  7.2 190.6 %copy-start.27 = (f32[2048]{0:T(1024)S(1)}, f32[2048]{0:T(1024)}, u32[]{:S(2)}) copy-start(f32[2048]{0:T(1024)} %param.19) | copy-start | bytes 24580
  7.2 246.7 %all-gather.6.cloned.1.call-start = ((), (), s32[]{:S(2)}) async-start(), calls=%async_computation.17 | async-start | bytes 2359296 | tf_op jit(solution)/shard_map/all_gather | solution.py:505
  10.3 195.4 %copy-start.32 = (f32[128]{0:T(128)}, f32[128]{0:T(128)S(1)}, u32[]{:S(2)}) copy-start(f32[128]{0:T(128)S(1)} %add_rsqrt_fusion.2) | copy-start | bytes 1540
  201.8 6.5 copy-start.35
  201.8 7.4 copy-start.39
  208.3 67.0 %copy-start.15 = (f32[128,4,128]{0,2,1:T(8,128)}, f32[128,4,128]{0,2,1:T(8,128)S(1)}, u32[]{:S(2)}) copy-start(f32[128,4,128]{0,2,1:T(8,128)S(1)} %get-tuple-element.166) | copy-start | bytes 786436
  219.5 245.1 %all-gather.8.cloned.1.call-start = ((), (), s32[]{:S(2)}) async-start(), calls=%async_computation.18 | async-start | bytes 17301504 | tf_op jit(solution)/shard_map/all_gather | solution.py:505
  256.7 31.0 %all-to-all-start.1 = ((s32[32,1,128]{2,1,0:T(1,128)}), s32[32,1,128]{2,1,0:T(1,128)}, u32[]{:S(2)}, u32[]{:S(2)}) async-start(s32[32,1,128]{2,1,0:T(1,128)} %bitcast.302), calls=%async_computation.1 | async-start | bytes 32768 | tf_op jit(solution)/shard_map/all_to_all | solution.py:508
  261.5 275.8 %all-gather.10.cloned.1.call-start = ((), (), s32[]{:S(2)}) async-start(), calls=%async_computation.19 | async-start | bytes 4718592 | tf_op jit(solution)/shard_map/all_gather | solution.py:505
  276.7 16.3 %copy-start.6 = (f32[128]{0:T(128)S(1)}, f32[128]{0:T(128)}, u32[]{:S(2)}) copy-start(f32[128]{0:T(128)} %param.23) | copy-start | bytes 1540
  296.1 12.8 %copy-start.11 = (bf16[1,128,2048]{2,1,0:T(8,128)(2,1)S(1)}, bf16[1,128,2048]{2,1,0:T(8,128)(2,1)}, u32[]{:S(2)}) copy-start(bf16[1,128,2048]{2,1,0:T(8,128)(2,1)} %param.16) | copy-start | bytes 1572868
  308.9 9.9 copy-start.2
  308.9 9.9 copy-start.7
  308.9 9.9 copy-start.30
  442.0 10.7 copy-start.40
  452.8 5.1 copy-start.42
  464.7 10.7 copy-start.19
  475.3 5.1 copy-start.9
  475.4 26.0 %copy-start.38 = (s32[32]{0:T(128)S(1)}, s32[32]{0:T(128)}, u32[]{:S(2)}) copy-start(s32[32]{0:T(128)} %select_reduce_fusion.2) | copy-start | bytes 388
  481.8 19.5 %all-to-all-start.4 = ((f32[32,1,128]{2,1,0:T(1,128)}), f32[32,1,128]{2,1,0:T(1,128)S(1)}, u32[]{:S(2)}, u32[]{:S(2)}) async-start(f32[32,1,128]{2,1,0:T(1,128)} %all_to_all.52), calls=%async_computation.5 | async-start | bytes 32768 | tf_op jit(solution)/shard_map/all_to_all | solution.py:508
  504.3 9.7 all-to-all-start.2
  514.0 23.2 %all-to-all-start.3 = ((bf16[8,128,512]{2,1,0:T(8,128)(2,1)}), bf16[8,128,512]{2,1,0:T(8,128)(2,1)}, u32[]{:S(2)}, u32[]{:S(2)}) async-start(bf16[8,128,512]{2,1,0:T(8,128)(2,1)} %bitcast.274), calls=%async_computation.3 | async-start | bytes 2097152 | tf_op jit(solution)/shard_map/all_to_all | solution.py:508
  541.0 26.0 %collective-permute-start.2 = (bf16[256,2048]{1,0:T(8,128)(2,1)}, bf16[256,2048]{1,0:T(8,128)(2,1)}, u32[]{:S(2)}, u32[]{:S(2)}) collective-permute-start(bf16[256,2048]{1,0:T(8,128)(2,1)} %get-tuple-element.138), channel_id=1, source_target_pairs={{0,3},{1,0},{2,1},{3,2},{4,7},{5,4},{6,5},{7,6},{8,11},{9,8},{10,9... | collective-permute-start | bytes 3145736 | tf_op jit(solution)/shard_map/ppermute | solution.py:666
  541.5 92.7 %collective-permute-start.1 = (bf16[256,2048]{1,0:T(8,128)(2,1)S(1)}, bf16[256,2048]{1,0:T(8,128)(2,1)}, u32[]{:S(2)}, u32[]{:S(2)}) collective-permute-start(bf16[256,2048]{1,0:T(8,128)(2,1)S(1)} %get-tuple-element.139), channel_id=1, source_target_pairs={{0,2},{1,3},{2,0},{3,1},{4,6},{5,7},{6,4},{7,5},{8,10},{9,11},{10,... | collective-permute-start | bytes 3145736 | tf_op jit(solution)/shard_map/ppermute | solution.py:666
  543.0 91.2 %collective-permute-start = (bf16[256,2048]{1,0:T(8,128)(2,1)S(1)}, bf16[256,2048]{1,0:T(8,128)(2,1)}, u32[]{:S(2)}, u32[]{:S(2)}) collective-permute-start(bf16[256,2048]{1,0:T(8,128)(2,1)S(1)} %get-tuple-element.140), channel_id=1, source_target_pairs={{0,1},{1,2},{2,3},{3,0},{4,5},{5,6},{6,7},{7,4},{8,9},{9,10},{10,1... | collective-permute-start | bytes 3145736 | tf_op jit(solution)/shard_map/ppermute | solution.py:666
  543.6 8.9 all-to-all-start
  547.8 145.5 %reduce-scatter.7.cloned.1.call-start = ((), (), s32[]{:S(2)}) async-start(), calls=%async_computation.20 | async-start | bytes 4718592 | tf_op jit(solution)/shard_map/reduce_scatter | solution.py:511
  642.7 53.3 %copy-start.18 = (bf16[1,128,2048]{2,1,0:T(8,128)(2,1)S(1)}, bf16[1,128,2048]{2,1,0:T(8,128)(2,1)}, u32[]{:S(2)}) copy-start(bf16[1,128,2048]{2,1,0:T(8,128)(2,1)} %param.31) | copy-start | bytes 1572868
  642.7 133.1 %reduce-scatter.11.cloned.1.call-start = ((), (), s32[]{:S(2)}) async-start(), calls=%async_computation.22 | async-start | bytes 2359296 | tf_op jit(solution)/shard_map/reduce_scatter | solution.py:511
  698.7 11.6 %copy-start.14 = (bf16[128,2048]{1,0:T(8,128)(2,1)}, bf16[128,2048]{1,0:T(8,128)(2,1)S(1)}, u32[]{:S(2)}) copy-start(bf16[128,2048]{1,0:T(8,128)(2,1)S(1)} %get-tuple-element.128) | copy-start | bytes 1572868
  698.7 11.7 %copy-start.8 = (bf16[128,4096]{1,0:T(8,128)(2,1)S(1)}, bf16[128,4096]{1,0:T(8,128)(2,1)}, u32[]{:S(2)}) copy-start(bf16[128,4096]{1,0:T(8,128)(2,1)} %copy-done.7) | copy-start | bytes 3145732
  711.4 23.8 %copy-start.26 = (f32[128,128]{1,0:T(8,128)S(1)}, f32[128,128]{1,0:T(8,128)}, u32[]{:S(2)}) copy-start(f32[128,128]{1,0:T(8,128)} %get-tuple-element.149) | copy-start | bytes 196612
  734.5 43.2 %copy-start.16 = (f32[128,4,128]{0,2,1:T(8,128)S(1)}, f32[128,4,128]{0,2,1:T(8,128)}, u32[]{:S(2)}) copy-start(f32[128,4,128]{0,2,1:T(8,128)} %copy-done.15) | copy-start | bytes 786436
  734.5 43.2 %copy-start.21 = (f32[128,128]{0,1:T(8,128)S(1)}, f32[128,128]{0,1:T(8,128)}, u32[]{:S(2)}) copy-start(f32[128,128]{0,1:T(8,128)} %copy.153) | copy-start | bytes 196612
  734.5 43.2 %copy-start.36 = (f32[128]{0:T(128)S(1)}, f32[128]{0:T(128)}, u32[]{:S(2)}) copy-start(f32[128]{0:T(128)} %param.24) | copy-start | bytes 1540
  734.6 251.3 %all-gather.12.cloned.1.call-start = ((), (), s32[]{:S(2)}) async-start(), calls=%async_computation.25 | async-start | bytes 4718592 | tf_op jit(solution)/shard_map/all_gather | solution.py:505
  778.5 12.3 %copy-start.24 = (bf16[128,4,128]{0,2,1:T(8,128)(2,1)}, bf16[128,4,128]{0,2,1:T(8,128)(2,1)S(1)}, u32[]{:S(2)}) copy-start(bf16[128,4,128]{0,2,1:T(8,128)(2,1)S(1)} %multiply_convert_fusion.4) | copy-start | bytes 393220
  779.2 11.6 %all-to-all-start.8 = ((bf16[8,128,128]{1,2,0:T(8,128)(2,1)}), bf16[8,128,128]{1,2,0:T(8,128)(2,1)S(1)}, u32[]{:S(2)}, u32[]{:S(2)}) async-start(bf16[8,128,128]{1,2,0:T(8,128)(2,1)} %maximum_bitcast_fusion), calls=%async_computation.12 | async-start | bytes 524288 | tf_op jit(solution)/shard_map/all_to_all | solution.py:508
  790.8 26.3 %all-to-all-start.6 = ((bf16[8,128,512]{2,1,0:T(8,128)(2,1)}), bf16[8,128,512]{2,1,0:T(8,128)(2,1)S(1)}, u32[]{:S(2)}, u32[]{:S(2)}) async-start(bf16[8,128,512]{2,1,0:T(8,128)(2,1)} %bitcast.254), calls=%async_computation.9 | async-start | bytes 2097152 | tf_op jit(solution)/shard_map/all_to_all | solution.py:508
  794.4 239.3 %reduce-scatter.15.cloned.1.call-start = ((), (), s32[]{:S(2)}) async-start(), calls=%async_computation.24 | async-start | bytes 655360 | tf_op jit(solution)/shard_map/reduce_scatter | solution.py:511
  799.0 247.1 %reduce-scatter.13.cloned.1.call-start = ((), (), s32[]{:S(2)}) async-start(), calls=%async_computation.23 | async-start | bytes 2621440 | tf_op jit(solution)/shard_map/reduce_scatter | solution.py:511
  824.6 237.7 %reduce-scatter.9.cloned.1.call-start = ((), (), s32[]{:S(2)}) async-start(), calls=%async_computation.21 | async-start | bytes 4718592 | tf_op jit(solution)/shard_map/reduce_scatter | solution.py:511
  831.6 31.7 %collective-permute-start.5 = (bf16[256,2048]{1,0:T(8,128)(2,1)S(1)}, bf16[256,2048]{1,0:T(8,128)(2,1)S(1)}, u32[]{:S(2)}, u32[]{:S(2)}) collective-permute-start(bf16[256,2048]{1,0:T(8,128)(2,1)S(1)} %get-tuple-element.134), channel_id=1, source_target_pairs={{0,3},{1,0},{2,1},{3,2},{4,7},{5,4},{6,5},{7,6},{8,11},{9,8},{10,9... | collective-permute-start | bytes 3145736 | tf_op jit(solution)/shard_map/ppermute | solution.py:666
  835.0 124.3 %collective-permute-start.4 = (bf16[256,2048]{1,0:T(8,128)(2,1)S(1)}, bf16[256,2048]{1,0:T(8,128)(2,1)S(1)}, u32[]{:S(2)}, u32[]{:S(2)}) collective-permute-start(bf16[256,2048]{1,0:T(8,128)(2,1)S(1)} %get-tuple-element.135), channel_id=1, source_target_pairs={{0,2},{1,3},{2,0},{3,1},{4,6},{5,7},{6,4},{7,5},{8,10},{9,11},{10,... | collective-permute-start | bytes 3145736 | tf_op jit(solution)/shard_map/ppermute | solution.py:666
  835.0 124.3 %collective-permute-start.3 = (bf16[256,2048]{1,0:T(8,128)(2,1)S(1)}, bf16[256,2048]{1,0:T(8,128)(2,1)S(1)}, u32[]{:S(2)}, u32[]{:S(2)}) collective-permute-start(bf16[256,2048]{1,0:T(8,128)(2,1)S(1)} %get-tuple-element.136), channel_id=1, source_target_pairs={{0,1},{1,2},{2,3},{3,0},{4,5},{5,6},{6,7},{7,4},{8,9},{9,10},{10,1... | collective-permute-start | bytes 3145736 | tf_op jit(solution)/shard_map/ppermute | solution.py:666
  968.1 40.6 %all-to-all-start.10 = ((f32[32,1,2048]{2,1,0:T(1,128)}), f32[32,1,2048]{2,1,0:T(1,128)S(1)}, u32[]{:S(2)}, u32[]{:S(2)}) async-start(f32[32,1,2048]{2,1,0:T(1,128)} %all_to_all.61), calls=%async_computation.16 | async-start | bytes 524288 | tf_op jit(solution)/shard_map/all_to_all | solution.py:508
  970.7 9.5 copy-start.51
  970.7 94.3 %reduce-scatter.17.cloned.1.call-start = ((), (), s32[]{:S(2)}) async-start(), calls=%async_computation.26 | async-start | bytes 2621440 | tf_op jit(solution)/shard_map/reduce_scatter | solution.py:511
  970.7 9.4 copy-start.45
  992.1 11.7 %copy-start.12 = (bf16[1,128,2048]{2,1,0:T(8,128)(2,1)S(1)}, bf16[1,128,2048]{2,1,0:T(8,128)(2,1)}, u32[]{:S(2)}) copy-start(bf16[1,128,2048]{2,1,0:T(8,128)(2,1)} %param.16) | copy-start | bytes 1572868
  992.1 11.7 %copy-start.23 = (bf16[128,4,1,128]{0,3,1,2:T(8,128)(2,1)S(1)}, bf16[128,4,1,128]{0,3,1,2:T(8,128)(2,1)}, u32[]{:S(2)}) copy-start(bf16[128,4,1,128]{0,3,1,2:T(8,128)(2,1)} %copy-done.22) | copy-start | bytes 393220
  992.1 11.7 %copy-start.25 = (bf16[128,4,128]{0,2,1:T(8,128)(2,1)S(1)}, bf16[128,4,128]{0,2,1:T(8,128)(2,1)}, u32[]{:S(2)}) copy-start(bf16[128,4,128]{0,2,1:T(8,128)(2,1)} %copy-done.24) | copy-start | bytes 393220
  992.1 11.7 %copy-start.28 = (f32[2048]{0:T(1024)S(1)}, f32[2048]{0:T(1024)}, u32[]{:S(2)}) copy-start(f32[2048]{0:T(1024)} %param.19) | copy-start | bytes 24580
  992.1 11.7 %copy-start.33 = (f32[128]{0:T(128)S(1)}, f32[128]{0:T(128)}, u32[]{:S(2)}) copy-start(f32[128]{0:T(128)} %copy-done.32) | copy-start | bytes 1540
  1003.7 5.0 copy-start.31
  1003.7 5.0 copy-start.37
  1009.8 23.0 %all-to-all-start.5 = ((f32[32,1,4352]{2,1,0:T(1,128)}), f32[32,1,4352]{2,1,0:T(1,128)S(1)}, u32[]{:S(2)}, u32[]{:S(2)}) async-start(f32[32,1,4352]{2,1,0:T(1,128)} %broadcast_in_dim.148), calls=%async_computation.8 | async-start | bytes 1114112 | tf_op jit(solution)/shard_map/all_to_all | solution.py:464
  1015.9 9.9 copy-start.17
  1015.9 9.9 copy-start.29
  1015.9 9.9 copy-start.34
  1033.7 12.4 %all-to-all-start.9 = ((bf16[8,64,128]{2,1,0:T(8,128)(2,1)}), bf16[8,64,128]{2,1,0:T(8,128)(2,1)S(1)}, u32[]{:S(2)}, u32[]{:S(2)}) async-start(bf16[8,64,128]{2,1,0:T(8,128)(2,1)} %bitcast.300), calls=%async_computation.14 | async-start | bytes 262144 | tf_op jit(solution)/shard_map/all_to_all | solution.py:508
  1046.1 13.9 %all-to-all-start.7 = ((bf16[8,64,512]{2,1,0:T(8,128)(2,1)}), bf16[8,64,512]{2,1,0:T(8,128)(2,1)}, u32[]{:S(2)}, u32[]{:S(2)}) async-start(bf16[8,64,512]{2,1,0:T(8,128)(2,1)} %bitcast.289), calls=%async_computation.11 | async-start | bytes 1048576 | tf_op jit(solution)/shard_map/all_to_all | solution.py:508
  1050.3 16.8 %copy-start.1 = (bf16[1,768,2048]{2,1,0:T(8,128)(2,1)S(1)}, bf16[1,768,2048]{2,1,0:T(8,128)(2,1)}, u32[]{:S(2)}) copy-start(bf16[1,768,2048]{2,1,0:T(8,128)(2,1)} %param.30) | copy-start | bytes 9437188
  (15 other events, 38.4 us)
Sparse Core Ops, SparseCore 0:
  219.7 34.2 all-gather.5
  256.8 155.5 all-gather.7
  463.2 44.6 all-gather.9
  642.8 50.4 reduce-scatter.6
  734.7 41.0 reduce-scatter.10
  777.5 44.0 all-gather.11
  824.0 62.2 reduce-scatter.14
  888.5 75.9 reduce-scatter.12
  967.8 50.8 reduce-scatter.8
  1020.9 44.0 reduce-scatter.16

commit v4 on v3

--- a/solution.py
+++ b/solution.py
@@ -510,13 +510,33 @@
     def scatter_sum(value, axes):
         return lax.psum_scatter(value, axes, scatter_dimension=0, tiled=True)
 
+    def turn(blocks):
+        arrived = []
+        for step in range(wt_size):
+            block = lax.dynamic_index_in_dim(
+                blocks, lax.rem(wt_index + step, wt_size), keepdims=False
+            )
+            if step:
+                pairs = [(w, (w + step) % wt_size) for w in range(wt_size)]
+                block = lax.ppermute(block, "wt", pairs)
+            arrived.append(block)
+        return arrived
+
+    def line_sum(blocks):
+        return sum(block.astype(jnp.float32) for block in turn(blocks))
+
     doc_ends = jnp.cumsum(doc_lengths[0])
     all_positions = jnp.arange(seq_len, dtype=jnp.int32)
     doc_all = jnp.sum((doc_ends[None, :] <= all_positions[:, None]).astype(jnp.int32), axis=1)
     first_pos = ctx_index * tokens
     my_positions = first_pos + jnp.arange(tokens, dtype=jnp.int32)
     my_docs = lax.dynamic_slice_in_dim(doc_all, first_pos, tokens)
-    cosine_table, sine_table = rotary_tables(my_positions, head_dim)
+    cosine_all, sine_all = rotary_tables(all_positions, head_dim)
+
+    def mine_of(rows):
+        return lax.dynamic_slice_in_dim(rows, first_pos, tokens)
+
+    cosine_table, sine_table = mine_of(cosine_all), mine_of(sine_all)
     cosine_rows = cosine_table[:, 0, :]
     first_half = jnp.arange(head_dim) < head_dim // 2
     sine_rows = jnp.where(first_half[None, :], -sine_table[:, 0, :], sine_table[:, 0, :])
@@ -524,9 +544,18 @@
     expert_ids = jnp.arange(expert_count, dtype=jnp.int32)
     hits = jnp.sum((routes[0][:, :, None] == expert_ids[None, None, :]).astype(jnp.int32), axis=1)
     local_rank = jnp.cumsum(hits, axis=0) - hits
-    counts = lax.all_gather(jnp.sum(hits, axis=0), "ctx")
+    assert expert_count <= tokens
+    counts = jnp.pad(jnp.sum(hits, axis=0), (0, tokens - expert_count))
+    plane_mine = jnp.concatenate(
+        [
+            hits.T.reshape(ctx_size, wt_size, tokens),
+            jnp.broadcast_to(counts, (ctx_size, 1, tokens)),
+        ],
+        axis=1,
+    )
+    plane = exchange(plane_mine, "ctx")
     earlier = jnp.arange(ctx_size, dtype=jnp.int32)[:, None] < ctx_index
-    offsets = jnp.sum(jnp.where(earlier, counts, 0), axis=0)
+    offsets = jnp.sum(jnp.where(earlier, plane[:, wt_size, :expert_count], 0), axis=0)
     kept = (hits > 0) & (local_rank + offsets[None, :] < capacity)
     keep_float = kept.astype(jnp.float32)
     hits_float = hits.astype(jnp.float32)
@@ -543,10 +572,8 @@
     slot_ids = jnp.arange(capacity, dtype=jnp.int32)
     place = slot_mine[:, None, :] == slot_ids[None, :, None]
     place_low = place.astype(jnp.bfloat16)
-    hit_plane = exchange(hits.T.reshape(ctx_size, wt_size, tokens), "ctx").transpose(1, 0, 2)
-    hit_plane = hit_plane.reshape(wt_size, seq_len)[
-        (wt_index - jnp.arange(wt_size)) % wt_size
-    ]
+    hit_plane = plane[:, :wt_size].transpose(1, 0, 2).reshape(wt_size, seq_len)
+    hit_plane = hit_plane[(wt_index - jnp.arange(wt_size)) % wt_size]
     slot_plane = jnp.cumsum(hit_plane, axis=1) - hit_plane
     slot_plane = jnp.where((hit_plane > 0) & (slot_plane < capacity), slot_plane, -1)
     spread_low = (slot_plane[:, None, :] == slot_ids[None, :, None]).astype(jnp.bfloat16)
@@ -554,6 +581,7 @@
     resid_in = hidden_in[0].astype(jnp.float32)
     normed_in = norm_rows(resid_in, gain_attn).astype(jnp.bfloat16)
     router_pad = -expert_count % head_dim
+    normed_in_all = gather(normed_in, "ctx")
     side_mine = jnp.concatenate(
         [key_weight, value_weight, jnp.pad(w_router, ((0, 0), (0, router_pad)))], axis=1
     )
@@ -566,26 +594,19 @@
         side_weights = gather(side_mine, both)
         query_full = gather(w_query, both)
         out_full = gather(w_out, both)
-    key_full = side_weights[:, :kv_width]
-    value_full = side_weights[:, kv_width : 2 * kv_width]
     router_full = side_weights[:, 2 * kv_width : 2 * kv_width + expert_count]
-    key_sum = matmul(normed_in, key_full).reshape(tokens, key_heads, head_dim)
-    value_low = matmul(normed_in, value_full).astype(jnp.bfloat16)
-    key_low = (
-        rotate(norm_rows(key_sum, gain_key), cosine_table, sine_table)
-        .reshape(tokens, kv_width)
-        .astype(jnp.bfloat16)
-    )
-
-    def interleave(left, right):
-        both_heads = jnp.stack(
-            [side.reshape(-1, key_heads, head_dim) for side in (left, right)], axis=2
-        )
-        return both_heads.reshape(-1, 2 * kv_width)
-
-    pairs_all = gather(interleave(key_low, value_low), "ctx")
+    pair_sums = lax.optimization_barrier(
+        matmul(normed_in_all, side_weights[:, : 2 * kv_width])
+    )
+    key_sums = pair_sums[:, :kv_width].reshape(seq_len, key_heads, head_dim)
+    key_low = rotate(norm_rows(key_sums, gain_key), cosine_all, sine_all).astype(jnp.bfloat16)
+    value_low = pair_sums[:, kv_width:].astype(jnp.bfloat16)
+    pairs_all = jnp.concatenate(
+        [key_low, value_low.reshape(seq_len, key_heads, head_dim)], axis=2
+    ).reshape(seq_len, 2 * kv_width)
+    key_sum = mine_of(key_sums)
     if small_plane:
-        cot_all = gather(after(out_grad[0], pairs_all), by_stream)
+        cot_all = gather(after(out_grad[0], query_full), by_stream)
     query_sum = lax.optimization_barrier(matmul(normed_in, query_full))
     mixed_low, query_low = attend(
         query_sum,
@@ -629,7 +650,6 @@
     if not small_plane:
         cot_all = gather(after(out_grad[0], filled), by_stream)
     cot_all = cot_all.reshape(wt_size, seq_len, model_width)
-    normed_in_all = gather(after(normed_in, filled), "ctx")
     mixed_columns = column_blocks(after(mixed_low, filled))
     gate_h = matmul(filled, expert_gate[0])
     up_h = matmul(filled, expert_up[0])
@@ -655,29 +675,19 @@
         contract_cols(gate_cot_h, expert_gate[0]) + contract_cols(up_cot_h, expert_up[0])
     ).astype(jnp.bfloat16)
 
-    def turn(blocks):
-        arrived = []
-        for step in range(wt_size):
-            block = lax.dynamic_index_in_dim(
-                blocks, lax.rem(wt_index + step, wt_size), keepdims=False
-            )
-            if step:
-                pairs = [(w, (w + step) % wt_size) for w in range(wt_size)]
-                block = lax.ppermute(block, "wt", pairs)
-            arrived.append(block)
-        return arrived
-
     def add_pairs(table, stream_rows):
         partial = contract_rows(
             table.reshape(wt_size * capacity, seq_len), jnp.concatenate(stream_rows, axis=0)
         ).astype(jnp.bfloat16)
         return scatter_sum(partial, "ctx").astype(jnp.float32)
 
-    gate_cot = from_owner_rows(exchange(gate_cot_mine.reshape(devices, tokens), by_stream))
     mixed_rows = (gate_rows[:, None] * result_rows.astype(jnp.float32)).astype(jnp.bfloat16)
-    in_rows_cot, normed_in_all, mixed_columns = lax.optimization_barrier(
-        (in_rows_cot, normed_in_all, mixed_columns)
-    )
+    in_rows_cot, mixed_columns, spread_low = lax.optimization_barrier(
+        (in_rows_cot, mixed_columns, spread_low)
+    )
+    gate_cot = from_owner_rows(exchange(
+        after(gate_cot_mine, in_rows_cot).reshape(devices, tokens), by_stream
+    ))
     blocks_shape = (wt_size, capacity, model_width)
     stream_cots = turn(in_rows_cot.reshape(blocks_shape))
     returned_cot = add_pairs(spread_low, stream_cots)
@@ -701,9 +711,8 @@
 
     mixed_cot = contract_cols(attn_cot, out_full)
     attn_cot_all = gather(attn_cot, "ctx")
-    grad_w_out = scatter_sum(
-        contract_rows(mixed_columns, attn_cot_all).astype(jnp.bfloat16), "wt"
-    ).astype(jnp.float32)
+    out_block = contract_rows(mixed_columns, attn_cot_all).astype(jnp.bfloat16)
+    grad_w_out = line_sum(out_block.reshape(wt_size, -1, model_width))
 
     query_cot_low, pair_cots, gain_query_terms = attend_back(
         query_sum,
@@ -735,8 +744,8 @@
         width = cots.shape[1] // ctx_size
         block = contract_rows(normed_in_all, column_blocks(cots)).astype(jnp.bfloat16)
         block = block.reshape(ctx_size, wt_size, -1, width).transpose(1, 0, 2, 3)
-        mine = scatter_sum(block.reshape(model_width, width), "wt")
-        rows = exchange(mine.reshape(ctx_size, -1, width), "ctx")
+        mine = line_sum(block).astype(jnp.bfloat16)
+        rows = exchange(mine, "ctx")
         return rows.transpose(1, 0, 2).reshape(-1, width * ctx_size).astype(jnp.float32)
 
     grad_w_query = weight_grad(query_cot_low)

time: 1080 us -> 1010 us (0.935)
  waiting for transfers between devices: 386 us -> 313 us
  starting transfers between devices: 62.5 us -> 74.2 us
    reduce_scatter x6 -> x3, waiting for transfers between devices: 90.4 us -> 38.9 us  [scatter_sum(): return lax.psum_scatter(value, axes, scatter_dimension=0, tiled=True)]
    all_gather x4 -> x3, waiting for transfers between devices: 34.4 us -> 0.04 us  [gather(): return lax.all_gather(value, axes, axis=0, tiled=True)]
    all_to_all x10, waiting for transfers between devices: 55.7 us -> 86.8 us  [exchange(): return lax.all_to_all(value, axes, split_axis=0, concat_axis=0, tiled=True)]
    ppermute x6 -> x15, waiting for transfers between devices: 201 us -> 176 us  [turn(): block = lax.ppermute(block, 'wt', pairs)]
    ppermute x6 -> x15, starting transfers between devices: 7.11 us -> 23.5 us  [turn(): block = lax.ppermute(block, 'wt', pairs)]
    dot_general x8 -> x7, matrix products: 39.7 us -> 35.1 us  [matmul(): return jnp.dot(left_side, right_side, preferred_element_type=jnp.float32)]
  transfers between devices with their start and end apart: 27 -> 32, of which waited for: 16 -> 11; matrix products, arithmetic and copies ran while one was open for 18% -> 22% of each run, Pallas kernels for 12% -> 32%
where the time goes in v4:
time: 1010 us; the launch traced here: 1000 us
  Pallas kernels  341 us (34%)
  waiting for transfers between devices  313 us (31%)
  matrix products  154 us (15%)
  starting transfers between devices  74.2 us (7%)
  other arithmetic  59.2 us (6%)
  local copies, waits for them, and re-layouts  44.4 us (4%)
  between operations  15.6 us (2%)
    pallas_call x2, Pallas kernels, spread(): pl.pallas_call(functools.partial(spread_kernel, splits, streams_first), o...  304 us
    ppermute x15, waiting for transfers between devices, turn(): block = lax.ppermute(block, 'wt', pairs)  176 us
    all_to_all x10, waiting for transfers between devices, exchange(): return lax.all_to_all(value, axes, split_axis=0, concat_axis=0, tiled=True)  86.8 us
    dot_general x9, matrix products, contract_rows(): lax.dot_general(left_side, right_side, (((0,), (0,)), ((), ())), preferre...  53.4 us
    all_to_all x10, starting transfers between devices, exchange(): return lax.all_to_all(value, axes, split_axis=0, concat_axis=0, tiled=True)  47 us
    dot_general x7, matrix products, contract_cols(): lax.dot_general(left_side, right_side, (((1,), (1,)), ((), ())), preferre...  44.1 us
    reduce_scatter x3, waiting for transfers between devices, scatter_sum(): return lax.psum_scatter(value, axes, scatter_dimension=0, tiled=True)  38.9 us
    dot_general x7, matrix products, matmul(): return jnp.dot(left_side, right_side, preferred_element_type=jnp.float32)  35.1 us
  transfers between devices with their start and end apart: 32, of which 11 were waited for; matrix products, arithmetic and copies ran while one was open for 22% of the time, Pallas kernels for 32%

profile of v4, /device:TPU:0, one launch (start us, length us, event | category | flops | bytes accessed | tf_op | source)
XLA Modules:
  0.0 1001.6 jit_solution(5736495791738190561)
XLA Ops:
  13.1 192.6 %shard_map.263 = (bf16[8,4,64,1152]{3,2,1,0:T(8,128)(2,1)}, bf16[8,4,64,4096]{3,2,1,0:T(8,128)(2,1)}, bf16[8,4,128,2048]{3,2,1,0:T(8,128)(2,1)}) custom-call(bf16[64,1152]{1,0:T(8,128)(2,1)} %fusion.92.refs_0_, bf16[64,4096]{1,0:T(8,128)(2,1)} %refs_1_.1, bf16[128,2048]{1,0:T(8,128)(2,1)} %refs_2_.1), custom_call_target="tpu_custom_call" | custom-call | bytes 76546048 | tf_op jit(solution)/shard_map/pallas_call | solution.py:198
  207.2 4.0 all-to-all-start.1
  215.0 9.8 fusion.74.query_ref
  229.9 4.0 all-to-all-start
  245.5 7.6 fusion.33
  258.0 3.1 reshape.488
  261.0 2.9 multiply_reduce_fusion
  267.8 2.6 fusion.49
  272.4 13.0 %attend.1 = (bf16[128,4096]{1,0:T(8,128)(2,1)S(1)}, bf16[128,4096]{1,0:T(8,128)(2,1)S(1)}) custom-call(f32[128,4096]{1,0:T(8,128)S(1)} %copy-done.4, bf16[1024,1024]{1,0:T(8,128)(2,1)S(1)} %bitcast.269, f32[1,128]{1,0:T(1,128)S(1)} %bitcast.273, f32[128,128]{1,0:T(8,128)S(1)} %get-tuple-element.209.cosine_ref, f32[128,128]{1,0:T(8,128)S(1)} %get-tuple-element.182.sine_ref, ...), custom_call_target="tpu_custom_call" | custom-call | flops 2147483648 | bytes 4194304 | tf_op jit(solution)/shard_map/attend/pallas_call | solution.py:353
  285.5 2.6 multiply_reduce_fusion.3
  290.1 111.8 %shard_map.264 = bf16[4,8,128,2048]{3,2,1,0:T(8,128)(2,1)} custom-call(bf16[128,2048]{1,0:T(8,128)(2,1)} %multiply_convert_fusion.3.refs_0_), custom_call_target="tpu_custom_call" | custom-call | bytes 33554432 | tf_op jit(solution)/shard_map/pallas_call | solution.py:198
  404.2 9.8 all-to-all-start.2
  414.1 10.7 %fusion.24 = bf16[4,256,2048]{2,1,0:T(8,128)(2,1)S(1)} fusion(bf16[4,1024,2048]{2,1,0:T(8,128)(2,1)} %bitcast.282, s32[4,1024]{1,0:T(4,128)S(1)} %and_select_fusion.1), kind=kOutput, calls=%fused_computation.35 | convolution fusion | flops 4298113024 | bytes 20987904 | tf_op jit(solution)/shard_map/wkt,wtd->wkd/dot_general | solution.py:644
  424.8 3.4 fusion.37
  428.2 5.1 multiply_convert_fusion
  434.4 4.2 all-to-all-start.3
  440.0 11.0 %fusion.23 = bf16[4,256,2048]{2,1,0:T(8,128)(2,1)S(1)} fusion(bf16[4,1024,2048]{2,1,0:T(8,128)(2,1)} %bitcast.322, s32[4,1024]{1,0:T(4,128)S(1)} %and_select_fusion.1), kind=kOutput, calls=%fused_computation.34 | convolution fusion | flops 4298113024 | bytes 20987904 | tf_op jit(solution)/shard_map/wkt,wtd->wkd/dot_general | solution.py:644
  451.0 5.1 fusion
  457.3 3.1 fusion.2
  461.4 4.4 multiply_convert_fusion.1
  465.8 3.4 fusion.35
  469.3 5.2 add_convert_fusion
  474.5 2.9 dynamic-slice_bitcast_fusion.7
  477.4 3.7 collective-permute-start.2
  482.1 22.6 %collective-permute-done.2 = bf16[256,2048]{1,0:T(8,128)(2,1)S(1)} collective-permute-done((bf16[256,2048]{1,0:T(8,128)(2,1)S(1)}, bf16[256,2048]{1,0:T(8,128)(2,1)S(1)}, u32[]{:S(2)}, u32[]{:S(2)}) %collective-permute-start.2) | collective-permute-done | bytes 1048608 | tf_op jit(solution)/shard_map/ppermute | solution.py:521
  504.7 66.8 %collective-permute-done.1 = bf16[256,2048]{1,0:T(8,128)(2,1)S(1)} collective-permute-done((bf16[256,2048]{1,0:T(8,128)(2,1)S(1)}, bf16[256,2048]{1,0:T(8,128)(2,1)S(1)}, u32[]{:S(2)}, u32[]{:S(2)}) %collective-permute-start.1) | collective-permute-done | bytes 1048608 | tf_op jit(solution)/shard_map/ppermute | solution.py:521
  571.5 6.1 fusion.28
  578.2 5.1 all-to-all-start.4
  583.6 6.8 all-to-all-done.4
  590.5 38.9 %reduce-scatter.4.cloned.1.call-done = bf16[128,2048]{1,0:T(8,128)(2,1)} async-done(((bf16[1024,2048]{1,0:T(8,128)(2,1)}), bf16[128,2048]{1,0:T(8,128)(2,1)}) %reduce-scatter.4.cloned.1.call-update) | async-done | bytes 524304 | tf_op jit(solution)/shard_map/reduce_scatter | solution.py:511
  631.2 2.8 fusion.102
  634.0 11.6 %convolution_convert_fusion.cot_ref = bf16[128,4096]{1,0:T(8,128)(2,1)S(1)} fusion(bf16[128,2048]{1,0:T(8,128)(2,1)} %get-tuple-element.156, bf16[4096,2048]{1,0:T(8,128)(2,1)} %bitcast.275), kind=kOutput, calls=%fused_computation.10 | convolution fusion | flops 2148007936 | bytes 18350080 | tf_op jit(solution)/shard_map/dot_general | solution.py:61
  646.8 23.3 %attend_back.1 = (bf16[128,4096]{1,0:T(8,128)(2,1)S(1)}, bf16[1024,1024]{1,0:T(8,128)(2,1)}, f32[32,128]{1,0:T(8,128)S(1)}) custom-call(f32[128,4096]{1,0:T(8,128)} %fusion.74.query_ref, bf16[128,4096]{1,0:T(8,128)(2,1)S(1)} %copy-done.8, bf16[128,4096]{1,0:T(8,128)(2,1)S(1)} %convolution_convert_fusion.cot_ref, bf16[1024,1024]{1,0:T(8,128)(2,1)} %bitcast.270, ...), custom_call_target="tpu_custom_call" | custom-call | flops 5368709120 | bytes 6291456 | tf_op jit(solution)/shard_map/attend_back/pallas_call | solution.py:409
  672.1 9.0 convolution_bitcast_fusion.2
  681.2 5.9 convolution_bitcast_fusion.1
  687.1 4.3 fusion.3
  693.6 3.3 collective-permute-start.5
  699.6 4.0 all-to-all-start.10
  703.6 9.0 convolution_bitcast_fusion
  712.6 80.0 %all-to-all-done.10 = f32[32,1,2048]{2,1,0:T(1,128)S(1)} async-done(((f32[32,1,2048]{2,1,0:T(1,128)}), f32[32,1,2048]{2,1,0:T(1,128)S(1)}, u32[]{:S(2)}, u32[]{:S(2)}) %all-to-all-start.10) | async-done | bytes 262176 | tf_op jit(solution)/shard_map/all_to_all | solution.py:508
  795.1 4.2 all-to-all-start.6
  799.6 9.1 fusion.25
  808.7 12.4 %fusion.109 = f32[128,2048]{1,0:T(8,128)} fusion(bf16[128,4096]{1,0:T(8,128)(2,1)S(1)} %get-tuple-element.41, bf16[2048,4096]{1,0:T(8,128)(2,1)} %bitcast.280), kind=kOutput, calls=%fused_computation.225 | convolution fusion | flops 2147483648 | bytes 18874368 | tf_op jit(solution)/shard_map/dot_general | solution.py:61
  821.1 5.4 convolution_convert_fusion.3
  827.7 4.4 collective-permute-start.8
  837.8 4.0 all-to-all-start.8
  841.8 3.0 collective-permute-done.8
  844.8 32.4 %collective-permute-done.7 = bf16[8,64,512]{2,1,0:T(8,128)(2,1)} collective-permute-done((bf16[8,64,512]{2,1,0:T(8,128)(2,1)}, bf16[8,64,512]{2,1,0:T(8,128)(2,1)}, u32[]{:S(2)}, u32[]{:S(2)}) %collective-permute-start.7) | collective-permute-done | bytes 524320 | tf_op jit(solution)/shard_map/ppermute | solution.py:521
  877.2 2.4 fusion.72
  879.7 3.7 all-to-all-start.7
  883.7 3.6 convolution_convert_fusion.4
  888.1 3.1 collective-permute-start.10
  894.5 9.7 collective-permute-done.10
  905.9 3.9 all-to-all-start.9
  909.9 5.4 fusion.64
  916.5 3.3 all-to-all-start.5
  920.4 2.6 fusion.63
  923.7 10.9 %all-to-all-done.5 = f32[32,1,4352]{2,1,0:T(1,128)S(1)} async-done(((f32[32,1,4352]{2,1,0:T(1,128)}), f32[32,1,4352]{2,1,0:T(1,128)S(1)}, u32[]{:S(2)}, u32[]{:S(2)}) %all-to-all-start.5) | async-done | bytes 557088 | tf_op jit(solution)/shard_map/all_to_all | solution.py:464
  935.6 4.9 convolution_convert_fusion.2
  943.0 3.0 collective-permute-start.14
  947.6 2.4 add_bitcast_fusion
  950.0 10.1 %collective-permute-done.14 = bf16[128,2048]{1,0:T(8,128)(2,1)} collective-permute-done((bf16[128,2048]{1,0:T(8,128)(2,1)}, bf16[128,2048]{1,0:T(8,128)(2,1)}, u32[]{:S(2)}, u32[]{:S(2)}) %collective-permute-start.14) | collective-permute-done | bytes 524320 | tf_op jit(solution)/shard_map/ppermute | solution.py:521
  960.1 31.6 %collective-permute-done.13 = bf16[128,2048]{1,0:T(8,128)(2,1)} collective-permute-done((bf16[128,2048]{1,0:T(8,128)(2,1)}, bf16[128,2048]{1,0:T(8,128)(2,1)}, u32[]{:S(2)}, u32[]{:S(2)}) %collective-permute-start.13) | collective-permute-done | bytes 524320 | tf_op jit(solution)/shard_map/ppermute | solution.py:521
  991.7 2.8 fusion.69
  (284 shorter events, 82.5 us)
Async XLA Ops:
  7.2 443.8 %copy-start = (bf16[1,768,2048]{2,1,0:T(8,128)(2,1)S(1)}, bf16[1,768,2048]{2,1,0:T(8,128)(2,1)}, u32[]{:S(2)}) copy-start(bf16[1,768,2048]{2,1,0:T(8,128)(2,1)} %param.30) | copy-start | bytes 9437188
  7.2 207.8 %copy-start.33 = (f32[2048]{0:T(1024)S(1)}, f32[2048]{0:T(1024)}, u32[]{:S(2)}) copy-start(f32[2048]{0:T(1024)} %param.19) | copy-start | bytes 24580
  7.2 204.0 %copy-start.47 = (s32[1,2]{1,0:T(1,128)S(1)}, s32[1,2]{1,0:T(1,128)}, u32[]{:S(2)}) copy-start(s32[1,2]{1,0:T(1,128)} %param.17) | copy-start | bytes 28
  7.2 238.3 %all-gather.4.cloned.1.call-start = ((), (), s32[]{:S(2)}) async-start(), calls=%async_computation.14 | async-start | bytes 4718592 | tf_op jit(solution)/shard_map/all_gather | solution.py:505
  8.7 216.1 %copy-start.39 = (f32[128]{0:T(128)}, f32[128]{0:T(128)S(1)}, u32[]{:S(2)}) copy-start(f32[128]{0:T(128)S(1)} %add_rsqrt_fusion.3) | copy-start | bytes 1540
  10.7 429.2 %all-gather.6.cloned.1.call-start = ((), (), s32[]{:S(2)}) async-start(), calls=%async_computation.15 | async-start | bytes 17301504 | tf_op jit(solution)/shard_map/all_gather | solution.py:505
  207.2 22.7 %all-to-all-start.1 = ((s32[8,5,128]{2,1,0:T(8,128)}), s32[8,5,128]{2,1,0:T(8,128)}, u32[]{:S(2)}, u32[]{:S(2)}) async-start(s32[8,5,128]{2,1,0:T(8,128)} %pad_add_fusion), calls=%async_computation.1 | async-start | bytes 65536 | tf_op jit(solution)/shard_map/all_to_all | solution.py:508
  229.9 12.8 %all-to-all-start = ((s32[32,1,128]{2,1,0:T(1,128)}), s32[32,1,128]{2,1,0:T(1,128)S(1)}, u32[]{:S(2)}, u32[]{:S(2)}) async-start(s32[32,1,128]{2,1,0:T(1,128)} %bitcast.15), calls=%async_computation | async-start | bytes 32768 | tf_op jit(solution)/shard_map/all_to_all | solution.py:508
  258.0 6.1 copy-start.37
  266.5 18.9 %slice-start = ((s8[16777216]{0:T(1024)(128)(4,1)}), s8[4194304]{0:T(1024)(128)(4,1)S(1)}, s32[]{:S(2)}) async-start(s8[16777216]{0:T(1024)(128)(4,1)} %bitcast.276), calls=%async_computation.20 | async-start | bytes 8388608
  267.8 17.7 %slice-start.1 = ((s8[16777216]{0:T(1024)(128)(4,1)}), s8[4194304]{0:T(1024)(128)(4,1)S(1)}, s32[]{:S(2)}) async-start(s8[16777216]{0:T(1024)(128)(4,1)} %bitcast.276), calls=%async_computation.21 | async-start | bytes 8388608
  267.8 17.7 %slice-start.2 = ((s8[16777216]{0:T(1024)(128)(4,1)}), s8[4194304]{0:T(1024)(128)(4,1)S(1)}, s32[]{:S(2)}) async-start(s8[16777216]{0:T(1024)(128)(4,1)} %bitcast.276), calls=%async_computation.22 | async-start | bytes 8388608
  271.5 13.9 %slice-start.3 = ((s8[16777216]{0:T(1024)(128)(4,1)}), s8[4194304]{0:T(1024)(128)(4,1)S(1)}, s32[]{:S(2)}) async-start(s8[16777216]{0:T(1024)(128)(4,1)} %bitcast.276), calls=%async_computation.23 | async-start | bytes 8388608
  272.1 16.1 %copy-start.5 = (bf16[128,8,4,256]{3,1,2,0:T(8,128)(2,1)}, bf16[128,8,4,256]{3,1,2,0:T(8,128)(2,1)S(1)}, u32[]{:S(2)}) copy-start(bf16[128,8,4,256]{3,1,2,0:T(8,128)(2,1)S(1)} %copy.214) | copy-start | bytes 6291460
  272.1 13.4 %copy-start.14 = (bf16[1,128,2048]{2,1,0:T(8,128)(2,1)S(1)}, bf16[1,128,2048]{2,1,0:T(8,128)(2,1)}, u32[]{:S(2)}) copy-start(bf16[1,128,2048]{2,1,0:T(8,128)(2,1)} %param.16) | copy-start | bytes 1572868
  290.1 113.4 %copy-start.36 = (s32[128,32]{0,1:T(8,128)S(1)}, s32[128,32]{0,1:T(8,128)}, u32[]{:S(2)}) copy-start(s32[128,32]{0,1:T(8,128)} %copy.182) | copy-start | bytes 49156
  290.1 113.4 %copy-start.42 = (s32[32]{0:T(128)S(1)}, s32[32]{0:T(128)}, u32[]{:S(2)}) copy-start(s32[32]{0:T(128)} %select_reduce_fusion.2) | copy-start | bytes 388
  404.2 30.2 %all-to-all-start.2 = ((f32[32,1,128]{2,1,0:T(1,128)}), f32[32,1,128]{2,1,0:T(1,128)S(1)}, u32[]{:S(2)}, u32[]{:S(2)}) async-start(f32[32,1,128]{2,1,0:T(1,128)} %bitcast.23), calls=%async_computation.2 | async-start | bytes 32768 | tf_op jit(solution)/shard_map/all_to_all | solution.py:508
  414.0 10.7 %copy-start.43 = (bf16[1,2048,768]{2,1,0:T(8,128)(2,1)S(1)}, bf16[1,2048,768]{2,1,0:T(8,128)(2,1)}, u32[]{:S(2)}) copy-start(bf16[1,2048,768]{2,1,0:T(8,128)(2,1)} %param.28) | copy-start | bytes 9437188
  434.4 40.1 %all-to-all-start.3 = ((bf16[8,128,512]{2,1,0:T(8,128)(2,1)}), bf16[8,128,512]{2,1,0:T(8,128)(2,1)}, u32[]{:S(2)}, u32[]{:S(2)}) async-start(bf16[8,128,512]{2,1,0:T(8,128)(2,1)} %bitcast.285), calls=%async_computation.3 | async-start | bytes 2097152 | tf_op jit(solution)/shard_map/all_to_all | solution.py:508
  438.7 190.7 %reduce-scatter.4.cloned.1.call-start = ((), (), s32[]{:S(2)}) async-start(), calls=%async_computation.16 | async-start | bytes 4718592 | tf_op jit(solution)/shard_map/reduce_scatter | solution.py:511
  440.0 11.0 %copy-start.26 = (bf16[1024,768]{1,0:T(8,128)(2,1)S(1)}, bf16[1024,768]{1,0:T(8,128)(2,1)}, u32[]{:S(2)}) copy-start(bf16[1024,768]{1,0:T(8,128)(2,1)} %get-tuple-element.203) | copy-start | bytes 4718596
  474.5 97.0 %copy-start.24 = (bf16[4,256,1024]{2,1,0:T(8,128)(2,1)S(1)}, bf16[4,256,1024]{2,1,0:T(8,128)(2,1)}, u32[]{:S(2)}) copy-start(bf16[4,256,1024]{2,1,0:T(8,128)(2,1)} %fusion.22) | copy-start | bytes 6291460
  477.4 27.3 %collective-permute-start.2 = (bf16[256,2048]{1,0:T(8,128)(2,1)S(1)}, bf16[256,2048]{1,0:T(8,128)(2,1)S(1)}, u32[]{:S(2)}, u32[]{:S(2)}) collective-permute-start(bf16[256,2048]{1,0:T(8,128)(2,1)S(1)} %get-tuple-element.167), channel_id=1, source_target_pairs={{0,3},{1,0},{2,1},{3,2},{4,7},{5,4},{6,5},{7,6},{8,11},{9,8},{10,9... | collective-permute-start | bytes 3145736 | tf_op jit(solution)/shard_map/ppermute | solution.py:521
  481.0 90.4 %collective-permute-start.1 = (bf16[256,2048]{1,0:T(8,128)(2,1)S(1)}, bf16[256,2048]{1,0:T(8,128)(2,1)S(1)}, u32[]{:S(2)}, u32[]{:S(2)}) collective-permute-start(bf16[256,2048]{1,0:T(8,128)(2,1)S(1)} %get-tuple-element.168), channel_id=1, source_target_pairs={{0,2},{1,3},{2,0},{3,1},{4,6},{5,7},{6,4},{7,5},{8,10},{9,11},{10,... | collective-permute-start | bytes 3145736 | tf_op jit(solution)/shard_map/ppermute | solution.py:521
  481.1 90.4 %collective-permute-start = (bf16[256,2048]{1,0:T(8,128)(2,1)S(1)}, bf16[256,2048]{1,0:T(8,128)(2,1)S(1)}, u32[]{:S(2)}, u32[]{:S(2)}) collective-permute-start(bf16[256,2048]{1,0:T(8,128)(2,1)S(1)} %get-tuple-element.169), channel_id=1, source_target_pairs={{0,1},{1,2},{2,3},{3,0},{4,5},{5,6},{6,7},{7,4},{8,9},{9,10},{10,1... | collective-permute-start | bytes 3145736 | tf_op jit(solution)/shard_map/ppermute | solution.py:521
  577.6 51.8 %copy-start.11 = (f32[128,2048]{1,0:T(8,128)S(1)}, f32[128,2048]{1,0:T(8,128)}, u32[]{:S(2)}) copy-start(f32[128,2048]{1,0:T(8,128)} %copy-done.10) | copy-start | bytes 3145732
  578.2 12.2 %all-to-all-start.4 = ((f32[32,1,128]{2,1,0:T(1,128)}), f32[32,1,128]{2,1,0:T(1,128)S(1)}, u32[]{:S(2)}, u32[]{:S(2)}) async-start(f32[32,1,128]{2,1,0:T(1,128)} %all_to_all.52), calls=%async_computation.5 | async-start | bytes 32768 | tf_op jit(solution)/shard_map/all_to_all | solution.py:508
  583.3 249.5 %reduce-scatter.8.cloned.1.call-start = ((), (), s32[]{:S(2)}) async-start(), calls=%async_computation.18 | async-start | bytes 2359296 | tf_op jit(solution)/shard_map/reduce_scatter | solution.py:511
  670.1 265.4 %all-gather.8.cloned.1.call-start = ((), (), s32[]{:S(2)}) async-start(), calls=%async_computation.19 | async-start | bytes 4718592 | tf_op jit(solution)/shard_map/all_gather | solution.py:505
  672.1 9.1 copy-start.49
  672.1 9.1 copy-start.55
  691.4 6.7 copy-start.16
  693.6 105.9 %collective-permute-start.5 = (bf16[256,2048]{1,0:T(8,128)(2,1)}, bf16[256,2048]{1,0:T(8,128)(2,1)}, u32[]{:S(2)}, u32[]{:S(2)}) collective-permute-start(bf16[256,2048]{1,0:T(8,128)(2,1)} %get-tuple-element.163), channel_id=1, source_target_pairs={{0,3},{1,0},{2,1},{3,2},{4,7},{5,4},{6,5},{7,6},{8,11},{9,8},{10,9... | collective-permute-start | bytes 3145736 | tf_op jit(solution)/shard_map/ppermute | solution.py:521
  697.0 102.6 %collective-permute-start.4 = (bf16[256,2048]{1,0:T(8,128)(2,1)}, bf16[256,2048]{1,0:T(8,128)(2,1)}, u32[]{:S(2)}, u32[]{:S(2)}) collective-permute-start(bf16[256,2048]{1,0:T(8,128)(2,1)} %get-tuple-element.164), channel_id=1, source_target_pairs={{0,2},{1,3},{2,0},{3,1},{4,6},{5,7},{6,4},{7,5},{8,10},{9,11},{10,... | collective-permute-start | bytes 3145736 | tf_op jit(solution)/shard_map/ppermute | solution.py:521
  697.0 102.6 %collective-permute-start.3 = (bf16[256,2048]{1,0:T(8,128)(2,1)}, bf16[256,2048]{1,0:T(8,128)(2,1)}, u32[]{:S(2)}, u32[]{:S(2)}) collective-permute-start(bf16[256,2048]{1,0:T(8,128)(2,1)} %get-tuple-element.165), channel_id=1, source_target_pairs={{0,1},{1,2},{2,3},{3,0},{4,5},{5,6},{6,7},{7,4},{8,9},{9,10},{10,1... | collective-permute-start | bytes 3145736 | tf_op jit(solution)/shard_map/ppermute | solution.py:521
  699.6 93.0 %all-to-all-start.10 = ((f32[32,1,2048]{2,1,0:T(1,128)}), f32[32,1,2048]{2,1,0:T(1,128)S(1)}, u32[]{:S(2)}, u32[]{:S(2)}) async-start(f32[32,1,2048]{2,1,0:T(1,128)} %all_to_all.61), calls=%async_computation.13 | async-start | bytes 524288 | tf_op jit(solution)/shard_map/all_to_all | solution.py:508
  712.6 87.0 %copy-start.28 = (bf16[256,2048]{1,0:T(8,128)(2,1)S(1)}, bf16[256,2048]{1,0:T(8,128)(2,1)}, u32[]{:S(2)}) copy-start(bf16[256,2048]{1,0:T(8,128)(2,1)} %get-tuple-element.162) | copy-start | bytes 3145732
  795.1 26.0 %all-to-all-start.6 = ((bf16[8,128,512]{2,1,0:T(8,128)(2,1)}), bf16[8,128,512]{2,1,0:T(8,128)(2,1)}, u32[]{:S(2)}, u32[]{:S(2)}) async-start(bf16[8,128,512]{2,1,0:T(8,128)(2,1)} %bitcast.261), calls=%async_computation.9 | async-start | bytes 2097152 | tf_op jit(solution)/shard_map/all_to_all | solution.py:508
  799.4 148.2 %reduce-scatter.6.cloned.1.call-start = ((), (), s32[]{:S(2)}) async-start(), calls=%async_computation.17 | async-start | bytes 4718592 | tf_op jit(solution)/shard_map/reduce_scatter | solution.py:511
  826.5 8.8 copy-start.38
  827.7 17.1 %collective-permute-start.8 = (bf16[8,64,512]{2,1,0:T(8,128)(2,1)}, bf16[8,64,512]{2,1,0:T(8,128)(2,1)}, u32[]{:S(2)}, u32[]{:S(2)}) collective-permute-start(bf16[8,64,512]{2,1,0:T(8,128)(2,1)} %get-tuple-element.174), channel_id=1, source_target_pairs={{0,3},{1,0},{2,1},{3,2},{4,7},{5,4},{6,5},{7,6},{8,11},{9,8},{10,9... | collective-permute-start | bytes 1572872 | tf_op jit(solution)/shard_map/ppermute | solution.py:521
  832.1 45.2 %collective-permute-start.7 = (bf16[8,64,512]{2,1,0:T(8,128)(2,1)}, bf16[8,64,512]{2,1,0:T(8,128)(2,1)}, u32[]{:S(2)}, u32[]{:S(2)}) collective-permute-start(bf16[8,64,512]{2,1,0:T(8,128)(2,1)} %get-tuple-element.175), channel_id=1, source_target_pairs={{0,2},{1,3},{2,0},{3,1},{4,6},{5,7},{6,4},{7,5},{8,10},{9,11},{10,... | collective-permute-start | bytes 1572872 | tf_op jit(solution)/shard_map/ppermute | solution.py:521
  832.1 45.2 %collective-permute-start.6 = (bf16[8,64,512]{2,1,0:T(8,128)(2,1)}, bf16[8,64,512]{2,1,0:T(8,128)(2,1)}, u32[]{:S(2)}, u32[]{:S(2)}) collective-permute-start(bf16[8,64,512]{2,1,0:T(8,128)(2,1)} %get-tuple-element.173), channel_id=1, source_target_pairs={{0,1},{1,2},{2,3},{3,0},{4,5},{5,6},{6,7},{7,4},{8,9},{9,10},{10,1... | collective-permute-start | bytes 1572872 | tf_op jit(solution)/shard_map/ppermute | solution.py:521
  836.1 47.5 %copy-start.30 = (bf16[128,4,128]{0,2,1:T(8,128)(2,1)}, bf16[128,4,128]{0,2,1:T(8,128)(2,1)S(1)}, u32[]{:S(2)}) copy-start(bf16[128,4,128]{0,2,1:T(8,128)(2,1)S(1)} %multiply_convert_fusion.4) | copy-start | bytes 393220
  837.8 41.9 %all-to-all-start.8 = ((bf16[8,128,128]{1,2,0:T(8,128)(2,1)}), bf16[8,128,128]{1,2,0:T(8,128)(2,1)S(1)}, u32[]{:S(2)}, u32[]{:S(2)}) async-start(bf16[8,128,128]{1,2,0:T(8,128)(2,1)} %maximum_bitcast_fusion), calls=%async_computation.11 | async-start | bytes 524288 | tf_op jit(solution)/shard_map/all_to_all | solution.py:508
  879.7 13.6 %all-to-all-start.7 = ((bf16[8,64,512]{2,1,0:T(8,128)(2,1)}), bf16[8,64,512]{2,1,0:T(8,128)(2,1)S(1)}, u32[]{:S(2)}, u32[]{:S(2)}) async-start(bf16[8,64,512]{2,1,0:T(8,128)(2,1)} %fusion.72), calls=%async_computation.10 | async-start | bytes 1048576 | tf_op jit(solution)/shard_map/all_to_all | solution.py:508
  883.6 26.3 %copy-start.15 = (bf16[1,128,2048]{2,1,0:T(8,128)(2,1)S(1)}, bf16[1,128,2048]{2,1,0:T(8,128)(2,1)}, u32[]{:S(2)}) copy-start(bf16[1,128,2048]{2,1,0:T(8,128)(2,1)} %param.16) | copy-start | bytes 1572868
  883.6 26.3 %copy-start.27 = (f32[128,2048]{1,0:T(8,128)S(1)}, f32[128,2048]{1,0:T(8,128)}, u32[]{:S(2)}) copy-start(f32[128,2048]{1,0:T(8,128)} %fusion.109) | copy-start | bytes 3145732
  883.6 26.3 %copy-start.29 = (bf16[128,4,1,128]{0,3,1,2:T(8,128)(2,1)S(1)}, bf16[128,4,1,128]{0,3,1,2:T(8,128)(2,1)}, u32[]{:S(2)}) copy-start(bf16[128,4,1,128]{0,3,1,2:T(8,128)(2,1)} %copy.205) | copy-start | bytes 393220
  883.6 26.3 %copy-start.31 = (bf16[128,4,128]{0,2,1:T(8,128)(2,1)S(1)}, bf16[128,4,128]{0,2,1:T(8,128)(2,1)}, u32[]{:S(2)}) copy-start(bf16[128,4,128]{0,2,1:T(8,128)(2,1)} %copy-done.30) | copy-start | bytes 393220
  883.6 26.3 %copy-start.34 = (f32[2048]{0:T(1024)S(1)}, f32[2048]{0:T(1024)}, u32[]{:S(2)}) copy-start(f32[2048]{0:T(1024)} %param.19) | copy-start | bytes 24580
  888.1 6.4 collective-permute-start.11
  888.1 16.0 %collective-permute-start.10 = (bf16[8,64,128]{2,1,0:T(8,128)(2,1)}, bf16[8,64,128]{2,1,0:T(8,128)(2,1)}, u32[]{:S(2)}, u32[]{:S(2)}) collective-permute-start(bf16[8,64,128]{2,1,0:T(8,128)(2,1)} %get-tuple-element.180), channel_id=1, source_target_pairs={{0,2},{1,3},{2,0},{3,1},{4,6},{5,7},{6,4},{7,5},{8,10},{9,11},{10,... | collective-permute-start | bytes 393224 | tf_op jit(solution)/shard_map/ppermute | solution.py:521
  891.3 12.9 %collective-permute-start.9 = (bf16[8,64,128]{2,1,0:T(8,128)(2,1)}, bf16[8,64,128]{2,1,0:T(8,128)(2,1)}, u32[]{:S(2)}, u32[]{:S(2)}) collective-permute-start(bf16[8,64,128]{2,1,0:T(8,128)(2,1)} %get-tuple-element.178), channel_id=1, source_target_pairs={{0,1},{1,2},{2,3},{3,0},{4,5},{5,6},{6,7},{7,4},{8,9},{9,10},{10,1... | collective-permute-start | bytes 393224 | tf_op jit(solution)/shard_map/ppermute | solution.py:521
  905.9 9.4 copy-start.40
  905.9 9.4 copy-start.41
  905.9 9.4 all-to-all-start.9
  909.9 10.5 %copy-start.19 = (f32[128,2048]{1,0:T(8,128)S(1)}, f32[128,2048]{1,0:T(8,128)}, u32[]{:S(2)}) copy-start(f32[128,2048]{1,0:T(8,128)} %get-tuple-element.157) | copy-start | bytes 3145732
  916.5 18.2 %all-to-all-start.5 = ((f32[32,1,4352]{2,1,0:T(1,128)}), f32[32,1,4352]{2,1,0:T(1,128)S(1)}, u32[]{:S(2)}, u32[]{:S(2)}) async-start(f32[32,1,4352]{2,1,0:T(1,128)} %broadcast_in_dim.152), calls=%async_computation.8 | async-start | bytes 1114112 | tf_op jit(solution)/shard_map/all_to_all | solution.py:464
  940.5 54.1 %copy-start.1 = (bf16[1,768,2048]{2,1,0:T(8,128)(2,1)S(1)}, bf16[1,768,2048]{2,1,0:T(8,128)(2,1)}, u32[]{:S(2)}) copy-start(bf16[1,768,2048]{2,1,0:T(8,128)(2,1)} %param.30) | copy-start | bytes 9437188
  943.0 17.1 %collective-permute-start.14 = (bf16[128,2048]{1,0:T(8,128)(2,1)}, bf16[128,2048]{1,0:T(8,128)(2,1)}, u32[]{:S(2)}, u32[]{:S(2)}) collective-permute-start(bf16[128,2048]{1,0:T(8,128)(2,1)} %get-tuple-element.171), channel_id=1, source_target_pairs={{0,3},{1,0},{2,1},{3,2},{4,7},{5,4},{6,5},{7,6},{8,11},{9,8},{10,9... | collective-permute-start | bytes 1572872 | tf_op jit(solution)/shard_map/ppermute | solution.py:521
  946.0 45.8 %collective-permute-start.13 = (bf16[128,2048]{1,0:T(8,128)(2,1)}, bf16[128,2048]{1,0:T(8,128)(2,1)}, u32[]{:S(2)}, u32[]{:S(2)}) collective-permute-start(bf16[128,2048]{1,0:T(8,128)(2,1)} %get-tuple-element.172), channel_id=1, source_target_pairs={{0,2},{1,3},{2,0},{3,1},{4,6},{5,7},{6,4},{7,5},{8,10},{9,11},{10,... | collective-permute-start | bytes 1572872 | tf_op jit(solution)/shard_map/ppermute | solution.py:521
  947.1 44.7 %collective-permute-start.12 = (bf16[128,2048]{1,0:T(8,128)(2,1)}, bf16[128,2048]{1,0:T(8,128)(2,1)}, u32[]{:S(2)}, u32[]{:S(2)}) collective-permute-start(bf16[128,2048]{1,0:T(8,128)(2,1)} %get-tuple-element.170), channel_id=1, source_target_pairs={{0,1},{1,2},{2,3},{3,0},{4,5},{5,6},{6,7},{7,4},{8,9},{9,10},{10,1... | collective-permute-start | bytes 1572872 | tf_op jit(solution)/shard_map/ppermute | solution.py:521
  (28 other events, 90.1 us)
Sparse Core Ops, SparseCore 0:
  10.8 53.1 all-gather.3
  205.8 136.3 all-gather.5
  577.7 51.6 reduce-scatter.3
  670.3 41.3 reduce-scatter.7
  713.4 36.2 all-gather.7
  808.8 56.3 reduce-scatter.5

commit v5 on v4

--- a/solution.py
+++ b/solution.py
@@ -229,14 +229,24 @@
     )
 
 
+def rotated(sums, gain_ref, cosine_ref, sine_ref):
+    rows = norm_rows(sums, gain_ref[...])
+    turned = pltpu.roll(rows, rows.shape[1] // 2, axis=1)
+    return (rows * cosine_ref[...] + turned * sine_ref[...]).astype(jnp.bfloat16)
+
+
 def attend_kernel(
     head_dim,
     together,
     query_ref,
-    pairs_ref,
+    key_ref,
+    value_ref,
     gain_ref,
     cosine_ref,
     sine_ref,
+    key_gain_ref,
+    key_cosine_ref,
+    key_sine_ref,
     query_pos_ref,
     query_doc_ref,
     key_pos_ref,
@@ -256,16 +266,14 @@
         )
         bias_ref[...] = jnp.where(allowed, 0.0, MASKED)
 
-    keys = pairs_ref[:, :head_dim]
-    values = pairs_ref[:, head_dim:]
+    keys = rotated(key_ref[...], key_gain_ref, key_cosine_ref, key_sine_ref)
+    values = value_ref[...].astype(jnp.bfloat16)
     for first in range(0, heads, together):
         for h in range(first, first + together):
             columns = slice(h * head_dim, (h + 1) * head_dim)
-            rows = query_ref[:, columns]
-            rows = norm_rows(rows, gain_ref[...])
-            turned = pltpu.roll(rows, head_dim // 2, axis=1)
-            rows = rows * cosine_ref[...] + turned * sine_ref[...]
-            query_low_ref[:, columns] = rows.astype(jnp.bfloat16)
+            query_low_ref[:, columns] = rotated(
+                query_ref[:, columns], gain_ref, cosine_ref, sine_ref
+            )
         queries = stack_heads(query_low_ref, first, head_dim, together)
         scores = contract_cols(queries, keys) * scale
         scores = scores + jnp.concatenate([bias_ref[...]] * together, axis=0)
@@ -283,10 +291,14 @@
     query_ref,
     query_low_ref,
     cot_ref,
-    pairs_ref,
+    key_ref,
+    value_ref,
     gain_ref,
     cosine_ref,
     sine_ref,
+    key_gain_ref,
+    key_cosine_ref,
+    key_sine_ref,
     query_pos_ref,
     query_doc_ref,
     key_pos_ref,
@@ -309,8 +321,8 @@
         )
         bias_ref[...] = jnp.where(allowed, 0.0, MASKED)
 
-    keys = pairs_ref[:, :head_dim]
-    values = pairs_ref[:, head_dim:]
+    keys = rotated(key_ref[...], key_gain_ref, key_cosine_ref, key_sine_ref)
+    values = value_ref[...].astype(jnp.bfloat16)
     for first in range(0, heads, together):
         queries = stack_heads(query_low_ref, first, head_dim, together)
         cots = stack_heads(cot_ref, first, head_dim, together)
@@ -342,10 +354,10 @@
     pair_cot_ref[:, head_dim:] = value_sum_ref[...].astype(jnp.bfloat16)
 
 
-def attend(query_sum, pairs_all, gain, cosine, sine, query_pos, query_doc, key_pos, key_doc):
+def attend(query_sum, pair_sums, gains, tables, query_rows, key_rows):
     tokens, q_width = query_sum.shape
-    seq_len, pair_width = pairs_all.shape
-    head_dim = gain.shape[0]
+    seq_len, pair_width = pair_sums.shape
+    head_dim = gains[0].shape[0]
     key_heads = pair_width // (2 * head_dim)
     group = q_width // key_heads
     whole = lambda shape: pl.BlockSpec(shape, lambda g: (0, 0))
@@ -355,10 +367,14 @@
         grid=(key_heads,),
         in_specs=[
             pl.BlockSpec((tokens, group), lambda g: (0, g)),
-            pl.BlockSpec((seq_len, 2 * head_dim), lambda g: (0, g)),
+            pl.BlockSpec((seq_len, head_dim), lambda g: (0, g)),
+            pl.BlockSpec((seq_len, head_dim), lambda g: (0, key_heads + g)),
             whole((1, head_dim)),
             whole((tokens, head_dim)),
             whole((tokens, head_dim)),
+            whole((1, head_dim)),
+            whole((seq_len, head_dim)),
+            whole((seq_len, head_dim)),
             whole((tokens, 1)),
             whole((tokens, 1)),
             whole((1, seq_len)),
@@ -367,40 +383,28 @@
         out_specs=[pl.BlockSpec((tokens, group), lambda g: (0, g))] * 2,
         out_shape=[jax.ShapeDtypeStruct((tokens, q_width), jnp.bfloat16)] * 2,
         scratch_shapes=[pltpu.VMEM((tokens, seq_len), jnp.float32)],
-        compiler_params=pltpu.CompilerParams(vmem_limit_bytes=32 << 20),
+        compiler_params=pltpu.CompilerParams(vmem_limit_bytes=48 << 20),
         cost_estimate=pl.CostEstimate(
             flops=flops, bytes_accessed=8 * tokens * q_width, transcendentals=0
         ),
         name="attend",
     )(
         query_sum,
-        pairs_all,
-        gain[None, :],
-        cosine,
-        sine,
-        query_pos[:, None],
-        query_doc[:, None],
-        key_pos[None, :],
-        key_doc[None, :],
-    )
-
-
-def attend_back(
-    query_sum,
-    query_low,
-    cots,
-    pairs_all,
-    gain,
-    cosine,
-    sine,
-    query_pos,
-    query_doc,
-    key_pos,
-    key_doc,
-):
+        pair_sums,
+        pair_sums,
+        gains[0][None, :],
+        *tables[:2],
+        gains[1][None, :],
+        *tables[2:],
+        *(row[:, None] for row in query_rows),
+        *(row[None, :] for row in key_rows),
+    )
+
+
+def attend_back(query_sum, query_low, cots, pair_sums, gains, tables, query_rows, key_rows):
     tokens, q_width = query_sum.shape
-    seq_len, pair_width = pairs_all.shape
-    head_dim = gain.shape[0]
+    seq_len, pair_width = pair_sums.shape
+    head_dim = gains[0].shape[0]
     key_heads = pair_width // (2 * head_dim)
     group = q_width // key_heads
     heads = group // head_dim
@@ -413,10 +417,14 @@
             pl.BlockSpec((tokens, group), lambda g: (0, g)),
             pl.BlockSpec((tokens, group), lambda g: (0, g)),
             pl.BlockSpec((tokens, group), lambda g: (0, g)),
-            pl.BlockSpec((seq_len, 2 * head_dim), lambda g: (0, g)),
+            pl.BlockSpec((seq_len, head_dim), lambda g: (0, g)),
+            pl.BlockSpec((seq_len, head_dim), lambda g: (0, key_heads + g)),
             whole((1, head_dim)),
             whole((tokens, head_dim)),
             whole((tokens, head_dim)),
+            whole((1, head_dim)),
+            whole((seq_len, head_dim)),
+            whole((seq_len, head_dim)),
             whole((1, tokens)),
             whole((1, tokens)),
             whole((seq_len, 1)),
@@ -437,7 +445,7 @@
             pltpu.VMEM((seq_len, head_dim), jnp.float32),
             pltpu.VMEM((seq_len, head_dim), jnp.float32),
         ],
-        compiler_params=pltpu.CompilerParams(vmem_limit_bytes=48 << 20),
+        compiler_params=pltpu.CompilerParams(vmem_limit_bytes=56 << 20),
         cost_estimate=pl.CostEstimate(
             flops=flops, bytes_accessed=12 * tokens * q_width, transcendentals=0
         ),
@@ -446,14 +454,14 @@
         query_sum,
         query_low,
         cots,
-        pairs_all,
-        gain[None, :],
-        cosine,
-        sine,
-        query_pos[None, :],
-        query_doc[None, :],
-        key_pos[:, None],
-        key_doc[:, None],
+        pair_sums,
+        pair_sums,
+        gains[0][None, :],
+        *tables[:2],
+        gains[1][None, :],
+        *tables[2:],
+        *(row[None, :] for row in query_rows),
+        *(row[:, None] for row in key_rows),
     )
 
 
@@ -522,8 +530,8 @@
             arrived.append(block)
         return arrived
 
-    def line_sum(blocks):
-        return sum(block.astype(jnp.float32) for block in turn(blocks))
+    def add_up(blocks):
+        return sum(block.astype(jnp.float32) for block in blocks)
 
     doc_ends = jnp.cumsum(doc_lengths[0])
     all_positions = jnp.arange(seq_len, dtype=jnp.int32)
@@ -537,9 +545,9 @@
         return lax.dynamic_slice_in_dim(rows, first_pos, tokens)
 
     cosine_table, sine_table = mine_of(cosine_all), mine_of(sine_all)
-    cosine_rows = cosine_table[:, 0, :]
     first_half = jnp.arange(head_dim) < head_dim // 2
-    sine_rows = jnp.where(first_half[None, :], -sine_table[:, 0, :], sine_table[:, 0, :])
+    turned_all = jnp.where(first_half[None, :], -sine_all[:, 0, :], sine_all[:, 0, :])
+    tables = (mine_of(cosine_all[:, 0, :]), mine_of(turned_all), cosine_all[:, 0, :], turned_all)
 
     expert_ids = jnp.arange(expert_count, dtype=jnp.int32)
     hits = jnp.sum((routes[0][:, :, None] == expert_ids[None, None, :]).astype(jnp.int32), axis=1)
@@ -598,27 +606,13 @@
     pair_sums = lax.optimization_barrier(
         matmul(normed_in_all, side_weights[:, : 2 * kv_width])
     )
-    key_sums = pair_sums[:, :kv_width].reshape(seq_len, key_heads, head_dim)
-    key_low = rotate(norm_rows(key_sums, gain_key), cosine_all, sine_all).astype(jnp.bfloat16)
-    value_low = pair_sums[:, kv_width:].astype(jnp.bfloat16)
-    pairs_all = jnp.concatenate(
-        [key_low, value_low.reshape(seq_len, key_heads, head_dim)], axis=2
-    ).reshape(seq_len, 2 * kv_width)
-    key_sum = mine_of(key_sums)
+    key_sum = mine_of(pair_sums)[:, :kv_width].reshape(tokens, key_heads, head_dim)
     if small_plane:
         cot_all = gather(after(out_grad[0], query_full), by_stream)
     query_sum = lax.optimization_barrier(matmul(normed_in, query_full))
-    mixed_low, query_low = attend(
-        query_sum,
-        pairs_all,
-        gain_query,
-        cosine_rows,
-        sine_rows,
-        my_positions,
-        my_docs,
-        all_positions,
-        doc_all,
-    )
+    gains = (gain_query, gain_key)
+    query_rows, key_rows = (my_positions, my_docs), (all_positions, doc_all)
+    mixed_low, query_low = attend(query_sum, pair_sums, gains, tables, query_rows, key_rows)
     resid_mid = resid_in + matmul(mixed_low, out_full)
     normed_mid = norm_rows(resid_mid, gain_moe).astype(jnp.bfloat16)
 
@@ -664,22 +658,18 @@
     gate_cot_mine = jnp.sum(jnp.where(place, gate_cot_rows[:, :, None], 0.0), axis=1)
     out_rows_cot = (gate_rows[:, None] * cot_rows.astype(jnp.float32)).astype(jnp.bfloat16)
     hidden_cot = contract_cols(out_rows_cot, expert_down[0])
-    grad_down = contract_rows(hidden_h, out_rows_cot)
     gate_cot_h = (hidden_cot * up_h * sigma_h * (1.0 + gate_h * (1.0 - sigma_h))).astype(
         jnp.bfloat16
     )
     up_cot_h = (hidden_cot * gate_h * sigma_h).astype(jnp.bfloat16)
-    grad_gate = contract_rows(filled, gate_cot_h)
-    grad_up = contract_rows(filled, up_cot_h)
     in_rows_cot = (
         contract_cols(gate_cot_h, expert_gate[0]) + contract_cols(up_cot_h, expert_up[0])
     ).astype(jnp.bfloat16)
 
     def add_pairs(table, stream_rows):
-        partial = contract_rows(
+        return contract_rows(
             table.reshape(wt_size * capacity, seq_len), jnp.concatenate(stream_rows, axis=0)
         ).astype(jnp.bfloat16)
-        return scatter_sum(partial, "ctx").astype(jnp.float32)
 
     mixed_rows = (gate_rows[:, None] * result_rows.astype(jnp.float32)).astype(jnp.bfloat16)
     in_rows_cot, mixed_columns, spread_low = lax.optimization_barrier(
@@ -690,7 +680,8 @@
     ))
     blocks_shape = (wt_size, capacity, model_width)
     stream_cots = turn(in_rows_cot.reshape(blocks_shape))
-    returned_cot = add_pairs(spread_low, stream_cots)
+    returned_cot = scatter_sum(add_pairs(spread_low, stream_cots), "ctx")
+    returned_cot = returned_cot.astype(jnp.float32)
     stream_mixed = turn(after(mixed_rows, stream_cots).reshape(blocks_shape))
     out_cot = out_grad[0].astype(jnp.float32)
 
@@ -706,29 +697,32 @@
     mid_norm_cot, gain_moe_terms = norm_back(resid_mid, gain_moe, mid_cot)
     resid_cot = out_cot + mid_norm_cot
     attn_cot = resid_cot.astype(jnp.bfloat16)
-    router_parts = exchange(contract_rows(normed_mid, logit_cot).reshape(devices, -1), both)
-    grad_w_router = jnp.sum(router_parts, axis=0).reshape(w_router.shape)
 
     mixed_cot = contract_cols(attn_cot, out_full)
     attn_cot_all = gather(attn_cot, "ctx")
-    out_block = contract_rows(mixed_columns, attn_cot_all).astype(jnp.bfloat16)
-    grad_w_out = line_sum(out_block.reshape(wt_size, -1, model_width))
-
     query_cot_low, pair_cots, gain_query_terms = attend_back(
         query_sum,
         query_low,
         mixed_cot.astype(jnp.bfloat16),
-        pairs_all,
-        gain_query,
-        cosine_rows,
-        sine_rows,
-        my_positions,
-        my_docs,
-        all_positions,
-        doc_all,
-    )
-    mixed_mine = add_pairs(after(spread_low, query_cot_low), stream_mixed)
+        pair_sums,
+        gains,
+        tables,
+        query_rows,
+        key_rows,
+    )
+    query_columns = column_blocks(query_cot_low)
+    filled, hidden_h = after((filled, hidden_h), query_cot_low)
+    normed_mid = after(normed_mid, query_columns)
+    grad_gate = contract_rows(filled, gate_cot_h)
+    grad_up = contract_rows(filled, up_cot_h)
+    grad_down = contract_rows(hidden_h, out_rows_cot)
+    router_parts = exchange(contract_rows(normed_mid, logit_cot).reshape(devices, -1), both)
+    grad_w_router = jnp.sum(router_parts, axis=0).reshape(w_router.shape)
+    mixed_partial = add_pairs(after(spread_low, query_cot_low), stream_mixed)
+    mixed_mine = scatter_sum(mixed_partial, "ctx").astype(jnp.float32)
     hidden_out = after(resid_mid, query_cot_low) + mixed_mine
+    out_block = contract_rows(after(mixed_columns, query_cot_low), attn_cot_all)
+    out_parts = turn(out_block.astype(jnp.bfloat16).reshape(wt_size, -1, model_width))
     pair_mine = scatter_sum(pair_cots, "ctx").reshape(tokens, key_heads, 2, head_dim)
     key_mine = pair_mine[:, :, 0].astype(jnp.float32)
     value_cot_low = pair_mine[:, :, 1].reshape(tokens, kv_width)
@@ -740,24 +734,30 @@
     key_cot_low = key_pre.reshape(tokens, kv_width).astype(jnp.bfloat16)
     pair_cot_low = jnp.concatenate([key_cot_low, value_cot_low], axis=1)
 
-    def weight_grad(cots):
-        width = cots.shape[1] // ctx_size
-        block = contract_rows(normed_in_all, column_blocks(cots)).astype(jnp.bfloat16)
+    def weight_parts(columns):
+        width = columns.shape[1]
+        block = contract_rows(normed_in_all, columns).astype(jnp.bfloat16)
         block = block.reshape(ctx_size, wt_size, -1, width).transpose(1, 0, 2, 3)
-        mine = line_sum(block).astype(jnp.bfloat16)
-        rows = exchange(mine, "ctx")
-        return rows.transpose(1, 0, 2).reshape(-1, width * ctx_size).astype(jnp.float32)
-
-    grad_w_query = weight_grad(query_cot_low)
-    grad_pair = weight_grad(pair_cot_low)
+        return turn(block), block
+
+    def weight_rows(parts):
+        rows = exchange(add_up(parts).astype(jnp.bfloat16), "ctx")
+        return rows.transpose(1, 0, 2).reshape(rows.shape[1], -1).astype(jnp.float32)
+
+    query_parts, query_block = weight_parts(after(query_columns, (out_block, mixed_partial)))
+    pair_parts, pair_block = weight_parts(column_blocks(after(pair_cot_low, query_block)))
+    in_cot = contract_cols(after(query_cot_low, query_block), query_full) + contract_cols(
+        pair_cot_low, side_weights[:, : 2 * kv_width]
+    )
+    query_parts = after(query_parts, (pair_block, in_cot))
+    grad_w_query = weight_rows(query_parts)
+    grad_w_out = add_up(after(out_parts, query_parts))
+    grad_pair = weight_rows(after(pair_parts, query_parts))
     grad_w_key = grad_pair[:, :kv_width]
     grad_w_value = grad_pair[:, kv_width:]
-    in_cot = contract_cols(query_cot_low, query_full) + contract_cols(
-        pair_cot_low, side_weights[:, : 2 * kv_width]
-    )
     in_norm_cot, gain_attn_terms = norm_back(resid_in, gain_attn, in_cot)
     grad_in = resid_cot + in_norm_cot
-    gains = sum_everywhere(
+    gain_sums = sum_everywhere(
         jnp.concatenate(
             [
                 jnp.sum(gain_attn_terms, axis=0),
@@ -767,10 +767,10 @@
             ]
         )
     )
-    grad_gain_attn = gains[:model_width]
-    grad_gain_query = gains[model_width : model_width + head_dim]
-    grad_gain_key = gains[model_width + head_dim : model_width + 2 * head_dim]
-    grad_gain_moe = gains[model_width + 2 * head_dim :]
+    grad_gain_attn = gain_sums[:model_width]
+    grad_gain_query = gain_sums[model_width : model_width + head_dim]
+    grad_gain_key = gain_sums[model_width + head_dim : model_width + 2 * head_dim]
+    grad_gain_moe = gain_sums[model_width + 2 * head_dim :]
     return (
         hidden_out[None],
         grad_in[None],

time: 1010 us -> 1040 us (1.030)
  Pallas kernels: 341 us -> 357 us
  starting transfers between devices: 74.2 us -> 88.7 us
  local copies, waits for them, and re-layouts: 44.4 us -> 32.1 us
  matrix products: 154 us -> 166 us
    all_to_all x10, waiting for transfers between devices: 86.8 us -> 26.2 us  [exchange(): return lax.all_to_all(value, axes, split_axis=0, concat_axis=0, tiled=True)]
    ppermute x15, waiting for transfers between devices: 176 us -> 215 us  [turn(): block = lax.ppermute(block, 'wt', pairs)]
    all_gather x3, waiting for transfers between devices: 0.04 us -> 31.7 us  [gather(): return lax.all_gather(value, axes, axis=0, tiled=True)]
    ppermute x15, starting transfers between devices: 23.5 us -> 37.6 us  [turn(): block = lax.ppermute(block, 'wt', pairs)]
  transfers between devices with their start and end apart: 32 -> 32, of which waited for: 11 -> 16; matrix products, arithmetic and copies ran while one was open for 22% -> 17% of each run, Pallas kernels for 32% -> 32%
where the time goes in v5:
time: 1040 us; the launch traced here: 1030 us
  Pallas kernels  357 us (34%)
  waiting for transfers between devices  321 us (31%)
  matrix products  166 us (16%)
  starting transfers between devices  88.7 us (9%)
  other arithmetic  50.3 us (5%)
  local copies, waits for them, and re-layouts  32.1 us (3%)
  between operations  15.4 us (1%)
    pallas_call x2, Pallas kernels, spread(): pl.pallas_call(functools.partial(spread_kernel, splits, streams_first), o...  311 us
    ppermute x15, waiting for transfers between devices, turn(): block = lax.ppermute(block, 'wt', pairs)  215 us
    dot_general x9, matrix products, contract_rows(): lax.dot_general(left_side, right_side, (((0,), (0,)), ((), ())), preferre...  55.8 us
    all_to_all x10, starting transfers between devices, exchange(): return lax.all_to_all(value, axes, split_axis=0, concat_axis=0, tiled=True)  44.7 us
    dot_general x7, matrix products, contract_cols(): lax.dot_general(left_side, right_side, (((1,), (1,)), ((), ())), preferre...  44.6 us
    dot_general x7, matrix products, matmul(): return jnp.dot(left_side, right_side, preferred_element_type=jnp.float32)  44.3 us
    reduce_scatter x3, waiting for transfers between devices, scatter_sum(): return lax.psum_scatter(value, axes, scatter_dimension=0, tiled=True)  38.9 us
    ppermute x15, starting transfers between devices, turn(): block = lax.ppermute(block, 'wt', pairs)  37.6 us
  transfers between devices with their start and end apart: 32, of which 16 were waited for; matrix products, arithmetic and copies ran while one was open for 17% of the time, Pallas kernels for 32%

profile of v5, /device:TPU:0, one launch (start us, length us, event | category | flops | bytes accessed | tf_op | source)
XLA Modules:
  0.0 1031.2 jit_solution(9744605285409914243)
XLA Ops:
  13.1 192.6 %shard_map.263 = (bf16[8,4,64,1152]{3,2,1,0:T(8,128)(2,1)}, bf16[8,4,64,4096]{3,2,1,0:T(8,128)(2,1)}, bf16[8,4,128,2048]{3,2,1,0:T(8,128)(2,1)}) custom-call(bf16[64,1152]{1,0:T(8,128)(2,1)} %fusion.82.refs_0_, bf16[64,4096]{1,0:T(8,128)(2,1)} %refs_1_.1, bf16[128,2048]{1,0:T(8,128)(2,1)} %refs_2_.1), custom_call_target="tpu_custom_call" | custom-call | bytes 76546048 | tf_op jit(solution)/shard_map/pallas_call | solution.py:198
  207.2 3.3 all-to-all-start.1
  211.7 3.0 fusion.75
  216.3 9.8 fusion.67.query_ref
  228.6 4.1 all-to-all-start
  237.2 2.9 all-to-all-done
  243.0 10.2 fusion.33.key_ref.value_ref
  253.3 16.4 %attend.1 = (bf16[128,4096]{1,0:T(8,128)(2,1)S(1)}, bf16[128,4096]{1,0:T(8,128)(2,1)S(1)}) custom-call(f32[128,4096]{1,0:T(8,128)S(1)} %copy-done.2, f32[1024,1024]{1,0:T(8,128)} %fusion.33.key_ref.value_ref, f32[1024,1024]{1,0:T(8,128)} %fusion.33.key_ref.value_ref, f32[1,128]{1,0:T(1,128)S(1)} %bitcast.312, f32[128,128]{1,0:T(8,128)S(1)} %get-tuple-element.221.cosine_ref, ...), custom_call_target="tpu_custom_call" | custom-call | flops 2147483648 | bytes 4194304 | tf_op jit(solution)/shard_map/attend/pallas_call | solution.py:365
  269.7 9.2 multiply_reduce_fusion.2
  280.8 118.6 %shard_map.264 = bf16[4,8,128,2048]{3,2,1,0:T(8,128)(2,1)} custom-call(bf16[128,2048]{1,0:T(8,128)(2,1)} %multiply_convert_fusion.3.refs_0_), custom_call_target="tpu_custom_call" | custom-call | bytes 33554432 | tf_op jit(solution)/shard_map/pallas_call | solution.py:198
  401.7 6.3 all-to-all-start.2
  408.0 10.7 %fusion.24 = bf16[4,256,2048]{2,1,0:T(8,128)(2,1)S(1)} fusion(bf16[4,1024,2048]{2,1,0:T(8,128)(2,1)} %bitcast.318, s32[4,1024]{1,0:T(4,128)S(1)} %and_select_fusion.1), kind=kOutput, calls=%fused_computation.35 | convolution fusion | flops 4298113024 | bytes 20987904 | tf_op jit(solution)/shard_map/wkt,wtd->wkd/dot_general | solution.py:638
  418.7 3.4 fusion.37
  422.2 5.1 multiply_convert_fusion
  428.4 4.2 all-to-all-start.3
  434.4 10.6 %fusion.23 = bf16[4,256,2048]{2,1,0:T(8,128)(2,1)S(1)} fusion(bf16[4,1024,2048]{2,1,0:T(8,128)(2,1)} %bitcast.361, s32[4,1024]{1,0:T(4,128)S(1)} %and_select_fusion.1), kind=kOutput, calls=%fused_computation.34 | convolution fusion | flops 4298113024 | bytes 20987904 | tf_op jit(solution)/shard_map/wkt,wtd->wkd/dot_general | solution.py:638
  445.0 5.0 fusion
  451.3 3.1 fusion.2
  455.4 4.4 multiply_convert_fusion.1
  459.8 3.4 fusion.35
  463.3 5.2 add_convert_fusion
  468.5 2.9 dynamic-slice_bitcast_fusion.7
  471.4 3.8 collective-permute-start.2
  476.2 22.6 %collective-permute-done.2 = bf16[256,2048]{1,0:T(8,128)(2,1)S(1)} collective-permute-done((bf16[256,2048]{1,0:T(8,128)(2,1)S(1)}, bf16[256,2048]{1,0:T(8,128)(2,1)S(1)}, u32[]{:S(2)}, u32[]{:S(2)}) %collective-permute-start.2) | collective-permute-done | bytes 1048608 | tf_op jit(solution)/shard_map/ppermute | solution.py:529
  498.8 66.8 %collective-permute-done.1 = bf16[256,2048]{1,0:T(8,128)(2,1)S(1)} collective-permute-done((bf16[256,2048]{1,0:T(8,128)(2,1)S(1)}, bf16[256,2048]{1,0:T(8,128)(2,1)S(1)}, u32[]{:S(2)}, u32[]{:S(2)}) %collective-permute-start.1) | collective-permute-done | bytes 1048608 | tf_op jit(solution)/shard_map/ppermute | solution.py:529
  565.6 6.1 fusion.28
  572.3 5.1 all-to-all-start.4
  579.0 5.5 all-to-all-done.4
  584.6 38.9 %reduce-scatter.4.cloned.1.call-done = bf16[128,2048]{1,0:T(8,128)(2,1)} async-done(((bf16[1024,2048]{1,0:T(8,128)(2,1)}), bf16[128,2048]{1,0:T(8,128)(2,1)}) %reduce-scatter.4.cloned.1.call-update) | async-done | bytes 524304 | tf_op jit(solution)/shard_map/reduce_scatter | solution.py:519
  625.3 2.4 fusion.92
  627.7 12.6 %convolution_convert_fusion.cot_ref = bf16[128,4096]{1,0:T(8,128)(2,1)} fusion(bf16[128,2048]{1,0:T(8,128)(2,1)S(1)} %get-tuple-element.167, bf16[4096,2048]{1,0:T(8,128)(2,1)} %bitcast.314), kind=kOutput, calls=%fused_computation.10 | convolution fusion | flops 2148007936 | bytes 18350080 | tf_op jit(solution)/shard_map/dot_general | solution.py:61
  641.1 29.7 %attend_back.1 = (bf16[128,4096]{1,0:T(8,128)(2,1)}, bf16[1024,1024]{1,0:T(8,128)(2,1)}, f32[32,128]{1,0:T(8,128)}) custom-call(f32[128,4096]{1,0:T(8,128)} %fusion.67.query_ref, bf16[128,4096]{1,0:T(8,128)(2,1)} %copy-done.15, bf16[128,4096]{1,0:T(8,128)(2,1)} %convolution_convert_fusion.cot_ref, f32[1024,1024]{1,0:T(8,128)} %fusion.33.key_ref.value_ref, ...), custom_call_target="tpu_custom_call" | custom-call | flops 5368709120 | bytes 6291456 | tf_op jit(solution)/shard_map/attend_back/pallas_call | solution.py:413
  670.9 6.3 fusion.3
  677.7 3.4 collective-permute-start.5
  682.2 22.5 %collective-permute-done.5 = bf16[256,2048]{1,0:T(8,128)(2,1)S(1)} collective-permute-done((bf16[256,2048]{1,0:T(8,128)(2,1)S(1)}, bf16[256,2048]{1,0:T(8,128)(2,1)S(1)}, u32[]{:S(2)}, u32[]{:S(2)}) %collective-permute-start.5) | collective-permute-done | bytes 1048608 | tf_op jit(solution)/shard_map/ppermute | solution.py:529
  704.7 66.1 %collective-permute-done.4 = bf16[256,2048]{1,0:T(8,128)(2,1)S(1)} collective-permute-done((bf16[256,2048]{1,0:T(8,128)(2,1)S(1)}, bf16[256,2048]{1,0:T(8,128)(2,1)S(1)}, u32[]{:S(2)}, u32[]{:S(2)}) %collective-permute-start.4) | collective-permute-done | bytes 1048608 | tf_op jit(solution)/shard_map/ppermute | solution.py:529
  770.8 6.2 fusion.25
  781.5 4.7 all-to-all-start.5
  786.2 9.5 convolution_bitcast_fusion.2
  796.1 9.0 convolution_bitcast_fusion.1
  808.8 6.1 all-to-all-start.10
  814.9 8.8 convolution_bitcast_fusion
  835.1 31.7 %all-gather.8.cloned.1.call-done = bf16[1024,2048]{1,0:T(8,128)(2,1)} async-done(((bf16[128,2048]{1,0:T(8,128)(2,1)}), bf16[1024,2048]{1,0:T(8,128)(2,1)}) %all-gather.8.cloned.1.call-update) | async-done | bytes 4194320 | tf_op jit(solution)/shard_map/all_gather | solution.py:513
  866.8 6.4 fusion.98
  873.2 5.0 convolution_convert_fusion.2
  878.1 11.7 %fusion.99 = f32[128,2048]{1,0:T(8,128)S(1)} fusion(bf16[128,4096]{1,0:T(8,128)(2,1)S(1)} %copy-done.23, bf16[2048,4096]{1,0:T(8,128)(2,1)} %bitcast.316), kind=kOutput, calls=%fused_computation.217 | convolution fusion | flops 2147483648 | bytes 18874368 | tf_op jit(solution)/shard_map/dot_general | solution.py:61
  889.9 5.5 fusion.62
  898.1 2.4 collective-permute-start.7
  902.7 3.4 all-to-all-start.8
  907.6 5.4 all-to-all-done.8
  913.0 3.5 convolution_convert_fusion.3
  917.7 2.7 collective-permute-start.11
  920.5 15.7 %collective-permute-done.7 = bf16[8,64,512]{2,1,0:T(8,128)(2,1)} collective-permute-done((bf16[8,64,512]{2,1,0:T(8,128)(2,1)}, bf16[8,64,512]{2,1,0:T(8,128)(2,1)}, u32[]{:S(2)}, u32[]{:S(2)}) %collective-permute-start.7) | collective-permute-done | bytes 524320 | tf_op jit(solution)/shard_map/ppermute | solution.py:529
  936.2 15.4 %collective-permute-start.12 = (bf16[128,2048]{1,0:T(8,128)(2,1)}, bf16[128,2048]{1,0:T(8,128)(2,1)}, u32[]{:S(2)}, u32[]{:S(2)}) collective-permute-start(bf16[128,2048]{1,0:T(8,128)(2,1)} %get-tuple-element.183), channel_id=1, source_target_pairs={{0,1},{1,2},{2,3},{3,0},{4,5},{5,6},{6,7},{7,4},{8,9},{9,10},{10,1... | collective-permute-start | bytes 1572872 | tf_op jit(solution)/shard_map/ppermute | solution.py:529
  951.6 3.4 collective-permute-start.13
  955.3 21.2 %collective-permute-done.10 = bf16[8,64,128]{2,1,0:T(8,128)(2,1)S(1)} collective-permute-done((bf16[8,64,128]{2,1,0:T(8,128)(2,1)S(1)}, bf16[8,64,128]{2,1,0:T(8,128)(2,1)S(1)}, u32[]{:S(2)}, u32[]{:S(2)}) %collective-permute-start.10) | collective-permute-done | bytes 131104 | tf_op jit(solution)/shard_map/ppermute | solution.py:529
  977.2 3.4 all-to-all-start.9
  980.6 2.4 add_convert_fusion.1
  983.0 3.0 all-to-all-done.9
  986.0 4.2 all-to-all-start.7
  991.7 8.2 all-to-all-done.7
  1001.0 5.8 all-to-all-start.6
  1006.8 3.0 convert_add_fusion
  1012.7 8.9 all-to-all-done.6
  (267 shorter events, 73.4 us)
Async XLA Ops:
  7.2 437.8 %copy-start = (bf16[1,768,2048]{2,1,0:T(8,128)(2,1)S(1)}, bf16[1,768,2048]{2,1,0:T(8,128)(2,1)}, u32[]{:S(2)}) copy-start(bf16[1,768,2048]{2,1,0:T(8,128)(2,1)} %param.30) | copy-start | bytes 9437188
  7.2 209.1 %copy-start.33 = (f32[2048]{0:T(1024)S(1)}, f32[2048]{0:T(1024)}, u32[]{:S(2)}) copy-start(f32[2048]{0:T(1024)} %param.19) | copy-start | bytes 24580
  7.2 203.3 %copy-start.48 = (s32[1,2]{1,0:T(1,128)S(1)}, s32[1,2]{1,0:T(1,128)}, u32[]{:S(2)}) copy-start(s32[1,2]{1,0:T(1,128)} %param.17) | copy-start | bytes 28
  7.2 235.7 %all-gather.4.cloned.1.call-start = ((), (), s32[]{:S(2)}) async-start(), calls=%async_computation.14 | async-start | bytes 4718592 | tf_op jit(solution)/shard_map/all_gather | solution.py:513
  8.7 217.5 %copy-start.37 = (f32[128]{0:T(128)}, f32[128]{0:T(128)S(1)}, u32[]{:S(2)}) copy-start(f32[128]{0:T(128)S(1)} %add_rsqrt_fusion.2) | copy-start | bytes 1540
  10.7 423.6 %all-gather.6.cloned.1.call-start = ((), (), s32[]{:S(2)}) async-start(), calls=%async_computation.15 | async-start | bytes 17301504 | tf_op jit(solution)/shard_map/all_gather | solution.py:513
  207.2 21.5 %all-to-all-start.1 = ((s32[8,5,128]{2,1,0:T(8,128)}), s32[8,5,128]{2,1,0:T(8,128)S(1)}, u32[]{:S(2)}, u32[]{:S(2)}) async-start(s32[8,5,128]{2,1,0:T(8,128)} %pad_add_fusion), calls=%async_computation.1 | async-start | bytes 65536 | tf_op jit(solution)/shard_map/all_to_all | solution.py:516
  216.3 36.9 %copy-start.9 = (f32[128,128]{1,0:T(8,128)}, f32[128,128]{1,0:T(8,128)S(1)}, u32[]{:S(2)}) copy-start(f32[128,128]{1,0:T(8,128)S(1)} %get-tuple-element.221.cosine_ref) | copy-start | bytes 196612
  216.3 36.9 %copy-start.11 = (f32[128,128]{1,0:T(8,128)}, f32[128,128]{1,0:T(8,128)S(1)}, u32[]{:S(2)}) copy-start(f32[128,128]{1,0:T(8,128)S(1)} %get-tuple-element.220.sine_ref) | copy-start | bytes 196612
  228.6 11.4 %all-to-all-start = ((s32[32,1,128]{2,1,0:T(1,128)}), s32[32,1,128]{2,1,0:T(1,128)S(1)}, u32[]{:S(2)}, u32[]{:S(2)}) async-start(s32[32,1,128]{2,1,0:T(1,128)} %bitcast.16), calls=%async_computation | async-start | bytes 32768 | tf_op jit(solution)/shard_map/all_to_all | solution.py:516
  242.9 10.3 copy-start.2
  242.9 10.3 copy-start.6
  242.9 10.3 copy-start.8
  242.9 10.3 copy-start.12
  243.0 10.3 copy-start.14
  253.3 16.4 %copy-start.19 = (bf16[1,128,2048]{2,1,0:T(8,128)(2,1)S(1)}, bf16[1,128,2048]{2,1,0:T(8,128)(2,1)}, u32[]{:S(2)}) copy-start(bf16[1,128,2048]{2,1,0:T(8,128)(2,1)} %param.16) | copy-start | bytes 1572868
  269.7 10.2 copy-start.35
  401.7 26.7 %all-to-all-start.2 = ((f32[32,1,128]{2,1,0:T(1,128)}), f32[32,1,128]{2,1,0:T(1,128)S(1)}, u32[]{:S(2)}, u32[]{:S(2)}) async-start(f32[32,1,128]{2,1,0:T(1,128)} %bitcast.24), calls=%async_computation.2 | async-start | bytes 32768 | tf_op jit(solution)/shard_map/all_to_all | solution.py:516
  408.0 10.7 %copy-start.44 = (bf16[1,2048,768]{2,1,0:T(8,128)(2,1)S(1)}, bf16[1,2048,768]{2,1,0:T(8,128)(2,1)}, u32[]{:S(2)}) copy-start(bf16[1,2048,768]{2,1,0:T(8,128)(2,1)} %param.28) | copy-start | bytes 9437188
  428.4 40.1 %all-to-all-start.3 = ((bf16[8,128,512]{2,1,0:T(8,128)(2,1)}), bf16[8,128,512]{2,1,0:T(8,128)(2,1)}, u32[]{:S(2)}, u32[]{:S(2)}) async-start(bf16[8,128,512]{2,1,0:T(8,128)(2,1)} %bitcast.321), calls=%async_computation.3 | async-start | bytes 2097152 | tf_op jit(solution)/shard_map/all_to_all | solution.py:516
  432.6 190.8 %reduce-scatter.4.cloned.1.call-start = ((), (), s32[]{:S(2)}) async-start(), calls=%async_computation.16 | async-start | bytes 4718592 | tf_op jit(solution)/shard_map/reduce_scatter | solution.py:519
  434.3 10.7 %copy-start.30 = (bf16[1024,768]{1,0:T(8,128)(2,1)S(1)}, bf16[1024,768]{1,0:T(8,128)(2,1)}, u32[]{:S(2)}) copy-start(bf16[1024,768]{1,0:T(8,128)(2,1)} %get-tuple-element.85) | copy-start | bytes 4718596
  468.5 97.1 %copy-start.25 = (bf16[4,256,1024]{2,1,0:T(8,128)(2,1)S(1)}, bf16[4,256,1024]{2,1,0:T(8,128)(2,1)}, u32[]{:S(2)}) copy-start(bf16[4,256,1024]{2,1,0:T(8,128)(2,1)} %fusion.22) | copy-start | bytes 6291460
  471.4 27.4 %collective-permute-start.2 = (bf16[256,2048]{1,0:T(8,128)(2,1)S(1)}, bf16[256,2048]{1,0:T(8,128)(2,1)S(1)}, u32[]{:S(2)}, u32[]{:S(2)}) collective-permute-start(bf16[256,2048]{1,0:T(8,128)(2,1)S(1)} %get-tuple-element.178), channel_id=1, source_target_pairs={{0,3},{1,0},{2,1},{3,2},{4,7},{5,4},{6,5},{7,6},{8,11},{9,8},{10,9... | collective-permute-start | bytes 3145736 | tf_op jit(solution)/shard_map/ppermute | solution.py:529
  475.1 90.4 %collective-permute-start.1 = (bf16[256,2048]{1,0:T(8,128)(2,1)S(1)}, bf16[256,2048]{1,0:T(8,128)(2,1)S(1)}, u32[]{:S(2)}, u32[]{:S(2)}) collective-permute-start(bf16[256,2048]{1,0:T(8,128)(2,1)S(1)} %get-tuple-element.179), channel_id=1, source_target_pairs={{0,2},{1,3},{2,0},{3,1},{4,6},{5,7},{6,4},{7,5},{8,10},{9,11},{10,... | collective-permute-start | bytes 3145736 | tf_op jit(solution)/shard_map/ppermute | solution.py:529
  475.1 90.4 %collective-permute-start = (bf16[256,2048]{1,0:T(8,128)(2,1)S(1)}, bf16[256,2048]{1,0:T(8,128)(2,1)S(1)}, u32[]{:S(2)}, u32[]{:S(2)}) collective-permute-start(bf16[256,2048]{1,0:T(8,128)(2,1)S(1)} %get-tuple-element.180), channel_id=1, source_target_pairs={{0,1},{1,2},{2,3},{3,0},{4,5},{5,6},{6,7},{7,4},{8,9},{9,10},{10,1... | collective-permute-start | bytes 3145736 | tf_op jit(solution)/shard_map/ppermute | solution.py:529
  571.7 51.8 %copy-start.17 = (f32[128,2048]{1,0:T(8,128)S(1)}, f32[128,2048]{1,0:T(8,128)}, u32[]{:S(2)}) copy-start(f32[128,2048]{1,0:T(8,128)} %copy-done.16) | copy-start | bytes 3145732
  571.7 53.6 %copy-start.29 = (bf16[1,128,2048]{2,1,0:T(8,128)(2,1)S(1)}, bf16[1,128,2048]{2,1,0:T(8,128)(2,1)}, u32[]{:S(2)}) copy-start(bf16[1,128,2048]{2,1,0:T(8,128)(2,1)} %param.31) | copy-start | bytes 1572868
  572.3 12.2 %all-to-all-start.4 = ((f32[32,1,128]{2,1,0:T(1,128)}), f32[32,1,128]{2,1,0:T(1,128)S(1)}, u32[]{:S(2)}, u32[]{:S(2)}) async-start(f32[32,1,128]{2,1,0:T(1,128)} %all_to_all.52), calls=%async_computation.5 | async-start | bytes 32768 | tf_op jit(solution)/shard_map/all_to_all | solution.py:516
  577.4 248.6 %reduce-scatter.8.cloned.1.call-start = ((), (), s32[]{:S(2)}) async-start(), calls=%async_computation.19 | async-start | bytes 2359296 | tf_op jit(solution)/shard_map/reduce_scatter | solution.py:519
  627.7 12.6 %copy-start.22 = (bf16[128,2048]{1,0:T(8,128)(2,1)}, bf16[128,2048]{1,0:T(8,128)(2,1)S(1)}, u32[]{:S(2)}) copy-start(bf16[128,2048]{1,0:T(8,128)(2,1)S(1)} %get-tuple-element.167) | copy-start | bytes 1572868
  670.8 162.1 %reduce-scatter.6.cloned.1.call-start = ((), (), s32[]{:S(2)}) async-start(), calls=%async_computation.17 | async-start | bytes 4718592 | tf_op jit(solution)/shard_map/reduce_scatter | solution.py:519
  677.1 93.7 %copy-start.26 = (bf16[4,256,1024]{2,1,0:T(8,128)(2,1)S(1)}, bf16[4,256,1024]{2,1,0:T(8,128)(2,1)}, u32[]{:S(2)}) copy-start(bf16[4,256,1024]{2,1,0:T(8,128)(2,1)} %fusion.22) | copy-start | bytes 6291460
  677.7 27.0 %collective-permute-start.5 = (bf16[256,2048]{1,0:T(8,128)(2,1)S(1)}, bf16[256,2048]{1,0:T(8,128)(2,1)S(1)}, u32[]{:S(2)}, u32[]{:S(2)}) collective-permute-start(bf16[256,2048]{1,0:T(8,128)(2,1)S(1)} %get-tuple-element.174), channel_id=1, source_target_pairs={{0,3},{1,0},{2,1},{3,2},{4,7},{5,4},{6,5},{7,6},{8,11},{9,8},{10,9... | collective-permute-start | bytes 3145736 | tf_op jit(solution)/shard_map/ppermute | solution.py:529
  681.1 89.7 %collective-permute-start.4 = (bf16[256,2048]{1,0:T(8,128)(2,1)S(1)}, bf16[256,2048]{1,0:T(8,128)(2,1)S(1)}, u32[]{:S(2)}, u32[]{:S(2)}) collective-permute-start(bf16[256,2048]{1,0:T(8,128)(2,1)S(1)} %get-tuple-element.175), channel_id=1, source_target_pairs={{0,2},{1,3},{2,0},{3,1},{4,6},{5,7},{6,4},{7,5},{8,10},{9,11},{10,... | collective-permute-start | bytes 3145736 | tf_op jit(solution)/shard_map/ppermute | solution.py:529
  681.1 89.7 %collective-permute-start.3 = (bf16[256,2048]{1,0:T(8,128)(2,1)S(1)}, bf16[256,2048]{1,0:T(8,128)(2,1)S(1)}, u32[]{:S(2)}, u32[]{:S(2)}) collective-permute-start(bf16[256,2048]{1,0:T(8,128)(2,1)S(1)} %get-tuple-element.176), channel_id=1, source_target_pairs={{0,1},{1,2},{2,3},{3,0},{4,5},{5,6},{6,7},{7,4},{8,9},{9,10},{10,1... | collective-permute-start | bytes 3145736 | tf_op jit(solution)/shard_map/ppermute | solution.py:529
  777.0 89.7 %all-gather.8.cloned.1.call-start = ((), (), s32[]{:S(2)}) async-start(), calls=%async_computation.18 | async-start | bytes 4718592 | tf_op jit(solution)/shard_map/all_gather | solution.py:513
  781.5 23.7 %all-to-all-start.5 = ((bf16[8,128,512]{2,1,0:T(8,128)(2,1)}), bf16[8,128,512]{2,1,0:T(8,128)(2,1)}, u32[]{:S(2)}, u32[]{:S(2)}) async-start(bf16[8,128,512]{2,1,0:T(8,128)(2,1)} %bitcast.322), calls=%async_computation.7 | async-start | bytes 2097152 | tf_op jit(solution)/shard_map/all_to_all | solution.py:516
  808.8 16.2 %all-to-all-start.10 = ((f32[32,1,2048]{2,1,0:T(1,128)}), f32[32,1,2048]{2,1,0:T(1,128)S(1)}, u32[]{:S(2)}, u32[]{:S(2)}) async-start(f32[32,1,2048]{2,1,0:T(1,128)} %all_to_all.61), calls=%async_computation.13 | async-start | bytes 524288 | tf_op jit(solution)/shard_map/all_to_all | solution.py:516
  878.1 11.7 %copy-start.20 = (bf16[1,128,2048]{2,1,0:T(8,128)(2,1)S(1)}, bf16[1,128,2048]{2,1,0:T(8,128)(2,1)}, u32[]{:S(2)}) copy-start(bf16[1,128,2048]{2,1,0:T(8,128)(2,1)} %param.16) | copy-start | bytes 1572868
  878.1 11.7 %copy-start.34 = (f32[2048]{0:T(1024)S(1)}, f32[2048]{0:T(1024)}, u32[]{:S(2)}) copy-start(f32[2048]{0:T(1024)} %param.19) | copy-start | bytes 24580
  878.1 11.8 %copy-start.38 = (f32[128]{0:T(128)S(1)}, f32[128]{0:T(128)}, u32[]{:S(2)}) copy-start(f32[128]{0:T(128)} %copy-done.37) | copy-start | bytes 1540
  895.4 10.7 %copy-start.27 = (bf16[512,2048]{1,0:T(8,128)(2,1)S(1)}, bf16[512,2048]{1,0:T(8,128)(2,1)}, u32[]{:S(2)}) copy-start(bf16[512,2048]{1,0:T(8,128)(2,1)} %fusion.98) | copy-start | bytes 6291460
  896.6 21.1 %collective-permute-start.6 = (bf16[8,64,512]{2,1,0:T(8,128)(2,1)}, bf16[8,64,512]{2,1,0:T(8,128)(2,1)}, u32[]{:S(2)}, u32[]{:S(2)}) collective-permute-start(bf16[8,64,512]{2,1,0:T(8,128)(2,1)} %get-tuple-element.187), channel_id=1, source_target_pairs={{0,1},{1,2},{2,3},{3,0},{4,5},{5,6},{6,7},{7,4},{8,9},{9,10},{10,1... | collective-permute-start | bytes 1572872 | tf_op jit(solution)/shard_map/ppermute | solution.py:529
  898.1 38.1 %collective-permute-start.7 = (bf16[8,64,512]{2,1,0:T(8,128)(2,1)}, bf16[8,64,512]{2,1,0:T(8,128)(2,1)}, u32[]{:S(2)}, u32[]{:S(2)}) collective-permute-start(bf16[8,64,512]{2,1,0:T(8,128)(2,1)} %get-tuple-element.186), channel_id=1, source_target_pairs={{0,2},{1,3},{2,0},{3,1},{4,6},{5,7},{6,4},{7,5},{8,10},{9,11},{10,... | collective-permute-start | bytes 1572872 | tf_op jit(solution)/shard_map/ppermute | solution.py:529
  900.5 51.0 %collective-permute-start.8 = (bf16[8,64,512]{2,1,0:T(8,128)(2,1)}, bf16[8,64,512]{2,1,0:T(8,128)(2,1)}, u32[]{:S(2)}, u32[]{:S(2)}) collective-permute-start(bf16[8,64,512]{2,1,0:T(8,128)(2,1)} %get-tuple-element.185), channel_id=1, source_target_pairs={{0,3},{1,0},{2,1},{3,2},{4,7},{5,4},{6,5},{7,6},{8,11},{9,8},{10,9... | collective-permute-start | bytes 1572872 | tf_op jit(solution)/shard_map/ppermute | solution.py:529
  902.7 10.3 all-to-all-start.8
  907.6 12.9 %copy-start.50 = (f32[128]{0:T(128)S(1)}, f32[128]{0:T(128)}, u32[]{:S(2)}) copy-start(f32[128]{0:T(128)} %get-tuple-element.159) | copy-start | bytes 1540
  907.6 12.9 %copy-start.40 = (f32[2048]{0:T(1024)S(1)}, f32[2048]{0:T(1024)}, u32[]{:S(2)}) copy-start(f32[2048]{0:T(1024)} %get-tuple-element.158) | copy-start | bytes 24580
  907.6 12.9 %copy-start.41 = (f32[128]{0:T(128)S(1)}, f32[128]{0:T(128)}, u32[]{:S(2)}) copy-start(f32[128]{0:T(128)} %get-tuple-element.160) | copy-start | bytes 1540
  907.6 12.9 %copy-start.42 = (f32[128]{0:T(128)S(1)}, f32[128]{0:T(128)}, u32[]{:S(2)}) copy-start(f32[128]{0:T(128)} %reduce_sum.233) | copy-start | bytes 1540
  916.5 73.7 %copy-start.24 = (f32[128,2048]{1,0:T(8,128)S(1)}, f32[128,2048]{1,0:T(8,128)}, u32[]{:S(2)}) copy-start(f32[128,2048]{1,0:T(8,128)} %get-tuple-element.168) | copy-start | bytes 3145732
  916.5 73.7 %copy-start.31 = (f32[128,2048]{1,0:T(8,128)S(1)}, f32[128,2048]{1,0:T(8,128)}, u32[]{:S(2)}) copy-start(f32[128,2048]{1,0:T(8,128)} %get-tuple-element.219) | copy-start | bytes 3145732
  916.5 73.7 %copy-start.39 = (f32[128]{0:T(128)S(1)}, f32[128]{0:T(128)}, u32[]{:S(2)}) copy-start(f32[128]{0:T(128)} %copy-done.37) | copy-start | bytes 1540
  916.6 38.4 %collective-permute-start.9 = (bf16[8,64,128]{2,1,0:T(8,128)(2,1)S(1)}, bf16[8,64,128]{2,1,0:T(8,128)(2,1)S(1)}, u32[]{:S(2)}, u32[]{:S(2)}) collective-permute-start(bf16[8,64,128]{2,1,0:T(8,128)(2,1)S(1)} %get-tuple-element.191), channel_id=1, source_target_pairs={{0,1},{1,2},{2,3},{3,0},{4,5},{5,6},{6,7},{7,4},{8,9},{9,10},{10,1... | collective-permute-start | bytes 393224 | tf_op jit(solution)/shard_map/ppermute | solution.py:529
  917.2 59.2 %collective-permute-start.10 = (bf16[8,64,128]{2,1,0:T(8,128)(2,1)S(1)}, bf16[8,64,128]{2,1,0:T(8,128)(2,1)S(1)}, u32[]{:S(2)}, u32[]{:S(2)}) collective-permute-start(bf16[8,64,128]{2,1,0:T(8,128)(2,1)S(1)} %get-tuple-element.190), channel_id=1, source_target_pairs={{0,2},{1,3},{2,0},{3,1},{4,6},{5,7},{6,4},{7,5},{8,10},{9,11},{10,... | collective-permute-start | bytes 393224 | tf_op jit(solution)/shard_map/ppermute | solution.py:529
  917.7 58.7 %collective-permute-start.11 = (bf16[8,64,128]{2,1,0:T(8,128)(2,1)S(1)}, bf16[8,64,128]{2,1,0:T(8,128)(2,1)S(1)}, u32[]{:S(2)}, u32[]{:S(2)}) collective-permute-start(bf16[8,64,128]{2,1,0:T(8,128)(2,1)S(1)} %get-tuple-element.189), channel_id=1, source_target_pairs={{0,3},{1,0},{2,1},{3,2},{4,7},{5,4},{6,5},{7,6},{8,11},{9,8},{10,9... | collective-permute-start | bytes 393224 | tf_op jit(solution)/shard_map/ppermute | solution.py:529
  936.2 55.3 %collective-permute-start.12 = (bf16[128,2048]{1,0:T(8,128)(2,1)}, bf16[128,2048]{1,0:T(8,128)(2,1)}, u32[]{:S(2)}, u32[]{:S(2)}) collective-permute-start(bf16[128,2048]{1,0:T(8,128)(2,1)} %get-tuple-element.183), channel_id=1, source_target_pairs={{0,1},{1,2},{2,3},{3,0},{4,5},{5,6},{6,7},{7,4},{8,9},{9,10},{10,1... | collective-permute-start | bytes 1572872 | tf_op jit(solution)/shard_map/ppermute | solution.py:529
  951.6 40.1 %collective-permute-start.13 = (bf16[128,2048]{1,0:T(8,128)(2,1)}, bf16[128,2048]{1,0:T(8,128)(2,1)}, u32[]{:S(2)}, u32[]{:S(2)}) collective-permute-start(bf16[128,2048]{1,0:T(8,128)(2,1)} %get-tuple-element.182), channel_id=1, source_target_pairs={{0,2},{1,3},{2,0},{3,1},{4,6},{5,7},{6,4},{7,5},{8,10},{9,11},{10,... | collective-permute-start | bytes 1572872 | tf_op jit(solution)/shard_map/ppermute | solution.py:529
  955.0 36.8 %collective-permute-start.14 = (bf16[128,2048]{1,0:T(8,128)(2,1)}, bf16[128,2048]{1,0:T(8,128)(2,1)}, u32[]{:S(2)}, u32[]{:S(2)}) collective-permute-start(bf16[128,2048]{1,0:T(8,128)(2,1)} %get-tuple-element.181), channel_id=1, source_target_pairs={{0,3},{1,0},{2,1},{3,2},{4,7},{5,4},{6,5},{7,6},{8,11},{9,8},{10,9... | collective-permute-start | bytes 1572872 | tf_op jit(solution)/shard_map/ppermute | solution.py:529
  977.2 8.8 all-to-all-start.9
  986.0 13.9 %all-to-all-start.7 = ((bf16[8,64,512]{2,1,0:T(8,128)(2,1)}), bf16[8,64,512]{2,1,0:T(8,128)(2,1)}, u32[]{:S(2)}, u32[]{:S(2)}) async-start(bf16[8,64,512]{2,1,0:T(8,128)(2,1)} %add_convert_fusion.1), calls=%async_computation.10 | async-start | bytes 1048576 | tf_op jit(solution)/shard_map/all_to_all | solution.py:516
  1001.0 20.6 %all-to-all-start.6 = ((f32[32,1,4352]{2,1,0:T(1,128)}), f32[32,1,4352]{2,1,0:T(1,128)}, u32[]{:S(2)}, u32[]{:S(2)}) async-start(f32[32,1,4352]{2,1,0:T(1,128)} %broadcast_in_dim.155), calls=%async_computation.9 | async-start | bytes 1114112 | tf_op jit(solution)/shard_map/all_to_all | solution.py:472
  1006.8 17.4 %copy-start.1 = (bf16[1,768,2048]{2,1,0:T(8,128)(2,1)S(1)}, bf16[1,768,2048]{2,1,0:T(8,128)(2,1)}, u32[]{:S(2)}) copy-start(bf16[1,768,2048]{2,1,0:T(8,128)(2,1)} %param.30) | copy-start | bytes 9437188
  (24 other events, 114.7 us)
Sparse Core Ops, SparseCore 0:
  10.8 53.1 all-gather.3
  205.8 147.5 all-gather.5
  571.8 51.6 reduce-scatter.3
  670.9 41.1 reduce-scatter.7
  777.1 51.7 reduce-scatter.5
  830.7 36.0 all-gather.7

commit v6 on v5

--- a/solution.py
+++ b/solution.py
@@ -518,17 +518,21 @@
     def scatter_sum(value, axes):
         return lax.psum_scatter(value, axes, scatter_dimension=0, tiled=True)
 
+    def cut(blocks):
+        return [
+            lax.dynamic_index_in_dim(blocks, lax.rem(wt_index + step, wt_size), keepdims=False)
+            for step in range(wt_size)
+        ]
+
+    def pass_on(cuts):
+        arrived = cuts[:1]
+        for step in range(1, wt_size):
+            pairs = [(w, (w + step) % wt_size) for w in range(wt_size)]
+            arrived.append(lax.ppermute(cuts[step], "wt", pairs))
+        return arrived
+
     def turn(blocks):
-        arrived = []
-        for step in range(wt_size):
-            block = lax.dynamic_index_in_dim(
-                blocks, lax.rem(wt_index + step, wt_size), keepdims=False
-            )
-            if step:
-                pairs = [(w, (w + step) % wt_size) for w in range(wt_size)]
-                block = lax.ppermute(block, "wt", pairs)
-            arrived.append(block)
-        return arrived
+        return pass_on(cut(blocks))
 
     def add_up(blocks):
         return sum(block.astype(jnp.float32) for block in blocks)
@@ -565,6 +569,10 @@
     earlier = jnp.arange(ctx_size, dtype=jnp.int32)[:, None] < ctx_index
     offsets = jnp.sum(jnp.where(earlier, plane[:, wt_size, :expert_count], 0), axis=0)
     kept = (hits > 0) & (local_rank + offsets[None, :] < capacity)
+    rank_lines = exchange(
+        jnp.where(kept, local_rank, -1).T.reshape(ctx_size, wt_size, tokens).transpose(1, 0, 2),
+        "wt",
+    )
     keep_float = kept.astype(jnp.float32)
     hits_float = hits.astype(jnp.float32)
 
@@ -577,9 +585,13 @@
     hit_mine = exchange(to_owner_rows(hits), by_stream).reshape(wt_size, seq_len)
     slot_mine = jnp.cumsum(hit_mine, axis=1) - hit_mine
     slot_mine = jnp.where((hit_mine > 0) & (slot_mine < capacity), slot_mine, -1)
+    send_slots = 2 * tokens * top_count // expert_count
+    send_ids = jnp.arange(send_slots, dtype=jnp.int32)
+    block_hits = jnp.sum(hit_mine.reshape(wt_size, ctx_size, tokens), axis=2)
+    block_first = jnp.cumsum(block_hits, axis=1) - block_hits
     slot_ids = jnp.arange(capacity, dtype=jnp.int32)
     place = slot_mine[:, None, :] == slot_ids[None, :, None]
-    place_low = place.astype(jnp.bfloat16)
+    place_low = after(place.astype(jnp.bfloat16), rank_lines)
     hit_plane = plane[:, :wt_size].transpose(1, 0, 2).reshape(wt_size, seq_len)
     hit_plane = hit_plane[(wt_index - jnp.arange(wt_size)) % wt_size]
     slot_plane = jnp.cumsum(hit_plane, axis=1) - hit_plane
@@ -672,17 +684,45 @@
         ).astype(jnp.bfloat16)
 
     mixed_rows = (gate_rows[:, None] * result_rows.astype(jnp.float32)).astype(jnp.bfloat16)
-    in_rows_cot, mixed_columns, spread_low = lax.optimization_barrier(
-        (in_rows_cot, mixed_columns, spread_low)
-    )
-    gate_cot = from_owner_rows(exchange(
-        after(gate_cot_mine, in_rows_cot).reshape(devices, tokens), by_stream
-    ))
-    blocks_shape = (wt_size, capacity, model_width)
-    stream_cots = turn(in_rows_cot.reshape(blocks_shape))
-    returned_cot = scatter_sum(add_pairs(spread_low, stream_cots), "ctx")
-    returned_cot = returned_cot.astype(jnp.float32)
-    stream_mixed = turn(after(mixed_rows, stream_cots).reshape(blocks_shape))
+    gate_cot = exchange(after(gate_cot_mine, mixed_columns).reshape(devices, tokens), by_stream)
+    in_rows_cot, gate_cot, mixed_columns = lax.optimization_barrier(
+        (in_rows_cot, gate_cot, mixed_columns)
+    )
+    gate_cot = from_owner_rows(gate_cot)
+    blocks_shape = (wt_size, capacity, -1)
+
+    half = model_width // 2
+    stream_cots = turn(in_rows_cot[:, :half].reshape(blocks_shape))
+    send_slot = jnp.where(
+        send_ids[None, None, :] < block_hits[:, :, None],
+        block_first[:, :, None] + send_ids[None, None, :],
+        -1,
+    ).reshape(wt_size, ctx_size * send_slots)
+    send_low = (send_slot[:, :, None] == slot_ids[None, None, :]).astype(jnp.bfloat16)
+    plane_sent = (
+        jnp.einsum(
+            "wjk,wkd->wjd",
+            send_low,
+            in_rows_cot[:, half:].reshape(blocks_shape),
+            preferred_element_type=jnp.float32,
+        )
+        .astype(jnp.bfloat16)
+        .reshape(wt_size, ctx_size, send_slots, half)
+        .transpose(1, 0, 2, 3)
+    )
+    plane_cots = exchange(plane_sent, "ctx")
+    first_part = scatter_sum(add_pairs(spread_low, stream_cots), "ctx")
+    line_low = (rank_lines[:, :, :, None] == send_ids).astype(jnp.bfloat16)
+    line_sent = jnp.einsum(
+        "sctj,csjd->std", line_low, plane_cots, preferred_element_type=jnp.float32
+    ).astype(jnp.bfloat16)
+    line_cots = turn(line_sent)
+    mixed_rows = after(mixed_rows, line_sent).reshape(blocks_shape)
+    mixed_cuts = cut(mixed_rows)
+    stream_mixed = pass_on(mixed_cuts)
+    returned_cot = after(
+        jnp.concatenate([first_part.astype(jnp.float32), add_up(line_cots)], axis=1), mixed_cuts
+    )
     out_cot = out_grad[0].astype(jnp.float32)
 
     kept_cot = gate_cot * keep_float

time: 1040 us -> 1020 us (0.981)
  waiting for transfers between devices: 321 us -> 258 us
  starting transfers between devices: 88.7 us -> 107 us
  local copies, waits for them, and re-layouts: 32.1 us -> 48.5 us
    all_to_all x10 -> x12, starting transfers between devices: 44.7 us -> 74.2 us  [exchange(): return lax.all_to_all(value, axes, split_axis=0, concat_axis=0, tiled=True)]
    ppermute x15 -> x18, waiting for transfers between devices: 215 us -> 188 us  [pass_on(): arrived.append(lax.ppermute(cuts[step], 'wt', pairs))]
    all_to_all x10 -> x12, waiting for transfers between devices: 26.2 us -> 4.62 us  [exchange(): return lax.all_to_all(value, axes, split_axis=0, concat_axis=0, tiled=True)]
    reduce_scatter x3, waiting for transfers between devices: 38.9 us -> 24.6 us  [scatter_sum(): return lax.psum_scatter(value, axes, scatter_dimension=0, tiled=True)]
    ppermute x15 -> x18, starting transfers between devices: 37.6 us -> 27.1 us  [pass_on(): arrived.append(lax.ppermute(cuts[step], 'wt', pairs))]
  transfers between devices with their start and end apart: 32 -> 37, of which waited for: 16 -> 14; matrix products, arithmetic and copies ran while one was open for 17% -> 21% of each run, Pallas kernels for 32% -> 32%
where the time goes in v6:
time: 1020 us; the launch traced here: 1010 us
  Pallas kernels  349 us (34%)
  waiting for transfers between devices  258 us (25%)
  matrix products  174 us (17%)
  starting transfers between devices  107 us (10%)
  other arithmetic  56.4 us (6%)
  local copies, waits for them, and re-layouts  48.5 us (5%)
  between operations  15.8 us (2%)
    pallas_call x2, Pallas kernels, spread(): pl.pallas_call(functools.partial(spread_kernel, splits, streams_first), o...  304 us
    ppermute x18, waiting for transfers between devices, pass_on(): arrived.append(lax.ppermute(cuts[step], 'wt', pairs))  188 us
    all_to_all x12, starting transfers between devices, exchange(): return lax.all_to_all(value, axes, split_axis=0, concat_axis=0, tiled=True)  74.2 us
    dot_general x9, matrix products, contract_rows(): lax.dot_general(left_side, right_side, (((0,), (0,)), ((), ())), preferre...  56.7 us
    dot_general x7, matrix products, contract_cols(): lax.dot_general(left_side, right_side, (((1,), (1,)), ((), ())), preferre...  46.2 us
    dot_general x7, matrix products, matmul(): return jnp.dot(left_side, right_side, preferred_element_type=jnp.float32)  44.6 us
    all_gather x3, waiting for transfers between devices, gather(): return lax.all_gather(value, axes, axis=0, tiled=True)  32 us
    pallas_call x1, Pallas kernels, attend_back(): pl.pallas_call(functools.partial(attend_back_kernel, head_dim, 2), grid=(...  29.5 us
  transfers between devices with their start and end apart: 37, of which 14 were waited for; matrix products, arithmetic and copies ran while one was open for 21% of the time, Pallas kernels for 32%

profile of v6, /device:TPU:0, one launch (start us, length us, event | category | flops | bytes accessed | tf_op | source)
XLA Modules:
  0.0 1010.3 jit_solution(17884295560560507137)
XLA Ops:
  13.1 192.6 %shard_map.263 = (bf16[8,4,64,1152]{3,2,1,0:T(8,128)(2,1)}, bf16[8,4,64,4096]{3,2,1,0:T(8,128)(2,1)}, bf16[8,4,128,2048]{3,2,1,0:T(8,128)(2,1)}) custom-call(bf16[64,1152]{1,0:T(8,128)(2,1)} %fusion.84.refs_0_, bf16[64,4096]{1,0:T(8,128)(2,1)} %refs_1_.1, bf16[128,2048]{1,0:T(8,128)(2,1)} %refs_2_.1), custom_call_target="tpu_custom_call" | custom-call | bytes 76546048 | tf_op jit(solution)/shard_map/pallas_call | solution.py:198
  207.2 3.3 all-to-all-start
  211.7 3.0 fusion.77
  216.3 9.8 fusion.67.query_ref
  229.1 3.9 all-to-all-start.1
  240.3 4.7 all-to-all-start.3
  252.0 10.2 %fusion.21.key_ref.value_ref = f32[1024,1024]{1,0:T(8,128)} fusion(bf16[1024,2048]{1,0:T(8,128)(2,1)} %all-gather.4.cloned.1.call-done, bf16[2048,1152]{1,0:T(8,128)(2,1)} %bitcast.389), kind=kOutput, calls=%fused_computation.38 | convolution fusion | flops 4294967296 | bytes 12582912 | tf_op jit(solution)/shard_map/dot_general | solution.py:51
  262.3 16.4 %attend.1 = (bf16[128,4096]{1,0:T(8,128)(2,1)S(1)}, bf16[128,4096]{1,0:T(8,128)(2,1)S(1)}) custom-call(f32[128,4096]{1,0:T(8,128)S(1)} %copy-done.2, f32[1024,1024]{1,0:T(8,128)} %fusion.21.key_ref.value_ref, f32[1024,1024]{1,0:T(8,128)} %fusion.21.key_ref.value_ref, f32[1,128]{1,0:T(1,128)S(1)} %bitcast.354, f32[128,128]{1,0:T(8,128)S(1)} %get-tuple-element.244.cosine_ref, ...), custom_call_target="tpu_custom_call" | custom-call | flops 2147483648 | bytes 4194304 | tf_op jit(solution)/shard_map/attend/pallas_call | solution.py:365
  278.7 9.2 multiply_reduce_fusion.2
  289.8 110.9 %shard_map.264 = bf16[4,8,128,2048]{3,2,1,0:T(8,128)(2,1)} custom-call(bf16[128,2048]{1,0:T(8,128)(2,1)} %multiply_convert_fusion.3.refs_0_), custom_call_target="tpu_custom_call" | custom-call | bytes 33554432 | tf_op jit(solution)/shard_map/pallas_call | solution.py:198
  403.1 11.3 %all-to-all-start.2 = ((f32[32,1,128]{2,1,0:T(1,128)}), f32[32,1,128]{2,1,0:T(1,128)S(1)}, u32[]{:S(2)}, u32[]{:S(2)}) async-start(f32[32,1,128]{2,1,0:T(1,128)} %bitcast.29), calls=%async_computation.2 | async-start | bytes 32768 | tf_op jit(solution)/shard_map/all_to_all | solution.py:516
  414.5 11.1 %convolution_convert_fusion.1 = bf16[4,256,2048]{2,1,0:T(8,128)(2,1)S(1)} fusion(bf16[4,256,1024]{2,1,0:T(8,128)(2,1)} %fusion.14, bf16[4,1024,2048]{2,1,0:T(8,128)(2,1)} %bitcast.361), kind=kOutput, calls=%fused_computation.33 | convolution fusion | flops 4297064448 | bytes 23068672 | tf_op jit(solution)/shard_map/wkt,wtd->wkd/dot_general | solution.py:650
  425.6 3.4 fusion.25
  429.0 5.2 multiply_convert_fusion
  435.3 4.2 all-to-all-start.4
  440.8 11.0 %convolution_convert_fusion.2 = bf16[4,256,2048]{2,1,0:T(8,128)(2,1)S(1)} fusion(bf16[4,256,1024]{2,1,0:T(8,128)(2,1)} %fusion.14, bf16[4,1024,2048]{2,1,0:T(8,128)(2,1)} %bitcast.407), kind=kOutput, calls=%fused_computation.34 | convolution fusion | flops 4297064448 | bytes 23068672 | tf_op jit(solution)/shard_map/wkt,wtd->wkd/dot_general | solution.py:650
  451.9 5.2 fusion
  459.1 6.5 all-to-all-start.5
  465.6 3.1 fusion.2
  469.7 4.3 multiply_convert_fusion.1
  474.1 3.4 fusion.23
  477.6 5.0 add_convert_fusion
  482.6 4.0 fusion.99
  490.5 4.7 all-to-all-start.6
  496.5 3.7 collective-permute-start.2
  502.8 10.1 collective-permute-done.2
  512.9 32.9 %collective-permute-done.1 = bf16[256,1024]{1,0:T(8,128)(2,1)S(1)} collective-permute-done((bf16[256,1024]{1,0:T(8,128)(2,1)}, bf16[256,1024]{1,0:T(8,128)(2,1)S(1)}, u32[]{:S(2)}, u32[]{:S(2)}) %collective-permute-start.1) | collective-permute-done | bytes 524320 | tf_op jit(solution)/shard_map/ppermute | solution.py:531
  545.9 4.8 fusion.44
  552.3 7.3 fusion.3
  559.7 3.2 bitcast_convert_fusion
  563.9 3.1 collective-permute-start.5
  567.9 24.6 %reduce-scatter.4.cloned.1.call-done = bf16[128,1024]{1,0:T(8,128)(2,1)} async-done(((bf16[1024,1024]{1,0:T(8,128)(2,1)}), bf16[128,1024]{1,0:T(8,128)(2,1)}) %reduce-scatter.4.cloned.1.call-update) | async-done | bytes 262160 | tf_op jit(solution)/shard_map/reduce_scatter | solution.py:519
  593.5 4.5 dynamic-slice_bitcast_fusion
  601.9 12.6 %convolution_convert_fusion.cot_ref = bf16[128,4096]{1,0:T(8,128)(2,1)} fusion(bf16[128,2048]{1,0:T(8,128)(2,1)S(1)} %fusion.96, bf16[4096,2048]{1,0:T(8,128)(2,1)} %bitcast.356), kind=kOutput, calls=%fused_computation.10 | convolution fusion | flops 2148007936 | bytes 18350080 | tf_op jit(solution)/shard_map/dot_general | solution.py:61
  615.3 29.5 %attend_back.1 = (bf16[128,4096]{1,0:T(8,128)(2,1)}, bf16[1024,1024]{1,0:T(8,128)(2,1)}, f32[32,128]{1,0:T(8,128)}) custom-call(f32[128,4096]{1,0:T(8,128)} %fusion.67.query_ref, bf16[128,4096]{1,0:T(8,128)(2,1)} %copy-done.15, bf16[128,4096]{1,0:T(8,128)(2,1)} %convolution_convert_fusion.cot_ref, f32[1024,1024]{1,0:T(8,128)} %fusion.21.key_ref.value_ref, ...), custom_call_target="tpu_custom_call" | custom-call | flops 5368709120 | bytes 6291456 | tf_op jit(solution)/shard_map/attend_back/pallas_call | solution.py:413
  644.8 3.4 collective-permute-start.8
  650.2 21.9 %collective-permute-done.8 = bf16[256,2048]{1,0:T(8,128)(2,1)S(1)} collective-permute-done((bf16[256,2048]{1,0:T(8,128)(2,1)}, bf16[256,2048]{1,0:T(8,128)(2,1)S(1)}, u32[]{:S(2)}, u32[]{:S(2)}) %collective-permute-start.8) | collective-permute-done | bytes 1048608 | tf_op jit(solution)/shard_map/ppermute | solution.py:531
  672.1 66.0 %collective-permute-done.7 = bf16[256,2048]{1,0:T(8,128)(2,1)S(1)} collective-permute-done((bf16[256,2048]{1,0:T(8,128)(2,1)}, bf16[256,2048]{1,0:T(8,128)(2,1)S(1)}, u32[]{:S(2)}, u32[]{:S(2)}) %collective-permute-start.7) | collective-permute-done | bytes 1048608 | tf_op jit(solution)/shard_map/ppermute | solution.py:531
  738.2 7.9 fusion.16
  751.7 4.3 all-to-all-start.7
  756.0 9.4 convolution_bitcast_fusion.1
  765.9 9.6 convolution_bitcast_fusion.2
  779.3 5.5 all-to-all-start.12
  784.8 8.8 convolution_bitcast_fusion
  804.0 32.0 %all-gather.8.cloned.1.call-done = bf16[1024,2048]{1,0:T(8,128)(2,1)} async-done(((bf16[128,2048]{1,0:T(8,128)(2,1)}), bf16[1024,2048]{1,0:T(8,128)(2,1)}) %all-gather.8.cloned.1.call-update) | async-done | bytes 4194320 | tf_op jit(solution)/shard_map/all_gather | solution.py:513
  836.0 6.4 fusion.104
  842.3 5.0 convolution_convert_fusion.4
  848.1 13.0 %fusion.105 = f32[128,2048]{1,0:T(8,128)} fusion(bf16[128,4096]{1,0:T(8,128)(2,1)} %get-tuple-element.71, bf16[2048,4096]{1,0:T(8,128)(2,1)} %bitcast.358), kind=kOutput, calls=%fused_computation.239 | convolution fusion | flops 2147483648 | bytes 18874368 | tf_op jit(solution)/shard_map/dot_general | solution.py:61
  861.1 5.7 fusion.61
  866.8 3.4 all-to-all-start.10
  870.2 3.0 dynamic-slice_bitcast_fusion.8
  873.3 3.3 collective-permute-start.11
  879.1 3.5 convolution_convert_fusion.6
  882.7 2.8 collective-permute-start.14
  890.1 38.5 %collective-permute-done.10 = bf16[8,64,512]{2,1,0:T(8,128)(2,1)} collective-permute-done((bf16[8,64,512]{2,1,0:T(8,128)(2,1)}, bf16[8,64,512]{2,1,0:T(8,128)(2,1)}, u32[]{:S(2)}, u32[]{:S(2)}) %collective-permute-start.10) | collective-permute-done | bytes 524320 | tf_op jit(solution)/shard_map/ppermute | solution.py:531
  928.6 2.9 collective-permute-start.16
  934.9 18.1 %all-to-all-start.11 = ((bf16[8,64,128]{2,1,0:T(8,128)(2,1)}), bf16[8,64,128]{2,1,0:T(8,128)(2,1)S(1)}, u32[]{:S(2)}, u32[]{:S(2)}) async-start(bf16[8,64,128]{2,1,0:T(8,128)(2,1)} %add_convert_fusion.2), calls=%async_computation.14 | async-start | bytes 262144 | tf_op jit(solution)/shard_map/all_to_all | solution.py:516
  955.6 2.9 all-to-all-done.11
  958.5 4.2 all-to-all-start.9
  962.7 2.8 fusion.60
  965.5 13.2 %collective-permute-done.16 = bf16[128,2048]{1,0:T(8,128)(2,1)} collective-permute-done((bf16[128,2048]{1,0:T(8,128)(2,1)}, bf16[128,2048]{1,0:T(8,128)(2,1)}, u32[]{:S(2)}, u32[]{:S(2)}) %collective-permute-start.16) | collective-permute-done | bytes 524320 | tf_op jit(solution)/shard_map/ppermute | solution.py:531
  979.7 5.9 all-to-all-start.8
  985.6 3.0 convert_add_fusion
  991.6 8.9 all-to-all-done.8
  (316 shorter events, 96.4 us)
Async XLA Ops:
  7.2 444.7 %copy-start = (bf16[1,768,2048]{2,1,0:T(8,128)(2,1)S(1)}, bf16[1,768,2048]{2,1,0:T(8,128)(2,1)}, u32[]{:S(2)}) copy-start(bf16[1,768,2048]{2,1,0:T(8,128)(2,1)} %param.30) | copy-start | bytes 9437188
  7.2 209.1 %copy-start.32 = (f32[2048]{0:T(1024)S(1)}, f32[2048]{0:T(1024)}, u32[]{:S(2)}) copy-start(f32[2048]{0:T(1024)} %param.19) | copy-start | bytes 24580
  7.2 203.3 %copy-start.55 = (s32[1,2]{1,0:T(1,128)S(1)}, s32[1,2]{1,0:T(1,128)}, u32[]{:S(2)}) copy-start(s32[1,2]{1,0:T(1,128)} %param.17) | copy-start | bytes 28
  7.2 244.7 %all-gather.4.cloned.1.call-start = ((), (), s32[]{:S(2)}) async-start(), calls=%async_computation.16 | async-start | bytes 4718592 | tf_op jit(solution)/shard_map/all_gather | solution.py:513
  8.7 217.5 %copy-start.39 = (f32[128]{0:T(128)}, f32[128]{0:T(128)S(1)}, u32[]{:S(2)}) copy-start(f32[128]{0:T(128)S(1)} %add_rsqrt_fusion.2) | copy-start | bytes 1540
  10.7 430.1 %all-gather.6.cloned.1.call-start = ((), (), s32[]{:S(2)}) async-start(), calls=%async_computation.17 | async-start | bytes 17301504 | tf_op jit(solution)/shard_map/all_gather | solution.py:513
  207.2 21.3 %all-to-all-start = ((s32[8,5,128]{2,1,0:T(8,128)}), s32[8,5,128]{2,1,0:T(8,128)S(1)}, u32[]{:S(2)}, u32[]{:S(2)}) async-start(s32[8,5,128]{2,1,0:T(8,128)} %pad_add_fusion), calls=%async_computation | async-start | bytes 65536 | tf_op jit(solution)/shard_map/all_to_all | solution.py:516
  216.3 45.9 %copy-start.9 = (f32[128,128]{1,0:T(8,128)}, f32[128,128]{1,0:T(8,128)S(1)}, u32[]{:S(2)}) copy-start(f32[128,128]{1,0:T(8,128)S(1)} %get-tuple-element.244.cosine_ref) | copy-start | bytes 196612
  216.3 45.9 %copy-start.11 = (f32[128,128]{1,0:T(8,128)}, f32[128,128]{1,0:T(8,128)S(1)}, u32[]{:S(2)}) copy-start(f32[128,128]{1,0:T(8,128)S(1)} %get-tuple-element.243.sine_ref) | copy-start | bytes 196612
  229.1 11.2 %all-to-all-start.1 = ((s32[32,1,128]{2,1,0:T(1,128)}), s32[32,1,128]{2,1,0:T(1,128)S(1)}, u32[]{:S(2)}, u32[]{:S(2)}) async-start(s32[32,1,128]{2,1,0:T(1,128)} %bitcast.23), calls=%async_computation.1 | async-start | bytes 32768 | tf_op jit(solution)/shard_map/all_to_all | solution.py:516
  240.3 11.5 %all-to-all-start.3 = ((s32[4,8,128]{2,1,0:T(8,128)}), s32[4,8,128]{2,1,0:T(8,128)}, u32[]{:S(2)}, u32[]{:S(2)}) async-start(s32[4,8,128]{2,1,0:T(8,128)} %copy.202), calls=%async_computation.3 | async-start | bytes 32768 | tf_op jit(solution)/shard_map/all_to_all | solution.py:516
  251.9 10.3 %copy-start.2 = (f32[128,4096]{1,0:T(8,128)S(1)}, f32[128,4096]{1,0:T(8,128)}, u32[]{:S(2)}) copy-start(f32[128,4096]{1,0:T(8,128)} %fusion.67.query_ref) | copy-start | bytes 6291460
  262.3 16.4 %copy-start.19 = (bf16[1,128,2048]{2,1,0:T(8,128)(2,1)S(1)}, bf16[1,128,2048]{2,1,0:T(8,128)(2,1)}, u32[]{:S(2)}) copy-start(bf16[1,128,2048]{2,1,0:T(8,128)(2,1)} %param.16) | copy-start | bytes 1572868
  287.9 112.8 %copy-start.41 = (f32[128]{0:T(128)}, f32[128]{0:T(128)S(1)}, u32[]{:S(2)}) copy-start(f32[128]{0:T(128)S(1)} %add_rsqrt_fusion.1) | copy-start | bytes 1540
  289.8 112.6 %copy-start.36 = (s32[128,32]{0,1:T(8,128)S(1)}, s32[128,32]{0,1:T(8,128)}, u32[]{:S(2)}) copy-start(s32[128,32]{0,1:T(8,128)} %copy.198) | copy-start | bytes 49156
  289.8 112.6 %copy-start.45 = (s32[32]{0:T(128)S(1)}, s32[32]{0:T(128)}, u32[]{:S(2)}) copy-start(s32[32]{0:T(128)} %copy-done.44) | copy-start | bytes 388
  403.1 32.2 %all-to-all-start.2 = ((f32[32,1,128]{2,1,0:T(1,128)}), f32[32,1,128]{2,1,0:T(1,128)S(1)}, u32[]{:S(2)}, u32[]{:S(2)}) async-start(f32[32,1,128]{2,1,0:T(1,128)} %bitcast.29), calls=%async_computation.2 | async-start | bytes 32768 | tf_op jit(solution)/shard_map/all_to_all | solution.py:516
  414.4 11.1 %copy-start.51 = (bf16[1,2048,768]{2,1,0:T(8,128)(2,1)S(1)}, bf16[1,2048,768]{2,1,0:T(8,128)(2,1)}, u32[]{:S(2)}) copy-start(bf16[1,2048,768]{2,1,0:T(8,128)(2,1)} %param.28) | copy-start | bytes 9437188
  435.3 23.1 %all-to-all-start.4 = ((bf16[8,128,512]{2,1,0:T(8,128)(2,1)}), bf16[8,128,512]{2,1,0:T(8,128)(2,1)}, u32[]{:S(2)}, u32[]{:S(2)}) async-start(bf16[8,128,512]{2,1,0:T(8,128)(2,1)} %bitcast.367), calls=%async_computation.4 | async-start | bytes 2097152 | tf_op jit(solution)/shard_map/all_to_all | solution.py:516
  440.8 11.1 %copy-start.27 = (bf16[1024,768]{1,0:T(8,128)(2,1)S(1)}, bf16[1024,768]{1,0:T(8,128)(2,1)}, u32[]{:S(2)}) copy-start(bf16[1024,768]{1,0:T(8,128)(2,1)} %get-tuple-element.89) | copy-start | bytes 4718596
  459.1 23.5 %all-to-all-start.5 = ((f32[32,1,128]{2,1,0:T(1,128)}), f32[32,1,128]{2,1,0:T(1,128)S(1)}, u32[]{:S(2)}, u32[]{:S(2)}) async-start(f32[32,1,128]{2,1,0:T(1,128)} %all_to_all.61), calls=%async_computation.5 | async-start | bytes 32768 | tf_op jit(solution)/shard_map/all_to_all | solution.py:516
  490.5 69.2 %all-to-all-start.6 = ((bf16[8,4,64,1024]{3,2,1,0:T(8,128)(2,1)}), bf16[8,4,64,1024]{3,2,1,0:T(8,128)(2,1)}, u32[]{:S(2)}, u32[]{:S(2)}) async-start(bf16[8,4,64,1024]{3,2,1,0:T(8,128)(2,1)} %bitcast.362), calls=%async_computation.7 | async-start | bytes 8388608 | tf_op jit(solution)/shard_map/all_to_all | solution.py:516
  495.2 97.3 %reduce-scatter.4.cloned.1.call-start = ((), (), s32[]{:S(2)}) async-start(), calls=%async_computation.18 | async-start | bytes 2359296 | tf_op jit(solution)/shard_map/reduce_scatter | solution.py:519
  496.5 16.4 %collective-permute-start.2 = (bf16[256,1024]{1,0:T(8,128)(2,1)}, bf16[256,1024]{1,0:T(8,128)(2,1)S(1)}, u32[]{:S(2)}, u32[]{:S(2)}) collective-permute-start(bf16[256,1024]{1,0:T(8,128)(2,1)} %get-tuple-element.206), channel_id=1, source_target_pairs={{0,3},{1,0},{2,1},{3,2},{4,7},{5,4},{6,5},{7,6},{8,11},{9,8},{10,9... | collective-permute-start | bytes 1572872 | tf_op jit(solution)/shard_map/ppermute | solution.py:531
  500.2 45.7 %collective-permute-start.1 = (bf16[256,1024]{1,0:T(8,128)(2,1)}, bf16[256,1024]{1,0:T(8,128)(2,1)S(1)}, u32[]{:S(2)}, u32[]{:S(2)}) collective-permute-start(bf16[256,1024]{1,0:T(8,128)(2,1)} %get-tuple-element.207), channel_id=1, source_target_pairs={{0,2},{1,3},{2,0},{3,1},{4,6},{5,7},{6,4},{7,5},{8,10},{9,11},{10,... | collective-permute-start | bytes 1572872 | tf_op jit(solution)/shard_map/ppermute | solution.py:531
  500.2 45.7 %collective-permute-start = (bf16[256,1024]{1,0:T(8,128)(2,1)S(1)}, bf16[256,1024]{1,0:T(8,128)(2,1)}, u32[]{:S(2)}, u32[]{:S(2)}) collective-permute-start(bf16[256,1024]{1,0:T(8,128)(2,1)S(1)} %get-tuple-element.208), channel_id=1, source_target_pairs={{0,1},{1,2},{2,3},{3,0},{4,5},{5,6},{6,7},{7,4},{8,9},{9,10},{10,1... | collective-permute-start | bytes 1572872 | tf_op jit(solution)/shard_map/ppermute | solution.py:531
  550.7 245.2 %reduce-scatter.8.cloned.1.call-start = ((), (), s32[]{:S(2)}) async-start(), calls=%async_computation.21 | async-start | bytes 2359296 | tf_op jit(solution)/shard_map/reduce_scatter | solution.py:519
  562.9 30.5 %copy-start.28 = (bf16[4,128,1024]{2,1,0:T(8,128)(2,1)}, bf16[4,128,1024]{2,1,0:T(8,128)(2,1)S(1)}, u32[]{:S(2)}) copy-start(bf16[4,128,1024]{2,1,0:T(8,128)(2,1)S(1)} %bitcast_convert_fusion) | copy-start | bytes 3145732
  563.0 34.9 %collective-permute-start.3 = (bf16[128,1024]{1,0:T(8,128)(2,1)S(1)}, bf16[128,1024]{1,0:T(8,128)(2,1)S(1)}, u32[]{:S(2)}, u32[]{:S(2)}) collective-permute-start(bf16[128,1024]{1,0:T(8,128)(2,1)S(1)} %get-tuple-element.209), channel_id=1, source_target_pairs={{0,1},{1,2},{2,3},{3,0},{4,5},{5,6},{6,7},{7,4},{8,9},{9,10},{10,1... | collective-permute-start | bytes 786440 | tf_op jit(solution)/shard_map/ppermute | solution.py:531
  563.9 34.1 %collective-permute-start.5 = (bf16[128,1024]{1,0:T(8,128)(2,1)S(1)}, bf16[128,1024]{1,0:T(8,128)(2,1)S(1)}, u32[]{:S(2)}, u32[]{:S(2)}) collective-permute-start(bf16[128,1024]{1,0:T(8,128)(2,1)S(1)} %get-tuple-element.210), channel_id=1, source_target_pairs={{0,3},{1,0},{2,1},{3,2},{4,7},{5,4},{6,5},{7,6},{8,11},{9,8},{10,9... | collective-permute-start | bytes 786440 | tf_op jit(solution)/shard_map/ppermute | solution.py:531
  566.9 31.1 %collective-permute-start.4 = (bf16[128,1024]{1,0:T(8,128)(2,1)S(1)}, bf16[128,1024]{1,0:T(8,128)(2,1)}, u32[]{:S(2)}, u32[]{:S(2)}) collective-permute-start(bf16[128,1024]{1,0:T(8,128)(2,1)S(1)} %get-tuple-element.211), channel_id=1, source_target_pairs={{0,2},{1,3},{2,0},{3,1},{4,6},{5,7},{6,4},{7,5},{8,10},{9,11},{10,... | collective-permute-start | bytes 786440 | tf_op jit(solution)/shard_map/ppermute | solution.py:531
  601.5 12.9 %copy-start.46 = (f32[128]{0:T(128)}, f32[128]{0:T(128)S(1)}, u32[]{:S(2)}) copy-start(f32[128]{0:T(128)S(1)} %broadcast_multiply_fusion.3) | copy-start | bytes 1540
  601.9 12.6 %copy-start.25 = (bf16[128,2048]{1,0:T(8,128)(2,1)}, bf16[128,2048]{1,0:T(8,128)(2,1)S(1)}, u32[]{:S(2)}) copy-start(bf16[128,2048]{1,0:T(8,128)(2,1)S(1)} %fusion.96) | copy-start | bytes 1572868
  644.8 157.1 %reduce-scatter.6.cloned.1.call-start = ((), (), s32[]{:S(2)}) async-start(), calls=%async_computation.19 | async-start | bytes 4718592 | tf_op jit(solution)/shard_map/reduce_scatter | solution.py:519
  644.8 27.3 %collective-permute-start.8 = (bf16[256,2048]{1,0:T(8,128)(2,1)}, bf16[256,2048]{1,0:T(8,128)(2,1)S(1)}, u32[]{:S(2)}, u32[]{:S(2)}) collective-permute-start(bf16[256,2048]{1,0:T(8,128)(2,1)} %get-tuple-element.191), channel_id=1, source_target_pairs={{0,3},{1,0},{2,1},{3,2},{4,7},{5,4},{6,5},{7,6},{8,11},{9,8},{10,9... | collective-permute-start | bytes 3145736 | tf_op jit(solution)/shard_map/ppermute | solution.py:531
  648.2 89.9 %collective-permute-start.7 = (bf16[256,2048]{1,0:T(8,128)(2,1)}, bf16[256,2048]{1,0:T(8,128)(2,1)S(1)}, u32[]{:S(2)}, u32[]{:S(2)}) collective-permute-start(bf16[256,2048]{1,0:T(8,128)(2,1)} %get-tuple-element.192), channel_id=1, source_target_pairs={{0,2},{1,3},{2,0},{3,1},{4,6},{5,7},{6,4},{7,5},{8,10},{9,11},{10,... | collective-permute-start | bytes 3145736 | tf_op jit(solution)/shard_map/ppermute | solution.py:531
  648.2 89.9 %collective-permute-start.6 = (bf16[256,2048]{1,0:T(8,128)(2,1)}, bf16[256,2048]{1,0:T(8,128)(2,1)S(1)}, u32[]{:S(2)}, u32[]{:S(2)}) collective-permute-start(bf16[256,2048]{1,0:T(8,128)(2,1)} %get-tuple-element.193), channel_id=1, source_target_pairs={{0,1},{1,2},{2,3},{3,0},{4,5},{5,6},{6,7},{7,4},{8,9},{9,10},{10,1... | collective-permute-start | bytes 3145736 | tf_op jit(solution)/shard_map/ppermute | solution.py:531
  746.1 89.9 %all-gather.8.cloned.1.call-start = ((), (), s32[]{:S(2)}) async-start(), calls=%async_computation.20 | async-start | bytes 4718592 | tf_op jit(solution)/shard_map/all_gather | solution.py:513
  751.7 23.8 %all-to-all-start.7 = ((bf16[8,128,512]{2,1,0:T(8,128)(2,1)}), bf16[8,128,512]{2,1,0:T(8,128)(2,1)}, u32[]{:S(2)}, u32[]{:S(2)}) async-start(bf16[8,128,512]{2,1,0:T(8,128)(2,1)} %bitcast.368), calls=%async_computation.9 | async-start | bytes 2097152 | tf_op jit(solution)/shard_map/all_to_all | solution.py:516
  779.3 15.7 %all-to-all-start.12 = ((f32[32,1,2048]{2,1,0:T(1,128)}), f32[32,1,2048]{2,1,0:T(1,128)S(1)}, u32[]{:S(2)}, u32[]{:S(2)}) async-start(f32[32,1,2048]{2,1,0:T(1,128)} %all_to_all.72), calls=%async_computation.15 | async-start | bytes 524288 | tf_op jit(solution)/shard_map/all_to_all | solution.py:516
  848.1 13.0 %copy-start.20 = (bf16[1,128,2048]{2,1,0:T(8,128)(2,1)S(1)}, bf16[1,128,2048]{2,1,0:T(8,128)(2,1)}, u32[]{:S(2)}) copy-start(bf16[1,128,2048]{2,1,0:T(8,128)(2,1)} %param.16) | copy-start | bytes 1572868
  848.1 13.0 %copy-start.33 = (f32[2048]{0:T(1024)S(1)}, f32[2048]{0:T(1024)}, u32[]{:S(2)}) copy-start(f32[2048]{0:T(1024)} %param.19) | copy-start | bytes 24580
  848.1 13.0 %copy-start.40 = (f32[128]{0:T(128)S(1)}, f32[128]{0:T(128)}, u32[]{:S(2)}) copy-start(f32[128]{0:T(128)} %copy-done.39) | copy-start | bytes 1540
  866.8 12.4 %all-to-all-start.10 = ((bf16[8,128,128]{2,1,0:T(8,128)(2,1)}), bf16[8,128,128]{2,1,0:T(8,128)(2,1)S(1)}, u32[]{:S(2)}, u32[]{:S(2)}) async-start(bf16[8,128,128]{2,1,0:T(8,128)(2,1)} %bitcast_bitcast_fusion.2), calls=%async_computation.13 | async-start | bytes 524288 | tf_op jit(solution)/shard_map/all_to_all | solution.py:516
  873.3 16.0 %collective-permute-start.11 = (bf16[8,64,512]{2,1,0:T(8,128)(2,1)}, bf16[8,64,512]{2,1,0:T(8,128)(2,1)}, u32[]{:S(2)}, u32[]{:S(2)}) collective-permute-start(bf16[8,64,512]{2,1,0:T(8,128)(2,1)} %get-tuple-element.201), channel_id=1, source_target_pairs={{0,3},{1,0},{2,1},{3,2},{4,7},{5,4},{6,5},{7,6},{8,11},{9,8},{10,9... | collective-permute-start | bytes 1572872 | tf_op jit(solution)/shard_map/ppermute | solution.py:531
  877.9 12.2 %copy-start.57 = (f32[128]{0:T(128)S(1)}, f32[128]{0:T(128)}, u32[]{:S(2)}) copy-start(f32[128]{0:T(128)} %get-tuple-element.177) | copy-start | bytes 1540
  877.9 12.2 %copy-start.37 = (f32[2048]{0:T(1024)S(1)}, f32[2048]{0:T(1024)}, u32[]{:S(2)}) copy-start(f32[2048]{0:T(1024)} %get-tuple-element.174) | copy-start | bytes 24580
  877.9 12.2 %copy-start.43 = (f32[2048]{0:T(1024)S(1)}, f32[2048]{0:T(1024)}, u32[]{:S(2)}) copy-start(f32[2048]{0:T(1024)} %get-tuple-element.176) | copy-start | bytes 24580
  877.9 12.2 %copy-start.48 = (f32[128]{0:T(128)S(1)}, f32[128]{0:T(128)}, u32[]{:S(2)}) copy-start(f32[128]{0:T(128)} %get-tuple-element.178) | copy-start | bytes 1540
  878.0 12.2 %copy-start.49 = (f32[128]{0:T(128)S(1)}, f32[128]{0:T(128)}, u32[]{:S(2)}) copy-start(f32[128]{0:T(128)} %reduce_sum.243) | copy-start | bytes 1540
  878.0 50.6 %collective-permute-start.10 = (bf16[8,64,512]{2,1,0:T(8,128)(2,1)}, bf16[8,64,512]{2,1,0:T(8,128)(2,1)}, u32[]{:S(2)}, u32[]{:S(2)}) collective-permute-start(bf16[8,64,512]{2,1,0:T(8,128)(2,1)} %get-tuple-element.202), channel_id=1, source_target_pairs={{0,2},{1,3},{2,0},{3,1},{4,6},{5,7},{6,4},{7,5},{8,10},{9,11},{10,... | collective-permute-start | bytes 1572872 | tf_op jit(solution)/shard_map/ppermute | solution.py:531
  878.0 50.6 %collective-permute-start.9 = (bf16[8,64,512]{2,1,0:T(8,128)(2,1)}, bf16[8,64,512]{2,1,0:T(8,128)(2,1)}, u32[]{:S(2)}, u32[]{:S(2)}) collective-permute-start(bf16[8,64,512]{2,1,0:T(8,128)(2,1)} %get-tuple-element.203), channel_id=1, source_target_pairs={{0,1},{1,2},{2,3},{3,0},{4,5},{5,6},{6,7},{7,4},{8,9},{9,10},{10,1... | collective-permute-start | bytes 1572872 | tf_op jit(solution)/shard_map/ppermute | solution.py:531
  882.6 80.0 %copy-start.24 = (bf16[1,128,2048]{2,1,0:T(8,128)(2,1)S(1)}, bf16[1,128,2048]{2,1,0:T(8,128)(2,1)}, u32[]{:S(2)}) copy-start(bf16[1,128,2048]{2,1,0:T(8,128)(2,1)} %param.31) | copy-start | bytes 1572868
  882.6 80.0 %copy-start.47 = (f32[128]{0:T(128)S(1)}, f32[128]{0:T(128)}, u32[]{:S(2)}) copy-start(f32[128]{0:T(128)} %copy-done.46) | copy-start | bytes 1540
  882.7 48.8 %collective-permute-start.14 = (bf16[8,64,128]{2,1,0:T(8,128)(2,1)S(1)}, bf16[8,64,128]{2,1,0:T(8,128)(2,1)S(1)}, u32[]{:S(2)}, u32[]{:S(2)}) collective-permute-start(bf16[8,64,128]{2,1,0:T(8,128)(2,1)S(1)} %get-tuple-element.212), channel_id=1, source_target_pairs={{0,3},{1,0},{2,1},{3,2},{4,7},{5,4},{6,5},{7,6},{8,11},{9,8},{10,9... | collective-permute-start | bytes 393224 | tf_op jit(solution)/shard_map/ppermute | solution.py:531
  885.6 48.6 %collective-permute-start.13 = (bf16[8,64,128]{2,1,0:T(8,128)(2,1)S(1)}, bf16[8,64,128]{2,1,0:T(8,128)(2,1)S(1)}, u32[]{:S(2)}, u32[]{:S(2)}) collective-permute-start(bf16[8,64,128]{2,1,0:T(8,128)(2,1)S(1)} %get-tuple-element.213), channel_id=1, source_target_pairs={{0,2},{1,3},{2,0},{3,1},{4,6},{5,7},{6,4},{7,5},{8,10},{9,11},{10,... | collective-permute-start | bytes 393224 | tf_op jit(solution)/shard_map/ppermute | solution.py:531
  889.3 44.9 %collective-permute-start.12 = (bf16[8,64,128]{2,1,0:T(8,128)(2,1)S(1)}, bf16[8,64,128]{2,1,0:T(8,128)(2,1)S(1)}, u32[]{:S(2)}, u32[]{:S(2)}) collective-permute-start(bf16[8,64,128]{2,1,0:T(8,128)(2,1)S(1)} %get-tuple-element.214), channel_id=1, source_target_pairs={{0,1},{1,2},{2,3},{3,0},{4,5},{5,6},{6,7},{7,4},{8,9},{9,10},{10,1... | collective-permute-start | bytes 393224 | tf_op jit(solution)/shard_map/ppermute | solution.py:531
  928.6 36.9 %collective-permute-start.17 = (bf16[128,2048]{1,0:T(8,128)(2,1)}, bf16[128,2048]{1,0:T(8,128)(2,1)}, u32[]{:S(2)}, u32[]{:S(2)}) collective-permute-start(bf16[128,2048]{1,0:T(8,128)(2,1)} %get-tuple-element.197), channel_id=1, source_target_pairs={{0,3},{1,0},{2,1},{3,2},{4,7},{5,4},{6,5},{7,6},{8,11},{9,8},{10,9... | collective-permute-start | bytes 1572872 | tf_op jit(solution)/shard_map/ppermute | solution.py:531
  928.6 50.0 %collective-permute-start.16 = (bf16[128,2048]{1,0:T(8,128)(2,1)}, bf16[128,2048]{1,0:T(8,128)(2,1)}, u32[]{:S(2)}, u32[]{:S(2)}) collective-permute-start(bf16[128,2048]{1,0:T(8,128)(2,1)} %get-tuple-element.198), channel_id=1, source_target_pairs={{0,2},{1,3},{2,0},{3,1},{4,6},{5,7},{6,4},{7,5},{8,10},{9,11},{10,... | collective-permute-start | bytes 1572872 | tf_op jit(solution)/shard_map/ppermute | solution.py:531
  931.5 47.1 %collective-permute-start.15 = (bf16[128,2048]{1,0:T(8,128)(2,1)}, bf16[128,2048]{1,0:T(8,128)(2,1)}, u32[]{:S(2)}, u32[]{:S(2)}) collective-permute-start(bf16[128,2048]{1,0:T(8,128)(2,1)} %get-tuple-element.199), channel_id=1, source_target_pairs={{0,1},{1,2},{2,3},{3,0},{4,5},{5,6},{6,7},{7,4},{8,9},{9,10},{10,1... | collective-permute-start | bytes 1572872 | tf_op jit(solution)/shard_map/ppermute | solution.py:531
  934.9 23.6 %all-to-all-start.11 = ((bf16[8,64,128]{2,1,0:T(8,128)(2,1)}), bf16[8,64,128]{2,1,0:T(8,128)(2,1)S(1)}, u32[]{:S(2)}, u32[]{:S(2)}) async-start(bf16[8,64,128]{2,1,0:T(8,128)(2,1)} %add_convert_fusion.2), calls=%async_computation.14 | async-start | bytes 262144 | tf_op jit(solution)/shard_map/all_to_all | solution.py:516
  958.5 20.1 %all-to-all-start.9 = ((bf16[8,64,512]{2,1,0:T(8,128)(2,1)}), bf16[8,64,512]{2,1,0:T(8,128)(2,1)}, u32[]{:S(2)}, u32[]{:S(2)}) async-start(bf16[8,64,512]{2,1,0:T(8,128)(2,1)} %add_convert_fusion.1), calls=%async_computation.12 | async-start | bytes 1048576 | tf_op jit(solution)/shard_map/all_to_all | solution.py:516
  979.7 20.7 %all-to-all-start.8 = ((f32[32,1,4352]{2,1,0:T(1,128)}), f32[32,1,4352]{2,1,0:T(1,128)}, u32[]{:S(2)}, u32[]{:S(2)}) async-start(f32[32,1,4352]{2,1,0:T(1,128)} %broadcast_in_dim.172), calls=%async_computation.11 | async-start | bytes 1114112 | tf_op jit(solution)/shard_map/all_to_all | solution.py:472
  985.6 17.4 %copy-start.1 = (bf16[1,768,2048]{2,1,0:T(8,128)(2,1)S(1)}, bf16[1,768,2048]{2,1,0:T(8,128)(2,1)}, u32[]{:S(2)}) copy-start(bf16[1,768,2048]{2,1,0:T(8,128)(2,1)} %param.30) | copy-start | bytes 9437188
  (36 other events, 187.6 us)
Sparse Core Ops, SparseCore 0:
  10.8 53.1 all-gather.3
  205.8 136.5 all-gather.5
  550.8 41.6 reduce-scatter.3
  644.9 41.1 reduce-scatter.7
  746.2 52.0 reduce-scatter.5
  800.1 35.8 all-gather.7

commit v7 on v6

--- a/solution.py
+++ b/solution.py
@@ -498,6 +498,7 @@
     devices = ctx_size * wt_size
     seq_len = tokens * ctx_size
     head_dim = gain_query.shape[0]
+    q_width = w_query.shape[1]
     kv_width = key_weight.shape[1]
     key_heads = kv_width // head_dim
     expert_count = w_router.shape[1]
@@ -656,14 +657,20 @@
     if not small_plane:
         cot_all = gather(after(out_grad[0], filled), by_stream)
     cot_all = cot_all.reshape(wt_size, seq_len, model_width)
-    mixed_columns = column_blocks(after(mixed_low, filled))
+    mixed_columns = column_blocks(mixed_low)
     gate_h = matmul(filled, expert_gate[0])
     up_h = matmul(filled, expert_up[0])
     sigma_h = jax.nn.sigmoid(gate_h)
     hidden_h = (gate_h * sigma_h * up_h).astype(jnp.bfloat16)
-    result_rows = matmul(hidden_h, expert_down[0]).astype(jnp.bfloat16)
+    result_rows = lax.optimization_barrier(
+        matmul(hidden_h, expert_down[0]).astype(jnp.bfloat16)
+    )
     cot_rows = pick_rows(cot_all)
     gate_rows = jnp.sum(jnp.where(place, gate_mine[:, None, :], 0.0), axis=2).reshape(-1)
+    mixed_rows = (gate_rows[:, None] * result_rows.astype(jnp.float32)).astype(jnp.bfloat16)
+    blocks_shape = (wt_size, capacity, -1)
+    half = model_width // 2
+    stream_mixed = turn(mixed_rows[:, :half].reshape(blocks_shape))
     gate_cot_rows = jnp.sum(
         result_rows.astype(jnp.float32) * cot_rows.astype(jnp.float32), axis=1
     ).reshape(wt_size, capacity)
@@ -674,8 +681,9 @@
         jnp.bfloat16
     )
     up_cot_h = (hidden_cot * gate_h * sigma_h).astype(jnp.bfloat16)
+    gate_part = contract_cols(gate_cot_h, expert_gate[0])
     in_rows_cot = (
-        contract_cols(gate_cot_h, expert_gate[0]) + contract_cols(up_cot_h, expert_up[0])
+        gate_part + contract_cols(up_cot_h, expert_up[0])
     ).astype(jnp.bfloat16)
 
     def add_pairs(table, stream_rows):
@@ -683,15 +691,8 @@
             table.reshape(wt_size * capacity, seq_len), jnp.concatenate(stream_rows, axis=0)
         ).astype(jnp.bfloat16)
 
-    mixed_rows = (gate_rows[:, None] * result_rows.astype(jnp.float32)).astype(jnp.bfloat16)
-    gate_cot = exchange(after(gate_cot_mine, mixed_columns).reshape(devices, tokens), by_stream)
-    in_rows_cot, gate_cot, mixed_columns = lax.optimization_barrier(
-        (in_rows_cot, gate_cot, mixed_columns)
-    )
-    gate_cot = from_owner_rows(gate_cot)
-    blocks_shape = (wt_size, capacity, -1)
-
-    half = model_width // 2
+    in_rows_cot, mixed_columns = lax.optimization_barrier((in_rows_cot, mixed_columns))
+
     stream_cots = turn(in_rows_cot[:, :half].reshape(blocks_shape))
     send_slot = jnp.where(
         send_ids[None, None, :] < block_hits[:, :, None],
@@ -712,14 +713,16 @@
     )
     plane_cots = exchange(plane_sent, "ctx")
     first_part = scatter_sum(add_pairs(spread_low, stream_cots), "ctx")
+    gate_cot = from_owner_rows(
+        exchange(after(gate_cot_mine, plane_cots).reshape(devices, tokens), by_stream)
+    )
     line_low = (rank_lines[:, :, :, None] == send_ids).astype(jnp.bfloat16)
     line_sent = jnp.einsum(
         "sctj,csjd->std", line_low, plane_cots, preferred_element_type=jnp.float32
     ).astype(jnp.bfloat16)
     line_cots = turn(line_sent)
-    mixed_rows = after(mixed_rows, line_sent).reshape(blocks_shape)
-    mixed_cuts = cut(mixed_rows)
-    stream_mixed = pass_on(mixed_cuts)
+    mixed_cuts = cut(after(mixed_rows[:, half:], line_sent).reshape(blocks_shape))
+    stream_mixed_late = pass_on(mixed_cuts)
     returned_cot = after(
         jnp.concatenate([first_part.astype(jnp.float32), add_up(line_cots)], axis=1), mixed_cuts
     )
@@ -756,11 +759,12 @@
     grad_gate = contract_rows(filled, gate_cot_h)
     grad_up = contract_rows(filled, up_cot_h)
     grad_down = contract_rows(hidden_h, out_rows_cot)
-    router_parts = exchange(contract_rows(normed_mid, logit_cot).reshape(devices, -1), both)
-    grad_w_router = jnp.sum(router_parts, axis=0).reshape(w_router.shape)
-    mixed_partial = add_pairs(after(spread_low, query_cot_low), stream_mixed)
+    grad_w_router = scatter_sum(contract_rows(normed_mid, logit_cot), both)
+    spread_late = after(spread_low, query_cot_low)
+    mixed_partial = jnp.concatenate(
+        [add_pairs(spread_late, part) for part in (stream_mixed, stream_mixed_late)], axis=1
+    )
     mixed_mine = scatter_sum(mixed_partial, "ctx").astype(jnp.float32)
-    hidden_out = after(resid_mid, query_cot_low) + mixed_mine
     out_block = contract_rows(after(mixed_columns, query_cot_low), attn_cot_all)
     out_parts = turn(out_block.astype(jnp.bfloat16).reshape(wt_size, -1, model_width))
     pair_mine = scatter_sum(pair_cots, "ctx").reshape(tokens, key_heads, 2, head_dim)
@@ -780,21 +784,11 @@
         block = block.reshape(ctx_size, wt_size, -1, width).transpose(1, 0, 2, 3)
         return turn(block), block
 
-    def weight_rows(parts):
-        rows = exchange(add_up(parts).astype(jnp.bfloat16), "ctx")
-        return rows.transpose(1, 0, 2).reshape(rows.shape[1], -1).astype(jnp.float32)
-
     query_parts, query_block = weight_parts(after(query_columns, (out_block, mixed_partial)))
     pair_parts, pair_block = weight_parts(column_blocks(after(pair_cot_low, query_block)))
     in_cot = contract_cols(after(query_cot_low, query_block), query_full) + contract_cols(
         pair_cot_low, side_weights[:, : 2 * kv_width]
     )
-    query_parts = after(query_parts, (pair_block, in_cot))
-    grad_w_query = weight_rows(query_parts)
-    grad_w_out = add_up(after(out_parts, query_parts))
-    grad_pair = weight_rows(after(pair_parts, query_parts))
-    grad_w_key = grad_pair[:, :kv_width]
-    grad_w_value = grad_pair[:, kv_width:]
     in_norm_cot, gain_attn_terms = norm_back(resid_in, gain_attn, in_cot)
     grad_in = resid_cot + in_norm_cot
     gain_sums = sum_everywhere(
@@ -807,6 +801,19 @@
             ]
         )
     )
+    query_parts = after(query_parts, (pair_block, gain_sums))
+    grad_w_out = add_up(after(out_parts, query_parts))
+    rows_mine = jnp.concatenate(
+        [add_up(query_parts), add_up(after(pair_parts, query_parts))], axis=2
+    ).astype(jnp.bfloat16)
+    hidden_out = after(resid_mid, rows_mine) + mixed_mine
+    grad_w_router = after(grad_w_router, rows_mine)
+    rows = exchange(rows_mine, "ctx").transpose(1, 0, 2).astype(jnp.float32)
+    query_columns = q_width // ctx_size
+    grad_w_query = rows[:, :, :query_columns].reshape(-1, q_width)
+    grad_pair = rows[:, :, query_columns:].reshape(-1, 2 * kv_width)
+    grad_w_key = grad_pair[:, :kv_width]
+    grad_w_value = grad_pair[:, kv_width:]
     grad_gain_attn = gain_sums[:model_width]
     grad_gain_query = gain_sums[model_width : model_width + head_dim]
     grad_gain_key = gain_sums[model_width + head_dim : model_width + 2 * head_dim]

time: 1020 us -> 1080 us (1.059)
  waiting for transfers between devices: 258 us -> 307 us
  blocking collectives: 0 us -> 18.5 us
    unnamed x6 -> x8, waiting for transfers between devices: 0.61 us -> 83.3 us
    ppermute x18 -> x21, waiting for transfers between devices: 188 us -> 112 us  [pass_on(): arrived.append(lax.ppermute(cuts[step], 'wt', pairs))]
    reduce_scatter x3, waiting for transfers between devices: 24.6 us -> 59.2 us  [scatter_sum(): return lax.psum_scatter(value, axes, scatter_dimension=0, tiled=True)]
    all_to_all x0 -> x1, blocking collectives: none -> 18.5 us  [exchange(): return lax.all_to_all(value, axes, split_axis=0, concat_axis=0, tiled=True)]
    all_to_all x12 -> x9, starting transfers between devices: 74.2 us -> 56.2 us  [exchange(): return lax.all_to_all(value, axes, split_axis=0, concat_axis=0, tiled=True)]
    dot_general x9, matrix products: 56.7 us -> 43.5 us  [contract_rows(): lax.dot_general(left_side, right_side, (((0,), (0,)), ((), ())), preferre...]
    all_to_all x1, waiting for transfers between devices: 8.92 us -> 20.8 us  [sum_everywhere(): lax.all_to_all(spread, ('ctx', 'wt'), split_axis=0, concat_axis=0, tiled=...]
    ppermute x18 -> x21, starting transfers between devices: 27.1 us -> 38.7 us  [pass_on(): arrived.append(lax.ppermute(cuts[step], 'wt', pairs))]
  transfers between devices with their start and end apart: 37 -> 38, of which waited for: 14 -> 12; matrix products, arithmetic and copies ran while one was open for 21% -> 22% of each run, Pallas kernels for 32% -> 30%
where the time goes in v7:
time: 1080 us; the launch traced here: 1060 us
  Pallas kernels  348 us (32%)
  waiting for transfers between devices  307 us (28%)
  matrix products  165 us (15%)
  starting transfers between devices  98.6 us (9%)
  other arithmetic  63.2 us (6%)
  local copies, waits for them, and re-layouts  46.1 us (4%)
  blocking collectives  18.5 us (2%)
  between operations  15.8 us (1%)
    pallas_call x2, Pallas kernels, spread(): pl.pallas_call(functools.partial(spread_kernel, splits, streams_first), o...  302 us
    ppermute x21, waiting for transfers between devices, pass_on(): arrived.append(lax.ppermute(cuts[step], 'wt', pairs))  112 us
    unnamed x8, waiting for transfers between devices  83.3 us
    reduce_scatter x3, waiting for transfers between devices, scatter_sum(): return lax.psum_scatter(value, axes, scatter_dimension=0, tiled=True)  59.2 us
    all_to_all x9, starting transfers between devices, exchange(): return lax.all_to_all(value, axes, split_axis=0, concat_axis=0, tiled=True)  56.2 us
    dot_general x7, matrix products, contract_cols(): lax.dot_general(left_side, right_side, (((1,), (1,)), ((), ())), preferre...  45.8 us
    dot_general x7, matrix products, matmul(): return jnp.dot(left_side, right_side, preferred_element_type=jnp.float32)  44.4 us
    dot_general x9, matrix products, contract_rows(): lax.dot_general(left_side, right_side, (((0,), (0,)), ((), ())), preferre...  43.5 us
  transfers between devices with their start and end apart: 38, of which 12 were waited for; matrix products, arithmetic and copies ran while one was open for 22% of the time, Pallas kernels for 30%

profile of v7, /device:TPU:0, one launch (start us, length us, event | category | flops | bytes accessed | tf_op | source)
XLA Modules:
  0.0 1062.6 jit_solution(11122181403572853328)
XLA Ops:
  13.1 192.6 %shard_map.263 = (bf16[8,4,64,1152]{3,2,1,0:T(8,128)(2,1)}, bf16[8,4,64,4096]{3,2,1,0:T(8,128)(2,1)}, bf16[8,4,128,2048]{3,2,1,0:T(8,128)(2,1)}) custom-call(bf16[64,1152]{1,0:T(8,128)(2,1)} %fusion.95.refs_0_, bf16[64,4096]{1,0:T(8,128)(2,1)} %refs_1_.1, bf16[128,2048]{1,0:T(8,128)(2,1)} %refs_2_.1), custom_call_target="tpu_custom_call" | custom-call | bytes 76546048 | tf_op jit(solution)/shard_map/pallas_call | solution.py:198
  207.2 3.3 all-to-all-start
  212.3 3.0 fusion.88
  216.9 9.8 fusion.78.query_ref
  230.5 3.9 all-to-all-start.1
  238.7 3.1 all-to-all-done.1
  241.8 4.1 all-to-all-start.3
  252.1 10.2 fusion.10.key_ref.value_ref
  262.5 16.4 %attend.1 = (bf16[128,4096]{1,0:T(8,128)(2,1)S(1)}, bf16[128,4096]{1,0:T(8,128)(2,1)S(1)}) custom-call(f32[128,4096]{1,0:T(8,128)S(1)} %copy-done.2, f32[1024,1024]{1,0:T(8,128)} %fusion.10.key_ref.value_ref, f32[1024,1024]{1,0:T(8,128)} %fusion.10.key_ref.value_ref, f32[1,128]{1,0:T(1,128)S(1)} %bitcast.362, f32[128,128]{1,0:T(8,128)S(1)} %get-tuple-element.164.cosine_ref, ...), custom_call_target="tpu_custom_call" | custom-call | flops 2147483648 | bytes 4194304 | tf_op jit(solution)/shard_map/attend/pallas_call | solution.py:365
  278.9 9.2 multiply_reduce_fusion.2
  290.1 109.8 %shard_map.264 = bf16[4,8,128,2048]{3,2,1,0:T(8,128)(2,1)} custom-call(bf16[128,2048]{1,0:T(8,128)(2,1)} %multiply_convert_fusion.3.refs_0_), custom_call_target="tpu_custom_call" | custom-call | bytes 33554432 | tf_op jit(solution)/shard_map/pallas_call | solution.py:198
  402.2 12.2 %all-to-all-start.2 = ((f32[32,1,128]{2,1,0:T(1,128)}), f32[32,1,128]{2,1,0:T(1,128)S(1)}, u32[]{:S(2)}, u32[]{:S(2)}) async-start(f32[32,1,128]{2,1,0:T(1,128)} %bitcast.29), calls=%async_computation.2 | async-start | bytes 32768 | tf_op jit(solution)/shard_map/all_to_all | solution.py:517
  414.5 11.1 %convolution_convert_fusion.1 = bf16[4,256,2048]{2,1,0:T(8,128)(2,1)S(1)} fusion(bf16[4,256,1024]{2,1,0:T(8,128)(2,1)} %fusion.6, bf16[4,1024,2048]{2,1,0:T(8,128)(2,1)} %bitcast.369), kind=kOutput, calls=%fused_computation.25 | convolution fusion | flops 4297064448 | bytes 23068672 | tf_op jit(solution)/shard_map/wkt,wtd->wkd/dot_general | solution.py:651
  425.6 3.4 fusion.14
  429.0 5.3 multiply_convert_fusion
  434.3 4.9 convolution_convert_fusion.3
  440.3 4.4 all-to-all-start.4
  446.0 14.2 %fusion.1 = (f32[1024]{0:T(1024)S(1)}, bf16[4,256,2048]{2,1,0:T(8,128)(2,1)}) fusion(bf16[1024,2048]{1,0:T(8,128)(2,1)} %convolution_convert_fusion.3, bf16[4,256,1024]{2,1,0:T(8,128)(2,1)} %fusion.6, bf16[4,1024,2048]{2,1,0:T(8,128)(2,1)} %bitcast.368), kind=kOutput, calls=%fused_computation.4 | convolution fusion | flops 4305452032 | bytes 27267072 | tf_op jit(solution)/shard_map/wkt,wtd->wkd/dot_general | solution.py:651
  461.5 3.1 fusion.2
  465.6 4.4 multiply_convert_fusion.1
  470.0 3.4 fusion.12
  473.5 5.2 add_convert_fusion
  478.8 4.0 fusion.112
  484.3 2.5 copy.276
  486.8 4.7 all-to-all-start.5
  496.4 2.4 collective-permute-start.1
  501.4 10.1 collective-permute-done
  511.5 22.1 %collective-permute-done.1 = bf16[256,1024]{1,0:T(8,128)(2,1)S(1)} collective-permute-done((bf16[256,1024]{1,0:T(8,128)(2,1)}, bf16[256,1024]{1,0:T(8,128)(2,1)S(1)}, u32[]{:S(2)}, u32[]{:S(2)}) %collective-permute-start.1) | collective-permute-done | bytes 524320 | tf_op jit(solution)/shard_map/ppermute | solution.py:532
  533.6 4.8 fusion.49
  539.9 6.3 fusion.3
  548.6 15.2 %all-to-all-start.6 = ((f32[32,1,128]{2,1,0:T(1,128)}), f32[32,1,128]{2,1,0:T(1,128)S(1)}, u32[]{:S(2)}, u32[]{:S(2)}) async-start(f32[32,1,128]{2,1,0:T(1,128)} %all_to_all.51), calls=%async_computation.7 | async-start | bytes 32768 | tf_op jit(solution)/shard_map/all_to_all | solution.py:517
  563.8 3.0 bitcast_convert_fusion
  570.4 2.4 collective-permute-start.4
  574.6 15.6 %reduce-scatter.7.cloned.1.call-done = bf16[128,1024]{1,0:T(8,128)(2,1)} async-done(((bf16[1024,1024]{1,0:T(8,128)(2,1)}), bf16[128,1024]{1,0:T(8,128)(2,1)}) %reduce-scatter.7.cloned.1.call-update) | async-done | bytes 262160 | tf_op jit(solution)/shard_map/reduce_scatter | solution.py:520
  594.7 12.6 %convolution_convert_fusion.cot_ref = bf16[128,4096]{1,0:T(8,128)(2,1)} fusion(bf16[128,2048]{1,0:T(8,128)(2,1)S(1)} %fusion.108, bf16[4096,2048]{1,0:T(8,128)(2,1)} %bitcast.364), kind=kOutput, calls=%fused_computation.10 | convolution fusion | flops 2148007936 | bytes 18350080 | tf_op jit(solution)/shard_map/dot_general | solution.py:61
  608.1 29.5 %attend_back.1 = (bf16[128,4096]{1,0:T(8,128)(2,1)}, bf16[1024,1024]{1,0:T(8,128)(2,1)}, f32[32,128]{1,0:T(8,128)}) custom-call(f32[128,4096]{1,0:T(8,128)} %fusion.78.query_ref, bf16[128,4096]{1,0:T(8,128)(2,1)} %copy-done.15, bf16[128,4096]{1,0:T(8,128)(2,1)} %convolution_convert_fusion.cot_ref, f32[1024,1024]{1,0:T(8,128)} %fusion.10.key_ref.value_ref, ...), custom_call_target="tpu_custom_call" | custom-call | flops 5368709120 | bytes 6291456 | tf_op jit(solution)/shard_map/attend_back/pallas_call | solution.py:413
  639.0 18.5 %all_to_all.68 = bf16[8,128,512]{2,1,0:T(8,128)(2,1)} all-to-all(bf16[8,128,512]{2,1,0:T(8,128)(2,1)S(1)} %bitcast.378), channel_id=1, replica_groups=mesh['ctx'=8,'wt'=4] {'ctx'}, dimensions={0} | all-to-all | bytes 2097152 | tf_op jit(solution)/shard_map/all_to_all | solution.py:517
  664.4 2.9 dynamic-slice_bitcast_fusion.11
  667.3 5.6 collective-permute-start.6
  675.9 2.9 collective-permute-start.11
  679.4 9.0 convolution_bitcast_fusion.1
  688.4 5.5 convolution_bitcast_fusion.2
  693.9 5.4 convolution_bitcast_fusion
  699.5 12.3 %collective-permute-done.7 = bf16[256,1024]{1,0:T(8,128)(2,1)} collective-permute-done((bf16[256,1024]{1,0:T(8,128)(2,1)}, bf16[256,1024]{1,0:T(8,128)(2,1)}, u32[]{:S(2)}, u32[]{:S(2)}) %collective-permute-start.7) | collective-permute-done | bytes 524320 | tf_op jit(solution)/shard_map/ppermute | solution.py:532
  711.9 3.8 fusion.55
  715.7 43.4 %collective-permute-done.10 = bf16[256,1024]{1,0:T(8,128)(2,1)} collective-permute-done((bf16[256,1024]{1,0:T(8,128)(2,1)}, bf16[256,1024]{1,0:T(8,128)(2,1)}, u32[]{:S(2)}, u32[]{:S(2)}) %collective-permute-start.10) | collective-permute-done | bytes 524320 | tf_op jit(solution)/shard_map/ppermute | solution.py:532
  759.1 3.7 fusion.52
  762.8 2.4 pad_maximum_fusion
  765.2 82.2 %reduce-scatter.13.cloned.1.call-done = f32[64,32]{1,0:T(8,128)} async-done(((f32[2048,32]{1,0:T(8,128)}), f32[64,32]{1,0:T(8,128)}) %reduce-scatter.13.cloned.1.call-update) | async-done | bytes 8208
  848.8 43.6 %reduce-scatter.9.cloned.1.call-done = bf16[128,1024]{1,0:T(8,128)(2,1)} async-done(((bf16[1024,1024]{1,0:T(8,128)(2,1)}), bf16[128,1024]{1,0:T(8,128)(2,1)}) %reduce-scatter.9.cloned.1.call-update) | async-done | bytes 262160 | tf_op jit(solution)/shard_map/reduce_scatter | solution.py:520
  901.9 28.8 %all-gather.8.cloned.1.call-done = bf16[1024,2048]{1,0:T(8,128)(2,1)} async-done(((bf16[128,2048]{1,0:T(8,128)(2,1)}), bf16[1024,2048]{1,0:T(8,128)(2,1)}) %all-gather.8.cloned.1.call-update) | async-done | bytes 4194320 | tf_op jit(solution)/shard_map/all_gather | solution.py:514
  930.8 6.4 fusion.117
  937.2 2.4 convolution_convert_fusion.4
  947.3 4.1 all-to-all-start.9
  951.4 13.5 %fusion.118 = f32[128,2048]{1,0:T(8,128)} fusion(bf16[128,4096]{1,0:T(8,128)(2,1)} %get-tuple-element.67, bf16[2048,4096]{1,0:T(8,128)(2,1)} %bitcast.366), kind=kOutput, calls=%fused_computation.257 | convolution fusion | flops 2147483648 | bytes 18874368 | tf_op jit(solution)/shard_map/dot_general | solution.py:61
  965.0 5.2 fusion.68
  971.3 3.3 all-to-all-start.8
  974.7 2.9 fusion.72
  977.6 2.4 convolution_convert_fusion.6
  982.4 2.5 collective-permute-start.16
  987.7 20.8 %all-to-all-done.8 = f32[32,1,4352]{2,1,0:T(1,128)} async-done(((f32[32,1,4352]{2,1,0:T(1,128)}), f32[32,1,4352]{2,1,0:T(1,128)}, u32[]{:S(2)}, u32[]{:S(2)}) %all-to-all-start.8) | async-done | bytes 557088 | tf_op jit(solution)/shard_map/all_to_all | solution.py:472
  1017.7 4.2 all-to-all-start.10
  1027.0 22.3 %collective-permute-done.19 = bf16[128,2048]{1,0:T(8,128)(2,1)} collective-permute-done((bf16[128,2048]{1,0:T(8,128)(2,1)}, bf16[128,2048]{1,0:T(8,128)(2,1)}, u32[]{:S(2)}, u32[]{:S(2)}) %collective-permute-start.19) | collective-permute-done | bytes 524320 | tf_op jit(solution)/shard_map/ppermute | solution.py:532
  1049.2 3.0 convert_add_fusion
  (335 shorter events, 111.6 us)
Async XLA Ops:
  7.2 427.1 %copy-start = (bf16[1,768,2048]{2,1,0:T(8,128)(2,1)S(1)}, bf16[1,768,2048]{2,1,0:T(8,128)(2,1)}, u32[]{:S(2)}) copy-start(bf16[1,768,2048]{2,1,0:T(8,128)(2,1)} %param.30) | copy-start | bytes 9437188
  7.2 209.7 %copy-start.37 = (f32[2048]{0:T(1024)S(1)}, f32[2048]{0:T(1024)}, u32[]{:S(2)}) copy-start(f32[2048]{0:T(1024)} %param.19) | copy-start | bytes 24580
  7.2 203.3 %copy-start.60 = (s32[1,2]{1,0:T(1,128)S(1)}, s32[1,2]{1,0:T(1,128)}, u32[]{:S(2)}) copy-start(s32[1,2]{1,0:T(1,128)} %param.17) | copy-start | bytes 28
  7.2 244.8 %all-gather.4.cloned.1.call-start = ((), (), s32[]{:S(2)}) async-start(), calls=%async_computation.15 | async-start | bytes 4718592 | tf_op jit(solution)/shard_map/all_gather | solution.py:514
  8.7 218.1 %copy-start.44 = (f32[128]{0:T(128)}, f32[128]{0:T(128)S(1)}, u32[]{:S(2)}) copy-start(f32[128]{0:T(128)S(1)} %add_rsqrt_fusion.2) | copy-start | bytes 1540
  10.7 435.3 %all-gather.6.cloned.1.call-start = ((), (), s32[]{:S(2)}) async-start(), calls=%async_computation.16 | async-start | bytes 17301504 | tf_op jit(solution)/shard_map/all_gather | solution.py:514
  207.2 23.3 %all-to-all-start = ((s32[8,5,128]{2,1,0:T(8,128)}), s32[8,5,128]{2,1,0:T(8,128)S(1)}, u32[]{:S(2)}, u32[]{:S(2)}) async-start(s32[8,5,128]{2,1,0:T(8,128)} %pad_add_fusion), calls=%async_computation | async-start | bytes 65536 | tf_op jit(solution)/shard_map/all_to_all | solution.py:517
  216.9 45.5 %copy-start.9 = (f32[128,128]{1,0:T(8,128)}, f32[128,128]{1,0:T(8,128)S(1)}, u32[]{:S(2)}) copy-start(f32[128,128]{1,0:T(8,128)S(1)} %get-tuple-element.164.cosine_ref) | copy-start | bytes 196612
  216.9 45.5 %copy-start.11 = (f32[128,128]{1,0:T(8,128)}, f32[128,128]{1,0:T(8,128)S(1)}, u32[]{:S(2)}) copy-start(f32[128,128]{1,0:T(8,128)S(1)} %get-tuple-element.163.sine_ref) | copy-start | bytes 196612
  230.5 31.9 %copy-start.40 = (s32[8,5,128]{2,1,0:T(8,128)}, s32[8,5,128]{2,1,0:T(8,128)S(1)}, u32[]{:S(2)}) copy-start(s32[8,5,128]{2,1,0:T(8,128)S(1)} %all-to-all-done) | copy-start | bytes 61444
  230.5 11.3 %all-to-all-start.1 = ((s32[32,1,128]{2,1,0:T(1,128)}), s32[32,1,128]{2,1,0:T(1,128)S(1)}, u32[]{:S(2)}, u32[]{:S(2)}) async-start(s32[32,1,128]{2,1,0:T(1,128)} %bitcast.409), calls=%async_computation.1 | async-start | bytes 32768 | tf_op jit(solution)/shard_map/all_to_all | solution.py:517
  241.8 10.2 all-to-all-start.3
  262.4 16.4 %copy-start.19 = (bf16[1,128,2048]{2,1,0:T(8,128)(2,1)S(1)}, bf16[1,128,2048]{2,1,0:T(8,128)(2,1)}, u32[]{:S(2)}) copy-start(bf16[1,128,2048]{2,1,0:T(8,128)(2,1)} %param.16) | copy-start | bytes 1572868
  288.1 306.2 %copy-start.46 = (f32[128]{0:T(128)}, f32[128]{0:T(128)S(1)}, u32[]{:S(2)}) copy-start(f32[128]{0:T(128)S(1)} %add_rsqrt_fusion.1) | copy-start | bytes 1540
  290.1 111.5 %copy-start.42 = (s32[128,32]{0,1:T(8,128)S(1)}, s32[128,32]{0,1:T(8,128)}, u32[]{:S(2)}) copy-start(s32[128,32]{0,1:T(8,128)} %copy.197) | copy-start | bytes 49156
  290.1 111.5 %copy-start.49 = (s32[32]{0:T(128)S(1)}, s32[32]{0:T(128)}, u32[]{:S(2)}) copy-start(s32[32]{0:T(128)} %copy-done.48) | copy-start | bytes 388
  402.2 38.1 %all-to-all-start.2 = ((f32[32,1,128]{2,1,0:T(1,128)}), f32[32,1,128]{2,1,0:T(1,128)S(1)}, u32[]{:S(2)}, u32[]{:S(2)}) async-start(f32[32,1,128]{2,1,0:T(1,128)} %bitcast.29), calls=%async_computation.2 | async-start | bytes 32768 | tf_op jit(solution)/shard_map/all_to_all | solution.py:517
  440.3 38.4 %all-to-all-start.4 = ((bf16[8,128,512]{2,1,0:T(8,128)(2,1)}), bf16[8,128,512]{2,1,0:T(8,128)(2,1)}, u32[]{:S(2)}, u32[]{:S(2)}) async-start(bf16[8,128,512]{2,1,0:T(8,128)(2,1)} %bitcast.377), calls=%async_computation.4 | async-start | bytes 2097152 | tf_op jit(solution)/shard_map/all_to_all | solution.py:517
  486.8 61.2 %all-to-all-start.5 = ((bf16[8,4,64,1024]{3,2,1,0:T(8,128)(2,1)}), bf16[8,4,64,1024]{3,2,1,0:T(8,128)(2,1)}, u32[]{:S(2)}, u32[]{:S(2)}) async-start(bf16[8,4,64,1024]{3,2,1,0:T(8,128)(2,1)} %bitcast.370), calls=%async_computation.6 | async-start | bytes 8388608 | tf_op jit(solution)/shard_map/all_to_all | solution.py:517
  491.5 98.7 %reduce-scatter.7.cloned.1.call-start = ((), (), s32[]{:S(2)}) async-start(), calls=%async_computation.17 | async-start | bytes 2359296 | tf_op jit(solution)/shard_map/reduce_scatter | solution.py:520
  494.6 16.9 %collective-permute-start = (bf16[256,1024]{1,0:T(8,128)(2,1)}, bf16[256,1024]{1,0:T(8,128)(2,1)S(1)}, u32[]{:S(2)}, u32[]{:S(2)}) collective-permute-start(bf16[256,1024]{1,0:T(8,128)(2,1)} %get-tuple-element.128), channel_id=1, source_target_pairs={{0,1},{1,2},{2,3},{3,0},{4,5},{5,6},{6,7},{7,4},{8,9},{9,10},{10,1... | collective-permute-start | bytes 1572872 | tf_op jit(solution)/shard_map/ppermute | solution.py:532
  496.4 37.1 %collective-permute-start.1 = (bf16[256,1024]{1,0:T(8,128)(2,1)}, bf16[256,1024]{1,0:T(8,128)(2,1)S(1)}, u32[]{:S(2)}, u32[]{:S(2)}) collective-permute-start(bf16[256,1024]{1,0:T(8,128)(2,1)} %get-tuple-element.127), channel_id=1, source_target_pairs={{0,2},{1,3},{2,0},{3,1},{4,6},{5,7},{6,4},{7,5},{8,10},{9,11},{10,... | collective-permute-start | bytes 1572872 | tf_op jit(solution)/shard_map/ppermute | solution.py:532
  498.9 34.7 %collective-permute-start.2 = (bf16[256,1024]{1,0:T(8,128)(2,1)S(1)}, bf16[256,1024]{1,0:T(8,128)(2,1)}, u32[]{:S(2)}, u32[]{:S(2)}) collective-permute-start(bf16[256,1024]{1,0:T(8,128)(2,1)S(1)} %get-tuple-element.126), channel_id=1, source_target_pairs={{0,3},{1,0},{2,1},{3,2},{4,7},{5,4},{6,5},{7,6},{8,11},{9,8},{10,9... | collective-permute-start | bytes 1572872 | tf_op jit(solution)/shard_map/ppermute | solution.py:532
  548.6 42.6 %all-to-all-start.6 = ((f32[32,1,128]{2,1,0:T(1,128)}), f32[32,1,128]{2,1,0:T(1,128)S(1)}, u32[]{:S(2)}, u32[]{:S(2)}) async-start(f32[32,1,128]{2,1,0:T(1,128)} %all_to_all.51), calls=%async_computation.7 | async-start | bytes 32768 | tf_op jit(solution)/shard_map/all_to_all | solution.py:517
  563.8 283.6 %reduce-scatter.13.cloned.1.call-start = ((), (), s32[]{:S(2)}) async-start(), calls=%async_computation.21 | async-start | bytes 1081344
  566.8 25.9 %copy-start.17 = (f32[128,2048]{1,0:T(8,128)S(1)}, f32[128,2048]{1,0:T(8,128)}, u32[]{:S(2)}) copy-start(f32[128,2048]{1,0:T(8,128)} %copy-done.16) | copy-start | bytes 3145732
  568.6 25.8 %copy-start.23 = (bf16[1,128,2048]{2,1,0:T(8,128)(2,1)S(1)}, bf16[1,128,2048]{2,1,0:T(8,128)(2,1)}, u32[]{:S(2)}) copy-start(bf16[1,128,2048]{2,1,0:T(8,128)(2,1)} %param.31) | copy-start | bytes 1572868
  568.6 22.8 %collective-permute-start.3 = (bf16[128,1024]{1,0:T(8,128)(2,1)S(1)}, bf16[128,1024]{1,0:T(8,128)(2,1)S(1)}, u32[]{:S(2)}, u32[]{:S(2)}) collective-permute-start(bf16[128,1024]{1,0:T(8,128)(2,1)S(1)} %get-tuple-element.129), channel_id=1, source_target_pairs={{0,1},{1,2},{2,3},{3,0},{4,5},{5,6},{6,7},{7,4},{8,9},{9,10},{10,1... | collective-permute-start | bytes 786440 | tf_op jit(solution)/shard_map/ppermute | solution.py:532
  570.4 20.9 %collective-permute-start.4 = (bf16[128,1024]{1,0:T(8,128)(2,1)S(1)}, bf16[128,1024]{1,0:T(8,128)(2,1)}, u32[]{:S(2)}, u32[]{:S(2)}) collective-permute-start(bf16[128,1024]{1,0:T(8,128)(2,1)S(1)} %get-tuple-element.131), channel_id=1, source_target_pairs={{0,2},{1,3},{2,0},{3,1},{4,6},{5,7},{6,4},{7,5},{8,10},{9,11},{10,... | collective-permute-start | bytes 786440 | tf_op jit(solution)/shard_map/ppermute | solution.py:532
  572.8 18.5 %collective-permute-start.5 = (bf16[128,1024]{1,0:T(8,128)(2,1)S(1)}, bf16[128,1024]{1,0:T(8,128)(2,1)}, u32[]{:S(2)}, u32[]{:S(2)}) collective-permute-start(bf16[128,1024]{1,0:T(8,128)(2,1)S(1)} %get-tuple-element.130), channel_id=1, source_target_pairs={{0,3},{1,0},{2,1},{3,2},{4,7},{5,4},{6,5},{7,6},{8,11},{9,8},{10,9... | collective-permute-start | bytes 786440 | tf_op jit(solution)/shard_map/ppermute | solution.py:532
  594.3 12.9 %copy-start.50 = (f32[128]{0:T(128)}, f32[128]{0:T(128)S(1)}, u32[]{:S(2)}) copy-start(f32[128]{0:T(128)S(1)} %broadcast_multiply_fusion.3) | copy-start | bytes 1540
  594.7 12.6 %copy-start.25 = (bf16[128,2048]{1,0:T(8,128)(2,1)}, bf16[128,2048]{1,0:T(8,128)(2,1)S(1)}, u32[]{:S(2)}) copy-start(bf16[128,2048]{1,0:T(8,128)(2,1)S(1)} %fusion.108) | copy-start | bytes 1572868
  637.5 19.9 %copy-start.21 = (bf16[128,2048]{1,0:T(8,128)(2,1)S(1)}, bf16[128,2048]{1,0:T(8,128)(2,1)}, u32[]{:S(2)}) copy-start(bf16[128,2048]{1,0:T(8,128)(2,1)} %multiply_convert_fusion.3.refs_0_) | copy-start | bytes 1572868
  638.9 22.1 %copy-start.13 = (f32[128]{0:T(128)S(1)}, f32[128]{0:T(128)}, u32[]{:S(2)}) copy-start(f32[128]{0:T(128)} %param.24) | copy-start | bytes 1540
  658.8 233.7 %reduce-scatter.9.cloned.1.call-start = ((), (), s32[]{:S(2)}) async-start(), calls=%async_computation.19 | async-start | bytes 2359296 | tf_op jit(solution)/shard_map/reduce_scatter | solution.py:520
  659.4 19.5 %copy-start.43 = (f32[32,128]{1,0:T(8,128)S(1)}, f32[32,128]{1,0:T(8,128)}, u32[]{:S(2)}) copy-start(f32[32,128]{1,0:T(8,128)} %get-tuple-element.69) | copy-start | bytes 49156
  659.4 271.4 %all-gather.8.cloned.1.call-start = ((), (), s32[]{:S(2)}) async-start(), calls=%async_computation.18 | async-start | bytes 4718592 | tf_op jit(solution)/shard_map/all_gather | solution.py:514
  659.9 362.0 %reduce-scatter.11.cloned.1.call-start = ((), (), s32[]{:S(2)}) async-start(), calls=%async_computation.20 | async-start | bytes 4718592 | tf_op jit(solution)/shard_map/reduce_scatter | solution.py:520
  667.3 32.0 %collective-permute-start.6 = (bf16[256,1024]{1,0:T(8,128)(2,1)}, bf16[256,1024]{1,0:T(8,128)(2,1)}, u32[]{:S(2)}, u32[]{:S(2)}) collective-permute-start(bf16[256,1024]{1,0:T(8,128)(2,1)} %get-tuple-element.120), channel_id=1, source_target_pairs={{0,1},{1,2},{2,3},{3,0},{4,5},{5,6},{6,7},{7,4},{8,9},{9,10},{10,1... | collective-permute-start | bytes 1572872 | tf_op jit(solution)/shard_map/ppermute | solution.py:532
  673.0 38.9 %collective-permute-start.7 = (bf16[256,1024]{1,0:T(8,128)(2,1)}, bf16[256,1024]{1,0:T(8,128)(2,1)}, u32[]{:S(2)}, u32[]{:S(2)}) collective-permute-start(bf16[256,1024]{1,0:T(8,128)(2,1)} %get-tuple-element.119), channel_id=1, source_target_pairs={{0,2},{1,3},{2,0},{3,1},{4,6},{5,7},{6,4},{7,5},{8,10},{9,11},{10,... | collective-permute-start | bytes 1572872 | tf_op jit(solution)/shard_map/ppermute | solution.py:532
  674.4 37.4 %collective-permute-start.8 = (bf16[256,1024]{1,0:T(8,128)(2,1)}, bf16[256,1024]{1,0:T(8,128)(2,1)}, u32[]{:S(2)}, u32[]{:S(2)}) collective-permute-start(bf16[256,1024]{1,0:T(8,128)(2,1)} %get-tuple-element.118), channel_id=1, source_target_pairs={{0,3},{1,0},{2,1},{3,2},{4,7},{5,4},{6,5},{7,6},{8,11},{9,8},{10,9... | collective-permute-start | bytes 1572872 | tf_op jit(solution)/shard_map/ppermute | solution.py:532
  675.3 83.8 %collective-permute-start.10 = (bf16[256,1024]{1,0:T(8,128)(2,1)}, bf16[256,1024]{1,0:T(8,128)(2,1)}, u32[]{:S(2)}, u32[]{:S(2)}) collective-permute-start(bf16[256,1024]{1,0:T(8,128)(2,1)} %get-tuple-element.122), channel_id=1, source_target_pairs={{0,2},{1,3},{2,0},{3,1},{4,6},{5,7},{6,4},{7,5},{8,10},{9,11},{10,... | collective-permute-start | bytes 1572872 | tf_op jit(solution)/shard_map/ppermute | solution.py:532
  675.9 83.2 %collective-permute-start.11 = (bf16[256,1024]{1,0:T(8,128)(2,1)}, bf16[256,1024]{1,0:T(8,128)(2,1)}, u32[]{:S(2)}, u32[]{:S(2)}) collective-permute-start(bf16[256,1024]{1,0:T(8,128)(2,1)} %get-tuple-element.121), channel_id=1, source_target_pairs={{0,3},{1,0},{2,1},{3,2},{4,7},{5,4},{6,5},{7,6},{8,11},{9,8},{10,9... | collective-permute-start | bytes 1572872 | tf_op jit(solution)/shard_map/ppermute | solution.py:532
  693.9 17.9 %copy-start.26 = (bf16[4,256,1024]{2,1,0:T(8,128)(2,1)S(1)}, bf16[4,256,1024]{2,1,0:T(8,128)(2,1)}, u32[]{:S(2)}) copy-start(bf16[4,256,1024]{2,1,0:T(8,128)(2,1)} %fusion.7) | copy-start | bytes 6291460
  693.9 17.9 %copy-start.36 = (bf16[256,1024]{1,0:T(8,128)(2,1)S(1)}, bf16[256,1024]{1,0:T(8,128)(2,1)}, u32[]{:S(2)}) copy-start(bf16[256,1024]{1,0:T(8,128)(2,1)} %get-tuple-element.117) | copy-start | bytes 1572868
  699.3 59.8 %collective-permute-start.9 = (bf16[256,1024]{1,0:T(8,128)(2,1)S(1)}, bf16[256,1024]{1,0:T(8,128)(2,1)S(1)}, u32[]{:S(2)}, u32[]{:S(2)}) collective-permute-start(bf16[256,1024]{1,0:T(8,128)(2,1)S(1)} %copy-done.35), channel_id=1, source_target_pairs={{0,1},{1,2},{2,3},{3,0},{4,5},{5,6},{6,7},{7,4},{8,9},{9,10},{10,1... | collective-permute-start | bytes 1572872 | tf_op jit(solution)/shard_map/ppermute | solution.py:532
  711.9 47.3 %copy-start.34 = (bf16[256,1024]{1,0:T(8,128)(2,1)S(1)}, bf16[256,1024]{1,0:T(8,128)(2,1)}, u32[]{:S(2)}) copy-start(bf16[256,1024]{1,0:T(8,128)(2,1)} %get-tuple-element.124) | copy-start | bytes 1572868
  765.2 133.0 %copy-start.10 = (f32[128,128]{1,0:T(8,128)S(1)}, f32[128,128]{1,0:T(8,128)}, u32[]{:S(2)}) copy-start(f32[128,128]{1,0:T(8,128)} %copy-done.9) | copy-start | bytes 196612
  941.0 43.9 %collective-permute-start.12 = (bf16[8,64,512]{2,1,0:T(8,128)(2,1)}, bf16[8,64,512]{2,1,0:T(8,128)(2,1)}, u32[]{:S(2)}, u32[]{:S(2)}) collective-permute-start(bf16[8,64,512]{2,1,0:T(8,128)(2,1)} %get-tuple-element.115), channel_id=1, source_target_pairs={{0,1},{1,2},{2,3},{3,0},{4,5},{5,6},{6,7},{7,4},{8,9},{9,10},{10,1... | collective-permute-start | bytes 1572872 | tf_op jit(solution)/shard_map/ppermute | solution.py:532
  942.7 67.1 %collective-permute-start.13 = (bf16[8,64,512]{2,1,0:T(8,128)(2,1)}, bf16[8,64,512]{2,1,0:T(8,128)(2,1)}, u32[]{:S(2)}, u32[]{:S(2)}) collective-permute-start(bf16[8,64,512]{2,1,0:T(8,128)(2,1)} %get-tuple-element.114), channel_id=1, source_target_pairs={{0,2},{1,3},{2,0},{3,1},{4,6},{5,7},{6,4},{7,5},{8,10},{9,11},{10,... | collective-permute-start | bytes 1572872 | tf_op jit(solution)/shard_map/ppermute | solution.py:532
  945.1 66.4 %collective-permute-start.14 = (bf16[8,64,512]{2,1,0:T(8,128)(2,1)}, bf16[8,64,512]{2,1,0:T(8,128)(2,1)}, u32[]{:S(2)}, u32[]{:S(2)}) collective-permute-start(bf16[8,64,512]{2,1,0:T(8,128)(2,1)} %get-tuple-element.113), channel_id=1, source_target_pairs={{0,3},{1,0},{2,1},{3,2},{4,7},{5,4},{6,5},{7,6},{8,11},{9,8},{10,9... | collective-permute-start | bytes 1572872 | tf_op jit(solution)/shard_map/ppermute | solution.py:532
  947.3 22.9 %all-to-all-start.9 = ((bf16[8,128,128]{2,1,0:T(8,128)(2,1)}), bf16[8,128,128]{2,1,0:T(8,128)(2,1)}, u32[]{:S(2)}, u32[]{:S(2)}) async-start(bf16[8,128,128]{2,1,0:T(8,128)(2,1)} %bitcast_bitcast_fusion.2), calls=%async_computation.11 | async-start | bytes 524288 | tf_op jit(solution)/shard_map/all_to_all | solution.py:517
  951.4 13.5 %copy-start.20 = (bf16[1,128,2048]{2,1,0:T(8,128)(2,1)S(1)}, bf16[1,128,2048]{2,1,0:T(8,128)(2,1)}, u32[]{:S(2)}) copy-start(bf16[1,128,2048]{2,1,0:T(8,128)(2,1)} %param.16) | copy-start | bytes 1572868
  951.4 13.5 %copy-start.33 = (bf16[128,512]{1,0:T(8,128)(2,1)S(1)}, bf16[128,512]{1,0:T(8,128)(2,1)}, u32[]{:S(2)}) copy-start(bf16[128,512]{1,0:T(8,128)(2,1)} %copy.215) | copy-start | bytes 393220
  951.4 13.5 %copy-start.38 = (f32[2048]{0:T(1024)S(1)}, f32[2048]{0:T(1024)}, u32[]{:S(2)}) copy-start(f32[2048]{0:T(1024)} %param.19) | copy-start | bytes 24580
  951.4 13.5 %copy-start.45 = (f32[128]{0:T(128)S(1)}, f32[128]{0:T(128)}, u32[]{:S(2)}) copy-start(f32[128]{0:T(128)} %copy-done.44) | copy-start | bytes 1540
  971.3 37.1 %all-to-all-start.8 = ((f32[32,1,4352]{2,1,0:T(1,128)}), f32[32,1,4352]{2,1,0:T(1,128)}, u32[]{:S(2)}, u32[]{:S(2)}) async-start(f32[32,1,4352]{2,1,0:T(1,128)} %broadcast_in_dim.170), calls=%async_computation.10 | async-start | bytes 1114112 | tf_op jit(solution)/shard_map/all_to_all | solution.py:472
  980.8 32.7 %collective-permute-start.15 = (bf16[8,64,128]{2,1,0:T(8,128)(2,1)}, bf16[8,64,128]{2,1,0:T(8,128)(2,1)S(1)}, u32[]{:S(2)}, u32[]{:S(2)}) collective-permute-start(bf16[8,64,128]{2,1,0:T(8,128)(2,1)} %get-tuple-element.134), channel_id=1, source_target_pairs={{0,1},{1,2},{2,3},{3,0},{4,5},{5,6},{6,7},{7,4},{8,9},{9,10},{10,1... | collective-permute-start | bytes 393224 | tf_op jit(solution)/shard_map/ppermute | solution.py:532
  982.4 31.6 %collective-permute-start.16 = (bf16[8,64,128]{2,1,0:T(8,128)(2,1)}, bf16[8,64,128]{2,1,0:T(8,128)(2,1)S(1)}, u32[]{:S(2)}, u32[]{:S(2)}) collective-permute-start(bf16[8,64,128]{2,1,0:T(8,128)(2,1)} %get-tuple-element.133), channel_id=1, source_target_pairs={{0,2},{1,3},{2,0},{3,1},{4,6},{5,7},{6,4},{7,5},{8,10},{9,11},{10,... | collective-permute-start | bytes 393224 | tf_op jit(solution)/shard_map/ppermute | solution.py:532
  984.9 29.1 %collective-permute-start.17 = (bf16[8,64,128]{2,1,0:T(8,128)(2,1)}, bf16[8,64,128]{2,1,0:T(8,128)(2,1)}, u32[]{:S(2)}, u32[]{:S(2)}) collective-permute-start(bf16[8,64,128]{2,1,0:T(8,128)(2,1)} %get-tuple-element.132), channel_id=1, source_target_pairs={{0,3},{1,0},{2,1},{3,2},{4,7},{5,4},{6,5},{7,6},{8,11},{9,8},{10,9... | collective-permute-start | bytes 393224 | tf_op jit(solution)/shard_map/ppermute | solution.py:532
  1009.9 17.1 %collective-permute-start.18 = (bf16[128,2048]{1,0:T(8,128)(2,1)}, bf16[128,2048]{1,0:T(8,128)(2,1)}, u32[]{:S(2)}, u32[]{:S(2)}) collective-permute-start(bf16[128,2048]{1,0:T(8,128)(2,1)} %get-tuple-element.111), channel_id=1, source_target_pairs={{0,1},{1,2},{2,3},{3,0},{4,5},{5,6},{6,7},{7,4},{8,9},{9,10},{10,1... | collective-permute-start | bytes 1572872 | tf_op jit(solution)/shard_map/ppermute | solution.py:532
  1011.6 37.7 %collective-permute-start.19 = (bf16[128,2048]{1,0:T(8,128)(2,1)}, bf16[128,2048]{1,0:T(8,128)(2,1)}, u32[]{:S(2)}, u32[]{:S(2)}) collective-permute-start(bf16[128,2048]{1,0:T(8,128)(2,1)} %get-tuple-element.110), channel_id=1, source_target_pairs={{0,2},{1,3},{2,0},{3,1},{4,6},{5,7},{6,4},{7,5},{8,10},{9,11},{10,... | collective-permute-start | bytes 1572872 | tf_op jit(solution)/shard_map/ppermute | solution.py:532
  1013.5 35.8 %collective-permute-start.20 = (bf16[128,2048]{1,0:T(8,128)(2,1)}, bf16[128,2048]{1,0:T(8,128)(2,1)}, u32[]{:S(2)}, u32[]{:S(2)}) collective-permute-start(bf16[128,2048]{1,0:T(8,128)(2,1)} %get-tuple-element.109), channel_id=1, source_target_pairs={{0,3},{1,0},{2,1},{3,2},{4,7},{5,4},{6,5},{7,6},{8,11},{9,8},{10,9... | collective-permute-start | bytes 1572872 | tf_op jit(solution)/shard_map/ppermute | solution.py:532
  1017.7 34.5 %all-to-all-start.10 = ((bf16[8,64,640]{2,1,0:T(8,128)(2,1)}), bf16[8,64,640]{2,1,0:T(8,128)(2,1)}, u32[]{:S(2)}, u32[]{:S(2)}) async-start(bf16[8,64,640]{2,1,0:T(8,128)(2,1)} %pad_maximum_fusion.2), calls=%async_computation.13 | async-start | bytes 1310720 | tf_op jit(solution)/shard_map/all_to_all | solution.py:517
  (43 other events, 260.3 us)
Sparse Core Ops, SparseCore 0:
  10.8 53.1 all-gather.3
  205.8 136.5 all-gather.5
  538.5 51.6 reduce-scatter.6
  658.9 188.4 reduce-scatter.12
  850.5 41.8 reduce-scatter.8
  894.2 36.5 all-gather.7
  934.1 54.1 reduce-scatter.10

commit v8 on v7

--- a/solution.py
+++ b/solution.py
@@ -465,12 +465,15 @@
     )
 
 
-def sum_everywhere(vector):
-    devices = lax.axis_size("ctx") * lax.axis_size("wt")
-    spread = jnp.broadcast_to(vector[None, :], (devices, vector.shape[0]))
-    return jnp.sum(
-        lax.all_to_all(spread, ("ctx", "wt"), split_axis=0, concat_axis=0, tiled=True), axis=0
-    )
+def sum_everywhere(own_parts, vector):
+    devices = own_parts.shape[0]
+    sent = jnp.concatenate(
+        [own_parts, jnp.broadcast_to(vector[None, :], (devices, vector.shape[0]))], axis=1
+    )
+    sums = jnp.sum(
+        lax.all_to_all(sent, ("ctx", "wt"), split_axis=0, concat_axis=0, tiled=True), axis=0
+    )
+    return sums
 
 
 def on_device(
@@ -691,7 +694,11 @@
             table.reshape(wt_size * capacity, seq_len), jnp.concatenate(stream_rows, axis=0)
         ).astype(jnp.bfloat16)
 
-    in_rows_cot, mixed_columns = lax.optimization_barrier((in_rows_cot, mixed_columns))
+    gate_cot = exchange(gate_cot_mine.reshape(devices, tokens), by_stream)
+    in_rows_cot, mixed_columns, gate_cot = lax.optimization_barrier(
+        (in_rows_cot, mixed_columns, gate_cot)
+    )
+    gate_cot = from_owner_rows(gate_cot)
 
     stream_cots = turn(in_rows_cot[:, :half].reshape(blocks_shape))
     send_slot = jnp.where(
@@ -713,18 +720,15 @@
     )
     plane_cots = exchange(plane_sent, "ctx")
     first_part = scatter_sum(add_pairs(spread_low, stream_cots), "ctx")
-    gate_cot = from_owner_rows(
-        exchange(after(gate_cot_mine, plane_cots).reshape(devices, tokens), by_stream)
-    )
     line_low = (rank_lines[:, :, :, None] == send_ids).astype(jnp.bfloat16)
     line_sent = jnp.einsum(
         "sctj,csjd->std", line_low, plane_cots, preferred_element_type=jnp.float32
     ).astype(jnp.bfloat16)
     line_cots = turn(line_sent)
-    mixed_cuts = cut(after(mixed_rows[:, half:], line_sent).reshape(blocks_shape))
+    mixed_cuts = cut(after(mixed_rows[:, half:], line_cots).reshape(blocks_shape))
     stream_mixed_late = pass_on(mixed_cuts)
-    returned_cot = after(
-        jnp.concatenate([first_part.astype(jnp.float32), add_up(line_cots)], axis=1), mixed_cuts
+    returned_cot = jnp.concatenate(
+        [first_part.astype(jnp.float32), add_up(line_cots)], axis=1
     )
     out_cot = out_grad[0].astype(jnp.float32)
 
@@ -754,18 +758,14 @@
         key_rows,
     )
     query_columns = column_blocks(query_cot_low)
-    filled, hidden_h = after((filled, hidden_h), query_cot_low)
     normed_mid = after(normed_mid, query_columns)
-    grad_gate = contract_rows(filled, gate_cot_h)
-    grad_up = contract_rows(filled, up_cot_h)
-    grad_down = contract_rows(hidden_h, out_rows_cot)
-    grad_w_router = scatter_sum(contract_rows(normed_mid, logit_cot), both)
-    spread_late = after(spread_low, query_cot_low)
+    router_parts = contract_rows(normed_mid, logit_cot).reshape(devices, -1)
+    out_block = contract_rows(after(mixed_columns, query_cot_low), attn_cot_all)
+    spread_late = after(spread_low, out_block)
     mixed_partial = jnp.concatenate(
         [add_pairs(spread_late, part) for part in (stream_mixed, stream_mixed_late)], axis=1
     )
     mixed_mine = scatter_sum(mixed_partial, "ctx").astype(jnp.float32)
-    out_block = contract_rows(after(mixed_columns, query_cot_low), attn_cot_all)
     out_parts = turn(out_block.astype(jnp.bfloat16).reshape(wt_size, -1, model_width))
     pair_mine = scatter_sum(pair_cots, "ctx").reshape(tokens, key_heads, 2, head_dim)
     key_mine = pair_mine[:, :, 0].astype(jnp.float32)
@@ -785,13 +785,18 @@
         return turn(block), block
 
     query_parts, query_block = weight_parts(after(query_columns, (out_block, mixed_partial)))
+    filled, hidden_h = after((filled, hidden_h), query_block)
+    grad_gate = contract_rows(filled, gate_cot_h)
+    grad_up = contract_rows(filled, up_cot_h)
+    grad_down = contract_rows(hidden_h, out_rows_cot)
     pair_parts, pair_block = weight_parts(column_blocks(after(pair_cot_low, query_block)))
     in_cot = contract_cols(after(query_cot_low, query_block), query_full) + contract_cols(
         pair_cot_low, side_weights[:, : 2 * kv_width]
     )
     in_norm_cot, gain_attn_terms = norm_back(resid_in, gain_attn, in_cot)
     grad_in = resid_cot + in_norm_cot
-    gain_sums = sum_everywhere(
+    sums = sum_everywhere(
+        router_parts,
         jnp.concatenate(
             [
                 jnp.sum(gain_attn_terms, axis=0),
@@ -799,21 +804,22 @@
                 jnp.sum(gain_key_terms, axis=(0, 1)),
                 jnp.sum(gain_moe_terms, axis=0),
             ]
-        )
-    )
-    query_parts = after(query_parts, (pair_block, gain_sums))
+        ),
+    )
+    query_parts = after(query_parts, (pair_block, sums))
+    router_sums, gain_sums = sums[: router_parts.shape[1]], sums[router_parts.shape[1] :]
     grad_w_out = add_up(after(out_parts, query_parts))
     rows_mine = jnp.concatenate(
         [add_up(query_parts), add_up(after(pair_parts, query_parts))], axis=2
     ).astype(jnp.bfloat16)
     hidden_out = after(resid_mid, rows_mine) + mixed_mine
-    grad_w_router = after(grad_w_router, rows_mine)
     rows = exchange(rows_mine, "ctx").transpose(1, 0, 2).astype(jnp.float32)
     query_columns = q_width // ctx_size
     grad_w_query = rows[:, :, :query_columns].reshape(-1, q_width)
     grad_pair = rows[:, :, query_columns:].reshape(-1, 2 * kv_width)
     grad_w_key = grad_pair[:, :kv_width]
     grad_w_value = grad_pair[:, kv_width:]
+    grad_w_router = router_sums.reshape(w_router.shape)
     grad_gain_attn = gain_sums[:model_width]
     grad_gain_query = gain_sums[model_width : model_width + head_dim]
     grad_gain_key = gain_sums[model_width + head_dim : model_width + 2 * head_dim]

time: 1080 us -> 948 us (0.88)
  waiting for transfers between devices: 307 us -> 190 us
  blocking collectives: 18.5 us -> 0 us
  matrix products: 165 us -> 176 us
    unnamed x8 -> x6, waiting for transfers between devices: 83.3 us -> 0.62 us
    ppermute x21, waiting for transfers between devices: 112 us -> 89.9 us  [pass_on(): arrived.append(lax.ppermute(cuts[step], 'wt', pairs))]
    reduce_scatter x3, waiting for transfers between devices: 59.2 us -> 40.4 us  [scatter_sum(): return lax.psum_scatter(value, axes, scatter_dimension=0, tiled=True)]
    all_to_all x1 -> x0, blocking collectives: 18.5 us -> none  [exchange(): return lax.all_to_all(value, axes, split_axis=0, concat_axis=0, tiled=True)]
    all_to_all x9 -> x10, starting transfers between devices: 56.2 us -> 51.4 us  [exchange(): return lax.all_to_all(value, axes, split_axis=0, concat_axis=0, tiled=True)]
    dot_general x9 -> x10, matrix products: 43.5 us -> 47.5 us  [contract_rows(): lax.dot_general(left_side, right_side, (((0,), (0,)), ((), ())), preferre...]
  transfers between devices with their start and end apart: 38 -> 38, of which waited for: 12 -> 11; matrix products, arithmetic and copies ran while one was open for 22% -> 26% of each run, Pallas kernels for 30% -> 34%
where the time goes in v8:
time: 948 us; the launch traced here: 932 us
  Pallas kernels  348 us (37%)
  waiting for transfers between devices  190 us (20%)
  matrix products  176 us (19%)
  starting transfers between devices  94.1 us (10%)
  other arithmetic  59.9 us (6%)
  local copies, waits for them, and re-layouts  47.8 us (5%)
  between operations  15.9 us (2%)
    pallas_call x2, Pallas kernels, spread(): pl.pallas_call(functools.partial(spread_kernel, splits, streams_first), o...  303 us
    ppermute x21, waiting for transfers between devices, pass_on(): arrived.append(lax.ppermute(cuts[step], 'wt', pairs))  89.9 us
    dot_general x7, matrix products, contract_cols(): lax.dot_general(left_side, right_side, (((1,), (1,)), ((), ())), preferre...  55 us
    all_to_all x10, starting transfers between devices, exchange(): return lax.all_to_all(value, axes, split_axis=0, concat_axis=0, tiled=True)  51.4 us
    dot_general x10, matrix products, contract_rows(): lax.dot_general(left_side, right_side, (((0,), (0,)), ((), ())), preferre...  47.5 us
    dot_general x7, matrix products, matmul(): return jnp.dot(left_side, right_side, preferred_element_type=jnp.float32)  44.2 us
    reduce_scatter x3, waiting for transfers between devices, scatter_sum(): return lax.psum_scatter(value, axes, scatter_dimension=0, tiled=True)  40.4 us
    ppermute x21, starting transfers between devices, pass_on(): arrived.append(lax.ppermute(cuts[step], 'wt', pairs))  37.5 us
  transfers between devices with their start and end apart: 38, of which 11 were waited for; matrix products, arithmetic and copies ran while one was open for 26% of the time, Pallas kernels for 34%

profile of v8, /device:TPU:0, one launch (start us, length us, event | category | flops | bytes accessed | tf_op | source)
XLA Modules:
  0.0 932.5 jit_solution(14354145340701515454)
XLA Ops:
  13.1 192.6 %shard_map.263 = (bf16[8,4,64,1152]{3,2,1,0:T(8,128)(2,1)}, bf16[8,4,64,4096]{3,2,1,0:T(8,128)(2,1)}, bf16[8,4,128,2048]{3,2,1,0:T(8,128)(2,1)}) custom-call(bf16[64,1152]{1,0:T(8,128)(2,1)} %fusion.96.refs_0_, bf16[64,4096]{1,0:T(8,128)(2,1)} %refs_1_.1, bf16[128,2048]{1,0:T(8,128)(2,1)} %refs_2_.1), custom_call_target="tpu_custom_call" | custom-call | bytes 76546048 | tf_op jit(solution)/shard_map/pallas_call | solution.py:198
  207.2 3.3 all-to-all-start
  212.2 3.0 fusion.89
  216.8 9.8 %fusion.78.query_ref = f32[128,4096]{1,0:T(8,128)} fusion(bf16[2048,4096]{1,0:T(8,128)(2,1)} %bitcast.365, bf16[1,128,2048]{2,1,0:T(8,128)(2,1)} %param.16, f32[2048]{0:T(1024)S(1)} %copy-done.37, f32[128]{0:T(128)S(1)} %add_rsqrt_fusion.2), kind=kOutput, calls=%fused_computation.117 | convolution fusion | flops 2148532224 | bytes 19407360 | tf_op jit(solution)/shard_map/dot_general | solution.py:51
  230.4 3.9 all-to-all-start.1
  238.1 3.6 all-to-all-done.1
  241.7 4.1 all-to-all-start.3
  252.2 10.1 %fusion.10.key_ref.value_ref = f32[1024,1024]{1,0:T(8,128)} fusion(bf16[1024,2048]{1,0:T(8,128)(2,1)} %all-gather.4.cloned.1.call-done, bf16[2048,1152]{1,0:T(8,128)(2,1)} %bitcast.400), kind=kOutput, calls=%fused_computation.30 | convolution fusion | flops 4294967296 | bytes 12582912 | tf_op jit(solution)/shard_map/dot_general | solution.py:51
  262.4 16.4 %attend.1 = (bf16[128,4096]{1,0:T(8,128)(2,1)S(1)}, bf16[128,4096]{1,0:T(8,128)(2,1)S(1)}) custom-call(f32[128,4096]{1,0:T(8,128)S(1)} %copy-done.2, f32[1024,1024]{1,0:T(8,128)} %fusion.10.key_ref.value_ref, f32[1024,1024]{1,0:T(8,128)} %fusion.10.key_ref.value_ref, f32[1,128]{1,0:T(1,128)S(1)} %bitcast.362, f32[128,128]{1,0:T(8,128)S(1)} %get-tuple-element.233.cosine_ref, ...), custom_call_target="tpu_custom_call" | custom-call | flops 2147483648 | bytes 4194304 | tf_op jit(solution)/shard_map/attend/pallas_call | solution.py:365
  278.8 9.2 multiply_reduce_fusion.2
  290.0 110.0 %shard_map.264 = bf16[4,8,128,2048]{3,2,1,0:T(8,128)(2,1)} custom-call(bf16[128,2048]{1,0:T(8,128)(2,1)} %multiply_convert_fusion.3.refs_0_), custom_call_target="tpu_custom_call" | custom-call | bytes 33554432 | tf_op jit(solution)/shard_map/pallas_call | solution.py:198
  402.3 11.9 %all-to-all-start.2 = ((f32[32,1,128]{2,1,0:T(1,128)}), f32[32,1,128]{2,1,0:T(1,128)S(1)}, u32[]{:S(2)}, u32[]{:S(2)}) async-start(f32[32,1,128]{2,1,0:T(1,128)} %bitcast.29), calls=%async_computation.2 | async-start | bytes 32768 | tf_op jit(solution)/shard_map/all_to_all | solution.py:520
  414.2 11.1 %convolution_convert_fusion.1 = bf16[4,256,2048]{2,1,0:T(8,128)(2,1)S(1)} fusion(bf16[4,256,1024]{2,1,0:T(8,128)(2,1)} %fusion.6, bf16[4,1024,2048]{2,1,0:T(8,128)(2,1)} %bitcast.369), kind=kOutput, calls=%fused_computation.25 | convolution fusion | flops 4297064448 | bytes 23068672 | tf_op jit(solution)/shard_map/wkt,wtd->wkd/dot_general | solution.py:654
  425.3 3.4 fusion.14
  428.7 5.2 multiply_convert_fusion
  434.0 4.9 convolution_convert_fusion.3
  440.0 4.4 all-to-all-start.4
  445.7 14.2 %fusion = (f32[1024]{0:T(1024)S(1)}, bf16[4,256,2048]{2,1,0:T(8,128)(2,1)}) fusion(bf16[1024,2048]{1,0:T(8,128)(2,1)} %convolution_convert_fusion.3, bf16[4,256,1024]{2,1,0:T(8,128)(2,1)} %fusion.6, bf16[4,1024,2048]{2,1,0:T(8,128)(2,1)} %bitcast.368), kind=kOutput, calls=%fused_computation.3 | convolution fusion | flops 4305452032 | bytes 27267072 | tf_op jit(solution)/shard_map/wkt,wtd->wkd/dot_general | solution.py:654
  461.2 3.1 fusion.2
  465.3 5.8 multiply_convert_fusion.1
  471.8 9.2 fusion.12
  481.0 6.6 all-to-all-start.5
  487.6 7.8 add_convert_fusion
  495.4 4.0 fusion.113
  501.0 2.4 copy.250
  503.4 4.7 all-to-all-start.6
  511.1 3.7 collective-permute-start.2
  517.1 10.5 %collective-permute-done.2 = bf16[256,1024]{1,0:T(8,128)(2,1)S(1)} collective-permute-done((bf16[256,1024]{1,0:T(8,128)(2,1)}, bf16[256,1024]{1,0:T(8,128)(2,1)S(1)}, u32[]{:S(2)}, u32[]{:S(2)}) %collective-permute-start.2) | collective-permute-done | bytes 524320 | tf_op jit(solution)/shard_map/ppermute | solution.py:535
  527.6 32.9 %collective-permute-done.1 = bf16[256,1024]{1,0:T(8,128)(2,1)S(1)} collective-permute-done((bf16[256,1024]{1,0:T(8,128)(2,1)}, bf16[256,1024]{1,0:T(8,128)(2,1)S(1)}, u32[]{:S(2)}, u32[]{:S(2)}) %collective-permute-start.1) | collective-permute-done | bytes 524320 | tf_op jit(solution)/shard_map/ppermute | solution.py:535
  560.5 4.8 fusion.49
  567.0 3.0 bitcast_convert_fusion
  571.0 2.8 collective-permute-start.4
  576.2 31.0 %reduce-scatter.4.cloned.1.call-done = bf16[128,1024]{1,0:T(8,128)(2,1)} async-done(((bf16[1024,1024]{1,0:T(8,128)(2,1)}), bf16[128,1024]{1,0:T(8,128)(2,1)}) %reduce-scatter.4.cloned.1.call-update) | async-done | bytes 262160 | tf_op jit(solution)/shard_map/reduce_scatter | solution.py:523
  611.5 12.6 %convolution_convert_fusion.cot_ref = bf16[128,4096]{1,0:T(8,128)(2,1)} fusion(bf16[128,2048]{1,0:T(8,128)(2,1)S(1)} %fusion.109, bf16[4096,2048]{1,0:T(8,128)(2,1)} %bitcast.364), kind=kOutput, calls=%fused_computation.10 | convolution fusion | flops 2148007936 | bytes 18350080 | tf_op jit(solution)/shard_map/dot_general | solution.py:61
  624.9 29.5 %attend_back.1 = (bf16[128,4096]{1,0:T(8,128)(2,1)}, bf16[1024,1024]{1,0:T(8,128)(2,1)}, f32[32,128]{1,0:T(8,128)}) custom-call(f32[128,4096]{1,0:T(8,128)} %fusion.78.query_ref, bf16[128,4096]{1,0:T(8,128)(2,1)} %copy-done.15, bf16[128,4096]{1,0:T(8,128)(2,1)} %convolution_convert_fusion.cot_ref, f32[1024,1024]{1,0:T(8,128)} %fusion.10.key_ref.value_ref, ...), custom_call_target="tpu_custom_call" | custom-call | flops 5368709120 | bytes 6291456 | tf_op jit(solution)/shard_map/attend_back/pallas_call | solution.py:413
  662.1 4.4 all-to-all-start.7
  666.6 6.4 fusion.3
  674.9 3.3 collective-permute-start.8
  687.2 2.4 reshape.515
  689.6 9.5 %reduce-scatter.6.cloned.1.call-done = bf16[128,1024]{1,0:T(8,128)(2,1)} async-done(((bf16[1024,1024]{1,0:T(8,128)(2,1)}), bf16[128,1024]{1,0:T(8,128)(2,1)}) %reduce-scatter.6.cloned.1.call-update) | async-done | bytes 262160 | tf_op jit(solution)/shard_map/reduce_scatter | solution.py:523
  705.0 32.4 %all-gather.8.cloned.1.call-done = bf16[1024,2048]{1,0:T(8,128)(2,1)} async-done(((bf16[128,2048]{1,0:T(8,128)(2,1)}), bf16[1024,2048]{1,0:T(8,128)(2,1)}) %all-gather.8.cloned.1.call-update) | async-done | bytes 4194320 | tf_op jit(solution)/shard_map/all_gather | solution.py:517
  737.4 6.4 fusion.118
  743.8 4.1 collective-permute-start.6
  747.9 21.1 %collective-permute-done.10 = bf16[256,1024]{1,0:T(8,128)(2,1)} collective-permute-done((bf16[256,1024]{1,0:T(8,128)(2,1)}, bf16[256,1024]{1,0:T(8,128)(2,1)}, u32[]{:S(2)}, u32[]{:S(2)}) %collective-permute-start.10) | collective-permute-done | bytes 524320 | tf_op jit(solution)/shard_map/ppermute | solution.py:535
  769.0 3.8 fusion.52
  772.8 3.6 fusion.55
  776.4 2.4 pad_maximum_fusion
  778.9 6.3 convolution_convert_fusion.4
  785.2 5.5 convolution_bitcast_fusion.2
  790.7 5.5 convolution_bitcast_fusion.1
  797.0 3.8 all-to-all-start.9
  800.8 2.9 dynamic-slice_bitcast_fusion.4
  803.7 4.1 collective-permute-start.14
  807.8 12.8 %fusion.120 = f32[128,2048]{1,0:T(8,128)} fusion(bf16[128,4096]{1,0:T(8,128)(2,1)} %get-tuple-element.65, bf16[2048,4096]{1,0:T(8,128)(2,1)} %bitcast.366), kind=kOutput, calls=%fused_computation.260 | convolution fusion | flops 2147483648 | bytes 18874368 | tf_op jit(solution)/shard_map/dot_general | solution.py:61
  820.7 5.2 fusion.68
  827.4 5.0 all-to-all-start.8
  832.5 8.9 convolution_bitcast_fusion
  847.9 2.4 collective-permute-start.16
  853.2 22.0 %all-to-all-done.8 = f32[32,1,6400]{2,1,0:T(1,128)} async-done(((f32[32,1,6400]{2,1,0:T(1,128)}), f32[32,1,6400]{2,1,0:T(1,128)}, u32[]{:S(2)}, u32[]{:S(2)}) %all-to-all-start.8) | async-done | bytes 819232 | tf_op jit(solution)/shard_map/all_to_all | solution.py:474
  876.8 2.8 collective-permute-start.18
  879.6 2.4 collective-permute-start.20
  885.6 4.2 all-to-all-start.10
  892.6 23.7 %collective-permute-done.19 = bf16[128,2048]{1,0:T(8,128)(2,1)S(1)} collective-permute-done((bf16[128,2048]{1,0:T(8,128)(2,1)}, bf16[128,2048]{1,0:T(8,128)(2,1)S(1)}, u32[]{:S(2)}, u32[]{:S(2)}) %collective-permute-start.19) | collective-permute-done | bytes 524320 | tf_op jit(solution)/shard_map/ppermute | solution.py:535
  922.7 2.4 add_bitcast_fusion
  (331 shorter events, 101.2 us)
Async XLA Ops:
  7.2 426.8 %copy-start = (bf16[1,768,2048]{2,1,0:T(8,128)(2,1)S(1)}, bf16[1,768,2048]{2,1,0:T(8,128)(2,1)}, u32[]{:S(2)}) copy-start(bf16[1,768,2048]{2,1,0:T(8,128)(2,1)} %param.30) | copy-start | bytes 9437188
  7.2 209.6 %copy-start.37 = (f32[2048]{0:T(1024)S(1)}, f32[2048]{0:T(1024)}, u32[]{:S(2)}) copy-start(f32[2048]{0:T(1024)} %param.19) | copy-start | bytes 24580
  7.2 203.3 %copy-start.59 = (s32[1,2]{1,0:T(1,128)S(1)}, s32[1,2]{1,0:T(1,128)}, u32[]{:S(2)}) copy-start(s32[1,2]{1,0:T(1,128)} %param.17) | copy-start | bytes 28
  7.2 244.9 %all-gather.4.cloned.1.call-start = ((), (), s32[]{:S(2)}) async-start(), calls=%async_computation.14 | async-start | bytes 4718592 | tf_op jit(solution)/shard_map/all_gather | solution.py:517
  8.7 218.0 %copy-start.44 = (f32[128]{0:T(128)}, f32[128]{0:T(128)S(1)}, u32[]{:S(2)}) copy-start(f32[128]{0:T(128)S(1)} %add_rsqrt_fusion.2) | copy-start | bytes 1540
  10.7 434.9 %all-gather.6.cloned.1.call-start = ((), (), s32[]{:S(2)}) async-start(), calls=%async_computation.15 | async-start | bytes 17301504 | tf_op jit(solution)/shard_map/all_gather | solution.py:517
  207.2 23.2 %all-to-all-start = ((s32[8,5,128]{2,1,0:T(8,128)}), s32[8,5,128]{2,1,0:T(8,128)S(1)}, u32[]{:S(2)}, u32[]{:S(2)}) async-start(s32[8,5,128]{2,1,0:T(8,128)} %pad_add_fusion), calls=%async_computation | async-start | bytes 65536 | tf_op jit(solution)/shard_map/all_to_all | solution.py:520
  216.8 45.5 %copy-start.9 = (f32[128,128]{1,0:T(8,128)}, f32[128,128]{1,0:T(8,128)S(1)}, u32[]{:S(2)}) copy-start(f32[128,128]{1,0:T(8,128)S(1)} %get-tuple-element.233.cosine_ref) | copy-start | bytes 196612
  216.8 45.5 %copy-start.11 = (f32[128,128]{1,0:T(8,128)}, f32[128,128]{1,0:T(8,128)S(1)}, u32[]{:S(2)}) copy-start(f32[128,128]{1,0:T(8,128)S(1)} %get-tuple-element.232.sine_ref) | copy-start | bytes 196612
  230.3 31.9 %copy-start.40 = (s32[8,5,128]{2,1,0:T(8,128)}, s32[8,5,128]{2,1,0:T(8,128)S(1)}, u32[]{:S(2)}) copy-start(s32[8,5,128]{2,1,0:T(8,128)S(1)} %all-to-all-done) | copy-start | bytes 61444
  230.4 11.3 %all-to-all-start.1 = ((s32[32,1,128]{2,1,0:T(1,128)}), s32[32,1,128]{2,1,0:T(1,128)S(1)}, u32[]{:S(2)}, u32[]{:S(2)}) async-start(s32[32,1,128]{2,1,0:T(1,128)} %bitcast.409), calls=%async_computation.1 | async-start | bytes 32768 | tf_op jit(solution)/shard_map/all_to_all | solution.py:520
  235.1 13.7 %copy-start.48 = (s32[32]{0:T(128)}, s32[32]{0:T(128)S(1)}, u32[]{:S(2)}) copy-start(s32[32]{0:T(128)S(1)} %select_reduce_fusion.2) | copy-start | bytes 388
  241.7 10.4 %all-to-all-start.3 = ((s32[4,8,128]{2,1,0:T(8,128)}), s32[4,8,128]{2,1,0:T(8,128)}, u32[]{:S(2)}, u32[]{:S(2)}) async-start(s32[4,8,128]{2,1,0:T(8,128)} %copy.176), calls=%async_computation.3 | async-start | bytes 32768 | tf_op jit(solution)/shard_map/all_to_all | solution.py:520
  262.3 16.4 %copy-start.18 = (bf16[1,128,2048]{2,1,0:T(8,128)(2,1)S(1)}, bf16[1,128,2048]{2,1,0:T(8,128)(2,1)}, u32[]{:S(2)}) copy-start(bf16[1,128,2048]{2,1,0:T(8,128)(2,1)} %param.16) | copy-start | bytes 1572868
  288.0 323.0 %copy-start.46 = (f32[128]{0:T(128)}, f32[128]{0:T(128)S(1)}, u32[]{:S(2)}) copy-start(f32[128]{0:T(128)S(1)} %add_rsqrt_fusion.1) | copy-start | bytes 1540
  290.0 111.6 %copy-start.42 = (s32[128,32]{0,1:T(8,128)S(1)}, s32[128,32]{0,1:T(8,128)}, u32[]{:S(2)}) copy-start(s32[128,32]{0,1:T(8,128)} %copy.172) | copy-start | bytes 49156
  290.0 111.6 %copy-start.49 = (s32[32]{0:T(128)S(1)}, s32[32]{0:T(128)}, u32[]{:S(2)}) copy-start(s32[32]{0:T(128)} %copy-done.48) | copy-start | bytes 388
  402.3 37.7 %all-to-all-start.2 = ((f32[32,1,128]{2,1,0:T(1,128)}), f32[32,1,128]{2,1,0:T(1,128)S(1)}, u32[]{:S(2)}, u32[]{:S(2)}) async-start(f32[32,1,128]{2,1,0:T(1,128)} %bitcast.29), calls=%async_computation.2 | async-start | bytes 32768 | tf_op jit(solution)/shard_map/all_to_all | solution.py:520
  440.0 41.0 %all-to-all-start.4 = ((bf16[8,128,512]{2,1,0:T(8,128)(2,1)}), bf16[8,128,512]{2,1,0:T(8,128)(2,1)}, u32[]{:S(2)}, u32[]{:S(2)}) async-start(bf16[8,128,512]{2,1,0:T(8,128)(2,1)} %bitcast.378), calls=%async_computation.4 | async-start | bytes 2097152 | tf_op jit(solution)/shard_map/all_to_all | solution.py:520
  471.8 15.9 %copy-start.58 = (bf16[1,2048,768]{2,1,0:T(8,128)(2,1)S(1)}, bf16[1,2048,768]{2,1,0:T(8,128)(2,1)}, u32[]{:S(2)}) copy-start(bf16[1,2048,768]{2,1,0:T(8,128)(2,1)} %param.29) | copy-start | bytes 9437188
  481.0 14.4 %all-to-all-start.5 = ((f32[32,1,128]{2,1,0:T(1,128)}), f32[32,1,128]{2,1,0:T(1,128)S(1)}, u32[]{:S(2)}, u32[]{:S(2)}) async-start(f32[32,1,128]{2,1,0:T(1,128)} %all_to_all.54), calls=%async_computation.5 | async-start | bytes 32768 | tf_op jit(solution)/shard_map/all_to_all | solution.py:520
  503.4 63.6 %all-to-all-start.6 = ((bf16[8,4,64,1024]{3,2,1,0:T(8,128)(2,1)}), bf16[8,4,64,1024]{3,2,1,0:T(8,128)(2,1)}, u32[]{:S(2)}, u32[]{:S(2)}) async-start(bf16[8,4,64,1024]{3,2,1,0:T(8,128)(2,1)} %bitcast.370), calls=%async_computation.7 | async-start | bytes 8388608 | tf_op jit(solution)/shard_map/all_to_all | solution.py:520
  508.1 99.1 %reduce-scatter.4.cloned.1.call-start = ((), (), s32[]{:S(2)}) async-start(), calls=%async_computation.16 | async-start | bytes 2359296 | tf_op jit(solution)/shard_map/reduce_scatter | solution.py:523
  511.1 16.5 %collective-permute-start.2 = (bf16[256,1024]{1,0:T(8,128)(2,1)}, bf16[256,1024]{1,0:T(8,128)(2,1)S(1)}, u32[]{:S(2)}, u32[]{:S(2)}) collective-permute-start(bf16[256,1024]{1,0:T(8,128)(2,1)} %get-tuple-element.194), channel_id=1, source_target_pairs={{0,3},{1,0},{2,1},{3,2},{4,7},{5,4},{6,5},{7,6},{8,11},{9,8},{10,9... | collective-permute-start | bytes 1572872 | tf_op jit(solution)/shard_map/ppermute | solution.py:535
  514.9 45.7 %collective-permute-start.1 = (bf16[256,1024]{1,0:T(8,128)(2,1)}, bf16[256,1024]{1,0:T(8,128)(2,1)S(1)}, u32[]{:S(2)}, u32[]{:S(2)}) collective-permute-start(bf16[256,1024]{1,0:T(8,128)(2,1)} %get-tuple-element.195), channel_id=1, source_target_pairs={{0,2},{1,3},{2,0},{3,1},{4,6},{5,7},{6,4},{7,5},{8,10},{9,11},{10,... | collective-permute-start | bytes 1572872 | tf_op jit(solution)/shard_map/ppermute | solution.py:535
  514.9 45.7 %collective-permute-start = (bf16[256,1024]{1,0:T(8,128)(2,1)S(1)}, bf16[256,1024]{1,0:T(8,128)(2,1)}, u32[]{:S(2)}, u32[]{:S(2)}) collective-permute-start(bf16[256,1024]{1,0:T(8,128)(2,1)S(1)} %get-tuple-element.196), channel_id=1, source_target_pairs={{0,1},{1,2},{2,3},{3,0},{4,5},{5,6},{6,7},{7,4},{8,9},{9,10},{10,1... | collective-permute-start | bytes 1572872 | tf_op jit(solution)/shard_map/ppermute | solution.py:535
  565.3 133.7 %reduce-scatter.6.cloned.1.call-start = ((), (), s32[]{:S(2)}) async-start(), calls=%async_computation.18 | async-start | bytes 2359296 | tf_op jit(solution)/shard_map/reduce_scatter | solution.py:523
  570.0 39.5 %copy-start.17 = (f32[128,2048]{1,0:T(8,128)S(1)}, f32[128,2048]{1,0:T(8,128)}, u32[]{:S(2)}) copy-start(f32[128,2048]{1,0:T(8,128)} %copy-done.16) | copy-start | bytes 3145732
  570.0 41.1 %copy-start.22 = (bf16[1,128,2048]{2,1,0:T(8,128)(2,1)S(1)}, bf16[1,128,2048]{2,1,0:T(8,128)(2,1)}, u32[]{:S(2)}) copy-start(bf16[1,128,2048]{2,1,0:T(8,128)(2,1)} %param.31) | copy-start | bytes 1572868
  571.0 37.2 %collective-permute-start.5 = (bf16[128,1024]{1,0:T(8,128)(2,1)}, bf16[128,1024]{1,0:T(8,128)(2,1)}, u32[]{:S(2)}, u32[]{:S(2)}) collective-permute-start(bf16[128,1024]{1,0:T(8,128)(2,1)} %get-tuple-element.198), channel_id=1, source_target_pairs={{0,3},{1,0},{2,1},{3,2},{4,7},{5,4},{6,5},{7,6},{8,11},{9,8},{10,9... | collective-permute-start | bytes 786440 | tf_op jit(solution)/shard_map/ppermute | solution.py:535
  571.0 37.2 %collective-permute-start.4 = (bf16[128,1024]{1,0:T(8,128)(2,1)}, bf16[128,1024]{1,0:T(8,128)(2,1)}, u32[]{:S(2)}, u32[]{:S(2)}) collective-permute-start(bf16[128,1024]{1,0:T(8,128)(2,1)} %get-tuple-element.199), channel_id=1, source_target_pairs={{0,2},{1,3},{2,0},{3,1},{4,6},{5,7},{6,4},{7,5},{8,10},{9,11},{10,... | collective-permute-start | bytes 786440 | tf_op jit(solution)/shard_map/ppermute | solution.py:535
  573.8 34.4 %collective-permute-start.3 = (bf16[128,1024]{1,0:T(8,128)(2,1)}, bf16[128,1024]{1,0:T(8,128)(2,1)}, u32[]{:S(2)}, u32[]{:S(2)}) collective-permute-start(bf16[128,1024]{1,0:T(8,128)(2,1)} %get-tuple-element.197), channel_id=1, source_target_pairs={{0,1},{1,2},{2,3},{3,0},{4,5},{5,6},{6,7},{7,4},{8,9},{9,10},{10,1... | collective-permute-start | bytes 786440 | tf_op jit(solution)/shard_map/ppermute | solution.py:535
  611.1 12.9 %copy-start.50 = (f32[128]{0:T(128)}, f32[128]{0:T(128)S(1)}, u32[]{:S(2)}) copy-start(f32[128]{0:T(128)S(1)} %broadcast_multiply_fusion.3) | copy-start | bytes 1540
  611.4 12.6 %copy-start.24 = (bf16[128,2048]{1,0:T(8,128)(2,1)}, bf16[128,2048]{1,0:T(8,128)(2,1)S(1)}, u32[]{:S(2)}) copy-start(bf16[128,2048]{1,0:T(8,128)(2,1)S(1)} %fusion.109) | copy-start | bytes 1572868
  624.9 31.6 %copy-start.13 = (f32[128]{0:T(128)S(1)}, f32[128]{0:T(128)}, u32[]{:S(2)}) copy-start(f32[128]{0:T(128)} %param.24) | copy-start | bytes 1540
  654.3 83.1 %all-gather.8.cloned.1.call-start = ((), (), s32[]{:S(2)}) async-start(), calls=%async_computation.17 | async-start | bytes 4718592 | tf_op jit(solution)/shard_map/all_gather | solution.py:517
  662.1 23.8 %all-to-all-start.7 = ((bf16[8,128,512]{2,1,0:T(8,128)(2,1)}), bf16[8,128,512]{2,1,0:T(8,128)(2,1)}, u32[]{:S(2)}, u32[]{:S(2)}) async-start(bf16[8,128,512]{2,1,0:T(8,128)(2,1)} %bitcast.377), calls=%async_computation.8 | async-start | bytes 2097152 | tf_op jit(solution)/shard_map/all_to_all | solution.py:520
  666.5 256.1 %reduce-scatter.8.cloned.1.call-start = ((), (), s32[]{:S(2)}) async-start(), calls=%async_computation.19 | async-start | bytes 4718592 | tf_op jit(solution)/shard_map/reduce_scatter | solution.py:523
  674.9 97.9 %collective-permute-start.8 = (bf16[256,1024]{1,0:T(8,128)(2,1)}, bf16[256,1024]{1,0:T(8,128)(2,1)}, u32[]{:S(2)}, u32[]{:S(2)}) collective-permute-start(bf16[256,1024]{1,0:T(8,128)(2,1)} %get-tuple-element.186), channel_id=1, source_target_pairs={{0,3},{1,0},{2,1},{3,2},{4,7},{5,4},{6,5},{7,6},{8,11},{9,8},{10,9... | collective-permute-start | bytes 1572872 | tf_op jit(solution)/shard_map/ppermute | solution.py:535
  678.3 94.6 %collective-permute-start.7 = (bf16[256,1024]{1,0:T(8,128)(2,1)}, bf16[256,1024]{1,0:T(8,128)(2,1)}, u32[]{:S(2)}, u32[]{:S(2)}) collective-permute-start(bf16[256,1024]{1,0:T(8,128)(2,1)} %get-tuple-element.187), channel_id=1, source_target_pairs={{0,2},{1,3},{2,0},{3,1},{4,6},{5,7},{6,4},{7,5},{8,10},{9,11},{10,... | collective-permute-start | bytes 1572872 | tf_op jit(solution)/shard_map/ppermute | solution.py:535
  679.6 22.9 %copy-start.10 = (f32[128,128]{1,0:T(8,128)S(1)}, f32[128,128]{1,0:T(8,128)}, u32[]{:S(2)}) copy-start(f32[128,128]{1,0:T(8,128)} %copy-done.9) | copy-start | bytes 196612
  679.6 22.9 %copy-start.36 = (f32[128,128]{1,0:T(8,128)S(1)}, f32[128,128]{1,0:T(8,128)}, u32[]{:S(2)}) copy-start(f32[128,128]{1,0:T(8,128)} %dynamic-slice_negate_fusion) | copy-start | bytes 196612
  679.6 64.2 %collective-permute-start.11 = (bf16[256,1024]{1,0:T(8,128)(2,1)}, bf16[256,1024]{1,0:T(8,128)(2,1)}, u32[]{:S(2)}, u32[]{:S(2)}) collective-permute-start(bf16[256,1024]{1,0:T(8,128)(2,1)} %get-tuple-element.190), channel_id=1, source_target_pairs={{0,3},{1,0},{2,1},{3,2},{4,7},{5,4},{6,5},{7,6},{8,11},{9,8},{10,9... | collective-permute-start | bytes 1572872 | tf_op jit(solution)/shard_map/ppermute | solution.py:535
  680.6 88.3 %collective-permute-start.10 = (bf16[256,1024]{1,0:T(8,128)(2,1)}, bf16[256,1024]{1,0:T(8,128)(2,1)}, u32[]{:S(2)}, u32[]{:S(2)}) collective-permute-start(bf16[256,1024]{1,0:T(8,128)(2,1)} %get-tuple-element.191), channel_id=1, source_target_pairs={{0,2},{1,3},{2,0},{3,1},{4,6},{5,7},{6,4},{7,5},{8,10},{9,11},{10,... | collective-permute-start | bytes 1572872 | tf_op jit(solution)/shard_map/ppermute | solution.py:535
  682.6 86.4 %collective-permute-start.9 = (bf16[256,1024]{1,0:T(8,128)(2,1)}, bf16[256,1024]{1,0:T(8,128)(2,1)}, u32[]{:S(2)}, u32[]{:S(2)}) collective-permute-start(bf16[256,1024]{1,0:T(8,128)(2,1)} %get-tuple-element.192), channel_id=1, source_target_pairs={{0,1},{1,2},{2,3},{3,0},{4,5},{5,6},{6,7},{7,4},{8,9},{9,10},{10,1... | collective-permute-start | bytes 1572872 | tf_op jit(solution)/shard_map/ppermute | solution.py:535
  737.4 31.5 %copy-start.25 = (bf16[4,256,1024]{2,1,0:T(8,128)(2,1)S(1)}, bf16[4,256,1024]{2,1,0:T(8,128)(2,1)}, u32[]{:S(2)}) copy-start(bf16[4,256,1024]{2,1,0:T(8,128)(2,1)} %fusion.7) | copy-start | bytes 6291460
  737.4 31.5 %copy-start.33 = (bf16[256,1024]{1,0:T(8,128)(2,1)S(1)}, bf16[256,1024]{1,0:T(8,128)(2,1)}, u32[]{:S(2)}) copy-start(bf16[256,1024]{1,0:T(8,128)(2,1)} %get-tuple-element.189) | copy-start | bytes 1572868
  743.8 29.0 %collective-permute-start.6 = (bf16[256,1024]{1,0:T(8,128)(2,1)}, bf16[256,1024]{1,0:T(8,128)(2,1)S(1)}, u32[]{:S(2)}, u32[]{:S(2)}) collective-permute-start(bf16[256,1024]{1,0:T(8,128)(2,1)} %get-tuple-element.188), channel_id=1, source_target_pairs={{0,1},{1,2},{2,3},{3,0},{4,5},{5,6},{6,7},{7,4},{8,9},{9,10},{10,1... | collective-permute-start | bytes 1572872 | tf_op jit(solution)/shard_map/ppermute | solution.py:535
  797.0 30.5 %all-to-all-start.9 = ((bf16[8,128,128]{2,1,0:T(8,128)(2,1)}), bf16[8,128,128]{2,1,0:T(8,128)(2,1)S(1)}, u32[]{:S(2)}, u32[]{:S(2)}) async-start(bf16[8,128,128]{2,1,0:T(8,128)(2,1)} %bitcast_bitcast_fusion.2), calls=%async_computation.11 | async-start | bytes 524288 | tf_op jit(solution)/shard_map/all_to_all | solution.py:520
  803.7 46.6 %collective-permute-start.12 = (bf16[8,64,512]{2,1,0:T(8,128)(2,1)}, bf16[8,64,512]{2,1,0:T(8,128)(2,1)}, u32[]{:S(2)}, u32[]{:S(2)}) collective-permute-start(bf16[8,64,512]{2,1,0:T(8,128)(2,1)} %get-tuple-element.183), channel_id=1, source_target_pairs={{0,1},{1,2},{2,3},{3,0},{4,5},{5,6},{6,7},{7,4},{8,9},{9,10},{10,1... | collective-permute-start | bytes 1572872 | tf_op jit(solution)/shard_map/ppermute | solution.py:535
  803.7 73.1 %collective-permute-start.13 = (bf16[8,64,512]{2,1,0:T(8,128)(2,1)}, bf16[8,64,512]{2,1,0:T(8,128)(2,1)}, u32[]{:S(2)}, u32[]{:S(2)}) collective-permute-start(bf16[8,64,512]{2,1,0:T(8,128)(2,1)} %get-tuple-element.182), channel_id=1, source_target_pairs={{0,2},{1,3},{2,0},{3,1},{4,6},{5,7},{6,4},{7,5},{8,10},{9,11},{10,... | collective-permute-start | bytes 1572872 | tf_op jit(solution)/shard_map/ppermute | solution.py:535
  803.7 17.0 %copy-start.19 = (bf16[1,128,2048]{2,1,0:T(8,128)(2,1)S(1)}, bf16[1,128,2048]{2,1,0:T(8,128)(2,1)}, u32[]{:S(2)}) copy-start(bf16[1,128,2048]{2,1,0:T(8,128)(2,1)} %param.16) | copy-start | bytes 1572868
  803.7 16.9 %copy-start.38 = (f32[2048]{0:T(1024)S(1)}, f32[2048]{0:T(1024)}, u32[]{:S(2)}) copy-start(f32[2048]{0:T(1024)} %param.19) | copy-start | bytes 24580
  803.7 16.9 %copy-start.45 = (f32[128]{0:T(128)S(1)}, f32[128]{0:T(128)}, u32[]{:S(2)}) copy-start(f32[128]{0:T(128)} %copy-done.44) | copy-start | bytes 1540
  803.7 75.8 %collective-permute-start.14 = (bf16[8,64,512]{2,1,0:T(8,128)(2,1)}, bf16[8,64,512]{2,1,0:T(8,128)(2,1)}, u32[]{:S(2)}, u32[]{:S(2)}) collective-permute-start(bf16[8,64,512]{2,1,0:T(8,128)(2,1)} %get-tuple-element.181), channel_id=1, source_target_pairs={{0,3},{1,0},{2,1},{3,2},{4,7},{5,4},{6,5},{7,6},{8,11},{9,8},{10,9... | collective-permute-start | bytes 1572872 | tf_op jit(solution)/shard_map/ppermute | solution.py:535
  827.4 47.8 %all-to-all-start.8 = ((f32[32,1,6400]{2,1,0:T(1,128)}), f32[32,1,6400]{2,1,0:T(1,128)}, u32[]{:S(2)}, u32[]{:S(2)}) async-start(f32[32,1,6400]{2,1,0:T(1,128)} %all_to_all.59), calls=%async_computation.10 | async-start | bytes 1638400 | tf_op jit(solution)/shard_map/all_to_all | solution.py:474
  845.4 37.6 %copy-start.27 = (bf16[8,64,512]{2,1,0:T(8,128)(2,1)S(1)}, bf16[8,64,512]{2,1,0:T(8,128)(2,1)}, u32[]{:S(2)}) copy-start(bf16[8,64,512]{2,1,0:T(8,128)(2,1)} %get-tuple-element.68) | copy-start | bytes 1572868
  846.2 33.4 %collective-permute-start.15 = (bf16[8,64,128]{2,1,0:T(8,128)(2,1)}, bf16[8,64,128]{2,1,0:T(8,128)(2,1)S(1)}, u32[]{:S(2)}, u32[]{:S(2)}) collective-permute-start(bf16[8,64,128]{2,1,0:T(8,128)(2,1)} %get-tuple-element.202), channel_id=1, source_target_pairs={{0,1},{1,2},{2,3},{3,0},{4,5},{5,6},{6,7},{7,4},{8,9},{9,10},{10,1... | collective-permute-start | bytes 393224 | tf_op jit(solution)/shard_map/ppermute | solution.py:535
  847.9 34.1 %collective-permute-start.16 = (bf16[8,64,128]{2,1,0:T(8,128)(2,1)}, bf16[8,64,128]{2,1,0:T(8,128)(2,1)S(1)}, u32[]{:S(2)}, u32[]{:S(2)}) collective-permute-start(bf16[8,64,128]{2,1,0:T(8,128)(2,1)} %get-tuple-element.201), channel_id=1, source_target_pairs={{0,2},{1,3},{2,0},{3,1},{4,6},{5,7},{6,4},{7,5},{8,10},{9,11},{10,... | collective-permute-start | bytes 393224 | tf_op jit(solution)/shard_map/ppermute | solution.py:535
  850.3 31.7 %collective-permute-start.17 = (bf16[8,64,128]{2,1,0:T(8,128)(2,1)}, bf16[8,64,128]{2,1,0:T(8,128)(2,1)}, u32[]{:S(2)}, u32[]{:S(2)}) collective-permute-start(bf16[8,64,128]{2,1,0:T(8,128)(2,1)} %get-tuple-element.200), channel_id=1, source_target_pairs={{0,3},{1,0},{2,1},{3,2},{4,7},{5,4},{6,5},{7,6},{8,11},{9,8},{10,9... | collective-permute-start | bytes 393224 | tf_op jit(solution)/shard_map/ppermute | solution.py:535
  876.8 15.8 %collective-permute-start.18 = (bf16[128,2048]{1,0:T(8,128)(2,1)}, bf16[128,2048]{1,0:T(8,128)(2,1)S(1)}, u32[]{:S(2)}, u32[]{:S(2)}) collective-permute-start(bf16[128,2048]{1,0:T(8,128)(2,1)} %get-tuple-element.179), channel_id=1, source_target_pairs={{0,1},{1,2},{2,3},{3,0},{4,5},{5,6},{6,7},{7,4},{8,9},{9,10},{10,1... | collective-permute-start | bytes 1572872 | tf_op jit(solution)/shard_map/ppermute | solution.py:535
  879.6 36.7 %collective-permute-start.19 = (bf16[128,2048]{1,0:T(8,128)(2,1)}, bf16[128,2048]{1,0:T(8,128)(2,1)S(1)}, u32[]{:S(2)}, u32[]{:S(2)}) collective-permute-start(bf16[128,2048]{1,0:T(8,128)(2,1)} %get-tuple-element.178), channel_id=1, source_target_pairs={{0,2},{1,3},{2,0},{3,1},{4,6},{5,7},{6,4},{7,5},{8,10},{9,11},{10,... | collective-permute-start | bytes 1572872 | tf_op jit(solution)/shard_map/ppermute | solution.py:535
  879.6 36.7 %collective-permute-start.20 = (bf16[128,2048]{1,0:T(8,128)(2,1)}, bf16[128,2048]{1,0:T(8,128)(2,1)}, u32[]{:S(2)}, u32[]{:S(2)}) collective-permute-start(bf16[128,2048]{1,0:T(8,128)(2,1)} %get-tuple-element.177), channel_id=1, source_target_pairs={{0,3},{1,0},{2,1},{3,2},{4,7},{5,4},{6,5},{7,6},{8,11},{9,8},{10,9... | collective-permute-start | bytes 1572872 | tf_op jit(solution)/shard_map/ppermute | solution.py:535
  885.6 33.8 %all-to-all-start.10 = ((bf16[8,64,640]{2,1,0:T(8,128)(2,1)}), bf16[8,64,640]{2,1,0:T(8,128)(2,1)}, u32[]{:S(2)}, u32[]{:S(2)}) async-start(bf16[8,64,640]{2,1,0:T(8,128)(2,1)} %pad_maximum_fusion.2), calls=%async_computation.13 | async-start | bytes 1310720 | tf_op jit(solution)/shard_map/all_to_all | solution.py:520
  (41 other events, 263.4 us)
Sparse Core Ops, SparseCore 0:
  10.8 53.1 all-gather.3
  205.8 136.3 all-gather.5
  565.5 41.6 reduce-scatter.3
  654.5 44.5 reduce-scatter.5
  700.8 36.5 all-gather.7
  779.0 50.9 reduce-scatter.7
